TPU v7x, 128 devices: a whole 4x4x4 slice. The times are simulated.
128 devices in a mesh: tm: 16 (over x, y), sector: 8 (over z, core).
Axes of the slice: x: 4, y: 4, z: 4, core: 2. Of those that a mesh axis runs over, the one named last changes fastest.
Arguments:
- propagator: bfloat16 [8, 16, 640, 640], P('sector', 'tm'), may hold values from -6 to 6
- rising_op: bfloat16 [8, 640, 640], P('sector'), may hold values from -0.25 to 0.25
- energies: float32 [8, 640], P('sector'), may hold values from 0.5 to 40
- hyb_particle: float32 [16], P('tm'), may hold values from 0.2 to 1
- hyb_hole: float32 [16], P('tm'), may hold values from 0.2 to 1
- sector_sizes: int32 [8], P('sector'), may hold values from 160 to 640, as said below
Outputs:
- new_prop: bfloat16 [8, 16, 640, 640], P('sector', 'tm')
Inputs may be any that keep to these rules, and one draw needn't show every extreme that they name: `sector_sizes`: one sector holds exactly 640 states.
All inputs are finite; a program needn't handle non-finite values.
Results may differ from a plain program's by a relative error of at most 0.0061.
Values may be sent and summed in bfloat16 or wider, within the bound.
No kernel may reach another device: no remote copies, remote signals or barrier semaphores. Data moves between devices by JAX's collectives and lax.ppermute only.
A program may use at most 128 MiB of HBM per device.

v0:
```python
import jax
import jax.numpy as jnp
from jax import lax
from jax.sharding import PartitionSpec as P


def shifted(block, axis, distance):
    devices = range(lax.axis_size(axis))
    route = [(i - distance, i) for i in devices if i - distance in devices]
    return lax.ppermute(block, axis, route)


def split_up(value, dim, size):
    before, after = (value.shape[:dim], value.shape[dim + 1 :])
    return jnp.moveaxis(value.reshape(*before, size, -1, *after), dim, 0)


def piece_ends(length, count):
    step = length // count
    if step >= 8:
        step -= step % 8
    return [step * k for k in range(1, count)]


def laid_out(pieces, dim):
    dims = list(pieces.shape[1:])
    dims[dim] *= pieces.shape[0]
    return jnp.moveaxis(pieces, 0, dim).reshape(dims)


def several_exchanges(value, axis, pieces, split_dim, concat_dim):
    blocks = split_up(value, split_dim, lax.axis_size(axis))
    cut = max(range(1, max(2, blocks.ndim - 1)), key=lambda d: blocks.shape[d])
    finished = []
    for share in jnp.split(blocks, piece_ends(blocks.shape[cut], pieces), axis=cut):
        if share.size:
            finished.append(lax.all_to_all(share, axis, split_axis=0, concat_axis=0, tiled=True))
    return laid_out(jnp.concatenate(finished, axis=cut), concat_dim)


def per_device(propagator, rising_op, energies, hyb_particle, hyb_hole, sector_sizes):
    t_dev = propagator.shape[1]
    states = propagator.shape[2]
    time_count = t_dev * lax.axis_size("tm")
    step_size = 1.0 / time_count
    positions = jnp.arange(states, dtype=jnp.int32)
    live_mask = positions < sector_sizes[0]
    square = live_mask[:, None] & live_mask[None, :]
    masked_prop = jnp.where(square[None], propagator[0], jnp.zeros((), jnp.bfloat16))
    operator = rising_op[0]
    raised = jnp.einsum(
        "ik,tkl->til", operator, masked_prop, preferred_element_type=jnp.float32
    ).astype(jnp.bfloat16)
    upward = jnp.einsum("tik,jk->tij", raised, operator, preferred_element_type=jnp.float32).astype(
        jnp.bfloat16
    )
    from_below = shifted(upward, "sector", 1)
    from_above = shifted(masked_prop, "sector", -1)
    lowered = jnp.einsum(
        "ki,tkl->til", operator, from_above, preferred_element_type=jnp.float32
    ).astype(jnp.bfloat16)
    downward = jnp.einsum("tik,kl->til", lowered, operator, preferred_element_type=jnp.float32)
    combined = (
        hyb_particle[:, None, None] * from_below.astype(jnp.float32)
        + hyb_hole[:, None, None] * downward
    )
    self_energy = jnp.where(square[None], combined, jnp.zeros((), jnp.float32)).astype(jnp.bfloat16)
    rows_each = states // lax.axis_size("tm")
    first_row = lax.axis_index("tm") * rows_each
    lag_rows = several_exchanges(self_energy, "tm", 2, 1, 0)
    history = lax.all_gather(masked_prop, "tm", axis=0, tiled=True)
    mirrored = jnp.concatenate([history[::-1], history], 0)
    slots = jnp.arange(time_count, dtype=jnp.int32)
    wide_slots = jnp.arange(time_count + 1, dtype=jnp.int32)

    def pair_step(lag, sums):
        forward, backward = sums
        other = time_count - 1 - lag
        window = lax.dynamic_slice_in_dim(mirrored, lag, time_count + 1, 0)
        near = lax.dynamic_index_in_dim(lag_rows, lag, 0, keepdims=False)
        far = lax.dynamic_index_in_dim(lag_rows, other, 0, keepdims=False)
        left = jnp.where((wide_slots < time_count - lag)[:, None, None], near[None], far[None])
        product = jnp.einsum("uik,ukl->uil", left, window, preferred_element_type=jnp.float32)
        backward = backward + jnp.where(
            (slots < time_count - lag)[:, None, None],
            product[:time_count],
            jnp.zeros((), jnp.float32),
        )
        forward = forward + jnp.where(
            (slots >= time_count - lag - 1)[:, None, None], product[1:], jnp.zeros((), jnp.float32)
        )
        return (forward, backward)

    empty_rows = jnp.zeros((time_count, rows_each, states), jnp.float32)
    forward, backward = lax.fori_loop(0, time_count // 2, pair_step, (empty_rows, empty_rows))
    convolved = step_size * (forward + backward[::-1])
    row_ids = first_row + jnp.arange(rows_each, dtype=jnp.int32)
    row_rates = lax.dynamic_slice_in_dim(energies[0], first_row, rows_each, 0)
    decay_rows = jnp.exp(-step_size * row_rates)

    def advance(running, term):
        running = decay_rows[:, None] * running + term
        return (running, running)

    _, summed = lax.scan(advance, jnp.zeros((rows_each, states), jnp.float32), convolved)
    moments = jnp.arange(time_count).astype(jnp.float32) * step_size
    live_rows = row_ids < sector_sizes[0]
    free_part = jnp.where(
        live_rows[None, :],
        jnp.exp(-row_rates[None, :] * moments[:, None]),
        jnp.zeros((), jnp.float32),
    )
    diagonal = jnp.where(
        (row_ids[:, None] == positions[None, :])[None],
        free_part[:, :, None],
        jnp.zeros((), jnp.float32),
    )
    new_rows = (diagonal - step_size * summed).astype(jnp.bfloat16)
    return lax.all_to_all(new_rows, "tm", split_axis=0, concat_axis=1, tiled=True)[None]


def solution(mesh):
    placed = (
        P("sector", "tm", None, None),
        P("sector", None, None),
        P("sector", None),
        P("tm"),
        P("tm"),
        P("sector"),
    )
    return jax.shard_map(
        per_device,
        mesh=mesh,
        in_specs=placed,
        out_specs=P("sector", "tm", None, None),
        check_vma=False,
    )
```

profile of v0, /device:TPU:32, one launch (start us, length us, event | category | flops | bytes accessed | tf_op | source)
XLA Modules:
  0.0 278.3 jit_solution(17964893264941335905)
XLA Ops:
  7.3 2.4 and_select_fusion.1
  9.7 1.9 collective-permute-start.1
  11.7 2.9 %fusion.15 = bf16[1,640,640]{2,1,0:T(8,128)(2,1)} fusion(bf16[1,1,640,640]{3,2,1,0:T(8,128)(2,1)S(1)} %copy-done.2, bf16[1,640,640]{2,1,0:T(8,128)(2,1)S(1)} %copy-done, pred[640]{0:T(1024)(128)(4,1)S(1)} %iota_compare_fusion.4), kind=kOutput, calls=%fused_computation.33 | convolution fusion | flops 1050214400 | bytes 2458240 | tf_op jit(solution)/shard_map/tik,jk->tij/dot_general | solution.py:54
  14.6 2.4 collective-permute-start
  18.3 3.6 %collective-permute-done.1 = bf16[1,640,640]{2,1,0:T(8,128)(2,1)S(1)} collective-permute-done((bf16[1,640,640]{2,1,0:T(8,128)(2,1)}, bf16[1,640,640]{2,1,0:T(8,128)(2,1)S(1)}, u32[]{:S(2)}, u32[]{:S(2)}) %collective-permute-start.1) | collective-permute-done | bytes 819232 | tf_op jit(solution)/shard_map/ppermute | solution.py:10
  21.8 6.6 %collective-permute-done = bf16[1,640,640]{2,1,0:T(8,128)(2,1)S(1)} collective-permute-done((bf16[1,640,640]{2,1,0:T(8,128)(2,1)}, bf16[1,640,640]{2,1,0:T(8,128)(2,1)S(1)}, u32[]{:S(2)}, u32[]{:S(2)}) %collective-permute-start) | collective-permute-done | bytes 819232 | tf_op jit(solution)/shard_map/ppermute | solution.py:10
  29.3 3.5 %fusion.13 = bf16[1,640,640]{2,1,0:T(8,128)(2,1)S(1)} fusion(bf16[1,640,640]{2,1,0:T(8,128)(2,1)} %copy-done.3, bf16[1,640,640]{2,1,0:T(8,128)(2,1)S(1)} %collective-permute-done.1, bf16[1,640,640]{2,1,0:T(8,128)(2,1)S(1)} %copy-done, f32[]{:T(128)} %bitcast.67, f32[]{:T(128)} %bitcast.66, pred[640]{0:T(1024)(128)(4,1)S(1)} %iota_compare_fusion.4), kind=kOutput, calls=%fused_computation.24 | convolution fusion | flops 1051852800 | bytes 3277448 | tf_op jit(solution)/shard_map/tik,kl->til/dot_general | solution.py:62
  33.5 7.0 %all-to-all-start = ((bf16[16,1,16,640]{3,2,1,0:T(8,128)(2,1)}), bf16[16,1,16,640]{3,2,1,0:T(8,128)(2,1)S(1)}, u32[]{:S(2)}, u32[]{:S(2)}) async-start(bf16[16,1,16,640]{3,2,1,0:T(8,128)(2,1)} %split.8), calls=%async_computation | async-start | bytes 655360 | tf_op jit(solution)/shard_map/all_to_all | solution.py:37
  42.2 7.4 %all-to-all-done = bf16[16,1,16,640]{3,2,1,0:T(8,128)(2,1)S(1)} async-done(((bf16[16,1,16,640]{3,2,1,0:T(8,128)(2,1)}), bf16[16,1,16,640]{3,2,1,0:T(8,128)(2,1)S(1)}, u32[]{:S(2)}, u32[]{:S(2)}) %all-to-all-start) | async-done | bytes 327712 | tf_op jit(solution)/shard_map/all_to_all | solution.py:37
  49.6 3.7 %all-to-all-start.1 = ((bf16[16,1,24,640]{3,2,1,0:T(8,128)(2,1)}), bf16[16,1,24,640]{3,2,1,0:T(8,128)(2,1)S(1)}, u32[]{:S(2)}, u32[]{:S(2)}) async-start(bf16[16,1,24,640]{3,2,1,0:T(8,128)(2,1)} %split.9), calls=%async_computation.1 | async-start | bytes 983040 | tf_op jit(solution)/shard_map/all_to_all | solution.py:37
  53.5 14.7 %all-to-all-done.1 = bf16[16,1,24,640]{3,2,1,0:T(8,128)(2,1)S(1)} async-done(((bf16[16,1,24,640]{3,2,1,0:T(8,128)(2,1)}), bf16[16,1,24,640]{3,2,1,0:T(8,128)(2,1)S(1)}, u32[]{:S(2)}, u32[]{:S(2)}) %all-to-all-start.1) | async-done | bytes 491552 | tf_op jit(solution)/shard_map/all_to_all | solution.py:37
  68.2 42.9 %all-gather.2.cloned.1.call-done = bf16[16,640,640]{2,1,0:T(8,128)(2,1)} async-done(((bf16[1,640,640]{2,1,0:T(8,128)(2,1)}), bf16[16,640,640]{2,1,0:T(8,128)(2,1)}) %all-gather.2.cloned.1.call-update) | async-done | bytes 13107216 | tf_op jit(solution)/shard_map/all_gather | solution.py:71
  111.1 10.8 %rev.6 = bf16[16,640,640]{2,1,0:T(8,128)(2,1)} reverse(bf16[16,640,640]{2,1,0:T(8,128)(2,1)} %all-gather.2.cloned.1.call-done), dimensions={0} | reverse | bytes 26214400 | tf_op jit(solution)/shard_map/rev | solution.py:72
  122.0 18.6 %pad_maximum_fusion = bf16[32,640,640]{2,1,0:T(8,128)(2,1)} fusion(bf16[16,640,640]{2,1,0:T(8,128)(2,1)} %all-gather.2.cloned.1.call-done, bf16[16,640,640]{2,1,0:T(8,128)(2,1)} %rev.6), kind=kLoop, calls=%fused_computation.21 | loop fusion | flops 13107200 | bytes 52428800 | tf_op jit(solution)/shard_map/concatenate | solution.py:72
  140.6 90.8 %while.35 = (s32[]{:T(128)}, f32[16,40,640]{2,1,0:T(8,128)}, f32[16,40,640]{2,1,0:T(8,128)}, bf16[16,40,640]{2,1,0:T(8,128)(2,1)S(1)}, bf16[32,640,640]{2,1,0:T(...) while((s32[]{:T(128)}, f32[16,40,640]{2,1,0:T(8,128)}, ...), condition=%wide.region_1.2_spmd.clone.clone, body=%wide.region_0.1_spmd.clone.clone.sunk | while | flops 559948800 | bytes 25805600 | solution.py:95
  140.6 7.3 %fusion.40 = f32[17,40,640]{2,1,0:T(8,128)S(1)} fusion(bf16[32,640,640]{2,1,0:T(8,128)(2,1)} %get-tuple-element.458, s32[]{:T(128)} %get-tuple-element.444, pred[17]{0:T(512)(128)(4,1)S(1)} %iota_compare_fusion.7, bf16[40,640]{1,0:T(8,128)(2,1)S(1)} %get-tuple-element.428, bf16[40,640]{1,0:T(8,128)(2,1)S(1)} %get-tuple-element.429), kind=kOutput, calls=%fused_computation.5.clone.1 | convolution fusion | flops 557491200 | bytes 15770129 | tf_op jit(solution)/shard_map/while/body/eval_jaxpr/uik,ukl->uil/dot_general | solution.py:83
  148.0 2.3 fusion.41
  150.3 7.3 %fusion.40 = f32[17,40,640]{2,1,0:T(8,128)S(1)} fusion(bf16[32,640,640]{2,1,0:T(8,128)(2,1)} %get-tuple-element.458, s32[]{:T(128)} %get-tuple-element.444, pred[17]{0:T(512)(128)(4,1)S(1)} %iota_compare_fusion.7, bf16[40,640]{1,0:T(8,128)(2,1)S(1)} %get-tuple-element.428, bf16[40,640]{1,0:T(8,128)(2,1)S(1)} %get-tuple-element.429), kind=kOutput, calls=%fused_computation.5.clone.1 | convolution fusion | flops 557491200 | bytes 15770129 | tf_op jit(solution)/shard_map/while/body/eval_jaxpr/uik,ukl->uil/dot_general | solution.py:83
  157.6 4.2 %fusion.41 = (f32[16,40,640]{2,1,0:T(8,128)}, f32[16,40,640]{2,1,0:T(8,128)}) fusion(f32[17,40,640]{2,1,0:T(8,128)S(1)} %fusion.40, f32[16,40,640]{2,1,0:T(8,128)} %get-tuple-element.446, pred[16]{0:T(512)(128)(4,1)S(1)} %get-tuple-element.430, pred[]{:T(512)S(6)} %compare.7, pred[16]{0:T(512)(128)(4,1)S(1)} %get-tuple-element.431, ...), kind=kLoop, calls=%fused_computation.8.clone.1 | loop fusion | flops 2457600 | bytes 9830433 | tf_op jit(solution)/shard_map/while/body/eval_jaxpr/add | solution.py:84
  161.9 7.3 %fusion.40 = f32[17,40,640]{2,1,0:T(8,128)S(1)} fusion(bf16[32,640,640]{2,1,0:T(8,128)(2,1)} %get-tuple-element.458, s32[]{:T(128)} %get-tuple-element.444, pred[17]{0:T(512)(128)(4,1)S(1)} %iota_compare_fusion.7, bf16[40,640]{1,0:T(8,128)(2,1)S(1)} %get-tuple-element.428, bf16[40,640]{1,0:T(8,128)(2,1)S(1)} %get-tuple-element.429), kind=kOutput, calls=%fused_computation.5.clone.1 | convolution fusion | flops 557491200 | bytes 15770129 | tf_op jit(solution)/shard_map/while/body/eval_jaxpr/uik,ukl->uil/dot_general | solution.py:83
  169.2 4.2 %fusion.41 = (f32[16,40,640]{2,1,0:T(8,128)}, f32[16,40,640]{2,1,0:T(8,128)}) fusion(f32[17,40,640]{2,1,0:T(8,128)S(1)} %fusion.40, f32[16,40,640]{2,1,0:T(8,128)} %get-tuple-element.446, pred[16]{0:T(512)(128)(4,1)S(1)} %get-tuple-element.430, pred[]{:T(512)S(6)} %compare.7, pred[16]{0:T(512)(128)(4,1)S(1)} %get-tuple-element.431, ...), kind=kLoop, calls=%fused_computation.8.clone.1 | loop fusion | flops 2457600 | bytes 9830433 | tf_op jit(solution)/shard_map/while/body/eval_jaxpr/add | solution.py:84
  173.5 7.3 %fusion.40 = f32[17,40,640]{2,1,0:T(8,128)S(1)} fusion(bf16[32,640,640]{2,1,0:T(8,128)(2,1)} %get-tuple-element.458, s32[]{:T(128)} %get-tuple-element.444, pred[17]{0:T(512)(128)(4,1)S(1)} %iota_compare_fusion.7, bf16[40,640]{1,0:T(8,128)(2,1)S(1)} %get-tuple-element.428, bf16[40,640]{1,0:T(8,128)(2,1)S(1)} %get-tuple-element.429), kind=kOutput, calls=%fused_computation.5.clone.1 | convolution fusion | flops 557491200 | bytes 15770129 | tf_op jit(solution)/shard_map/while/body/eval_jaxpr/uik,ukl->uil/dot_general | solution.py:83
  180.8 4.2 %fusion.41 = (f32[16,40,640]{2,1,0:T(8,128)}, f32[16,40,640]{2,1,0:T(8,128)}) fusion(f32[17,40,640]{2,1,0:T(8,128)S(1)} %fusion.40, f32[16,40,640]{2,1,0:T(8,128)} %get-tuple-element.446, pred[16]{0:T(512)(128)(4,1)S(1)} %get-tuple-element.430, pred[]{:T(512)S(6)} %compare.7, pred[16]{0:T(512)(128)(4,1)S(1)} %get-tuple-element.431, ...), kind=kLoop, calls=%fused_computation.8.clone.1 | loop fusion | flops 2457600 | bytes 9830433 | tf_op jit(solution)/shard_map/while/body/eval_jaxpr/add | solution.py:84
  185.1 7.3 %fusion.40 = f32[17,40,640]{2,1,0:T(8,128)S(1)} fusion(bf16[32,640,640]{2,1,0:T(8,128)(2,1)} %get-tuple-element.458, s32[]{:T(128)} %get-tuple-element.444, pred[17]{0:T(512)(128)(4,1)S(1)} %iota_compare_fusion.7, bf16[40,640]{1,0:T(8,128)(2,1)S(1)} %get-tuple-element.428, bf16[40,640]{1,0:T(8,128)(2,1)S(1)} %get-tuple-element.429), kind=kOutput, calls=%fused_computation.5.clone.1 | convolution fusion | flops 557491200 | bytes 15770129 | tf_op jit(solution)/shard_map/while/body/eval_jaxpr/uik,ukl->uil/dot_general | solution.py:83
  192.4 4.2 %fusion.41 = (f32[16,40,640]{2,1,0:T(8,128)}, f32[16,40,640]{2,1,0:T(8,128)}) fusion(f32[17,40,640]{2,1,0:T(8,128)S(1)} %fusion.40, f32[16,40,640]{2,1,0:T(8,128)} %get-tuple-element.446, pred[16]{0:T(512)(128)(4,1)S(1)} %get-tuple-element.430, pred[]{:T(512)S(6)} %compare.7, pred[16]{0:T(512)(128)(4,1)S(1)} %get-tuple-element.431, ...), kind=kLoop, calls=%fused_computation.8.clone.1 | loop fusion | flops 2457600 | bytes 9830433 | tf_op jit(solution)/shard_map/while/body/eval_jaxpr/add | solution.py:84
  196.7 7.3 %fusion.40 = f32[17,40,640]{2,1,0:T(8,128)S(1)} fusion(bf16[32,640,640]{2,1,0:T(8,128)(2,1)} %get-tuple-element.458, s32[]{:T(128)} %get-tuple-element.444, pred[17]{0:T(512)(128)(4,1)S(1)} %iota_compare_fusion.7, bf16[40,640]{1,0:T(8,128)(2,1)S(1)} %get-tuple-element.428, bf16[40,640]{1,0:T(8,128)(2,1)S(1)} %get-tuple-element.429), kind=kOutput, calls=%fused_computation.5.clone.1 | convolution fusion | flops 557491200 | bytes 15770129 | tf_op jit(solution)/shard_map/while/body/eval_jaxpr/uik,ukl->uil/dot_general | solution.py:83
  204.0 4.2 %fusion.41 = (f32[16,40,640]{2,1,0:T(8,128)}, f32[16,40,640]{2,1,0:T(8,128)}) fusion(f32[17,40,640]{2,1,0:T(8,128)S(1)} %fusion.40, f32[16,40,640]{2,1,0:T(8,128)} %get-tuple-element.446, pred[16]{0:T(512)(128)(4,1)S(1)} %get-tuple-element.430, pred[]{:T(512)S(6)} %compare.7, pred[16]{0:T(512)(128)(4,1)S(1)} %get-tuple-element.431, ...), kind=kLoop, calls=%fused_computation.8.clone.1 | loop fusion | flops 2457600 | bytes 9830433 | tf_op jit(solution)/shard_map/while/body/eval_jaxpr/add | solution.py:84
  208.2 7.3 %fusion.40 = f32[17,40,640]{2,1,0:T(8,128)S(1)} fusion(bf16[32,640,640]{2,1,0:T(8,128)(2,1)} %get-tuple-element.458, s32[]{:T(128)} %get-tuple-element.444, pred[17]{0:T(512)(128)(4,1)S(1)} %iota_compare_fusion.7, bf16[40,640]{1,0:T(8,128)(2,1)S(1)} %get-tuple-element.428, bf16[40,640]{1,0:T(8,128)(2,1)S(1)} %get-tuple-element.429), kind=kOutput, calls=%fused_computation.5.clone.1 | convolution fusion | flops 557491200 | bytes 15770129 | tf_op jit(solution)/shard_map/while/body/eval_jaxpr/uik,ukl->uil/dot_general | solution.py:83
  215.6 4.2 %fusion.41 = (f32[16,40,640]{2,1,0:T(8,128)}, f32[16,40,640]{2,1,0:T(8,128)}) fusion(f32[17,40,640]{2,1,0:T(8,128)S(1)} %fusion.40, f32[16,40,640]{2,1,0:T(8,128)} %get-tuple-element.446, pred[16]{0:T(512)(128)(4,1)S(1)} %get-tuple-element.430, pred[]{:T(512)S(6)} %compare.7, pred[16]{0:T(512)(128)(4,1)S(1)} %get-tuple-element.431, ...), kind=kLoop, calls=%fused_computation.8.clone.1 | loop fusion | flops 2457600 | bytes 9830433 | tf_op jit(solution)/shard_map/while/body/eval_jaxpr/add | solution.py:84
  219.8 7.3 %fusion.40 = f32[17,40,640]{2,1,0:T(8,128)S(1)} fusion(bf16[32,640,640]{2,1,0:T(8,128)(2,1)} %get-tuple-element.458, s32[]{:T(128)} %get-tuple-element.444, pred[17]{0:T(512)(128)(4,1)S(1)} %iota_compare_fusion.7, bf16[40,640]{1,0:T(8,128)(2,1)S(1)} %get-tuple-element.428, bf16[40,640]{1,0:T(8,128)(2,1)S(1)} %get-tuple-element.429), kind=kOutput, calls=%fused_computation.5.clone.1 | convolution fusion | flops 557491200 | bytes 15770129 | tf_op jit(solution)/shard_map/while/body/eval_jaxpr/uik,ukl->uil/dot_general | solution.py:83
  227.1 4.2 %fusion.41 = (f32[16,40,640]{2,1,0:T(8,128)}, f32[16,40,640]{2,1,0:T(8,128)}) fusion(f32[17,40,640]{2,1,0:T(8,128)S(1)} %fusion.40, f32[16,40,640]{2,1,0:T(8,128)} %get-tuple-element.446, pred[16]{0:T(512)(128)(4,1)S(1)} %get-tuple-element.430, pred[]{:T(512)S(6)} %compare.7, pred[16]{0:T(512)(128)(4,1)S(1)} %get-tuple-element.431, ...), kind=kLoop, calls=%fused_computation.8.clone.1 | loop fusion | flops 2457600 | bytes 9830433 | tf_op jit(solution)/shard_map/while/body/eval_jaxpr/add | solution.py:84
  231.4 3.3 %add_multiply_fusion = f32[16,40,640]{2,1,0:T(8,128)} fusion(f32[16,40,640]{2,1,0:T(8,128)} %get-tuple-element.265, f32[16,40,640]{2,1,0:T(8,128)} %get-tuple-element.266), kind=kLoop, calls=%fused_computation.27 | loop fusion | flops 819200 | bytes 4915200 | tf_op jit(solution)/shard_map/mul | solution.py:96
  234.7 16.0 %while.34 = (s32[]{:T(128)}, f32[40,640]{1,0:T(8,128)S(1)}, f32[16,40,640]{2,1,0:T(8,128)S(1)}, f32[40]{0:T(128)S(1)}, f32[16,40,640]{2,1,0:T(8,128)}, /*index=5*/s32[]{:T(128)}, s32[]{:T(128)}) while((s32[]{:T(128)}, f32[40,640]{1,0:T(8,128)S(1)}, f32[16,40,640]{2,1,0:T(8,128)S(1)}, f32[40]{0:T(128)S(1)}, ...), condition=%wide.region_3.4_spmd.clone, body=%wide.region_2.3_spmd.clone.sunk | while | flops 76803 | bytes 410203 | solution.py:105
  234.8 1.0 bitcast_dynamic-update-slice_fusion.2
  235.8 1.0 bitcast_dynamic-update-slice_fusion.2
  236.8 1.0 bitcast_dynamic-update-slice_fusion.2
  237.8 1.0 bitcast_dynamic-update-slice_fusion.2
  239.8 1.0 bitcast_dynamic-update-slice_fusion.2
  240.8 1.0 bitcast_dynamic-update-slice_fusion.2
  241.8 1.0 bitcast_dynamic-update-slice_fusion.2
  242.8 1.0 bitcast_dynamic-update-slice_fusion.2
  243.8 1.0 bitcast_dynamic-update-slice_fusion.2
  244.8 1.0 bitcast_dynamic-update-slice_fusion.2
  245.8 1.0 bitcast_dynamic-update-slice_fusion.2
  246.8 1.0 bitcast_dynamic-update-slice_fusion.2
  247.8 1.0 bitcast_dynamic-update-slice_fusion.2
  248.8 1.0 bitcast_dynamic-update-slice_fusion.2
  251.1 19.5 %all_to_all.19 = bf16[16,40,640]{2,1,0:T(8,128)(2,1)S(1)} all-to-all(bf16[16,40,640]{2,1,0:T(8,128)(2,1)S(1)} %subtract_convert_fusion), channel_id=1, replica_groups=mesh['tm'=16,'sector'=8] {'tm'}, dimensions={0} | all-to-all | bytes 1638400 | tf_op jit(solution)/shard_map/all_to_all | solution.py:119
  (52 shorter events, 7.0 us)
Async XLA Ops:
  6.5 5.1 %copy-start = (bf16[1,640,640]{2,1,0:T(8,128)(2,1)S(1)}, bf16[1,640,640]{2,1,0:T(8,128)(2,1)}, u32[]{:S(2)}) copy-start(bf16[1,640,640]{2,1,0:T(8,128)(2,1)} %param.11) | copy-start | bytes 2457604
  6.5 5.1 %copy-start.2 = (bf16[1,1,640,640]{3,2,1,0:T(8,128)(2,1)S(1)}, bf16[1,1,640,640]{3,2,1,0:T(8,128)(2,1)}, u32[]{:S(2)}) copy-start(bf16[1,1,640,640]{3,2,1,0:T(8,128)(2,1)} %param.10) | copy-start | bytes 2457604
  6.5 104.6 %all-gather.2.cloned.1.call-start = ((), (), s32[]{:S(2)}) async-start(), calls=%async_computation.3 | async-start | bytes 13926400 | tf_op jit(solution)/shard_map/all_gather | solution.py:71
  9.7 12.1 %collective-permute-start.1 = (bf16[1,640,640]{2,1,0:T(8,128)(2,1)}, bf16[1,640,640]{2,1,0:T(8,128)(2,1)S(1)}, u32[]{:S(2)}, u32[]{:S(2)}) collective-permute-start(bf16[1,640,640]{2,1,0:T(8,128)(2,1)} %and_select_fusion.1), channel_id=1, source_target_pairs={{1,0},{2,1},{3,2},{4,3},{5,4},{6,5},{7,6},{9,8},{10,9},{11,10},{12... | collective-permute-start | bytes 2457608 | tf_op jit(solution)/shard_map/ppermute | solution.py:10
  14.6 13.9 %collective-permute-start = (bf16[1,640,640]{2,1,0:T(8,128)(2,1)}, bf16[1,640,640]{2,1,0:T(8,128)(2,1)S(1)}, u32[]{:S(2)}, u32[]{:S(2)}) collective-permute-start(bf16[1,640,640]{2,1,0:T(8,128)(2,1)} %fusion.15), channel_id=1, source_target_pairs={{0,1},{1,2},{2,3},{3,4},{4,5},{5,6},{6,7},{8,9},{9,10},{10,11},{11... | collective-permute-start | bytes 2457608 | tf_op jit(solution)/shard_map/ppermute | solution.py:10
  28.4 0.9 copy-start.3
  33.5 16.0 %all-to-all-start = ((bf16[16,1,16,640]{3,2,1,0:T(8,128)(2,1)}), bf16[16,1,16,640]{3,2,1,0:T(8,128)(2,1)S(1)}, u32[]{:S(2)}, u32[]{:S(2)}) async-start(bf16[16,1,16,640]{3,2,1,0:T(8,128)(2,1)} %split.8), calls=%async_computation | async-start | bytes 655360 | tf_op jit(solution)/shard_map/all_to_all | solution.py:37
  49.6 18.6 %all-to-all-start.1 = ((bf16[16,1,24,640]{3,2,1,0:T(8,128)(2,1)}), bf16[16,1,24,640]{3,2,1,0:T(8,128)(2,1)S(1)}, u32[]{:S(2)}, u32[]{:S(2)}) async-start(bf16[16,1,24,640]{3,2,1,0:T(8,128)(2,1)} %split.9), calls=%async_computation.1 | async-start | bytes 983040 | tf_op jit(solution)/shard_map/all_to_all | solution.py:37
  250.8 20.7 %copy-start.1 = (bf16[1,640,640]{2,1,0:T(8,128)(2,1)S(1)}, bf16[1,640,640]{2,1,0:T(8,128)(2,1)}, u32[]{:S(2)}) copy-start(bf16[1,640,640]{2,1,0:T(8,128)(2,1)} %param.11) | copy-start | bytes 2457604
Sparse Core Ops, SparseCore 0:
  9.8 101.2 all-gather.1
where the time goes:
time: 280 us; the launch traced here: 278 us
  waiting for transfers between devices  75.2 us (27%)
  other arithmetic  73.3 us (26%)
  matrix products  64.8 us (23%)
  blocking collectives  19.5 us (7%)
  between operations  15.6 us (6%)
  starting transfers between devices  15 us (5%)
  local copies, waits for them, and re-layouts  14.4 us (5%)
    dot_general x8, matrix products, pair_step(): jnp.einsum('uik,ukl->uil', left, window, preferred_element_type=jnp.float32)  58.4 us
    all_gather x1, waiting for transfers between devices, per_device(): history = lax.all_gather(masked_prop, 'tm', axis=0, tiled=True)  42.9 us
    add x8, other arithmetic, pair_step(): backward + jnp.where((slots < time_count - lag)[:, None, None], product[:...  31.9 us
    all_to_all x2, waiting for transfers between devices, several_exchanges(): lax.all_to_all(share, axis, split_axis=0, concat_axis=0, tiled=True)  22 us
    all_to_all x1, blocking collectives, per_device(): lax.all_to_all(new_rows, 'tm', split_axis=0, concat_axis=1, tiled=True)  19.5 us
    concatenate x1, other arithmetic, per_device(): mirrored = jnp.concatenate([history[::-1], history], 0)  18.6 us
    dynamic_update_slice x16, other arithmetic, per_device(): lax.scan(advance, jnp.zeros((rows_each, states), jnp.float32), convolved)  15.7 us
    rev x1, local copies, waits for them, and re-layouts, per_device(): mirrored = jnp.concatenate([history[::-1], history], 0)  10.8 us
  transfers between devices with their start and end apart: 5, of which 5 were waited for; matrix products, arithmetic and copies ran while one was open for 3% of the time, Pallas kernels for 0%

commit v1 on v0

v1 whole, which is shorter than its diff:
```python
import functools

import jax
import jax.numpy as jnp
import numpy as np
from jax import lax
from jax.experimental import pallas as pl
from jax.experimental.pallas import tpu as pltpu
from jax.sharding import Mesh
from jax.sharding import PartitionSpec as P


def shifted(block, axis, distance):
    devices = range(lax.axis_size(axis))
    route = [(i - distance, i) for i in devices if i - distance in devices]
    return lax.ppermute(block, axis, route)


def ring(block, axis, distance):
    n = lax.axis_size(axis)
    return lax.ppermute(block, axis, [(i, (i + distance) % n) for i in range(n)])


def ring_gather(block, axis):
    half = block.shape[0] // 2
    first, second = block[:half], block[half:]
    below_a = ring(first, axis, 1)
    above_a = ring(second, axis, -1)
    below_b = ring(second, axis, 1)
    above_b = ring(first, axis, -1)
    far_a = ring(below_a, axis, 1)
    far_b = ring(above_a, axis, -1)
    return [
        (-1, 0, below_a),
        (1, 1, above_a),
        (-1, 1, below_b),
        (1, 0, above_b),
        (2, 0, far_a),
        (2, 1, far_b),
    ]


def convolve_kernel(
    plan_e, plan_g, sides, step_size, scalars, rates, *refs
):
    n = sides
    count = 1 + len(plan_e)
    e_parts = refs[:count]
    g_parts = refs[count : 2 * count]
    out, e_all, g_all, total, sems = refs[2 * count :]
    rows = out.shape[1] * n
    here_x, here_y, size = scalars[0], scalars[1], scalars[2]

    copies = []
    for parts, plan, here, target in (
        (e_parts, plan_e, here_y, e_all),
        (g_parts, plan_g, here_x, g_all),
    ):
        copies.append((parts[0], target.at[here]))
        for part, (offset, half, length) in zip(parts[1:], plan):
            source = lax.rem(here + offset + n, n)
            copies.append((part, target.at[source, pl.ds(half * length, length)]))
    started = [
        pltpu.make_async_copy(src, dst, sems.at[i]) for i, (src, dst) in enumerate(copies)
    ]
    for copy in started:
        copy.start()
    total[...] = jnp.zeros_like(total)
    for copy in started:
        copy.wait()

    @pl.loop(0, n)
    def _(source):
        for v in range(n * n):
            lane, first = v % n, v // n

            @pl.when(v - source >= 0)
            def _():
                u = v - source
                left = e_all[source, : n - first].reshape((n - first) * rows, -1)
                right = g_all[u // n, lax.rem(u, n)]
                product = lax.dot_general(
                    left, right, (((1,), (1,)), ((), ())), preferred_element_type=jnp.float32
                )
                total[lane, first * rows :, :] += product

    rate = rates[...]
    decay = jnp.exp(-step_size * rate)
    row = lax.broadcasted_iota(jnp.int32, (rows, rows), 0)
    column = lax.broadcasted_iota(jnp.int32, (rows, rows), 1)
    on_diagonal = (row == column) & (here_x == here_y) & (row + here_x * rows < size)
    running = jnp.zeros((rows, rows), jnp.float32)
    quarter = rows // n
    for t in range(n * n):
        lane, first = t % n, t // n
        running = decay * running + step_size * total[lane, first * rows : (first + 1) * rows, :]
        free = jnp.where(on_diagonal, jnp.exp(-rate * (t * step_size)), 0.0)
        fresh = free - step_size * running
        for b in range(n):
            out[t, :, b * rows : (b + 1) * rows] = fresh[b * quarter : (b + 1) * quarter].astype(
                jnp.bfloat16
            )


def convolve(own_e, rest_e, own_g, rest_g, scalars, rates, n, step_size):
    plan_e = [(o, h, p.shape[0]) for o, h, p in rest_e]
    plan_g = [(o, h, p.shape[0]) for o, h, p in rest_g]
    parts = [own_e] + [p for _, _, p in rest_e] + [own_g] + [p for _, _, p in rest_g]
    _, rows, states = own_e.shape
    anywhere = pl.BlockSpec(memory_space=pl.ANY)
    return pl.pallas_call(
        functools.partial(convolve_kernel, plan_e, plan_g, n, step_size),
        out_shape=jax.ShapeDtypeStruct((n * n, rows // n, states), jnp.bfloat16),
        in_specs=[
            pl.BlockSpec(memory_space=pltpu.SMEM),
            pl.BlockSpec(memory_space=pltpu.VMEM),
        ]
        + [anywhere] * len(parts),
        out_specs=pl.BlockSpec(memory_space=pltpu.VMEM),
        scratch_shapes=[
            pltpu.VMEM((n, n, rows, states), jnp.bfloat16),
            pltpu.VMEM((n, n, rows, states), jnp.bfloat16),
            pltpu.VMEM((n, n * rows, rows), jnp.float32),
            pltpu.SemaphoreType.DMA((len(parts),)),
        ],
        compiler_params=pltpu.CompilerParams(vmem_limit_bytes=40 * 1024 * 1024),
        cost_estimate=pl.CostEstimate(
            flops=2 * 136 * rows * rows * states,
            bytes_accessed=4 * n * n * rows * states,
            transcendentals=0,
        ),
        name="convolve",
    )(scalars, rates, *parts)


def assemble_kernel(n, packets, out):
    quarter, states = packets.shape[1:]
    rows = states // n
    for x in range(n):
        for b in range(n):
            out[x * rows + b * quarter : x * rows + (b + 1) * quarter, :] = jnp.concatenate(
                [packets[x * n + y, :, b * rows : (b + 1) * rows] for y in range(n)], axis=1
            )


def assemble(packets, n):
    states = packets.shape[2]
    return pl.pallas_call(
        functools.partial(assemble_kernel, n),
        out_shape=jax.ShapeDtypeStruct((states, states), jnp.bfloat16),
        in_specs=[pl.BlockSpec(memory_space=pltpu.VMEM)],
        out_specs=pl.BlockSpec(memory_space=pltpu.VMEM),
        name="assemble",
    )(packets)


def per_device(propagator, rising_op, energies, hyb_particle, hyb_hole, sector_sizes):
    states = propagator.shape[2]
    n = lax.axis_size("tx")
    step_size = 1.0 / (n * n)
    rows = states // n
    here_x, here_y = lax.axis_index("tx"), lax.axis_index("ty")
    positions = jnp.arange(states, dtype=jnp.int32)
    live_mask = positions < sector_sizes[0]
    square = live_mask[:, None] & live_mask[None, :]
    zero = jnp.zeros((), jnp.bfloat16)
    masked = jnp.where(square, propagator[0, 0], zero)
    operator = rising_op[0]

    columns = lax.all_to_all(masked.T.reshape(n, rows, states), "ty", 0, 0, tiled=True)

    from_above = shifted(masked, "sector", -1)
    raised = jnp.dot(operator, masked, preferred_element_type=jnp.float32).astype(jnp.bfloat16)
    upward = jnp.einsum("ik,jk->ij", raised, operator, preferred_element_type=jnp.float32).astype(
        jnp.bfloat16
    )
    from_below = shifted(upward, "sector", 1)
    lowered = jnp.einsum(
        "ki,kl->il", operator, from_above, preferred_element_type=jnp.float32
    ).astype(jnp.bfloat16)
    downward = jnp.dot(lowered, operator, preferred_element_type=jnp.float32)
    combined = hyb_particle[0] * from_below.astype(jnp.float32) + hyb_hole[0] * downward
    self_energy = jnp.where(square, combined, 0.0).astype(jnp.bfloat16)

    lines = lax.all_to_all(self_energy.reshape(n, rows, states), "tx", 0, 0, tiled=True)

    rest_g = ring_gather(columns, "tx")
    rest_e = ring_gather(lines, "ty")
    rates = lax.dynamic_slice_in_dim(energies[0], here_x * rows, rows, 0)[:, None]
    scalars = jnp.stack([here_x, here_y, sector_sizes[0]]).astype(jnp.int32)
    packets = convolve(lines, rest_e, columns, rest_g, scalars, rates, n, step_size)
    packets = lax.all_to_all(packets, ("tx", "ty"), 0, 0, tiled=True)
    return assemble(packets, n)[None, None]


def solution(mesh):
    n = math_root(mesh.shape["tm"])
    split = Mesh(
        np.asarray(mesh.devices).reshape(n, n, mesh.shape["sector"]), ("tx", "ty", "sector")
    )
    times = ("tx", "ty")
    placed = (
        P("sector", times, None, None),
        P("sector", None, None),
        P("sector", None),
        P(times),
        P(times),
        P("sector"),
    )
    return jax.shard_map(
        per_device,
        mesh=split,
        in_specs=placed,
        out_specs=P("sector", times, None, None),
        check_vma=False,
    )


def math_root(count):
    return int(round(count**0.5))
```

time: 280 us -> 138 us (0.49)
  other arithmetic: 73.3 us -> 0.71 us
  matrix products: 64.8 us -> 8.7 us
  waiting for transfers between devices: 75.2 us -> 46 us
  Pallas kernels: 0 us -> 26.1 us
  between operations: 15.6 us -> 2.11 us
  starting transfers between devices: 15 us -> 27.9 us
  local copies, waits for them, and re-layouts: 14.4 us -> 4.53 us
    dot_general x10 -> x2, matrix products: 64.8 us -> 8.7 us  [the longest x1 4.6 us: per_device(): downward = jnp.dot(lowered, operator, preferred_element_type=jnp.float32)]
    all_gather x1 -> x0, waiting for transfers between devices: 42.9 us -> none  [per_device(): history = lax.all_gather(masked_prop, 'tm', axis=0, tiled=True)]
    ppermute x0 -> x12, waiting for transfers between devices: none -> 38.8 us  [ring(): lax.ppermute(block, axis, [(i, (i + distance) % n) for i in range(n)])]
    add x9 -> x0, other arithmetic: 31.9 us -> none  [the longest x8 31.9 us: pair_step(): backward + jnp.where((slots < time_count - lag)[:, None, None], product[:...]
    pallas_call x0 -> x2, Pallas kernels: none -> 26.1 us  [the longest x1 23.7 us: convolve(): pl.pallas_call(functools.partial(convolve_kernel, plan_e, plan_g, n, step...]
    concatenate x1 -> x0, other arithmetic: 18.6 us -> none  [per_device(): mirrored = jnp.concatenate([history[::-1], history], 0)]
    all_to_all x2, waiting for transfers between devices: 22 us -> 4.74 us  [the longest x1 4.73 us: per_device(): lax.all_to_all(masked.T.reshape(n, rows, states), 'ty', 0, 0, tiled=True)]
    dynamic_update_slice x16 -> x0, other arithmetic: 15.7 us -> none  [per_device(): lax.scan(advance, jnp.zeros((rows_each, states), jnp.float32), convolved)]
  transfers between devices with their start and end apart: 5 -> 16, of which waited for: 5 -> 10; matrix products, arithmetic and copies ran while one was open for 3% -> 7% of each run, Pallas kernels for 0% -> 0%
where the time goes in v1:
time: 138 us; the launch traced here: 136 us
  waiting for transfers between devices  46 us (33%)
  starting transfers between devices  27.9 us (20%)
  Pallas kernels  26.1 us (19%)
  blocking collectives  19.6 us (14%)
  matrix products  8.7 us (6%)
  local copies, waits for them, and re-layouts  4.53 us (3%)
  between operations  2.11 us (2%)
    ppermute x12, waiting for transfers between devices, ring(): lax.ppermute(block, axis, [(i, (i + distance) % n) for i in range(n)])  38.8 us
    pallas_call x1, Pallas kernels, convolve(): pl.pallas_call(functools.partial(convolve_kernel, plan_e, plan_g, n, step...  23.7 us
    all_to_all x1, blocking collectives, per_device(): packets = lax.all_to_all(packets, ('tx', 'ty'), 0, 0, tiled=True)  19.6 us
    ppermute x12, starting transfers between devices, ring(): lax.ppermute(block, axis, [(i, (i + distance) % n) for i in range(n)])  13.6 us
    ppermute x2, starting transfers between devices, shifted(): return lax.ppermute(block, axis, route)  5.55 us
    all_to_all x1, waiting for transfers between devices, per_device(): lax.all_to_all(masked.T.reshape(n, rows, states), 'ty', 0, 0, tiled=True)  4.73 us
    dot_general x1, matrix products, per_device(): downward = jnp.dot(lowered, operator, preferred_element_type=jnp.float32)  4.6 us
    all_to_all x1, starting transfers between devices, per_device(): lax.all_to_all(masked.T.reshape(n, rows, states), 'ty', 0, 0, tiled=True)  4.46 us
  transfers between devices with their start and end apart: 16, of which 10 were waited for; matrix products, arithmetic and copies ran while one was open for 7% of the time, Pallas kernels for 0%

profile of v1, /device:TPU:32, one launch (start us, length us, event | category | flops | bytes accessed | tf_op | source)
XLA Modules:
  0.0 135.7 jit_solution(475595556960620304)
XLA Ops:
  0.0 0.0 copy-start
  0.7 0.4 copy-done
  1.2 4.1 %convolution_convert_fusion.1 = bf16[640,640]{1,0:T(8,128)(2,1)} fusion(bf16[1,1,640,640]{3,2,1,0:T(8,128)(2,1)} %param.6, bf16[1,640,640]{2,1,0:T(8,128)(2,1)S(1)} %copy-done, pred[640]{0:T(1024)(128)(4,1)S(1)} %iota_compare_fusion), kind=kOutput, calls=%fused_computation.5 | convolution fusion | flops 1050214400 | bytes 2458240 | tf_op jit(solution)/shard_map/ik,jk->ij/dot_general | solution.py:174
  5.3 1.9 %collective-permute-start = (bf16[640,640]{1,0:T(8,128)(2,1)}, bf16[640,640]{1,0:T(8,128)(2,1)}, u32[]{:S(2)}, u32[]{:S(2)}) collective-permute-start(bf16[640,640]{1,0:T(8,128)(2,1)} %convolution_convert_fusion.1), channel_id=1, source_target_pairs={{0,1},{1,2},{2,3},{3,4},{4,5},{5,6},{6,7},{8,9},{9,10},{10,11},{11... | collective-permute-start | bytes 2457608 | tf_op jit(solution)/shard_map/ppermute | solution.py:16
  7.2 0.0 copy-done.1
  7.2 0.3 and_select_fusion.1
  7.5 3.6 %collective-permute-start.1 = (bf16[640,640]{1,0:T(8,128)(2,1)S(1)}, bf16[640,640]{1,0:T(8,128)(2,1)}, u32[]{:S(2)}, u32[]{:S(2)}) collective-permute-start(bf16[640,640]{1,0:T(8,128)(2,1)S(1)} %and_select_fusion.1), channel_id=1, source_target_pairs={{1,0},{2,1},{3,2},{4,3},{5,4},{6,5},{7,6},{9,8},{10,9},{11,10},{12... | collective-permute-start | bytes 2457608 | tf_op jit(solution)/shard_map/ppermute | solution.py:16
  11.2 0.3 fusion.19
  11.5 1.3 copy.8
  12.8 4.5 %all-to-all-start.1 = ((bf16[4,160,640]{2,1,0:T(8,128)(2,1)}), bf16[4,160,640]{2,1,0:T(8,128)(2,1)S(1)}, u32[]{:S(2)}, u32[]{:S(2)}) async-start(bf16[4,160,640]{2,1,0:T(8,128)(2,1)} %bitcast.11), calls=%async_computation.1 | async-start | bytes 1638400 | tf_op jit(solution)/shard_map/all_to_all | solution.py:170
  18.5 0.7 collective-permute-done
  19.2 1.8 %collective-permute-done.1 = bf16[640,640]{1,0:T(8,128)(2,1)} collective-permute-done((bf16[640,640]{1,0:T(8,128)(2,1)S(1)}, bf16[640,640]{1,0:T(8,128)(2,1)}, u32[]{:S(2)}, u32[]{:S(2)}) %collective-permute-start.1) | collective-permute-done | bytes 819232 | tf_op jit(solution)/shard_map/ppermute | solution.py:16
  21.0 4.6 %fusion = bf16[640,640]{1,0:T(8,128)(2,1)} fusion(bf16[640,640]{1,0:T(8,128)(2,1)} %collective-permute-done, bf16[640,640]{1,0:T(8,128)(2,1)} %collective-permute-done.1, bf16[1,640,640]{2,1,0:T(8,128)(2,1)S(1)} %copy-done, f32[]{:T(128)} %bitcast.29, f32[]{:T(128)} %bitcast.28, pred[640]{0:T(1024)(128)(4,1)S(1)} %iota_compare_fusion), kind=kOutput, calls=%fused_computation.2 | convolution fusion | flops 1051852800 | bytes 3277448 | tf_op jit(solution)/shard_map/dot_general | solution.py:181
  25.6 4.7 %all-to-all-done.1.refs_7_ = bf16[4,160,640]{2,1,0:T(8,128)(2,1)S(1)} async-done(((bf16[4,160,640]{2,1,0:T(8,128)(2,1)}), bf16[4,160,640]{2,1,0:T(8,128)(2,1)S(1)}, u32[]{:S(2)}, u32[]{:S(2)}) %all-to-all-start.1) | async-done | bytes 819232 | tf_op jit(solution)/shard_map/all_to_all | solution.py:170
  30.3 4.3 %all-to-all-start = ((bf16[4,160,640]{2,1,0:T(8,128)(2,1)}), bf16[4,160,640]{2,1,0:T(8,128)(2,1)S(1)}, u32[]{:S(2)}, u32[]{:S(2)}) async-start(bf16[4,160,640]{2,1,0:T(8,128)(2,1)} %bitcast.9), calls=%async_computation | async-start | bytes 1638400 | tf_op jit(solution)/shard_map/all_to_all | solution.py:185
  34.6 1.0 fusion.16
  35.6 3.2 %collective-permute-start.9 = (bf16[2,160,640]{2,1,0:T(8,128)(2,1)}, bf16[2,160,640]{2,1,0:T(8,128)(2,1)S(1)}, u32[]{:S(2)}, u32[]{:S(2)}) collective-permute-start(bf16[2,160,640]{2,1,0:T(8,128)(2,1)} %get-tuple-element.5), channel_id=1, source_target_pairs={{0,96},{32,0},{64,32},{96,64},{1,97},{33,1},{65,33},{97,65},{2,98}... | collective-permute-start | bytes 1228808 | tf_op jit(solution)/shard_map/ppermute | solution.py:21
  38.8 0.0 collective-permute-start.10
  38.8 3.2 %collective-permute-start.11 = (bf16[2,160,640]{2,1,0:T(8,128)(2,1)}, bf16[2,160,640]{2,1,0:T(8,128)(2,1)}, u32[]{:S(2)}, u32[]{:S(2)}) collective-permute-start(bf16[2,160,640]{2,1,0:T(8,128)(2,1)} %get-tuple-element.6), channel_id=1, source_target_pairs={{0,96},{32,0},{64,32},{96,64},{1,97},{33,1},{65,33},{97,65},{2,98}... | collective-permute-start | bytes 1228808 | tf_op jit(solution)/shard_map/ppermute | solution.py:21
  42.1 0.0 collective-permute-start.8
  42.1 13.9 %collective-permute-done.9.refs_9_ = bf16[2,160,640]{2,1,0:T(8,128)(2,1)S(1)} collective-permute-done((bf16[2,160,640]{2,1,0:T(8,128)(2,1)}, bf16[2,160,640]{2,1,0:T(8,128)(2,1)S(1)}, u32[]{:S(2)}, u32[]{:S(2)}) %collective-permute-start.9) | collective-permute-done | bytes 409632 | tf_op jit(solution)/shard_map/ppermute | solution.py:21
  56.0 0.9 collective-permute-start.13
  56.9 0.0 all-to-all-done.refs_0_
  56.9 1.0 fusion.17
  57.9 1.2 collective-permute-start.3
  59.1 0.0 collective-permute-done.10.refs_10_
  59.1 0.8 collective-permute-start.2
  59.9 4.1 %collective-permute-done.8.refs_8_ = bf16[2,160,640]{2,1,0:T(8,128)(2,1)} collective-permute-done((bf16[2,160,640]{2,1,0:T(8,128)(2,1)}, bf16[2,160,640]{2,1,0:T(8,128)(2,1)}, u32[]{:S(2)}, u32[]{:S(2)}) %collective-permute-start.8) | collective-permute-done | bytes 409632 | tf_op jit(solution)/shard_map/ppermute | solution.py:21
  64.0 0.0 collective-permute-start.12
  64.0 0.9 collective-permute-done.11.refs_11_
  64.9 0.6 collective-permute-start.4
  65.5 6.1 %collective-permute-done.13.refs_13_ = bf16[2,160,640]{2,1,0:T(8,128)(2,1)} collective-permute-done((bf16[2,160,640]{2,1,0:T(8,128)(2,1)S(1)}, bf16[2,160,640]{2,1,0:T(8,128)(2,1)}, u32[]{:S(2)}, u32[]{:S(2)}) %collective-permute-start.13) | collective-permute-done | bytes 409632 | tf_op jit(solution)/shard_map/ppermute | solution.py:21
  71.5 1.6 %collective-permute-start.5 = (bf16[2,160,640]{2,1,0:T(8,128)(2,1)}, bf16[2,160,640]{2,1,0:T(8,128)(2,1)}, u32[]{:S(2)}, u32[]{:S(2)}) collective-permute-start(bf16[2,160,640]{2,1,0:T(8,128)(2,1)} %get-tuple-element.8), channel_id=1, source_target_pairs={{0,24},{8,0},{16,8},{24,16},{1,25},{9,1},{17,9},{25,17},{2,26},{10... | collective-permute-start | bytes 1228808 | tf_op jit(solution)/shard_map/ppermute | solution.py:21
  73.2 0.0 collective-permute-done.3.refs_2_
  73.2 0.7 collective-permute-start.7
  73.9 0.0 collective-permute-done.2.refs_1_
  73.9 1.3 collective-permute-start.6
  75.2 0.8 dynamic-slice_bitcast_fusion
  76.0 0.1 copy.9.rates
  76.1 0.1 pad_add_fusion.scalars
  76.2 0.0 collective-permute-done.12.refs_12_
  76.2 4.0 %collective-permute-done.4.refs_3_ = bf16[2,160,640]{2,1,0:T(8,128)(2,1)} collective-permute-done((bf16[2,160,640]{2,1,0:T(8,128)(2,1)}, bf16[2,160,640]{2,1,0:T(8,128)(2,1)}, u32[]{:S(2)}, u32[]{:S(2)}) %collective-permute-start.4) | collective-permute-done | bytes 409632 | tf_op jit(solution)/shard_map/ppermute | solution.py:21
  80.2 4.0 %collective-permute-done.5.refs_4_ = bf16[2,160,640]{2,1,0:T(8,128)(2,1)} collective-permute-done((bf16[2,160,640]{2,1,0:T(8,128)(2,1)}, bf16[2,160,640]{2,1,0:T(8,128)(2,1)}, u32[]{:S(2)}, u32[]{:S(2)}) %collective-permute-start.5) | collective-permute-done | bytes 409632 | tf_op jit(solution)/shard_map/ppermute | solution.py:21
  84.3 5.7 %collective-permute-done.7.refs_6_ = bf16[2,160,640]{2,1,0:T(8,128)(2,1)} collective-permute-done((bf16[2,160,640]{2,1,0:T(8,128)(2,1)}, bf16[2,160,640]{2,1,0:T(8,128)(2,1)}, u32[]{:S(2)}, u32[]{:S(2)}) %collective-permute-start.7) | collective-permute-done | bytes 409632 | tf_op jit(solution)/shard_map/ppermute | solution.py:21
  90.0 0.0 collective-permute-done.6.refs_5_
  90.0 23.7 %convolve.1 = bf16[16,40,640]{2,1,0:T(8,128)(2,1)S(1)} custom-call(s32[3]{0:T(128)S(1)} %pad_add_fusion.scalars, f32[160,1]{1,0:T(8,128)S(1)} %copy.9.rates, bf16[4,160,640]{2,1,0:T(8,128)(2,1)S(1)} %all-to-all-done.refs_0_, bf16[2,160,640]{2,1,0:T(8,128)(2,1)} %collective-permute-done.2.refs_1_, bf16[2,160,640]{2,1,0:T(8,128)(2,1)} %collective-permute-done.3.refs_2_, ...), custom_call_target="tpu_custom_call" | custom-call | flops 4456448000 | bytes 6553600 | tf_op jit(solution)/shard_map/convolve/pallas_call | solution.py:111
  113.7 19.6 %all_to_all.15.packets = bf16[16,40,640]{2,1,0:T(8,128)(2,1)} all-to-all(bf16[16,40,640]{2,1,0:T(8,128)(2,1)S(1)} %convolve.1), channel_id=1, replica_groups=mesh['tx'=4,'ty'=4,'sector'=8] {'tx','ty'}, dimensions={0} | all-to-all | bytes 1638400 | tf_op jit(solution)/shard_map/all_to_all | solution.py:192
  133.3 2.4 %assemble.1 = bf16[640,640]{1,0:T(8,128)(2,1)} custom-call(bf16[16,40,640]{2,1,0:T(8,128)(2,1)} %all_to_all.15.packets), custom_call_target="tpu_custom_call" | custom-call | tf_op jit(solution)/shard_map/assemble/pallas_call | solution.py:148
  (2 shorter events, 0.0 us)
Async XLA Ops:
  0.0 1.2 copy-start
  1.2 6.0 %copy-start.1 = (bf16[1,1,640,640]{3,2,1,0:T(8,128)(2,1)S(1)}, bf16[1,1,640,640]{3,2,1,0:T(8,128)(2,1)}, u32[]{:S(2)}) copy-start(bf16[1,1,640,640]{3,2,1,0:T(8,128)(2,1)} %param.6) | copy-start | bytes 2457604
  5.3 14.0 %collective-permute-start = (bf16[640,640]{1,0:T(8,128)(2,1)}, bf16[640,640]{1,0:T(8,128)(2,1)}, u32[]{:S(2)}, u32[]{:S(2)}) collective-permute-start(bf16[640,640]{1,0:T(8,128)(2,1)} %convolution_convert_fusion.1), channel_id=1, source_target_pairs={{0,1},{1,2},{2,3},{3,4},{4,5},{5,6},{6,7},{8,9},{9,10},{10,11},{11... | collective-permute-start | bytes 2457608 | tf_op jit(solution)/shard_map/ppermute | solution.py:16
  7.5 13.5 %collective-permute-start.1 = (bf16[640,640]{1,0:T(8,128)(2,1)S(1)}, bf16[640,640]{1,0:T(8,128)(2,1)}, u32[]{:S(2)}, u32[]{:S(2)}) collective-permute-start(bf16[640,640]{1,0:T(8,128)(2,1)S(1)} %and_select_fusion.1), channel_id=1, source_target_pairs={{1,0},{2,1},{3,2},{4,3},{5,4},{6,5},{7,6},{9,8},{10,9},{11,10},{12... | collective-permute-start | bytes 2457608 | tf_op jit(solution)/shard_map/ppermute | solution.py:16
  12.8 17.6 %all-to-all-start.1 = ((bf16[4,160,640]{2,1,0:T(8,128)(2,1)}), bf16[4,160,640]{2,1,0:T(8,128)(2,1)S(1)}, u32[]{:S(2)}, u32[]{:S(2)}) async-start(bf16[4,160,640]{2,1,0:T(8,128)(2,1)} %bitcast.11), calls=%async_computation.1 | async-start | bytes 1638400 | tf_op jit(solution)/shard_map/all_to_all | solution.py:170
  30.3 26.5 %all-to-all-start = ((bf16[4,160,640]{2,1,0:T(8,128)(2,1)}), bf16[4,160,640]{2,1,0:T(8,128)(2,1)S(1)}, u32[]{:S(2)}, u32[]{:S(2)}) async-start(bf16[4,160,640]{2,1,0:T(8,128)(2,1)} %bitcast.9), calls=%async_computation | async-start | bytes 1638400 | tf_op jit(solution)/shard_map/all_to_all | solution.py:185
  35.6 20.4 %collective-permute-start.9 = (bf16[2,160,640]{2,1,0:T(8,128)(2,1)}, bf16[2,160,640]{2,1,0:T(8,128)(2,1)S(1)}, u32[]{:S(2)}, u32[]{:S(2)}) collective-permute-start(bf16[2,160,640]{2,1,0:T(8,128)(2,1)} %get-tuple-element.5), channel_id=1, source_target_pairs={{0,96},{32,0},{64,32},{96,64},{1,97},{33,1},{65,33},{97,65},{2,98}... | collective-permute-start | bytes 1228808 | tf_op jit(solution)/shard_map/ppermute | solution.py:21
  38.8 20.2 %collective-permute-start.10 = (bf16[2,160,640]{2,1,0:T(8,128)(2,1)}, bf16[2,160,640]{2,1,0:T(8,128)(2,1)S(1)}, u32[]{:S(2)}, u32[]{:S(2)}) collective-permute-start(bf16[2,160,640]{2,1,0:T(8,128)(2,1)} %get-tuple-element.5), channel_id=1, source_target_pairs={{0,32},{32,64},{64,96},{96,0},{1,33},{33,65},{65,97},{97,1},{2,34}... | collective-permute-start | bytes 1228808 | tf_op jit(solution)/shard_map/ppermute | solution.py:21
  38.8 26.1 %collective-permute-start.11 = (bf16[2,160,640]{2,1,0:T(8,128)(2,1)}, bf16[2,160,640]{2,1,0:T(8,128)(2,1)}, u32[]{:S(2)}, u32[]{:S(2)}) collective-permute-start(bf16[2,160,640]{2,1,0:T(8,128)(2,1)} %get-tuple-element.6), channel_id=1, source_target_pairs={{0,96},{32,0},{64,32},{96,64},{1,97},{33,1},{65,33},{97,65},{2,98}... | collective-permute-start | bytes 1228808 | tf_op jit(solution)/shard_map/ppermute | solution.py:21
  42.1 21.9 %collective-permute-start.8 = (bf16[2,160,640]{2,1,0:T(8,128)(2,1)}, bf16[2,160,640]{2,1,0:T(8,128)(2,1)}, u32[]{:S(2)}, u32[]{:S(2)}) collective-permute-start(bf16[2,160,640]{2,1,0:T(8,128)(2,1)} %get-tuple-element.6), channel_id=1, source_target_pairs={{0,32},{32,64},{64,96},{96,0},{1,33},{33,65},{65,97},{97,1},{2,34}... | collective-permute-start | bytes 1228808 | tf_op jit(solution)/shard_map/ppermute | solution.py:21
  56.0 15.5 %collective-permute-start.13 = (bf16[2,160,640]{2,1,0:T(8,128)(2,1)S(1)}, bf16[2,160,640]{2,1,0:T(8,128)(2,1)}, u32[]{:S(2)}, u32[]{:S(2)}) collective-permute-start(bf16[2,160,640]{2,1,0:T(8,128)(2,1)S(1)} %collective-permute-done.9.refs_9_), channel_id=1, source_target_pairs={{0,96},{32,0},{64,32},{96,64},{1,97},{33,1},{65,33},{97,65},{2,98}... | collective-permute-start | bytes 1228808 | tf_op jit(solution)/shard_map/ppermute | solution.py:21
  57.9 15.3 %collective-permute-start.3 = (bf16[2,160,640]{2,1,0:T(8,128)(2,1)}, bf16[2,160,640]{2,1,0:T(8,128)(2,1)}, u32[]{:S(2)}, u32[]{:S(2)}) collective-permute-start(bf16[2,160,640]{2,1,0:T(8,128)(2,1)} %get-tuple-element.7), channel_id=1, source_target_pairs={{0,24},{8,0},{16,8},{24,16},{1,25},{9,1},{17,9},{25,17},{2,26},{10... | collective-permute-start | bytes 1228808 | tf_op jit(solution)/shard_map/ppermute | solution.py:21
  59.1 14.9 %collective-permute-start.2 = (bf16[2,160,640]{2,1,0:T(8,128)(2,1)}, bf16[2,160,640]{2,1,0:T(8,128)(2,1)}, u32[]{:S(2)}, u32[]{:S(2)}) collective-permute-start(bf16[2,160,640]{2,1,0:T(8,128)(2,1)} %get-tuple-element.8), channel_id=1, source_target_pairs={{0,8},{8,16},{16,24},{24,0},{1,9},{9,17},{17,25},{25,1},{2,10},{10... | collective-permute-start | bytes 1228808 | tf_op jit(solution)/shard_map/ppermute | solution.py:21
  64.0 12.2 %collective-permute-start.12 = (bf16[2,160,640]{2,1,0:T(8,128)(2,1)}, bf16[2,160,640]{2,1,0:T(8,128)(2,1)}, u32[]{:S(2)}, u32[]{:S(2)}) collective-permute-start(bf16[2,160,640]{2,1,0:T(8,128)(2,1)} %collective-permute-done.8.refs_8_), channel_id=1, source_target_pairs={{0,32},{32,64},{64,96},{96,0},{1,33},{33,65},{65,97},{97,1},{2,34}... | collective-permute-start | bytes 1228808 | tf_op jit(solution)/shard_map/ppermute | solution.py:21
  64.9 15.3 %collective-permute-start.4 = (bf16[2,160,640]{2,1,0:T(8,128)(2,1)}, bf16[2,160,640]{2,1,0:T(8,128)(2,1)}, u32[]{:S(2)}, u32[]{:S(2)}) collective-permute-start(bf16[2,160,640]{2,1,0:T(8,128)(2,1)} %get-tuple-element.7), channel_id=1, source_target_pairs={{0,8},{8,16},{16,24},{24,0},{1,9},{9,17},{17,25},{25,1},{2,10},{10... | collective-permute-start | bytes 1228808 | tf_op jit(solution)/shard_map/ppermute | solution.py:21
  71.5 12.7 %collective-permute-start.5 = (bf16[2,160,640]{2,1,0:T(8,128)(2,1)}, bf16[2,160,640]{2,1,0:T(8,128)(2,1)}, u32[]{:S(2)}, u32[]{:S(2)}) collective-permute-start(bf16[2,160,640]{2,1,0:T(8,128)(2,1)} %get-tuple-element.8), channel_id=1, source_target_pairs={{0,24},{8,0},{16,8},{24,16},{1,25},{9,1},{17,9},{25,17},{2,26},{10... | collective-permute-start | bytes 1228808 | tf_op jit(solution)/shard_map/ppermute | solution.py:21
  73.2 16.8 %collective-permute-start.7 = (bf16[2,160,640]{2,1,0:T(8,128)(2,1)}, bf16[2,160,640]{2,1,0:T(8,128)(2,1)}, u32[]{:S(2)}, u32[]{:S(2)}) collective-permute-start(bf16[2,160,640]{2,1,0:T(8,128)(2,1)} %collective-permute-done.3.refs_2_), channel_id=1, source_target_pairs={{0,24},{8,0},{16,8},{24,16},{1,25},{9,1},{17,9},{25,17},{2,26},{10... | collective-permute-start | bytes 1228808 | tf_op jit(solution)/shard_map/ppermute | solution.py:21
  73.9 16.0 %collective-permute-start.6 = (bf16[2,160,640]{2,1,0:T(8,128)(2,1)}, bf16[2,160,640]{2,1,0:T(8,128)(2,1)}, u32[]{:S(2)}, u32[]{:S(2)}) collective-permute-start(bf16[2,160,640]{2,1,0:T(8,128)(2,1)} %collective-permute-done.2.refs_1_), channel_id=1, source_target_pairs={{0,8},{8,16},{16,24},{24,0},{1,9},{9,17},{17,25},{25,1},{2,10},{10... | collective-permute-start | bytes 1228808 | tf_op jit(solution)/shard_map/ppermute | solution.py:21

commit v2 on v1

v2 whole, which is shorter than its diff:
```python
import functools

import jax
import jax.numpy as jnp
import numpy as np
from jax import lax
from jax.experimental import pallas as pl
from jax.experimental.pallas import tpu as pltpu
from jax.sharding import Mesh
from jax.sharding import PartitionSpec as P

MIB = 1024 * 1024
VMEM = pl.BlockSpec(memory_space=pltpu.VMEM)
SMEM = pl.BlockSpec(memory_space=pltpu.SMEM)
ANY = pl.BlockSpec(memory_space=pl.ANY)
NT = (((1,), (1,)), ((), ()))


def shifted(block, axis, distance):
    devices = range(lax.axis_size(axis))
    route = [(i - distance, i) for i in devices if i - distance in devices]
    return lax.ppermute(block, axis, route)


def ring(block, axis, distance):
    n = lax.axis_size(axis)
    return lax.ppermute(block, axis, [(i, (i + distance) % n) for i in range(n)])


def tied(value, *others):
    return lax.optimization_barrier((value, *others))[0]


def halves_gather(first, second, axis):
    below_a = ring(first, axis, 1)
    above_b = ring(second, axis, -1)
    below_b = ring(second, axis, 1)
    above_a = ring(first, axis, -1)
    far_a = ring(below_a, axis, 1)
    far_b = ring(above_b, axis, -1)
    return [
        (-1, 0, below_a),
        (1, 1, above_b),
        (-1, 1, below_b),
        (1, 0, above_a),
        (2, 0, far_a),
        (2, 1, far_b),
    ]


def live(shape, size, first_row=0):
    row = lax.broadcasted_iota(jnp.int32, shape, 0) + first_row
    column = lax.broadcasted_iota(jnp.int32, shape, 1)
    return (row < size) & (column < size)


def masked_block(value, size, first_row=0):
    wide = value.astype(jnp.float32)
    return jnp.where(live(value.shape, size, first_row), wide, 0.0).astype(jnp.bfloat16)


def dot(a, b):
    return jnp.dot(a, b, preferred_element_type=jnp.float32)


def turn_kernel(scalars, prop, turned):
    turned[...] = masked_block(prop[...], scalars[2]).T


def turn(scalars, prop):
    return pl.pallas_call(
        turn_kernel,
        out_shape=jax.ShapeDtypeStruct(prop.shape, jnp.bfloat16),
        in_specs=[SMEM, VMEM],
        out_specs=VMEM,
        cost_estimate=pl.CostEstimate(flops=0, bytes_accessed=4 * prop.size, transcendentals=0),
        name="turn",
    )(scalars, prop)


def raise_kernel(scalars, prop, operator, upward, flipped):
    inner = masked_block(prop[...], scalars[2])
    r = operator[...]
    raised = dot(r, inner).astype(jnp.bfloat16)
    upward[...] = lax.dot_general(raised, r, NT, preferred_element_type=jnp.float32).astype(
        jnp.bfloat16
    )
    flipped[...] = r.T


def raise_terms(scalars, prop, operator):
    states = prop.shape[0]
    square = jax.ShapeDtypeStruct((states, states), jnp.bfloat16)
    return pl.pallas_call(
        raise_kernel,
        out_shape=(square, square),
        in_specs=[SMEM, VMEM, VMEM],
        out_specs=(VMEM, VMEM),
        cost_estimate=pl.CostEstimate(
            flops=4 * states**3, bytes_accessed=8 * states**2, transcendentals=0
        ),
        name="raise_terms",
    )(scalars, prop, operator)


def energy_kernel(scalars, weights, above, below, operator, flipped, *outs):
    n = len(outs)
    rows = outs[0].shape[0]
    here_x, size, size_above = scalars[0], scalars[2], scalars[3]
    inner = masked_block(above[...], size_above)
    r = operator[...]
    for d in (2, 1, 3, 0):
        first = pl.multiple_of(lax.rem(here_x + d, n) * rows, 32)
        lowered = dot(flipped[pl.ds(first, rows), :], inner).astype(jnp.bfloat16)
        downward = dot(lowered, r)
        raised = below[pl.ds(first, rows), :].astype(jnp.float32)
        both = weights[0] * raised + weights[1] * downward
        outs[d][...] = jnp.where(live(both.shape, size, first), both, 0.0).astype(jnp.bfloat16)


def energy_blocks(scalars, weights, above, below, operator, flipped, n):
    states = above.shape[0]
    block = jax.ShapeDtypeStruct((states // n, states), jnp.bfloat16)
    return pl.pallas_call(
        energy_kernel,
        out_shape=(block,) * n,
        in_specs=[SMEM, SMEM, VMEM, VMEM, VMEM, VMEM],
        out_specs=(VMEM,) * n,
        cost_estimate=pl.CostEstimate(
            flops=4 * states**3, bytes_accessed=10 * states**2, transcendentals=0
        ),
        name="energy_blocks",
    )(scalars, weights, above, below, operator, flipped)


def convolve_kernel(plan, n, step_size, scalars, rates, *refs):
    parts = refs[: len(plan)]
    out, e_all, g_all, total, sems = refs[len(plan) :]
    rows = out.shape[1] * n
    here_x, here_y, size = scalars[0], scalars[1], scalars[2]

    def around(here, offset):
        return lax.rem(here + offset + n, n)

    copies = []
    for part, (kind, dx, dy, half) in zip(parts, plan):
        x, y = around(here_x, dx), around(here_y, dy)
        if kind == "block":
            copies.append((part, e_all.at[x, y]))
        elif kind == "rest":
            tall = part.shape[1]
            for d in range(1, n):
                room = e_all.at[around(here_x, -d), y, pl.ds(half * tall, tall)]
                copies.append((part.at[d - 1], room))
        elif kind == "column":
            copies.append((part, g_all.at[x]))
        else:
            some = part.shape[0]
            copies.append((part, g_all.at[x, pl.ds(half * some, some)]))
    started = [
        pltpu.make_async_copy(src, dst, sems.at[i]) for i, (src, dst) in enumerate(copies)
    ]
    for copy in started:
        copy.start()
    for copy in started:
        copy.wait()

    lags = e_all.reshape(n * n, *e_all.shape[2:])
    for u in range(n * n):
        right = g_all[u // n, u % n]
        for first in range(0, n * n - u, n):
            some = min(n, n * n - u - first)
            left = lags[first : first + some].reshape(some * rows, -1)
            product = lax.dot_general(left, right, NT, preferred_element_type=jnp.float32)
            where = slice((u + first) * rows, (u + first + some) * rows)
            if u == 0:
                total[where] = product
            else:
                total[where] += product

    quarter = rows // n
    scale = step_size * step_size
    for b in range(n):
        row = lax.broadcasted_iota(jnp.int32, (quarter, rows), 0) + b * quarter
        column = lax.broadcasted_iota(jnp.int32, (quarter, rows), 1)
        starts = (row == column) & (here_x == here_y) & (row + here_x * rows < size)
        rate = rates[b * quarter : (b + 1) * quarter]
        decay = jnp.broadcast_to(jnp.exp(-step_size * rate), (quarter, rows))
        for t in range(n * n):
            term = scale * total[t * rows + b * quarter : t * rows + (b + 1) * quarter]
            fresh = (jnp.where(starts, 1.0, 0.0) if t == 0 else decay * fresh) - term
            out[t, :, b * rows : (b + 1) * rows] = fresh.astype(jnp.bfloat16)


def convolve(parts, plan, scalars, rates, n, step_size):
    rows, states = parts[0].shape
    copies = sum(n - 1 if kind == "rest" else 1 for kind, *_ in plan)
    return pl.pallas_call(
        functools.partial(convolve_kernel, plan, n, step_size),
        out_shape=jax.ShapeDtypeStruct((n * n, rows // n, states), jnp.bfloat16),
        in_specs=[SMEM, VMEM] + [ANY] * len(parts),
        out_specs=VMEM,
        scratch_shapes=[
            pltpu.VMEM((n, n, rows, states), jnp.bfloat16),
            pltpu.VMEM((n, n, rows, states), jnp.bfloat16),
            pltpu.VMEM((n * n * rows, rows), jnp.float32),
            pltpu.SemaphoreType.DMA((copies,)),
        ],
        compiler_params=pltpu.CompilerParams(vmem_limit_bytes=32 * MIB),
        cost_estimate=pl.CostEstimate(
            flops=n * n * (n * n + 1) * rows * rows * states,
            bytes_accessed=4 * n * n * rows * states,
            transcendentals=0,
        ),
        name="convolve",
    )(scalars, rates, *parts)


def assemble_kernel(n, packets, out):
    quarter, states = packets.shape[1:]
    rows = states // n
    for x in range(n):
        for b in range(n):
            out[x * rows + b * quarter : x * rows + (b + 1) * quarter, :] = jnp.concatenate(
                [packets[x * n + y, :, b * rows : (b + 1) * rows] for y in range(n)], axis=1
            )


def assemble(packets, n):
    states = packets.shape[2]
    return pl.pallas_call(
        functools.partial(assemble_kernel, n),
        out_shape=jax.ShapeDtypeStruct((states, states), jnp.bfloat16),
        in_specs=[VMEM],
        out_specs=VMEM,
        name="assemble",
    )(packets)


def per_device(propagator, rising_op, energies, hyb_particle, hyb_hole, sector_sizes):
    states = propagator.shape[2]
    n = lax.axis_size("tx")
    step_size = 1.0 / (n * n)
    rows = states // n
    here_x, here_y = lax.axis_index("tx"), lax.axis_index("ty")
    raw, operator = propagator[0, 0], rising_op[0]

    above = shifted(raw, "sector", -1)
    size_above = shifted(sector_sizes, "sector", -1)
    scalars = jnp.stack([here_x, here_y, sector_sizes[0]]).astype(jnp.int32)
    turned = turn(scalars, raw)
    columns = lax.all_to_all(turned.reshape(n, rows, states), "ty", 0, 0, tiled=True)

    upward, flipped = raise_terms(scalars, tied(raw, turned), operator)
    below = shifted(upward, "sector", 1)
    scalars = jnp.stack([here_x, here_y, sector_sizes[0], size_above[0]]).astype(jnp.int32)
    weights = jnp.concatenate([hyb_particle, hyb_hole])
    own, *away = energy_blocks(scalars, weights, above, below, operator, flipped, n)

    crossed = [ring(away[d - 1], "tx", d) for d in (2, 1, 3)]
    crossed = [crossed[1], crossed[0], crossed[2]]
    parts, plan = [own], [("block", 0, 0, 0)]
    spread = [ring(own, "ty", d) for d in (1, -1, 2)]
    *crossed, a, b, c = lax.optimization_barrier((*crossed, *spread))
    for d, piece in zip((1, -1, 2), (a, b, c)):
        parts.append(piece)
        plan.append(("block", 0, -d, 0))
    for d in range(1, n):
        parts.append(crossed[d - 1])
        plan.append(("block", -d, 0, 0))
    half = rows // 2
    first = jnp.stack([block[:half] for block in crossed])
    second = jnp.stack([block[half:] for block in crossed])
    for offset, which, piece in halves_gather(first, second, "ty"):
        parts.append(piece)
        plan.append(("rest", 0, offset, which))

    parts.append(columns)
    plan.append(("column", 0, 0, 0))
    for offset, which, piece in halves_gather(columns[: n // 2], columns[n // 2 :], "tx"):
        parts.append(piece)
        plan.append(("columns", offset, 0, which))

    rates = lax.dynamic_slice_in_dim(energies[0], here_x * rows, rows, 0)[:, None]
    packets = convolve(parts, plan, scalars, rates, n, step_size)
    packets = lax.all_to_all(packets, ("tx", "ty"), 0, 0, tiled=True)
    return assemble(packets, n)[None, None]


def solution(mesh):
    n = round(mesh.shape["tm"] ** 0.5)
    split = Mesh(
        np.asarray(mesh.devices).reshape(n, n, mesh.shape["sector"]), ("tx", "ty", "sector")
    )
    times = ("tx", "ty")
    placed = (
        P("sector", times, None, None),
        P("sector", None, None),
        P("sector", None),
        P(times),
        P(times),
        P("sector"),
    )
    return jax.shard_map(
        per_device,
        mesh=split,
        in_specs=placed,
        out_specs=P("sector", times, None, None),
        check_vma=False,
    )
```

time: 138 us -> 127 us (0.920); the launches traced: 136 us -> 127 us
  waiting for transfers between devices: 46 us -> 26.8 us
  starting transfers between devices: 27.9 us -> 42 us
  matrix products: 8.7 us -> 0 us
  other arithmetic: 0.71 us -> 3.37 us
  local copies, waits for them, and re-layouts: 4.53 us -> 6.92 us
  blocking collectives: 19.6 us -> 17.3 us
  Pallas kernels: 26.1 us -> 28.1 us
    ppermute x12 -> x18, starting transfers between devices: 13.6 us -> 30.3 us  [ring(): lax.ppermute(block, axis, [(i, (i + distance) % n) for i in range(n)])]
    ppermute x12 -> x18, waiting for transfers between devices: 38.8 us -> 25.8 us  [ring(): lax.ppermute(block, axis, [(i, (i + distance) % n) for i in range(n)])]
    dot_general x2 -> x0, matrix products: 8.7 us -> none  [the longest x1 4.6 us: per_device(): downward = jnp.dot(lowered, operator, preferred_element_type=jnp.float32)]
    unnamed x4 -> x22, local copies, waits for them, and re-layouts: 0.42 us -> 6.61 us
    all_to_all x2 -> x1, waiting for transfers between devices: 4.74 us -> 0.01 us  [per_device(): lax.all_to_all(turned.reshape(n, rows, states), 'ty', 0, 0, tiled=True)]
    all_to_all x2 -> x1, starting transfers between devices: 8.75 us -> 4.48 us  [per_device(): lax.all_to_all(turned.reshape(n, rows, states), 'ty', 0, 0, tiled=True)]
    all_to_all x1, blocking collectives: 19.6 us -> 17.3 us  [per_device(): packets = lax.all_to_all(packets, ('tx', 'ty'), 0, 0, tiled=True)]
    another operation x0 -> x3, other arithmetic: none -> 2.09 us  [the longest x1 1.28 us: per_device(): jnp.stack([here_x, here_y, sector_sizes[0], size_above[0]])]
  transfers between devices with their start and end apart: 16 -> 22, of which waited for: 10 -> 7; matrix products, arithmetic and copies ran while one was open for 7% -> 3% of each run, Pallas kernels for 0% -> 9%
where the time goes in v2:
time: 127 us
  starting transfers between devices  42 us (33%)
  Pallas kernels  28.1 us (22%)
  waiting for transfers between devices  26.8 us (21%)
  blocking collectives  17.3 us (14%)
  local copies, waits for them, and re-layouts  6.92 us (5%)
  other arithmetic  3.37 us (3%)
  between operations  2.05 us (2%)
    ppermute x18, starting transfers between devices, ring(): lax.ppermute(block, axis, [(i, (i + distance) % n) for i in range(n)])  30.3 us
    ppermute x18, waiting for transfers between devices, ring(): lax.ppermute(block, axis, [(i, (i + distance) % n) for i in range(n)])  25.8 us
    all_to_all x1, blocking collectives, per_device(): packets = lax.all_to_all(packets, ('tx', 'ty'), 0, 0, tiled=True)  17.3 us
    pallas_call x1, Pallas kernels, convolve(): pl.pallas_call(functools.partial(convolve_kernel, plan, n, step_size), ou...  14.8 us
    ppermute x3, starting transfers between devices, shifted(): return lax.ppermute(block, axis, route)  7.3 us
    unnamed x22, local copies, waits for them, and re-layouts  6.61 us
    all_to_all x1, starting transfers between devices, per_device(): lax.all_to_all(turned.reshape(n, rows, states), 'ty', 0, 0, tiled=True)  4.48 us
    pallas_call x1, Pallas kernels, energy_blocks(): pl.pallas_call(energy_kernel, out_shape=(block,) * n, in_specs=[SMEM, SME...  4.42 us
  transfers between devices with their start and end apart: 22, of which 7 were waited for; matrix products, arithmetic and copies ran while one was open for 3% of the time, Pallas kernels for 9%

profile of v2, /device:TPU:32, one launch (start us, length us, event | category | flops | bytes accessed | tf_op | source)
XLA Modules:
  0.0 126.6 jit_solution(6782837229226058213)
XLA Ops:
  0.0 2.0 %collective-permute-start.1 = (bf16[640,640]{1,0:T(8,128)(2,1)}, bf16[640,640]{1,0:T(8,128)(2,1)S(1)}, u32[]{:S(2)}, u32[]{:S(2)}) collective-permute-start(bf16[640,640]{1,0:T(8,128)(2,1)} %bitcast.20), channel_id=1, source_target_pairs={{1,0},{2,1},{3,2},{4,3},{5,4},{6,5},{7,6},{9,8},{10,9},{11,10},{12... | collective-permute-start | bytes 2457608 | tf_op jit(solution)/shard_map/ppermute | solution.py:22
  2.7 0.7 pad_add_fusion.1.scalars
  3.4 2.4 %turn.1 = bf16[640,640]{1,0:T(8,128)(2,1)} custom-call(s32[3]{0:T(128)} %pad_add_fusion.1.scalars, bf16[640,640]{1,0:T(8,128)(2,1)} %bitcast.21), custom_call_target="tpu_custom_call" | custom-call | bytes 1638400 | tf_op jit(solution)/shard_map/turn/pallas_call | solution.py:71
  5.7 4.1 %raise_terms.1 = (bf16[640,640]{1,0:T(8,128)(2,1)}, bf16[640,640]{1,0:T(8,128)(2,1)}) custom-call(s32[3]{0:T(128)} %pad_add_fusion.1.scalars, bf16[640,640]{1,0:T(8,128)(2,1)} %bitcast.22, bf16[640,640]{1,0:T(8,128)(2,1)} %bitcast.23), custom_call_target="tpu_custom_call" | custom-call | flops 1048576000 | bytes 3276800 | tf_op jit(solution)/shard_map/raise_terms/pallas_call | solution.py:94
  9.9 2.4 %collective-permute-start.2 = (bf16[640,640]{1,0:T(8,128)(2,1)}, bf16[640,640]{1,0:T(8,128)(2,1)S(1)}, u32[]{:S(2)}, u32[]{:S(2)}) collective-permute-start(bf16[640,640]{1,0:T(8,128)(2,1)} %get-tuple-element.19), channel_id=1, source_target_pairs={{0,1},{1,2},{2,3},{3,4},{4,5},{5,6},{6,7},{8,9},{9,10},{10,11},{11... | collective-permute-start | bytes 2457608 | tf_op jit(solution)/shard_map/ppermute | solution.py:22
  12.3 4.5 %all-to-all-start = ((bf16[4,160,640]{2,1,0:T(8,128)(2,1)}), bf16[4,160,640]{2,1,0:T(8,128)(2,1)S(1)}, u32[]{:S(2)}, u32[]{:S(2)}) async-start(bf16[4,160,640]{2,1,0:T(8,128)(2,1)} %bitcast.11), calls=%async_computation | async-start | bytes 1638400 | tf_op jit(solution)/shard_map/all_to_all | solution.py:252
  16.7 2.9 %collective-permute-start = (s32[1]{0:T(128)}, s32[1]{0:T(128)}, u32[]{:S(2)}, u32[]{:S(2)}) collective-permute-start(s32[1]{0:T(128)} %param.11), channel_id=1, source_target_pairs={{1,0},{2,1},{3,2},{4,3},{5,4},{6,5},{7,6},{9,8},{10,9},{11,10},{12... | collective-permute-start | bytes 20 | tf_op jit(solution)/shard_map/ppermute | solution.py:22
  20.9 0.6 pad_maximum_fusion.2.weights
  21.5 1.3 %pad_add_fusion.scalars = s32[4]{0:T(128)} fusion(s32[1]{0:T(128)} %collective-permute-done, s32[1]{0:T(128)S(6)} %copy.10, s32[1]{0:T(128)} %bitcast.1, s32[1]{0:T(128)} %bitcast), kind=kLoop, calls=%fused_computation.9 | loop fusion | flops 12 | bytes 32 | tf_op jit(solution)/shard_map/stack | solution.py:256
  22.8 0.9 collective-permute-done.2.below
  23.7 0.9 copy-done.10
  24.6 4.4 %energy_blocks.1 = (bf16[160,640]{1,0:T(8,128)(2,1)}, bf16[160,640]{1,0:T(8,128)(2,1)}, bf16[160,640]{1,0:T(8,128)(2,1)}, bf16[160,640]{1,0:T(8,128)(2,1)}) custom-call(s32[4]{0:T(128)} %pad_add_fusion.scalars, f32[2]{0:T(128)} %pad_maximum_fusion.2.weights, bf16[640,640]{1,0:T(8,128)(2,1)} %copy-done.9, bf16[640,640]{1,0:T(8,128)(2,1)} %copy-done.10, ...), custom_call_target="tpu_custom_call" | custom-call | flops 1048576000 | bytes 4096000 | tf_op jit(solution)/shard_map/energy_blocks/pallas_call | solution.py:124
  29.0 1.5 %collective-permute-start.3 = (bf16[160,640]{1,0:T(8,128)(2,1)}, bf16[160,640]{1,0:T(8,128)(2,1)S(1)}, u32[]{:S(2)}, u32[]{:S(2)}) collective-permute-start(bf16[160,640]{1,0:T(8,128)(2,1)} %get-tuple-element.22), channel_id=1, source_target_pairs={{0,32},{32,64},{64,96},{96,0},{1,33},{33,65},{65,97},{97,1},{2,34}... | collective-permute-start | bytes 614408 | tf_op jit(solution)/shard_map/ppermute | solution.py:27
  30.5 3.2 %collective-permute-start.8 = (bf16[160,640]{1,0:T(8,128)(2,1)}, bf16[160,640]{1,0:T(8,128)(2,1)S(1)}, u32[]{:S(2)}, u32[]{:S(2)}) collective-permute-start(bf16[160,640]{1,0:T(8,128)(2,1)} %get-tuple-element.21.refs_0_), channel_id=1, source_target_pairs={{0,16},{8,24},{16,0},{24,8},{1,17},{9,25},{17,1},{25,9},{2,18},{10... | collective-permute-start | bytes 614408 | tf_op jit(solution)/shard_map/ppermute | solution.py:27
  33.7 1.1 collective-permute-start.7
  34.8 1.0 collective-permute-start.6
  35.8 2.7 %collective-permute-start.4 = (bf16[160,640]{1,0:T(8,128)(2,1)}, bf16[160,640]{1,0:T(8,128)(2,1)S(1)}, u32[]{:S(2)}, u32[]{:S(2)}) collective-permute-start(bf16[160,640]{1,0:T(8,128)(2,1)} %get-tuple-element.23), channel_id=1, source_target_pairs={{0,64},{32,96},{64,0},{96,32},{1,65},{33,97},{65,1},{97,33},{2,66}... | collective-permute-start | bytes 614408 | tf_op jit(solution)/shard_map/ppermute | solution.py:27
  38.5 1.4 %collective-permute-start.5 = (bf16[160,640]{1,0:T(8,128)(2,1)}, bf16[160,640]{1,0:T(8,128)(2,1)S(1)}, u32[]{:S(2)}, u32[]{:S(2)}) collective-permute-start(bf16[160,640]{1,0:T(8,128)(2,1)} %get-tuple-element.24), channel_id=1, source_target_pairs={{0,96},{32,0},{64,32},{96,64},{1,97},{33,1},{65,33},{97,65},{2,98}... | collective-permute-start | bytes 614408 | tf_op jit(solution)/shard_map/ppermute | solution.py:27
  40.0 4.5 %collective-permute-done.4.refs_5_ = bf16[160,640]{1,0:T(8,128)(2,1)S(1)} collective-permute-done((bf16[160,640]{1,0:T(8,128)(2,1)}, bf16[160,640]{1,0:T(8,128)(2,1)S(1)}, u32[]{:S(2)}, u32[]{:S(2)}) %collective-permute-start.4) | collective-permute-done | bytes 204832 | tf_op jit(solution)/shard_map/ppermute | solution.py:27
  44.5 2.4 %collective-permute-start.17 = (bf16[2,160,640]{2,1,0:T(8,128)(2,1)S(1)}, bf16[2,160,640]{2,1,0:T(8,128)(2,1)S(1)}, u32[]{:S(2)}, u32[]{:S(2)}) collective-permute-start(bf16[2,160,640]{2,1,0:T(8,128)(2,1)S(1)} %get-tuple-element.31), channel_id=1, source_target_pairs={{0,32},{32,64},{64,96},{96,0},{1,33},{33,65},{65,97},{97,1},{2,34}... | collective-permute-start | bytes 1228808 | tf_op jit(solution)/shard_map/ppermute | solution.py:27
  46.9 1.0 collective-permute-done.5.refs_6_
  48.0 2.7 %collective-permute-start.16 = (bf16[2,160,640]{2,1,0:T(8,128)(2,1)S(1)}, bf16[2,160,640]{2,1,0:T(8,128)(2,1)S(1)}, u32[]{:S(2)}, u32[]{:S(2)}) collective-permute-start(bf16[2,160,640]{2,1,0:T(8,128)(2,1)S(1)} %get-tuple-element.31), channel_id=1, source_target_pairs={{0,96},{32,0},{64,32},{96,64},{1,97},{33,1},{65,33},{97,65},{2,98}... | collective-permute-start | bytes 1228808 | tf_op jit(solution)/shard_map/ppermute | solution.py:27
  50.6 0.7 copy-done.3
  51.3 1.0 collective-permute-start.18
  52.3 0.7 copy-done.5
  53.0 1.1 collective-permute-start.15
  54.1 0.6 copy-done.7
  54.8 2.4 %collective-permute-start.12 = (bf16[3,80,640]{2,1,0:T(8,128)(2,1)S(1)}, bf16[3,80,640]{2,1,0:T(8,128)(2,1)S(1)}, u32[]{:S(2)}, u32[]{:S(2)}) collective-permute-start(bf16[3,80,640]{2,1,0:T(8,128)(2,1)S(1)} %pad_maximum_fusion), channel_id=1, source_target_pairs={{0,24},{8,0},{16,8},{24,16},{1,25},{9,1},{17,9},{25,17},{2,26},{10... | collective-permute-start | bytes 921608 | tf_op jit(solution)/shard_map/ppermute | solution.py:27
  57.2 0.8 pad_maximum_fusion.1
  58.0 0.5 collective-permute-start.9
  58.5 2.1 %collective-permute-done.16.refs_15_ = bf16[2,160,640]{2,1,0:T(8,128)(2,1)S(1)} collective-permute-done((bf16[2,160,640]{2,1,0:T(8,128)(2,1)S(1)}, bf16[2,160,640]{2,1,0:T(8,128)(2,1)S(1)}, u32[]{:S(2)}, u32[]{:S(2)}) %collective-permute-start.16) | collective-permute-done | bytes 409632 | tf_op jit(solution)/shard_map/ppermute | solution.py:27
  60.6 2.4 %collective-permute-start.10 = (bf16[3,80,640]{2,1,0:T(8,128)(2,1)}, bf16[3,80,640]{2,1,0:T(8,128)(2,1)}, u32[]{:S(2)}, u32[]{:S(2)}) collective-permute-start(bf16[3,80,640]{2,1,0:T(8,128)(2,1)} %pad_maximum_fusion.1), channel_id=1, source_target_pairs={{0,24},{8,0},{16,8},{24,16},{1,25},{9,1},{17,9},{25,17},{2,26},{10... | collective-permute-start | bytes 921608 | tf_op jit(solution)/shard_map/ppermute | solution.py:27
  63.0 5.8 %collective-permute-done.18.refs_17_ = bf16[2,160,640]{2,1,0:T(8,128)(2,1)S(1)} collective-permute-done((bf16[2,160,640]{2,1,0:T(8,128)(2,1)S(1)}, bf16[2,160,640]{2,1,0:T(8,128)(2,1)S(1)}, u32[]{:S(2)}, u32[]{:S(2)}) %collective-permute-start.18) | collective-permute-done | bytes 409632 | tf_op jit(solution)/shard_map/ppermute | solution.py:27
  68.8 3.2 %collective-permute-start.20 = (bf16[2,160,640]{2,1,0:T(8,128)(2,1)S(1)}, bf16[2,160,640]{2,1,0:T(8,128)(2,1)}, u32[]{:S(2)}, u32[]{:S(2)}) collective-permute-start(bf16[2,160,640]{2,1,0:T(8,128)(2,1)S(1)} %collective-permute-done.16.refs_15_), channel_id=1, source_target_pairs={{0,96},{32,0},{64,32},{96,64},{1,97},{33,1},{65,33},{97,65},{2,98}... | collective-permute-start | bytes 1228808 | tf_op jit(solution)/shard_map/ppermute | solution.py:27
  72.0 0.5 collective-permute-start.11
  72.5 0.5 collective-permute-start.13
  73.0 2.8 %collective-permute-start.14 = (bf16[3,80,640]{2,1,0:T(8,128)(2,1)}, bf16[3,80,640]{2,1,0:T(8,128)(2,1)}, u32[]{:S(2)}, u32[]{:S(2)}) collective-permute-start(bf16[3,80,640]{2,1,0:T(8,128)(2,1)} %collective-permute-done.10.refs_8_), channel_id=1, source_target_pairs={{0,24},{8,0},{16,8},{24,16},{1,25},{9,1},{17,9},{25,17},{2,26},{10... | collective-permute-start | bytes 921608 | tf_op jit(solution)/shard_map/ppermute | solution.py:27
  75.8 0.1 dynamic-slice_bitcast_fusion
  75.8 0.1 copy.7.rates
  76.0 7.9 %collective-permute-done.11.refs_9_ = bf16[3,80,640]{2,1,0:T(8,128)(2,1)} collective-permute-done((bf16[3,80,640]{2,1,0:T(8,128)(2,1)}, bf16[3,80,640]{2,1,0:T(8,128)(2,1)}, u32[]{:S(2)}, u32[]{:S(2)}) %collective-permute-start.11) | collective-permute-done | bytes 307232 | tf_op jit(solution)/shard_map/ppermute | solution.py:27
  83.9 4.5 %collective-permute-done.13.refs_11_ = bf16[3,80,640]{2,1,0:T(8,128)(2,1)} collective-permute-done((bf16[3,80,640]{2,1,0:T(8,128)(2,1)}, bf16[3,80,640]{2,1,0:T(8,128)(2,1)}, u32[]{:S(2)}, u32[]{:S(2)}) %collective-permute-start.13) | collective-permute-done | bytes 307232 | tf_op jit(solution)/shard_map/ppermute | solution.py:27
  88.3 0.9 copy-done.2
  89.3 0.9 copy-done.4
  90.2 0.9 copy-done.6
  91.1 0.9 copy-done.8
  92.0 14.8 %convolve.1 = bf16[16,40,640]{2,1,0:T(8,128)(2,1)S(1)} custom-call(s32[4]{0:T(128)S(1)} %copy-done.1, f32[160,1]{1,0:T(8,128)S(1)} %copy.7.rates, bf16[160,640]{1,0:T(8,128)(2,1)S(1)} %copy-done.2, bf16[160,640]{1,0:T(8,128)(2,1)S(1)} %copy-done.8, bf16[160,640]{1,0:T(8,128)(2,1)S(1)} %copy-done.6, bf16[160,640]{1,0:T(8,128)(2,1)S(1)} %copy-done.4, ...), custom_call_target="tpu_custom_call" | custom-call | flops 4456448000 | bytes 6553600 | tf_op jit(solution)/shard_map/convolve/pallas_call | solution.py:198
  106.8 17.3 %all_to_all.10.packets = bf16[16,40,640]{2,1,0:T(8,128)(2,1)} all-to-all(bf16[16,40,640]{2,1,0:T(8,128)(2,1)S(1)} %convolve.1), channel_id=1, replica_groups=mesh['tx'=4,'ty'=4,'sector'=8] {'tx','ty'}, dimensions={0} | all-to-all | bytes 1638400 | tf_op jit(solution)/shard_map/all_to_all | solution.py:286
  124.2 2.4 %assemble.1 = bf16[640,640]{1,0:T(8,128)(2,1)} custom-call(bf16[16,40,640]{2,1,0:T(8,128)(2,1)} %all_to_all.10.packets), custom_call_target="tpu_custom_call" | custom-call | tf_op jit(solution)/shard_map/assemble/pallas_call | solution.py:231
  (34 shorter events, 0.2 us)
Async XLA Ops:
  0.0 75.8 %copy-start = (f32[1,640]{1,0:T(1,128)S(1)}, f32[1,640]{1,0:T(1,128)}, u32[]{:S(2)}) copy-start(f32[1,640]{1,0:T(1,128)} %param.8) | copy-start | bytes 7684
  0.0 22.8 %collective-permute-start.1 = (bf16[640,640]{1,0:T(8,128)(2,1)}, bf16[640,640]{1,0:T(8,128)(2,1)S(1)}, u32[]{:S(2)}, u32[]{:S(2)}) collective-permute-start(bf16[640,640]{1,0:T(8,128)(2,1)} %bitcast.20), channel_id=1, source_target_pairs={{1,0},{2,1},{3,2},{4,3},{5,4},{6,5},{7,6},{9,8},{10,9},{11,10},{12... | collective-permute-start | bytes 2457608 | tf_op jit(solution)/shard_map/ppermute | solution.py:22
  9.9 13.9 %collective-permute-start.2 = (bf16[640,640]{1,0:T(8,128)(2,1)}, bf16[640,640]{1,0:T(8,128)(2,1)S(1)}, u32[]{:S(2)}, u32[]{:S(2)}) collective-permute-start(bf16[640,640]{1,0:T(8,128)(2,1)} %get-tuple-element.19), channel_id=1, source_target_pairs={{0,1},{1,2},{2,3},{3,4},{4,5},{5,6},{6,7},{8,9},{9,10},{10,11},{11... | collective-permute-start | bytes 2457608 | tf_op jit(solution)/shard_map/ppermute | solution.py:22
  12.3 27.7 %all-to-all-start = ((bf16[4,160,640]{2,1,0:T(8,128)(2,1)}), bf16[4,160,640]{2,1,0:T(8,128)(2,1)S(1)}, u32[]{:S(2)}, u32[]{:S(2)}) async-start(bf16[4,160,640]{2,1,0:T(8,128)(2,1)} %bitcast.11), calls=%async_computation | async-start | bytes 1638400 | tf_op jit(solution)/shard_map/all_to_all | solution.py:252
  16.7 4.8 %collective-permute-start = (s32[1]{0:T(128)}, s32[1]{0:T(128)}, u32[]{:S(2)}, u32[]{:S(2)}) collective-permute-start(s32[1]{0:T(128)} %param.11), channel_id=1, source_target_pairs={{1,0},{2,1},{3,2},{4,3},{5,4},{6,5},{7,6},{9,8},{10,9},{11,10},{12... | collective-permute-start | bytes 20 | tf_op jit(solution)/shard_map/ppermute | solution.py:22
  22.8 0.9 copy-start.9
  23.7 0.9 copy-start.10
  29.0 9.5 %collective-permute-start.3 = (bf16[160,640]{1,0:T(8,128)(2,1)}, bf16[160,640]{1,0:T(8,128)(2,1)S(1)}, u32[]{:S(2)}, u32[]{:S(2)}) collective-permute-start(bf16[160,640]{1,0:T(8,128)(2,1)} %get-tuple-element.22), channel_id=1, source_target_pairs={{0,32},{32,64},{64,96},{96,0},{1,33},{33,65},{65,97},{97,1},{2,34}... | collective-permute-start | bytes 614408 | tf_op jit(solution)/shard_map/ppermute | solution.py:27
  30.5 20.1 %collective-permute-start.8 = (bf16[160,640]{1,0:T(8,128)(2,1)}, bf16[160,640]{1,0:T(8,128)(2,1)S(1)}, u32[]{:S(2)}, u32[]{:S(2)}) collective-permute-start(bf16[160,640]{1,0:T(8,128)(2,1)} %get-tuple-element.21.refs_0_), channel_id=1, source_target_pairs={{0,16},{8,24},{16,0},{24,8},{1,17},{9,25},{17,1},{25,9},{2,18},{10... | collective-permute-start | bytes 614408 | tf_op jit(solution)/shard_map/ppermute | solution.py:27
  33.7 18.5 %collective-permute-start.7 = (bf16[160,640]{1,0:T(8,128)(2,1)}, bf16[160,640]{1,0:T(8,128)(2,1)S(1)}, u32[]{:S(2)}, u32[]{:S(2)}) collective-permute-start(bf16[160,640]{1,0:T(8,128)(2,1)} %get-tuple-element.21.refs_0_), channel_id=1, source_target_pairs={{0,24},{8,0},{16,8},{24,16},{1,25},{9,1},{17,9},{25,17},{2,26},{10... | collective-permute-start | bytes 614408 | tf_op jit(solution)/shard_map/ppermute | solution.py:27
  34.8 19.2 %collective-permute-start.6 = (bf16[160,640]{1,0:T(8,128)(2,1)}, bf16[160,640]{1,0:T(8,128)(2,1)S(1)}, u32[]{:S(2)}, u32[]{:S(2)}) collective-permute-start(bf16[160,640]{1,0:T(8,128)(2,1)} %get-tuple-element.21.refs_0_), channel_id=1, source_target_pairs={{0,8},{8,16},{16,24},{24,0},{1,9},{9,17},{17,25},{25,1},{2,10},{10... | collective-permute-start | bytes 614408 | tf_op jit(solution)/shard_map/ppermute | solution.py:27
  35.8 8.7 %collective-permute-start.4 = (bf16[160,640]{1,0:T(8,128)(2,1)}, bf16[160,640]{1,0:T(8,128)(2,1)S(1)}, u32[]{:S(2)}, u32[]{:S(2)}) collective-permute-start(bf16[160,640]{1,0:T(8,128)(2,1)} %get-tuple-element.23), channel_id=1, source_target_pairs={{0,64},{32,96},{64,0},{96,32},{1,65},{33,97},{65,1},{97,33},{2,66}... | collective-permute-start | bytes 614408 | tf_op jit(solution)/shard_map/ppermute | solution.py:27
  38.5 9.5 %collective-permute-start.5 = (bf16[160,640]{1,0:T(8,128)(2,1)}, bf16[160,640]{1,0:T(8,128)(2,1)S(1)}, u32[]{:S(2)}, u32[]{:S(2)}) collective-permute-start(bf16[160,640]{1,0:T(8,128)(2,1)} %get-tuple-element.24), channel_id=1, source_target_pairs={{0,96},{32,0},{64,32},{96,64},{1,97},{33,1},{65,33},{97,65},{2,98}... | collective-permute-start | bytes 614408 | tf_op jit(solution)/shard_map/ppermute | solution.py:27
  44.5 13.5 %collective-permute-start.17 = (bf16[2,160,640]{2,1,0:T(8,128)(2,1)S(1)}, bf16[2,160,640]{2,1,0:T(8,128)(2,1)S(1)}, u32[]{:S(2)}, u32[]{:S(2)}) collective-permute-start(bf16[2,160,640]{2,1,0:T(8,128)(2,1)S(1)} %get-tuple-element.31), channel_id=1, source_target_pairs={{0,32},{32,64},{64,96},{96,0},{1,33},{33,65},{65,97},{97,1},{2,34}... | collective-permute-start | bytes 1228808 | tf_op jit(solution)/shard_map/ppermute | solution.py:27
  48.0 12.7 %collective-permute-start.16 = (bf16[2,160,640]{2,1,0:T(8,128)(2,1)S(1)}, bf16[2,160,640]{2,1,0:T(8,128)(2,1)S(1)}, u32[]{:S(2)}, u32[]{:S(2)}) collective-permute-start(bf16[2,160,640]{2,1,0:T(8,128)(2,1)S(1)} %get-tuple-element.31), channel_id=1, source_target_pairs={{0,96},{32,0},{64,32},{96,64},{1,97},{33,1},{65,33},{97,65},{2,98}... | collective-permute-start | bytes 1228808 | tf_op jit(solution)/shard_map/ppermute | solution.py:27
  50.6 0.7 copy-start.3
  51.3 17.5 %collective-permute-start.18 = (bf16[2,160,640]{2,1,0:T(8,128)(2,1)S(1)}, bf16[2,160,640]{2,1,0:T(8,128)(2,1)S(1)}, u32[]{:S(2)}, u32[]{:S(2)}) collective-permute-start(bf16[2,160,640]{2,1,0:T(8,128)(2,1)S(1)} %get-tuple-element.32), channel_id=1, source_target_pairs={{0,96},{32,0},{64,32},{96,64},{1,97},{33,1},{65,33},{97,65},{2,98}... | collective-permute-start | bytes 1228808 | tf_op jit(solution)/shard_map/ppermute | solution.py:27
  52.3 0.7 copy-start.5
  53.0 19.1 %collective-permute-start.15 = (bf16[2,160,640]{2,1,0:T(8,128)(2,1)S(1)}, bf16[2,160,640]{2,1,0:T(8,128)(2,1)S(1)}, u32[]{:S(2)}, u32[]{:S(2)}) collective-permute-start(bf16[2,160,640]{2,1,0:T(8,128)(2,1)S(1)} %get-tuple-element.32), channel_id=1, source_target_pairs={{0,32},{32,64},{64,96},{96,0},{1,33},{33,65},{65,97},{97,1},{2,34}... | collective-permute-start | bytes 1228808 | tf_op jit(solution)/shard_map/ppermute | solution.py:27
  54.0 0.7 copy-start.7
  54.8 17.3 %collective-permute-start.12 = (bf16[3,80,640]{2,1,0:T(8,128)(2,1)S(1)}, bf16[3,80,640]{2,1,0:T(8,128)(2,1)S(1)}, u32[]{:S(2)}, u32[]{:S(2)}) collective-permute-start(bf16[3,80,640]{2,1,0:T(8,128)(2,1)S(1)} %pad_maximum_fusion), channel_id=1, source_target_pairs={{0,24},{8,0},{16,8},{24,16},{1,25},{9,1},{17,9},{25,17},{2,26},{10... | collective-permute-start | bytes 921608 | tf_op jit(solution)/shard_map/ppermute | solution.py:27
  58.0 14.5 %collective-permute-start.9 = (bf16[3,80,640]{2,1,0:T(8,128)(2,1)S(1)}, bf16[3,80,640]{2,1,0:T(8,128)(2,1)}, u32[]{:S(2)}, u32[]{:S(2)}) collective-permute-start(bf16[3,80,640]{2,1,0:T(8,128)(2,1)S(1)} %pad_maximum_fusion), channel_id=1, source_target_pairs={{0,8},{8,16},{16,24},{24,0},{1,9},{9,17},{17,25},{25,1},{2,10},{10... | collective-permute-start | bytes 921608 | tf_op jit(solution)/shard_map/ppermute | solution.py:27
  60.6 12.4 %collective-permute-start.10 = (bf16[3,80,640]{2,1,0:T(8,128)(2,1)}, bf16[3,80,640]{2,1,0:T(8,128)(2,1)}, u32[]{:S(2)}, u32[]{:S(2)}) collective-permute-start(bf16[3,80,640]{2,1,0:T(8,128)(2,1)} %pad_maximum_fusion.1), channel_id=1, source_target_pairs={{0,24},{8,0},{16,8},{24,16},{1,25},{9,1},{17,9},{25,17},{2,26},{10... | collective-permute-start | bytes 921608 | tf_op jit(solution)/shard_map/ppermute | solution.py:27
  68.8 15.0 %collective-permute-start.20 = (bf16[2,160,640]{2,1,0:T(8,128)(2,1)S(1)}, bf16[2,160,640]{2,1,0:T(8,128)(2,1)}, u32[]{:S(2)}, u32[]{:S(2)}) collective-permute-start(bf16[2,160,640]{2,1,0:T(8,128)(2,1)S(1)} %collective-permute-done.16.refs_15_), channel_id=1, source_target_pairs={{0,96},{32,0},{64,32},{96,64},{1,97},{33,1},{65,33},{97,65},{2,98}... | collective-permute-start | bytes 1228808 | tf_op jit(solution)/shard_map/ppermute | solution.py:27
  72.0 11.8 %collective-permute-start.19 = (bf16[2,160,640]{2,1,0:T(8,128)(2,1)S(1)}, bf16[2,160,640]{2,1,0:T(8,128)(2,1)}, u32[]{:S(2)}, u32[]{:S(2)}) collective-permute-start(bf16[2,160,640]{2,1,0:T(8,128)(2,1)S(1)} %collective-permute-done.15.refs_14_), channel_id=1, source_target_pairs={{0,32},{32,64},{64,96},{96,0},{1,33},{33,65},{65,97},{97,1},{2,34}... | collective-permute-start | bytes 1228808 | tf_op jit(solution)/shard_map/ppermute | solution.py:27
  72.0 11.8 %collective-permute-start.11 = (bf16[3,80,640]{2,1,0:T(8,128)(2,1)}, bf16[3,80,640]{2,1,0:T(8,128)(2,1)}, u32[]{:S(2)}, u32[]{:S(2)}) collective-permute-start(bf16[3,80,640]{2,1,0:T(8,128)(2,1)} %pad_maximum_fusion.1), channel_id=1, source_target_pairs={{0,8},{8,16},{16,24},{24,0},{1,9},{9,17},{17,25},{25,1},{2,10},{10... | collective-permute-start | bytes 921608 | tf_op jit(solution)/shard_map/ppermute | solution.py:27
  72.5 15.8 %collective-permute-start.13 = (bf16[3,80,640]{2,1,0:T(8,128)(2,1)}, bf16[3,80,640]{2,1,0:T(8,128)(2,1)}, u32[]{:S(2)}, u32[]{:S(2)}) collective-permute-start(bf16[3,80,640]{2,1,0:T(8,128)(2,1)} %collective-permute-done.9.refs_7_), channel_id=1, source_target_pairs={{0,8},{8,16},{16,24},{24,0},{1,9},{9,17},{17,25},{25,1},{2,10},{10... | collective-permute-start | bytes 921608 | tf_op jit(solution)/shard_map/ppermute | solution.py:27
  73.0 15.3 %collective-permute-start.14 = (bf16[3,80,640]{2,1,0:T(8,128)(2,1)}, bf16[3,80,640]{2,1,0:T(8,128)(2,1)}, u32[]{:S(2)}, u32[]{:S(2)}) collective-permute-start(bf16[3,80,640]{2,1,0:T(8,128)(2,1)} %collective-permute-done.10.refs_8_), channel_id=1, source_target_pairs={{0,24},{8,0},{16,8},{24,16},{1,25},{9,1},{17,9},{25,17},{2,26},{10... | collective-permute-start | bytes 921608 | tf_op jit(solution)/shard_map/ppermute | solution.py:27
  75.8 12.5 %copy-start.1 = (s32[4]{0:T(128)S(1)}, s32[4]{0:T(128)}, u32[]{:S(2)}) copy-start(s32[4]{0:T(128)} %pad_add_fusion.scalars) | copy-start | bytes 52
  88.3 0.9 copy-start.2
  89.3 0.9 copy-start.4
  90.2 0.9 copy-start.6
  91.1 0.9 copy-start.8

commit v3 on v2

v3 whole, which is shorter than its diff:
```python
import functools

import jax
import jax.numpy as jnp
import numpy as np
from jax import lax
from jax.experimental import pallas as pl
from jax.experimental.pallas import tpu as pltpu
from jax.sharding import Mesh
from jax.sharding import PartitionSpec as P

MIB = 1024 * 1024
VMEM = pl.BlockSpec(memory_space=pltpu.VMEM)
SMEM = pl.BlockSpec(memory_space=pltpu.SMEM)
ANY = pl.BlockSpec(memory_space=pl.ANY)
NT = (((1,), (1,)), ((), ()))


def shifted(block, axis, distance):
    devices = range(lax.axis_size(axis))
    route = [(i - distance, i) for i in devices if i - distance in devices]
    return lax.ppermute(block, axis, route)


def ring(block, axis, distance):
    n = lax.axis_size(axis)
    return lax.ppermute(block, axis, [(i, (i + distance) % n) for i in range(n)])


def tied(value, *others):
    return lax.optimization_barrier((value, *others))[0]


def spread(block, axis):
    return [(-d, ring(block, axis, d)) for d in (1, -1, 2)]


def halves_gather(first, second, axis):
    below_a = ring(first, axis, 1)
    above_b = ring(second, axis, -1)
    below_b = ring(second, axis, 1)
    above_a = ring(first, axis, -1)
    far_a = ring(below_a, axis, 1)
    far_b = ring(above_b, axis, -1)
    return [
        (-1, 0, below_a),
        (1, 1, above_b),
        (-1, 1, below_b),
        (1, 0, above_a),
        (2, 0, far_a),
        (2, 1, far_b),
    ]


def stacked_halves(blocks):
    half = blocks[0].shape[0] // 2
    return jnp.stack([b[:half] for b in blocks]), jnp.stack([b[half:] for b in blocks])


def live(shape, size, first_row=0):
    row = lax.broadcasted_iota(jnp.int32, shape, 0) + first_row
    column = lax.broadcasted_iota(jnp.int32, shape, 1)
    return (row < size) & (column < size)


def dot(a, b):
    return jnp.dot(a, b, preferred_element_type=jnp.float32)


def turn_kernel(masked, *outs):
    n = len(outs)
    rows = outs[0].shape[0]
    here_y = lax.axis_index("ty")
    for k in range(n):
        block = masked[:, k * rows : (k + 1) * rows].T
        for d in range(n):

            @pl.when(lax.rem(here_y + d, n) == k)
            def _():
                outs[d][...] = block


def turn_blocks(masked, n):
    states = masked.shape[0]
    block = jax.ShapeDtypeStruct((states // n, states), jnp.bfloat16)
    return pl.pallas_call(
        turn_kernel,
        out_shape=(block,) * n,
        in_specs=[VMEM],
        out_specs=(VMEM,) * n,
        cost_estimate=pl.CostEstimate(flops=0, bytes_accessed=4 * states**2, transcendentals=0),
        name="turn_blocks",
    )(masked)


def raise_kernel(masked, operator, upward, flipped):
    r = operator[...]
    raised = dot(r, masked[...]).astype(jnp.bfloat16)
    upward[...] = lax.dot_general(raised, r, NT, preferred_element_type=jnp.float32).astype(
        jnp.bfloat16
    )
    flipped[...] = r.T


def raise_terms(masked, operator):
    states = masked.shape[0]
    square = jax.ShapeDtypeStruct((states, states), jnp.bfloat16)
    return pl.pallas_call(
        raise_kernel,
        out_shape=(square, square),
        in_specs=[VMEM, VMEM],
        out_specs=(VMEM, VMEM),
        cost_estimate=pl.CostEstimate(
            flops=4 * states**3, bytes_accessed=8 * states**2, transcendentals=0
        ),
        name="raise_terms",
    )(masked, operator)


def energy_kernel(sizes, particle, hole, above, below, operator, flipped, *outs):
    n = len(outs)
    rows = outs[0].shape[0]
    here_x = lax.axis_index("tx")
    inner = above[...]
    r = operator[...]
    for d in (2, 1, 3, 0):
        first = pl.multiple_of(lax.rem(here_x + d, n) * rows, 32)
        lowered = dot(flipped[pl.ds(first, rows), :], inner).astype(jnp.bfloat16)
        downward = dot(lowered, r)
        raised = below[pl.ds(first, rows), :].astype(jnp.float32)
        both = particle[0] * raised + hole[0] * downward
        kept = live(both.shape, sizes[0], first)
        outs[d][...] = jnp.where(kept, both, 0.0).astype(jnp.bfloat16)


def energy_blocks(sizes, particle, hole, above, below, operator, flipped, n):
    states = above.shape[0]
    block = jax.ShapeDtypeStruct((states // n, states), jnp.bfloat16)
    return pl.pallas_call(
        energy_kernel,
        out_shape=(block,) * n,
        in_specs=[SMEM] * 3 + [VMEM] * 4,
        out_specs=(VMEM,) * n,
        cost_estimate=pl.CostEstimate(
            flops=4 * states**3, bytes_accessed=10 * states**2, transcendentals=0
        ),
        name="energy_blocks",
    )(sizes, particle, hole, above, below, operator, flipped)


def convolve_kernel(plan, n, step_size, sizes, rates, *refs):
    parts = refs[: len(plan)]
    out, e_all, g_all, total, sems = refs[len(plan) :]
    rows = out.shape[1] * n
    here_x, here_y, size = lax.axis_index("tx"), lax.axis_index("ty"), sizes[0]

    def around(here, offset):
        return lax.rem(here + offset + n, n)

    copies = []
    for part, (kind, far, near, half) in zip(parts, plan):
        room = e_all if kind == "e" else g_all

        def place(cross, ring_step):
            if kind == "e":
                return around(here_x, cross), around(here_y, ring_step)
            return around(here_x, ring_step), around(here_y, cross)

        if half is None:
            copies.append((part, room.at[place(far, near)]))
        else:
            tall = part.shape[1]
            for d in range(1, n):
                copies.append(
                    (part.at[d - 1], room.at[(*place(-d, near), pl.ds(half * tall, tall))])
                )
    started = [
        pltpu.make_async_copy(src, dst, sems.at[i]) for i, (src, dst) in enumerate(copies)
    ]
    for copy in started:
        copy.start()
    for copy in started:
        copy.wait()

    lags = e_all.reshape(n * n, *e_all.shape[2:])
    for u in range(n * n):
        right = g_all[u // n, u % n]
        for first in range(0, n * n - u, n):
            some = min(n, n * n - u - first)
            left = lags[first : first + some].reshape(some * rows, -1)
            product = lax.dot_general(left, right, NT, preferred_element_type=jnp.float32)
            where = slice((u + first) * rows, (u + first + some) * rows)
            if u == 0:
                total[where] = product
            else:
                total[where] += product

    quarter = rows // n
    scale = step_size * step_size
    for b in range(n):
        row = lax.broadcasted_iota(jnp.int32, (quarter, rows), 0) + b * quarter
        column = lax.broadcasted_iota(jnp.int32, (quarter, rows), 1)
        starts = (row == column) & (here_x == here_y) & (row + here_x * rows < size)
        rate = rates[b * quarter : (b + 1) * quarter]
        decay = jnp.broadcast_to(jnp.exp(-step_size * rate), (quarter, rows))
        for t in range(n * n):
            term = scale * total[t * rows + b * quarter : t * rows + (b + 1) * quarter]
            fresh = (jnp.where(starts, 1.0, 0.0) if t == 0 else decay * fresh) - term
            out[t, :, b * rows : (b + 1) * rows] = fresh.astype(jnp.bfloat16)


def convolve(parts, plan, sizes, rates, n, step_size):
    rows, states = parts[0].shape
    copies = sum(1 if half is None else n - 1 for *_, half in plan)
    return pl.pallas_call(
        functools.partial(convolve_kernel, plan, n, step_size),
        out_shape=jax.ShapeDtypeStruct((n * n, rows // n, states), jnp.bfloat16),
        in_specs=[SMEM, VMEM] + [ANY] * len(parts),
        out_specs=VMEM,
        scratch_shapes=[
            pltpu.VMEM((n, n, rows, states), jnp.bfloat16),
            pltpu.VMEM((n, n, rows, states), jnp.bfloat16),
            pltpu.VMEM((n * n * rows, rows), jnp.float32),
            pltpu.SemaphoreType.DMA((copies,)),
        ],
        compiler_params=pltpu.CompilerParams(vmem_limit_bytes=50 * MIB),
        cost_estimate=pl.CostEstimate(
            flops=n * n * (n * n + 1) * rows * rows * states,
            bytes_accessed=4 * n * n * rows * states,
            transcendentals=0,
        ),
        name="convolve",
    )(sizes, rates, *parts)


def assemble_kernel(n, packets, out):
    quarter, states = packets.shape[1:]
    rows = states // n
    for x in range(n):
        for b in range(n):
            out[x * rows + b * quarter : x * rows + (b + 1) * quarter, :] = jnp.concatenate(
                [packets[x * n + y, :, b * rows : (b + 1) * rows] for y in range(n)], axis=1
            )


def assemble(packets, n):
    states = packets.shape[2]
    return pl.pallas_call(
        functools.partial(assemble_kernel, n),
        out_shape=jax.ShapeDtypeStruct((states, states), jnp.bfloat16),
        in_specs=[VMEM],
        out_specs=VMEM,
        name="assemble",
    )(packets)


def per_device(propagator, rising_op, energies, hyb_particle, hyb_hole, sector_sizes):
    states = propagator.shape[2]
    n = lax.axis_size("tx")
    step_size = 1.0 / (n * n)
    rows = states // n
    here_x = lax.axis_index("tx")
    operator = rising_op[0]
    live_mask = jnp.arange(states, dtype=jnp.int32) < sector_sizes[0]
    square = live_mask[:, None] & live_mask[None, :]
    masked = jnp.where(square, propagator[0, 0], jnp.zeros((), jnp.bfloat16))

    above = shifted(masked, "sector", -1)
    upward, flipped = raise_terms(masked, operator)
    below = shifted(upward, "sector", 1)

    own_g, *away_g = turn_blocks(tied(masked, upward), n)
    crossed_g = {d: ring(away_g[d - 1], "ty", d) for d in (2, 1, 3)}
    spread_g = spread(own_g, "tx")

    operator_late = tied(operator, own_g)
    own_e, *away_e = energy_blocks(
        sector_sizes, hyb_particle, hyb_hole, above, below, operator_late, flipped, n
    )
    crossed_e = {d: ring(away_e[d - 1], "tx", d) for d in (2, 1, 3)}
    spread_e = spread(own_e, "ty")

    parts, plan = [], []

    def add(kind, far, near, half, piece):
        parts.append(piece)
        plan.append((kind, far, near, half))

    crossed_e = [crossed_e[d] for d in range(1, n)]
    crossed_g = [crossed_g[d] for d in range(1, n)]
    arrived = lax.optimization_barrier((crossed_e, crossed_g, [p for _, p in spread_e]))
    crossed_e, crossed_g, pieces_e = arrived
    for kind, own, crossed, near in (
        ("e", own_e, crossed_e, list(zip([o for o, _ in spread_e], pieces_e))),
        ("g", own_g, crossed_g, spread_g),
    ):
        add(kind, 0, 0, None, own)
        for d in range(1, n):
            add(kind, -d, 0, None, crossed[d - 1])
        for offset, piece in near:
            add(kind, 0, offset, None, piece)
        axis = "ty" if kind == "e" else "tx"
        for offset, half, piece in halves_gather(*stacked_halves(crossed), axis):
            add(kind, 0, offset, half, piece)

    rates = lax.dynamic_slice_in_dim(energies[0], here_x * rows, rows, 0)[:, None]
    packets = convolve(parts, plan, sector_sizes, rates, n, step_size)
    packets = lax.all_to_all(packets, ("tx", "ty"), 0, 0, tiled=True)
    return assemble(packets, n)[None, None]


def solution(mesh):
    n = round(mesh.shape["tm"] ** 0.5)
    split = Mesh(
        np.asarray(mesh.devices).reshape(n, n, mesh.shape["sector"]), ("tx", "ty", "sector")
    )
    times = ("tx", "ty")
    placed = (
        P("sector", times, None, None),
        P("sector", None, None),
        P("sector", None),
        P(times),
        P(times),
        P("sector"),
    )
    return jax.shard_map(
        per_device,
        mesh=split,
        in_specs=placed,
        out_specs=P("sector", times, None, None),
        check_vma=False,
    )
```

time: 127 us -> 120 us (0.945); the launches traced: 127 us -> 118 us
  waiting for transfers between devices: 26.8 us -> 16.3 us
  Pallas kernels: 28.1 us -> 31.8 us
  local copies, waits for them, and re-layouts: 6.92 us -> 4.48 us
  starting transfers between devices: 42 us -> 43.3 us
    ppermute x18 -> x24, waiting for transfers between devices: 25.8 us -> 14.9 us  [ring(): lax.ppermute(block, axis, [(i, (i + distance) % n) for i in range(n)])]
    ppermute x18 -> x24, starting transfers between devices: 30.3 us -> 39 us  [ring(): lax.ppermute(block, axis, [(i, (i + distance) % n) for i in range(n)])]
    all_to_all x1 -> x0, starting transfers between devices: 4.48 us -> none  [per_device(): lax.all_to_all(turned.reshape(n, rows, states), 'ty', 0, 0, tiled=True)]
    pallas_call x1, Pallas kernels: 14.8 us -> 17.9 us  [convolve(): pl.pallas_call(functools.partial(convolve_kernel, plan, n, step_size), ou...]
    ppermute x3 -> x2, starting transfers between devices: 7.3 us -> 4.31 us  [shifted(): return lax.ppermute(block, axis, route)]
    unnamed x22 -> x24, local copies, waits for them, and re-layouts: 6.61 us -> 4.15 us
    another operation x4, other arithmetic: 2.75 us -> 0.9 us  [the longest x2 0.81 us: stacked_halves(): jnp.stack([b[half:] for b in blocks])]
    select_n x0 -> x1, other arithmetic: none -> 1.46 us  [per_device(): masked = jnp.where(square, propagator[0, 0], jnp.zeros((), jnp.bfloat16))]
  transfers between devices with their start and end apart: 22 -> 26, of which waited for: 7 -> 10; matrix products, arithmetic and copies ran while one was open for 3% -> 1% of each run, Pallas kernels for 9% -> 10%
where the time goes in v3:
time: 120 us; the launch traced here: 118 us
  starting transfers between devices  43.3 us (36%)
  Pallas kernels  31.8 us (26%)
  blocking collectives  17.6 us (15%)
  waiting for transfers between devices  16.3 us (14%)
  local copies, waits for them, and re-layouts  4.48 us (4%)
  other arithmetic  2.36 us (2%)
  between operations  2.12 us (2%)
    ppermute x24, starting transfers between devices, ring(): lax.ppermute(block, axis, [(i, (i + distance) % n) for i in range(n)])  39 us
    pallas_call x1, Pallas kernels, convolve(): pl.pallas_call(functools.partial(convolve_kernel, plan, n, step_size), ou...  17.9 us
    all_to_all x1, blocking collectives, per_device(): packets = lax.all_to_all(packets, ('tx', 'ty'), 0, 0, tiled=True)  17.6 us
    ppermute x24, waiting for transfers between devices, ring(): lax.ppermute(block, axis, [(i, (i + distance) % n) for i in range(n)])  14.9 us
    pallas_call x1, Pallas kernels, energy_blocks(): pl.pallas_call(energy_kernel, out_shape=(block,) * n, in_specs=[SMEM] * 3...  4.39 us
    ppermute x2, starting transfers between devices, shifted(): return lax.ppermute(block, axis, route)  4.31 us
    pallas_call x1, Pallas kernels, raise_terms(): pl.pallas_call(raise_kernel, out_shape=(square, square), in_specs=[VMEM,...  4.19 us
    unnamed x24, local copies, waits for them, and re-layouts  4.15 us
  transfers between devices with their start and end apart: 26, of which 10 were waited for; matrix products, arithmetic and copies ran while one was open for 1% of the time, Pallas kernels for 10%

profile of v3, /device:TPU:32, one launch (start us, length us, event | category | flops | bytes accessed | tf_op | source)
XLA Modules:
  0.0 118.0 jit_solution(5993516441622800819)
XLA Ops:
  0.7 1.5 %and_select_fusion.masked = bf16[640,640]{1,0:T(8,128)(2,1)S(1)} fusion(bf16[1,1,640,640]{3,2,1,0:T(8,128)(2,1)} %param.6, pred[640]{0:T(1024)(128)(4,1)S(1)} %iota_compare_fusion), kind=kLoop, calls=%fused_computation | loop fusion | flops 819200 | bytes 1639040 | tf_op jit(solution)/shard_map/jit(_where)/select_n | solution.py:266
  2.2 1.9 %collective-permute-start = (bf16[640,640]{1,0:T(8,128)(2,1)S(1)}, bf16[640,640]{1,0:T(8,128)(2,1)S(1)}, u32[]{:S(2)}, u32[]{:S(2)}) collective-permute-start(bf16[640,640]{1,0:T(8,128)(2,1)S(1)} %and_select_fusion.masked), channel_id=1, source_target_pairs={{1,0},{2,1},{3,2},{4,3},{5,4},{6,5},{7,6},{9,8},{10,9},{11,10},{12... | collective-permute-start | bytes 2457608 | tf_op jit(solution)/shard_map/ppermute | solution.py:22
  4.1 4.2 %raise_terms.1 = (bf16[640,640]{1,0:T(8,128)(2,1)}, bf16[640,640]{1,0:T(8,128)(2,1)}) custom-call(bf16[640,640]{1,0:T(8,128)(2,1)} %copy-done.7, bf16[640,640]{1,0:T(8,128)(2,1)} %bitcast.32), custom_call_target="tpu_custom_call" | custom-call | flops 1048576000 | bytes 3276800 | tf_op jit(solution)/shard_map/raise_terms/pallas_call | solution.py:108
  8.3 2.4 %collective-permute-start.1 = (bf16[640,640]{1,0:T(8,128)(2,1)}, bf16[640,640]{1,0:T(8,128)(2,1)S(1)}, u32[]{:S(2)}, u32[]{:S(2)}) collective-permute-start(bf16[640,640]{1,0:T(8,128)(2,1)} %get-tuple-element.26), channel_id=1, source_target_pairs={{0,1},{1,2},{2,3},{3,4},{4,5},{5,6},{6,7},{8,9},{9,10},{10,11},{11... | collective-permute-start | bytes 2457608 | tf_op jit(solution)/shard_map/ppermute | solution.py:22
  10.7 2.9 %turn_blocks.1 = (bf16[160,640]{1,0:T(8,128)(2,1)}, bf16[160,640]{1,0:T(8,128)(2,1)}, bf16[160,640]{1,0:T(8,128)(2,1)}, bf16[160,640]{1,0:T(8,128)(2,1)}) custom-call(bf16[640,640]{1,0:T(8,128)(2,1)} %copy-done.7), custom_call_target="tpu_custom_call" | custom-call | bytes 1638400 | tf_op jit(solution)/shard_map/turn_blocks/pallas_call | solution.py:86
  13.6 1.6 %collective-permute-start.5 = (bf16[160,640]{1,0:T(8,128)(2,1)}, bf16[160,640]{1,0:T(8,128)(2,1)S(1)}, u32[]{:S(2)}, u32[]{:S(2)}) collective-permute-start(bf16[160,640]{1,0:T(8,128)(2,1)} %get-tuple-element.35), channel_id=1, source_target_pairs={{0,8},{8,16},{16,24},{24,0},{1,9},{9,17},{17,25},{25,1},{2,10},{10... | collective-permute-start | bytes 614408 | tf_op jit(solution)/shard_map/ppermute | solution.py:27
  15.2 2.9 %collective-permute-start.6 = (bf16[160,640]{1,0:T(8,128)(2,1)}, bf16[160,640]{1,0:T(8,128)(2,1)S(1)}, u32[]{:S(2)}, u32[]{:S(2)}) collective-permute-start(bf16[160,640]{1,0:T(8,128)(2,1)} %get-tuple-element.36), channel_id=1, source_target_pairs={{0,16},{8,24},{16,0},{24,8},{1,17},{9,25},{17,1},{25,9},{2,18},{10... | collective-permute-start | bytes 614408 | tf_op jit(solution)/shard_map/ppermute | solution.py:27
  18.1 1.3 %collective-permute-start.7 = (bf16[160,640]{1,0:T(8,128)(2,1)}, bf16[160,640]{1,0:T(8,128)(2,1)S(1)}, u32[]{:S(2)}, u32[]{:S(2)}) collective-permute-start(bf16[160,640]{1,0:T(8,128)(2,1)} %get-tuple-element.37), channel_id=1, source_target_pairs={{0,24},{8,0},{16,8},{24,16},{1,25},{9,1},{17,9},{25,17},{2,26},{10... | collective-permute-start | bytes 614408 | tf_op jit(solution)/shard_map/ppermute | solution.py:27
  20.8 1.4 %collective-permute-done.1.below = bf16[640,640]{1,0:T(8,128)(2,1)S(1)} collective-permute-done((bf16[640,640]{1,0:T(8,128)(2,1)}, bf16[640,640]{1,0:T(8,128)(2,1)S(1)}, u32[]{:S(2)}, u32[]{:S(2)}) %collective-permute-start.1) | collective-permute-done | bytes 819232 | tf_op jit(solution)/shard_map/ppermute | solution.py:22
  22.1 0.9 copy-done.9
  23.1 4.4 %energy_blocks.1 = (bf16[160,640]{1,0:T(8,128)(2,1)}, bf16[160,640]{1,0:T(8,128)(2,1)}, bf16[160,640]{1,0:T(8,128)(2,1)}, bf16[160,640]{1,0:T(8,128)(2,1)}) custom-call(s32[1]{0:T(128)} %copy.10.sizes, f32[1]{0:T(128)S(6)} %copy.8.particle, f32[1]{0:T(128)S(6)} %copy.9.hole, bf16[640,640]{1,0:T(8,128)(2,1)} %copy-done.8, bf16[640,640]{1,0:T(8,128)(2,1)} %copy-done.9, ...), custom_call_target="tpu_custom_call" | custom-call | flops 1048576000 | bytes 4096000 | tf_op jit(solution)/shard_map/energy_blocks/pallas_call | solution.py:139
  27.4 1.5 %collective-permute-start.2 = (bf16[160,640]{1,0:T(8,128)(2,1)}, bf16[160,640]{1,0:T(8,128)(2,1)S(1)}, u32[]{:S(2)}, u32[]{:S(2)}) collective-permute-start(bf16[160,640]{1,0:T(8,128)(2,1)} %get-tuple-element.32), channel_id=1, source_target_pairs={{0,32},{32,64},{64,96},{96,0},{1,33},{33,65},{65,97},{97,1},{2,34}... | collective-permute-start | bytes 614408 | tf_op jit(solution)/shard_map/ppermute | solution.py:27
  28.9 2.7 %collective-permute-start.3 = (bf16[160,640]{1,0:T(8,128)(2,1)}, bf16[160,640]{1,0:T(8,128)(2,1)S(1)}, u32[]{:S(2)}, u32[]{:S(2)}) collective-permute-start(bf16[160,640]{1,0:T(8,128)(2,1)} %get-tuple-element.33), channel_id=1, source_target_pairs={{0,64},{32,96},{64,0},{96,32},{1,65},{33,97},{65,1},{97,33},{2,66}... | collective-permute-start | bytes 614408 | tf_op jit(solution)/shard_map/ppermute | solution.py:27
  31.6 1.4 %collective-permute-start.4 = (bf16[160,640]{1,0:T(8,128)(2,1)}, bf16[160,640]{1,0:T(8,128)(2,1)S(1)}, u32[]{:S(2)}, u32[]{:S(2)}) collective-permute-start(bf16[160,640]{1,0:T(8,128)(2,1)} %get-tuple-element.34), channel_id=1, source_target_pairs={{0,96},{32,0},{64,32},{96,64},{1,97},{33,1},{65,33},{97,65},{2,98}... | collective-permute-start | bytes 614408 | tf_op jit(solution)/shard_map/ppermute | solution.py:27
  33.1 3.2 %collective-permute-start.10 = (bf16[160,640]{1,0:T(8,128)(2,1)}, bf16[160,640]{1,0:T(8,128)(2,1)S(1)}, u32[]{:S(2)}, u32[]{:S(2)}) collective-permute-start(bf16[160,640]{1,0:T(8,128)(2,1)} %get-tuple-element.31.refs_0_), channel_id=1, source_target_pairs={{0,16},{8,24},{16,0},{24,8},{1,17},{9,25},{17,1},{25,9},{2,18},{10... | collective-permute-start | bytes 614408 | tf_op jit(solution)/shard_map/ppermute | solution.py:27
  36.3 1.1 collective-permute-start.9
  37.4 1.0 collective-permute-start.8
  38.3 2.5 %collective-permute-done.3.refs_2_ = bf16[160,640]{1,0:T(8,128)(2,1)S(1)} collective-permute-done((bf16[160,640]{1,0:T(8,128)(2,1)}, bf16[160,640]{1,0:T(8,128)(2,1)S(1)}, u32[]{:S(2)}, u32[]{:S(2)}) %collective-permute-start.3) | collective-permute-done | bytes 204832 | tf_op jit(solution)/shard_map/ppermute | solution.py:27
  40.9 0.8 collective-permute-start.19
  41.7 0.4 collective-permute-done.4.refs_3_
  42.1 2.7 %collective-permute-start.18 = (bf16[160,640]{1,0:T(8,128)(2,1)S(1)}, bf16[160,640]{1,0:T(8,128)(2,1)S(1)}, u32[]{:S(2)}, u32[]{:S(2)}) collective-permute-start(bf16[160,640]{1,0:T(8,128)(2,1)S(1)} %copy-done.1), channel_id=1, source_target_pairs={{0,96},{32,0},{64,32},{96,64},{1,97},{33,1},{65,33},{97,65},{2,98}... | collective-permute-start | bytes 614408 | tf_op jit(solution)/shard_map/ppermute | solution.py:27
  44.8 0.6 collective-permute-done.9.refs_5_
  45.5 1.4 %collective-permute-start.13 = (bf16[3,80,640]{2,1,0:T(8,128)(2,1)S(1)}, bf16[3,80,640]{2,1,0:T(8,128)(2,1)S(1)}, u32[]{:S(2)}, u32[]{:S(2)}) collective-permute-start(bf16[3,80,640]{2,1,0:T(8,128)(2,1)S(1)} %pad_maximum_fusion.1), channel_id=1, source_target_pairs={{0,8},{8,16},{16,24},{24,0},{1,9},{9,17},{17,25},{25,1},{2,10},{10... | collective-permute-start | bytes 921608 | tf_op jit(solution)/shard_map/ppermute | solution.py:27
  46.9 1.9 %collective-permute-start.12 = (bf16[3,80,640]{2,1,0:T(8,128)(2,1)S(1)}, bf16[3,80,640]{2,1,0:T(8,128)(2,1)S(1)}, u32[]{:S(2)}, u32[]{:S(2)}) collective-permute-start(bf16[3,80,640]{2,1,0:T(8,128)(2,1)S(1)} %pad_maximum_fusion.1), channel_id=1, source_target_pairs={{0,24},{8,0},{16,8},{24,16},{1,25},{9,1},{17,9},{25,17},{2,26},{10... | collective-permute-start | bytes 921608 | tf_op jit(solution)/shard_map/ppermute | solution.py:27
  48.9 0.8 pad_maximum_fusion.3
  49.7 0.7 collective-permute-done.19.refs_19_
  50.4 3.0 %collective-permute-start.14 = (bf16[3,80,640]{2,1,0:T(8,128)(2,1)S(1)}, bf16[3,80,640]{2,1,0:T(8,128)(2,1)S(1)}, u32[]{:S(2)}, u32[]{:S(2)}) collective-permute-start(bf16[3,80,640]{2,1,0:T(8,128)(2,1)S(1)} %pad_maximum_fusion), channel_id=1, source_target_pairs={{0,24},{8,0},{16,8},{24,16},{1,25},{9,1},{17,9},{25,17},{2,26},{10... | collective-permute-start | bytes 921608 | tf_op jit(solution)/shard_map/ppermute | solution.py:27
  53.4 0.7 copy-done.3
  54.1 0.7 copy-done.5
  54.8 1.3 %collective-permute-start.23 = (bf16[3,80,640]{2,1,0:T(8,128)(2,1)S(1)}, bf16[3,80,640]{2,1,0:T(8,128)(2,1)S(1)}, u32[]{:S(2)}, u32[]{:S(2)}) collective-permute-start(bf16[3,80,640]{2,1,0:T(8,128)(2,1)S(1)} %pad_maximum_fusion.2), channel_id=1, source_target_pairs={{0,96},{32,0},{64,32},{96,64},{1,97},{33,1},{65,33},{97,65},{2,98}... | collective-permute-start | bytes 921608 | tf_op jit(solution)/shard_map/ppermute | solution.py:27
  56.1 0.8 collective-permute-start.20
  56.8 0.3 collective-permute-done.12.refs_8_
  57.1 2.9 %collective-permute-start.21 = (bf16[3,80,640]{2,1,0:T(8,128)(2,1)}, bf16[3,80,640]{2,1,0:T(8,128)(2,1)}, u32[]{:S(2)}, u32[]{:S(2)}) collective-permute-start(bf16[3,80,640]{2,1,0:T(8,128)(2,1)} %pad_maximum_fusion.3), channel_id=1, source_target_pairs={{0,96},{32,0},{64,32},{96,64},{1,97},{33,1},{65,33},{97,65},{2,98}... | collective-permute-start | bytes 921608 | tf_op jit(solution)/shard_map/ppermute | solution.py:27
  60.1 1.9 %collective-permute-done.14.refs_10_ = bf16[3,80,640]{2,1,0:T(8,128)(2,1)S(1)} collective-permute-done((bf16[3,80,640]{2,1,0:T(8,128)(2,1)S(1)}, bf16[3,80,640]{2,1,0:T(8,128)(2,1)S(1)}, u32[]{:S(2)}, u32[]{:S(2)}) %collective-permute-start.14) | collective-permute-done | bytes 307232 | tf_op jit(solution)/shard_map/ppermute | solution.py:27
  61.9 0.6 collective-permute-start.22
  62.5 2.9 %collective-permute-start.16 = (bf16[3,80,640]{2,1,0:T(8,128)(2,1)S(1)}, bf16[3,80,640]{2,1,0:T(8,128)(2,1)}, u32[]{:S(2)}, u32[]{:S(2)}) collective-permute-start(bf16[3,80,640]{2,1,0:T(8,128)(2,1)S(1)} %collective-permute-done.12.refs_8_), channel_id=1, source_target_pairs={{0,24},{8,0},{16,8},{24,16},{1,25},{9,1},{17,9},{25,17},{2,26},{10... | collective-permute-start | bytes 921608 | tf_op jit(solution)/shard_map/ppermute | solution.py:27
  65.5 0.2 collective-permute-start.15
  65.7 0.5 collective-permute-start.24
  66.3 2.4 %collective-permute-done.21.refs_21_ = bf16[3,80,640]{2,1,0:T(8,128)(2,1)} collective-permute-done((bf16[3,80,640]{2,1,0:T(8,128)(2,1)}, bf16[3,80,640]{2,1,0:T(8,128)(2,1)}, u32[]{:S(2)}, u32[]{:S(2)}) %collective-permute-start.21) | collective-permute-done | bytes 307232 | tf_op jit(solution)/shard_map/ppermute | solution.py:27
  68.7 3.2 %collective-permute-start.25 = (bf16[3,80,640]{2,1,0:T(8,128)(2,1)}, bf16[3,80,640]{2,1,0:T(8,128)(2,1)}, u32[]{:S(2)}, u32[]{:S(2)}) collective-permute-start(bf16[3,80,640]{2,1,0:T(8,128)(2,1)} %collective-permute-done.21.refs_21_), channel_id=1, source_target_pairs={{0,96},{32,0},{64,32},{96,64},{1,97},{33,1},{65,33},{97,65},{2,98}... | collective-permute-start | bytes 921608 | tf_op jit(solution)/shard_map/ppermute | solution.py:27
  72.0 0.1 copy.7.rates
  72.1 1.6 %collective-permute-done.22.refs_22_ = bf16[3,80,640]{2,1,0:T(8,128)(2,1)} collective-permute-done((bf16[3,80,640]{2,1,0:T(8,128)(2,1)}, bf16[3,80,640]{2,1,0:T(8,128)(2,1)}, u32[]{:S(2)}, u32[]{:S(2)}) %collective-permute-start.22) | collective-permute-done | bytes 307232 | tf_op jit(solution)/shard_map/ppermute | solution.py:27
  73.7 4.5 %collective-permute-done.24.refs_24_ = bf16[3,80,640]{2,1,0:T(8,128)(2,1)} collective-permute-done((bf16[3,80,640]{2,1,0:T(8,128)(2,1)}, bf16[3,80,640]{2,1,0:T(8,128)(2,1)}, u32[]{:S(2)}, u32[]{:S(2)}) %collective-permute-start.24) | collective-permute-done | bytes 307232 | tf_op jit(solution)/shard_map/ppermute | solution.py:27
  78.2 0.9 copy-done.4
  79.2 0.9 copy-done.6
  80.1 17.9 %convolve.1 = bf16[16,40,640]{2,1,0:T(8,128)(2,1)} custom-call(s32[1]{0:T(128)} %copy.10.sizes, f32[160,1]{1,0:T(8,128)S(1)} %copy.7.rates, bf16[160,640]{1,0:T(8,128)(2,1)S(1)} %copy-done.2, bf16[160,640]{1,0:T(8,128)(2,1)S(1)} %collective-permute-done.2.refs_1_, bf16[160,640]{1,0:T(8,128)(2,1)S(1)} %collective-permute-done.3.refs_2_, ...), custom_call_target="tpu_custom_call" | custom-call | flops 4456448000 | bytes 6553600 | tf_op jit(solution)/shard_map/convolve/pallas_call | solution.py:215
  98.0 17.6 %all_to_all.5.packets = bf16[16,40,640]{2,1,0:T(8,128)(2,1)} all-to-all(bf16[16,40,640]{2,1,0:T(8,128)(2,1)} %convolve.1), channel_id=1, replica_groups=mesh['tx'=4,'ty'=4,'sector'=8] {'tx','ty'}, dimensions={0} | all-to-all | bytes 1638400 | tf_op jit(solution)/shard_map/all_to_all | solution.py:308
  115.6 2.4 %assemble.1 = bf16[640,640]{1,0:T(8,128)(2,1)} custom-call(bf16[16,40,640]{2,1,0:T(8,128)(2,1)} %all_to_all.5.packets), custom_call_target="tpu_custom_call" | custom-call | tf_op jit(solution)/shard_map/assemble/pallas_call | solution.py:248
  (45 shorter events, 0.4 us)
Async XLA Ops:
  0.0 71.9 %copy-start = (f32[1,640]{1,0:T(1,128)S(1)}, f32[1,640]{1,0:T(1,128)}, u32[]{:S(2)}) copy-start(f32[1,640]{1,0:T(1,128)} %param.8) | copy-start | bytes 7684
  2.1 1.9 %copy-start.7 = (bf16[640,640]{1,0:T(8,128)(2,1)}, bf16[640,640]{1,0:T(8,128)(2,1)S(1)}, u32[]{:S(2)}) copy-start(bf16[640,640]{1,0:T(8,128)(2,1)S(1)} %and_select_fusion.masked) | copy-start | bytes 2457604
  2.2 18.6 %collective-permute-start = (bf16[640,640]{1,0:T(8,128)(2,1)S(1)}, bf16[640,640]{1,0:T(8,128)(2,1)S(1)}, u32[]{:S(2)}, u32[]{:S(2)}) collective-permute-start(bf16[640,640]{1,0:T(8,128)(2,1)S(1)} %and_select_fusion.masked), channel_id=1, source_target_pairs={{1,0},{2,1},{3,2},{4,3},{5,4},{6,5},{7,6},{9,8},{10,9},{11,10},{12... | collective-permute-start | bytes 2457608 | tf_op jit(solution)/shard_map/ppermute | solution.py:22
  8.3 13.9 %collective-permute-start.1 = (bf16[640,640]{1,0:T(8,128)(2,1)}, bf16[640,640]{1,0:T(8,128)(2,1)S(1)}, u32[]{:S(2)}, u32[]{:S(2)}) collective-permute-start(bf16[640,640]{1,0:T(8,128)(2,1)} %get-tuple-element.26), channel_id=1, source_target_pairs={{0,1},{1,2},{2,3},{3,4},{4,5},{5,6},{6,7},{8,9},{9,10},{10,11},{11... | collective-permute-start | bytes 2457608 | tf_op jit(solution)/shard_map/ppermute | solution.py:22
  13.6 18.0 %collective-permute-start.5 = (bf16[160,640]{1,0:T(8,128)(2,1)}, bf16[160,640]{1,0:T(8,128)(2,1)S(1)}, u32[]{:S(2)}, u32[]{:S(2)}) collective-permute-start(bf16[160,640]{1,0:T(8,128)(2,1)} %get-tuple-element.35), channel_id=1, source_target_pairs={{0,8},{8,16},{16,24},{24,0},{1,9},{9,17},{17,25},{25,1},{2,10},{10... | collective-permute-start | bytes 614408 | tf_op jit(solution)/shard_map/ppermute | solution.py:27
  15.2 17.9 %collective-permute-start.6 = (bf16[160,640]{1,0:T(8,128)(2,1)}, bf16[160,640]{1,0:T(8,128)(2,1)S(1)}, u32[]{:S(2)}, u32[]{:S(2)}) collective-permute-start(bf16[160,640]{1,0:T(8,128)(2,1)} %get-tuple-element.36), channel_id=1, source_target_pairs={{0,16},{8,24},{16,0},{24,8},{1,17},{9,25},{17,1},{25,9},{2,18},{10... | collective-permute-start | bytes 614408 | tf_op jit(solution)/shard_map/ppermute | solution.py:27
  18.1 18.2 %collective-permute-start.7 = (bf16[160,640]{1,0:T(8,128)(2,1)}, bf16[160,640]{1,0:T(8,128)(2,1)S(1)}, u32[]{:S(2)}, u32[]{:S(2)}) collective-permute-start(bf16[160,640]{1,0:T(8,128)(2,1)} %get-tuple-element.37), channel_id=1, source_target_pairs={{0,24},{8,0},{16,8},{24,16},{1,25},{9,1},{17,9},{25,17},{2,26},{10... | collective-permute-start | bytes 614408 | tf_op jit(solution)/shard_map/ppermute | solution.py:27
  20.8 2.3 %copy-start.8 = (bf16[640,640]{1,0:T(8,128)(2,1)}, bf16[640,640]{1,0:T(8,128)(2,1)S(1)}, u32[]{:S(2)}) copy-start(bf16[640,640]{1,0:T(8,128)(2,1)S(1)} %collective-permute-done.above) | copy-start | bytes 2457604
  22.1 0.9 copy-start.9
  23.0 17.8 %copy-start.1 = (bf16[160,640]{1,0:T(8,128)(2,1)S(1)}, bf16[160,640]{1,0:T(8,128)(2,1)}, u32[]{:S(2)}) copy-start(bf16[160,640]{1,0:T(8,128)(2,1)} %get-tuple-element.28.refs_13_) | copy-start | bytes 614404
  27.4 9.9 %collective-permute-start.2 = (bf16[160,640]{1,0:T(8,128)(2,1)}, bf16[160,640]{1,0:T(8,128)(2,1)S(1)}, u32[]{:S(2)}, u32[]{:S(2)}) collective-permute-start(bf16[160,640]{1,0:T(8,128)(2,1)} %get-tuple-element.32), channel_id=1, source_target_pairs={{0,32},{32,64},{64,96},{96,0},{1,33},{33,65},{65,97},{97,1},{2,34}... | collective-permute-start | bytes 614408 | tf_op jit(solution)/shard_map/ppermute | solution.py:27
  28.9 11.9 %collective-permute-start.3 = (bf16[160,640]{1,0:T(8,128)(2,1)}, bf16[160,640]{1,0:T(8,128)(2,1)S(1)}, u32[]{:S(2)}, u32[]{:S(2)}) collective-permute-start(bf16[160,640]{1,0:T(8,128)(2,1)} %get-tuple-element.33), channel_id=1, source_target_pairs={{0,64},{32,96},{64,0},{96,32},{1,65},{33,97},{65,1},{97,33},{2,66}... | collective-permute-start | bytes 614408 | tf_op jit(solution)/shard_map/ppermute | solution.py:27
  31.6 10.5 %collective-permute-start.4 = (bf16[160,640]{1,0:T(8,128)(2,1)}, bf16[160,640]{1,0:T(8,128)(2,1)S(1)}, u32[]{:S(2)}, u32[]{:S(2)}) collective-permute-start(bf16[160,640]{1,0:T(8,128)(2,1)} %get-tuple-element.34), channel_id=1, source_target_pairs={{0,96},{32,0},{64,32},{96,64},{1,97},{33,1},{65,33},{97,65},{2,98}... | collective-permute-start | bytes 614408 | tf_op jit(solution)/shard_map/ppermute | solution.py:27
  33.1 11.7 %collective-permute-start.10 = (bf16[160,640]{1,0:T(8,128)(2,1)}, bf16[160,640]{1,0:T(8,128)(2,1)S(1)}, u32[]{:S(2)}, u32[]{:S(2)}) collective-permute-start(bf16[160,640]{1,0:T(8,128)(2,1)} %get-tuple-element.31.refs_0_), channel_id=1, source_target_pairs={{0,16},{8,24},{16,0},{24,8},{1,17},{9,25},{17,1},{25,9},{2,18},{10... | collective-permute-start | bytes 614408 | tf_op jit(solution)/shard_map/ppermute | solution.py:27
  36.3 9.1 %collective-permute-start.9 = (bf16[160,640]{1,0:T(8,128)(2,1)}, bf16[160,640]{1,0:T(8,128)(2,1)S(1)}, u32[]{:S(2)}, u32[]{:S(2)}) collective-permute-start(bf16[160,640]{1,0:T(8,128)(2,1)} %get-tuple-element.31.refs_0_), channel_id=1, source_target_pairs={{0,24},{8,0},{16,8},{24,16},{1,25},{9,1},{17,9},{25,17},{2,26},{10... | collective-permute-start | bytes 614408 | tf_op jit(solution)/shard_map/ppermute | solution.py:27
  37.4 8.0 %collective-permute-start.8 = (bf16[160,640]{1,0:T(8,128)(2,1)}, bf16[160,640]{1,0:T(8,128)(2,1)S(1)}, u32[]{:S(2)}, u32[]{:S(2)}) collective-permute-start(bf16[160,640]{1,0:T(8,128)(2,1)} %get-tuple-element.31.refs_0_), channel_id=1, source_target_pairs={{0,8},{8,16},{16,24},{24,0},{1,9},{9,17},{17,25},{25,1},{2,10},{10... | collective-permute-start | bytes 614408 | tf_op jit(solution)/shard_map/ppermute | solution.py:27
  40.9 9.5 %collective-permute-start.19 = (bf16[160,640]{1,0:T(8,128)(2,1)S(1)}, bf16[160,640]{1,0:T(8,128)(2,1)S(1)}, u32[]{:S(2)}, u32[]{:S(2)}) collective-permute-start(bf16[160,640]{1,0:T(8,128)(2,1)S(1)} %copy-done.1), channel_id=1, source_target_pairs={{0,64},{32,96},{64,0},{96,32},{1,65},{33,97},{65,1},{97,33},{2,66}... | collective-permute-start | bytes 614408 | tf_op jit(solution)/shard_map/ppermute | solution.py:27
  42.1 11.3 %collective-permute-start.18 = (bf16[160,640]{1,0:T(8,128)(2,1)S(1)}, bf16[160,640]{1,0:T(8,128)(2,1)S(1)}, u32[]{:S(2)}, u32[]{:S(2)}) collective-permute-start(bf16[160,640]{1,0:T(8,128)(2,1)S(1)} %copy-done.1), channel_id=1, source_target_pairs={{0,96},{32,0},{64,32},{96,64},{1,97},{33,1},{65,33},{97,65},{2,98}... | collective-permute-start | bytes 614408 | tf_op jit(solution)/shard_map/ppermute | solution.py:27
  44.8 9.3 %collective-permute-start.17 = (bf16[160,640]{1,0:T(8,128)(2,1)S(1)}, bf16[160,640]{1,0:T(8,128)(2,1)S(1)}, u32[]{:S(2)}, u32[]{:S(2)}) collective-permute-start(bf16[160,640]{1,0:T(8,128)(2,1)S(1)} %copy-done.1), channel_id=1, source_target_pairs={{0,32},{32,64},{64,96},{96,0},{1,33},{33,65},{65,97},{97,1},{2,34}... | collective-permute-start | bytes 614408 | tf_op jit(solution)/shard_map/ppermute | solution.py:27
  45.5 10.6 %collective-permute-start.13 = (bf16[3,80,640]{2,1,0:T(8,128)(2,1)S(1)}, bf16[3,80,640]{2,1,0:T(8,128)(2,1)S(1)}, u32[]{:S(2)}, u32[]{:S(2)}) collective-permute-start(bf16[3,80,640]{2,1,0:T(8,128)(2,1)S(1)} %pad_maximum_fusion.1), channel_id=1, source_target_pairs={{0,8},{8,16},{16,24},{24,0},{1,9},{9,17},{17,25},{25,1},{2,10},{10... | collective-permute-start | bytes 921608 | tf_op jit(solution)/shard_map/ppermute | solution.py:27
  46.9 10.2 %collective-permute-start.12 = (bf16[3,80,640]{2,1,0:T(8,128)(2,1)S(1)}, bf16[3,80,640]{2,1,0:T(8,128)(2,1)S(1)}, u32[]{:S(2)}, u32[]{:S(2)}) collective-permute-start(bf16[3,80,640]{2,1,0:T(8,128)(2,1)S(1)} %pad_maximum_fusion.1), channel_id=1, source_target_pairs={{0,24},{8,0},{16,8},{24,16},{1,25},{9,1},{17,9},{25,17},{2,26},{10... | collective-permute-start | bytes 921608 | tf_op jit(solution)/shard_map/ppermute | solution.py:27
  49.7 28.5 %copy-start.2 = (bf16[160,640]{1,0:T(8,128)(2,1)S(1)}, bf16[160,640]{1,0:T(8,128)(2,1)}, u32[]{:S(2)}) copy-start(bf16[160,640]{1,0:T(8,128)(2,1)} %get-tuple-element.31.refs_0_) | copy-start | bytes 614404
  50.4 11.6 %collective-permute-start.14 = (bf16[3,80,640]{2,1,0:T(8,128)(2,1)S(1)}, bf16[3,80,640]{2,1,0:T(8,128)(2,1)S(1)}, u32[]{:S(2)}, u32[]{:S(2)}) collective-permute-start(bf16[3,80,640]{2,1,0:T(8,128)(2,1)S(1)} %pad_maximum_fusion), channel_id=1, source_target_pairs={{0,24},{8,0},{16,8},{24,16},{1,25},{9,1},{17,9},{25,17},{2,26},{10... | collective-permute-start | bytes 921608 | tf_op jit(solution)/shard_map/ppermute | solution.py:27
  53.4 0.7 copy-start.3
  54.1 8.4 %collective-permute-start.11 = (bf16[3,80,640]{2,1,0:T(8,128)(2,1)S(1)}, bf16[3,80,640]{2,1,0:T(8,128)(2,1)S(1)}, u32[]{:S(2)}, u32[]{:S(2)}) collective-permute-start(bf16[3,80,640]{2,1,0:T(8,128)(2,1)S(1)} %pad_maximum_fusion), channel_id=1, source_target_pairs={{0,8},{8,16},{16,24},{24,0},{1,9},{9,17},{17,25},{25,1},{2,10},{10... | collective-permute-start | bytes 921608 | tf_op jit(solution)/shard_map/ppermute | solution.py:27
  54.1 0.7 copy-start.5
  54.8 10.7 %collective-permute-start.23 = (bf16[3,80,640]{2,1,0:T(8,128)(2,1)S(1)}, bf16[3,80,640]{2,1,0:T(8,128)(2,1)S(1)}, u32[]{:S(2)}, u32[]{:S(2)}) collective-permute-start(bf16[3,80,640]{2,1,0:T(8,128)(2,1)S(1)} %pad_maximum_fusion.2), channel_id=1, source_target_pairs={{0,96},{32,0},{64,32},{96,64},{1,97},{33,1},{65,33},{97,65},{2,98}... | collective-permute-start | bytes 921608 | tf_op jit(solution)/shard_map/ppermute | solution.py:27
  56.1 9.6 %collective-permute-start.20 = (bf16[3,80,640]{2,1,0:T(8,128)(2,1)S(1)}, bf16[3,80,640]{2,1,0:T(8,128)(2,1)}, u32[]{:S(2)}, u32[]{:S(2)}) collective-permute-start(bf16[3,80,640]{2,1,0:T(8,128)(2,1)S(1)} %pad_maximum_fusion.2), channel_id=1, source_target_pairs={{0,32},{32,64},{64,96},{96,0},{1,33},{33,65},{65,97},{97,1},{2,34}... | collective-permute-start | bytes 921608 | tf_op jit(solution)/shard_map/ppermute | solution.py:27
  57.1 11.6 %collective-permute-start.21 = (bf16[3,80,640]{2,1,0:T(8,128)(2,1)}, bf16[3,80,640]{2,1,0:T(8,128)(2,1)}, u32[]{:S(2)}, u32[]{:S(2)}) collective-permute-start(bf16[3,80,640]{2,1,0:T(8,128)(2,1)} %pad_maximum_fusion.3), channel_id=1, source_target_pairs={{0,96},{32,0},{64,32},{96,64},{1,97},{33,1},{65,33},{97,65},{2,98}... | collective-permute-start | bytes 921608 | tf_op jit(solution)/shard_map/ppermute | solution.py:27
  61.9 3.8 %copy-start.10 = (bf16[3,80,640]{2,1,0:T(8,128)(2,1)}, bf16[3,80,640]{2,1,0:T(8,128)(2,1)S(1)}, u32[]{:S(2)}) copy-start(bf16[3,80,640]{2,1,0:T(8,128)(2,1)S(1)} %collective-permute-done.14.refs_10_) | copy-start | bytes 921604
  61.9 11.7 %collective-permute-start.22 = (bf16[3,80,640]{2,1,0:T(8,128)(2,1)}, bf16[3,80,640]{2,1,0:T(8,128)(2,1)}, u32[]{:S(2)}, u32[]{:S(2)}) collective-permute-start(bf16[3,80,640]{2,1,0:T(8,128)(2,1)} %pad_maximum_fusion.3), channel_id=1, source_target_pairs={{0,32},{32,64},{64,96},{96,0},{1,33},{33,65},{65,97},{97,1},{2,34}... | collective-permute-start | bytes 921608 | tf_op jit(solution)/shard_map/ppermute | solution.py:27
  62.5 11.2 %collective-permute-start.16 = (bf16[3,80,640]{2,1,0:T(8,128)(2,1)S(1)}, bf16[3,80,640]{2,1,0:T(8,128)(2,1)}, u32[]{:S(2)}, u32[]{:S(2)}) collective-permute-start(bf16[3,80,640]{2,1,0:T(8,128)(2,1)S(1)} %collective-permute-done.12.refs_8_), channel_id=1, source_target_pairs={{0,24},{8,0},{16,8},{24,16},{1,25},{9,1},{17,9},{25,17},{2,26},{10... | collective-permute-start | bytes 921608 | tf_op jit(solution)/shard_map/ppermute | solution.py:27
  65.5 0.8 copy-start.11
  65.5 8.2 %collective-permute-start.15 = (bf16[3,80,640]{2,1,0:T(8,128)(2,1)S(1)}, bf16[3,80,640]{2,1,0:T(8,128)(2,1)}, u32[]{:S(2)}, u32[]{:S(2)}) collective-permute-start(bf16[3,80,640]{2,1,0:T(8,128)(2,1)S(1)} %collective-permute-done.11.refs_7_), channel_id=1, source_target_pairs={{0,8},{8,16},{16,24},{24,0},{1,9},{9,17},{17,25},{25,1},{2,10},{10... | collective-permute-start | bytes 921608 | tf_op jit(solution)/shard_map/ppermute | solution.py:27
  65.7 12.5 %collective-permute-start.24 = (bf16[3,80,640]{2,1,0:T(8,128)(2,1)}, bf16[3,80,640]{2,1,0:T(8,128)(2,1)}, u32[]{:S(2)}, u32[]{:S(2)}) collective-permute-start(bf16[3,80,640]{2,1,0:T(8,128)(2,1)} %collective-permute-done.20.refs_20_), channel_id=1, source_target_pairs={{0,32},{32,64},{64,96},{96,0},{1,33},{33,65},{65,97},{97,1},{2,34}... | collective-permute-start | bytes 921608 | tf_op jit(solution)/shard_map/ppermute | solution.py:27
  68.7 9.5 %collective-permute-start.25 = (bf16[3,80,640]{2,1,0:T(8,128)(2,1)}, bf16[3,80,640]{2,1,0:T(8,128)(2,1)}, u32[]{:S(2)}, u32[]{:S(2)}) collective-permute-start(bf16[3,80,640]{2,1,0:T(8,128)(2,1)} %collective-permute-done.21.refs_21_), channel_id=1, source_target_pairs={{0,96},{32,0},{64,32},{96,64},{1,97},{33,1},{65,33},{97,65},{2,98}... | collective-permute-start | bytes 921608 | tf_op jit(solution)/shard_map/ppermute | solution.py:27
  78.2 0.9 copy-start.4
  79.2 0.9 copy-start.6

commit v4 on v3

v4 whole, which is shorter than its diff:
```python
import functools

import jax
import jax.numpy as jnp
import numpy as np
from jax import lax
from jax.experimental import pallas as pl
from jax.experimental.pallas import tpu as pltpu
from jax.sharding import Mesh
from jax.sharding import PartitionSpec as P

MIB = 1024 * 1024
VMEM = pl.BlockSpec(memory_space=pltpu.VMEM)
SMEM = pl.BlockSpec(memory_space=pltpu.SMEM)
HBM = pl.BlockSpec(memory_space=pltpu.HBM)
NT = (((1,), (1,)), ((), ()))


def shifted(block, axis, distance):
    devices = range(lax.axis_size(axis))
    route = [(i - distance, i) for i in devices if i - distance in devices]
    return lax.ppermute(block, axis, route)


def ring(block, axis, distance):
    n = lax.axis_size(axis)
    return lax.ppermute(block, axis, [(i, (i + distance) % n) for i in range(n)])


def tied(value, *others):
    return lax.optimization_barrier((value, *others))[0]


def spread(block, axis):
    return [(-d, ring(block, axis, d)) for d in (1, -1, 2)]


def relay_gather(block, axis):
    half = block.shape[0] // 2
    below, above = ring(block, axis, 1), ring(block, axis, -1)
    return below, above, ring(below[:half], axis, 1), ring(above[half:], axis, -1)


def live(shape, size, first_row=0):
    row = lax.broadcasted_iota(jnp.int32, shape, 0) + first_row
    column = lax.broadcasted_iota(jnp.int32, shape, 1)
    return (row < size) & (column < size)


def dot(a, b):
    return jnp.dot(a, b, preferred_element_type=jnp.float32)


def raise_kernel(sizes, prop, operator, masked, upward):
    inner = prop[...].astype(jnp.float32)
    inner = jnp.where(live(inner.shape, sizes[0]), inner, 0.0).astype(jnp.bfloat16)
    masked[...] = inner
    r = operator[...]
    raised = dot(r, inner).astype(jnp.bfloat16)
    upward[...] = lax.dot_general(raised, r, NT, preferred_element_type=jnp.float32).astype(
        jnp.bfloat16
    )


def raise_terms(sizes, prop, operator):
    states = prop.shape[0]
    square = jax.ShapeDtypeStruct((states, states), jnp.bfloat16)
    return pl.pallas_call(
        raise_kernel,
        out_shape=(square, square),
        in_specs=[SMEM, VMEM, VMEM],
        out_specs=(VMEM, VMEM),
        cost_estimate=pl.CostEstimate(
            flops=4 * states**3, bytes_accessed=8 * states**2, transcendentals=0
        ),
        name="raise_terms",
    )(sizes, prop, operator)


def turn_kernel(masked, operator, turned, flipped):
    turned[...] = masked[...].T
    flipped[...] = operator[...].T


def turn(masked, operator):
    states = masked.shape[0]
    square = jax.ShapeDtypeStruct((states, states), jnp.bfloat16)
    return pl.pallas_call(
        turn_kernel,
        out_shape=(square, square),
        in_specs=[VMEM, VMEM],
        out_specs=(VMEM, VMEM),
        cost_estimate=pl.CostEstimate(flops=0, bytes_accessed=8 * states**2, transcendentals=0),
        name="turn",
    )(masked, operator)


def energy_kernel(sizes, particle, hole, *refs):
    sources, (*outs,), copies, sems = refs[:4], refs[4:-5], refs[-5:-1], refs[-1]
    moves = [
        pltpu.make_async_copy(src, dst, sems.at[i])
        for i, (src, dst) in enumerate(zip(sources, copies))
    ]
    for move in moves:
        move.start()
    n = len(outs)
    rows = outs[0].shape[0]
    here_x = lax.axis_index("tx")
    for move in moves:
        move.wait()
    flipped, above, operator, below = copies
    inner = above[...]
    r = operator[...]
    for d in (2, 1, 3, 0):
        first = pl.multiple_of(lax.rem(here_x + d, n) * rows, 32)
        lowered = dot(flipped[pl.ds(first, rows), :], inner).astype(jnp.bfloat16)
        downward = dot(lowered, r)
        raised = below[pl.ds(first, rows), :].astype(jnp.float32)
        both = particle[0] * raised + hole[0] * downward
        kept = live(both.shape, sizes[0], first)
        outs[d][...] = jnp.where(kept, both, 0.0).astype(jnp.bfloat16)


def energy_blocks(sizes, particle, hole, above, below, operator, flipped, n):
    states = above.shape[0]
    block = jax.ShapeDtypeStruct((states // n, states), jnp.bfloat16)
    return pl.pallas_call(
        energy_kernel,
        out_shape=(block,) * n,
        in_specs=[SMEM] * 3 + [HBM] * 4,
        out_specs=(VMEM,) * n,
        scratch_shapes=[pltpu.VMEM((states, states), jnp.bfloat16)] * 4
        + [pltpu.SemaphoreType.DMA((4,))],
        cost_estimate=pl.CostEstimate(
            flops=4 * states**3, bytes_accessed=10 * states**2, transcendentals=0
        ),
        name="energy_blocks",
    )(sizes, particle, hole, flipped, above, operator, below)


def around(here, offset, n):
    return lax.rem(here + offset + n, n)


def placed(parts, plan, n, e_all, g_all, pad, sems):
    here_x = lax.axis_index("tx")
    copies = []
    for part, (kind, offset, slot) in zip(parts, plan):
        if kind == "e":
            copies.append((part, e_all.at[slot, around(here_x, offset, n)]))
        elif kind == "rest":
            for d in range(1, n):
                copies.append((part.at[d - 1], e_all.at[slot, around(here_x, -d, n)]))
        else:
            some = part.shape[0]
            start = pad + around(here_x, offset, n) * n + slot * some
            copies.append((part, g_all.at[pl.ds(start, some)]))
    moves = [
        pltpu.make_async_copy(src, dst, sems.at[i]) for i, (src, dst) in enumerate(copies)
    ]
    for move in moves:
        move.start()
    return moves


def near_kernel(plan, n, *refs):
    parts = refs[: len(plan)]
    total, e_all, g_all, sems = refs[len(plan) :]
    rows = total.shape[2]
    moves = placed(parts, plan, n, e_all, g_all, n - 1, sems)
    g_all[: n - 1] = jnp.zeros((n - 1, *g_all.shape[1:]), jnp.bfloat16)
    here_y = lax.axis_index("ty")
    for move in moves:
        move.wait()

    for slot in range(n - 1):
        source = lax.rem(here_y + slot + slot // 2, n)
        for v in range(n * n):
            lane, first = v % n, v // n
            left = e_all[slot, : n - first].reshape((n - first) * rows, -1)
            right = g_all[v - source + n - 1]
            product = lax.dot_general(left, right, NT, preferred_element_type=jnp.float32)
            if slot == 0 and first == 0:
                total[lane] = product
            else:
                total[lane, first * rows :, :] += product


def far_kernel(plan, n, step_size, sizes, rates, near, *refs):
    parts = refs[: len(plan)]
    out, e_all, g_all, total, sems = refs[len(plan) :]
    rows = total.shape[2]
    moves = placed(parts, plan, n, e_all, g_all, n - 1, sems)
    g_all[: n - 1] = jnp.zeros((n - 1, *g_all.shape[1:]), jnp.bfloat16)
    here_x, here_y, size = lax.axis_index("tx"), lax.axis_index("ty"), sizes[0]
    source = lax.rem(here_y + n // 2, n)
    for move in moves:
        move.wait()
    for v in range(n * n):
        lane, first = v % n, v // n
        left = e_all[0, : n - first].reshape((n - first) * rows, -1)
        right = g_all[v - source + n - 1]
        product = lax.dot_general(left, right, NT, preferred_element_type=jnp.float32)
        if first == 0:
            total[lane] = near[lane] + product
        else:
            total[lane, first * rows :, :] += product

    quarter = rows // n
    scale = step_size * step_size
    for b in range(n):
        row = lax.broadcasted_iota(jnp.int32, (quarter, rows), 0) + b * quarter
        column = lax.broadcasted_iota(jnp.int32, (quarter, rows), 1)
        starts = (row == column) & (here_x == here_y) & (row + here_x * rows < size)
        rate = rates[b * quarter : (b + 1) * quarter]
        decay = jnp.broadcast_to(jnp.exp(-step_size * rate), (quarter, rows))
        for t in range(n * n):
            top = t // n * rows + b * quarter
            term = scale * total[t % n, top : top + quarter]
            fresh = (jnp.where(starts, 1.0, 0.0) if t == 0 else decay * fresh) - term
            out[t, :, b * rows : (b + 1) * rows] = fresh.astype(jnp.bfloat16)


def copies_of(plan, n):
    return sum(n - 1 if kind == "rest" else 1 for kind, *_ in plan)


def convolve_near(entries, n):
    plan, parts = [e[:3] for e in entries], [e[3] for e in entries]
    rows, states = parts[0].shape
    return pl.pallas_call(
        functools.partial(near_kernel, plan, n),
        out_shape=jax.ShapeDtypeStruct((n, n * rows, rows), jnp.float32),
        in_specs=[HBM] * len(parts),
        out_specs=VMEM,
        scratch_shapes=[
            pltpu.VMEM((n - 1, n, rows, states), jnp.bfloat16),
            pltpu.VMEM((n * n + n - 1, rows, states), jnp.bfloat16),
            pltpu.SemaphoreType.DMA((copies_of(plan, n),)),
        ],
        compiler_params=pltpu.CompilerParams(vmem_limit_bytes=52 * MIB),
        cost_estimate=pl.CostEstimate(
            flops=200 * rows * rows * states,
            bytes_accessed=56 * rows * states,
            transcendentals=0,
        ),
        name="convolve_near",
    )(*parts)


def convolve_far(entries, near, sizes, rates, n, step_size):
    plan, parts = [e[:3] for e in entries], [e[3] for e in entries]
    rows, states = parts[0].shape
    return pl.pallas_call(
        functools.partial(far_kernel, plan, n, step_size),
        out_shape=jax.ShapeDtypeStruct((n * n, rows // n, states), jnp.bfloat16),
        in_specs=[SMEM, VMEM, VMEM] + [HBM] * len(parts),
        out_specs=VMEM,
        scratch_shapes=[
            pltpu.VMEM((1, n, rows, states), jnp.bfloat16),
            pltpu.VMEM((n * n + n - 1, rows, states), jnp.bfloat16),
            pltpu.VMEM((n, n * rows, rows), jnp.float32),
            pltpu.SemaphoreType.DMA((copies_of(plan, n),)),
        ],
        compiler_params=pltpu.CompilerParams(vmem_limit_bytes=52 * MIB),
        cost_estimate=pl.CostEstimate(
            flops=72 * rows * rows * states,
            bytes_accessed=60 * rows * states,
            transcendentals=0,
        ),
        name="convolve_far",
    )(sizes, rates, near, *parts)


def assemble_kernel(n, packets, out):
    quarter, states = packets.shape[1:]
    rows = states // n
    for x in range(n):
        for b in range(n):
            out[x * rows + b * quarter : x * rows + (b + 1) * quarter, :] = jnp.concatenate(
                [packets[x * n + y, :, b * rows : (b + 1) * rows] for y in range(n)], axis=1
            )


def assemble(packets, n):
    states = packets.shape[2]
    return pl.pallas_call(
        functools.partial(assemble_kernel, n),
        out_shape=jax.ShapeDtypeStruct((states, states), jnp.bfloat16),
        in_specs=[VMEM],
        out_specs=VMEM,
        name="assemble",
    )(packets)


def per_device(propagator, rising_op, energies, hyb_particle, hyb_hole, sector_sizes):
    states = propagator.shape[2]
    n = lax.axis_size("tx")
    step_size = 1.0 / (n * n)
    rows = states // n
    here_x = lax.axis_index("tx")
    operator = rising_op[0]

    masked, upward = raise_terms(sector_sizes, propagator[0, 0], operator)
    below = shifted(upward, "sector", 1)
    above = shifted(masked, "sector", -1)

    turned, flipped = turn(masked, operator)
    columns = lax.all_to_all(turned.reshape(n, rows, states), "ty", 0, 0, tiled=True)

    own, *away = energy_blocks(
        sector_sizes, hyb_particle, hyb_hole, above, below, operator, flipped, n
    )
    crossed = {d: ring(away[d - 1], "tx", d) for d in (2, 1, 3)}
    crossed = [crossed[d] for d in range(1, n)]
    down, up, across = (ring(own, "ty", d) for d in (1, -1, 2))
    crossed, down, up, across = lax.optimization_barrier((crossed, down, up, across))

    previous_g, next_g, far_first, far_second = relay_gather(columns, "tx")

    rest = jnp.stack(crossed)
    rest_down, rest_up = ring(rest, "ty", 1), ring(rest, "ty", -1)
    rest_late = tied(rest, rest_down, rest_up)
    rest_across = ring(rest_late, "ty", 2)

    entries_g = [
        ("g", 0, 0, columns),
        ("g", -1, 0, previous_g),
        ("g", 1, 0, next_g),
        ("g", 2, 0, far_first),
        ("g", 2, 1, far_second),
    ]
    entries_near = (
        [("e", 0, 0, own)]
        + [("e", -d, 0, crossed[d - 1]) for d in range(1, n)]
        + [("e", 0, 2, down), ("rest", None, 2, rest_down)]
        + [("e", 0, 1, up), ("rest", None, 1, rest_up)]
        + entries_g
    )
    entries_far = [("e", 0, 0, across), ("rest", None, 0, rest_across)] + entries_g
    rates = lax.dynamic_slice_in_dim(energies[0], here_x * rows, rows, 0)[:, None]
    near = convolve_near(entries_near, n)
    packets = convolve_far(entries_far, near, sector_sizes, rates, n, step_size)
    packets = lax.all_to_all(packets, ("tx", "ty"), 0, 0, tiled=True)
    return assemble(packets, n)[None, None]


def solution(mesh):
    n = round(mesh.shape["tm"] ** 0.5)
    split = Mesh(
        np.asarray(mesh.devices).reshape(n, n, mesh.shape["sector"]), ("tx", "ty", "sector")
    )
    times = ("tx", "ty")
    placed = (
        P("sector", times, None, None),
        P("sector", None, None),
        P("sector", None),
        P(times),
        P(times),
        P("sector"),
    )
    return jax.shard_map(
        per_device,
        mesh=split,
        in_specs=placed,
        out_specs=P("sector", times, None, None),
        check_vma=False,
    )
```

time: 120 us -> 121 us (level)
  the two profiles are of different devices: /device:TPU:32 before, /device:TPU:0 now
where the time goes in v4:
time: 121 us
  Pallas kernels  35.4 us (29%)
  starting transfers between devices  30.9 us (26%)
  waiting for transfers between devices  25.4 us (21%)
  blocking collectives  20.1 us (17%)
  local copies, waits for them, and re-layouts  5.54 us (5%)
  between operations  2.13 us (2%)
    ppermute x13, waiting for transfers between devices, ring(): lax.ppermute(block, axis, [(i, (i + distance) % n) for i in range(n)])  25.4 us
    ppermute x13, starting transfers between devices, ring(): lax.ppermute(block, axis, [(i, (i + distance) % n) for i in range(n)])  22 us
    all_to_all x1, blocking collectives, per_device(): packets = lax.all_to_all(packets, ('tx', 'ty'), 0, 0, tiled=True)  20.1 us
    pallas_call x1, Pallas kernels, convolve_near(): pl.pallas_call(functools.partial(near_kernel, plan, n), out_shape=jax.Sha...  13.3 us
    pallas_call x1, Pallas kernels, convolve_far(): pl.pallas_call(functools.partial(far_kernel, plan, n, step_size), out_sha...  8.41 us
    all_to_all x1, starting transfers between devices, per_device(): lax.all_to_all(turned.reshape(n, rows, states), 'ty', 0, 0, tiled=True)  4.54 us
    pallas_call x1, Pallas kernels, energy_blocks(): pl.pallas_call(energy_kernel, out_shape=(block,) * n, in_specs=[SMEM] * 3...  4.42 us
    unnamed x20, local copies, waits for them, and re-layouts  4.37 us
  transfers between devices with their start and end apart: 16, of which 6 were waited for; matrix products, arithmetic and copies ran while one was open for 2% of the time, Pallas kernels for 17%

profile of v4, /device:TPU:0, one launch (start us, length us, event | category | flops | bytes accessed | tf_op | source)
XLA Modules:
  0.0 120.5 jit_solution(17636420963049814755)
XLA Ops:
  0.7 4.0 %raise_terms.1 = (bf16[640,640]{1,0:T(8,128)(2,1)}, bf16[640,640]{1,0:T(8,128)(2,1)}) custom-call(s32[1]{0:T(128)S(6)} %copy.10.sizes, bf16[640,640]{1,0:T(8,128)(2,1)} %bitcast.16, bf16[640,640]{1,0:T(8,128)(2,1)} %bitcast.12), custom_call_target="tpu_custom_call" | custom-call | flops 1048576000 | bytes 3276800 | tf_op jit(solution)/shard_map/raise_terms/pallas_call | solution.py:68
  4.7 1.3 %collective-permute-start = (bf16[640,640]{1,0:T(8,128)(2,1)}, bf16[640,640]{1,0:T(8,128)(2,1)S(1)}, u32[]{:S(2)}, u32[]{:S(2)}) collective-permute-start(bf16[640,640]{1,0:T(8,128)(2,1)} %get-tuple-element.20.masked), channel_id=1, source_target_pairs={{1,0},{2,1},{3,2},{4,3},{5,4},{6,5},{7,6},{9,8},{10,9},{11,10},{12... | collective-permute-start | bytes 2457608 | tf_op jit(solution)/shard_map/ppermute | solution.py:22
  5.9 3.1 %collective-permute-start.1 = (bf16[640,640]{1,0:T(8,128)(2,1)}, bf16[640,640]{1,0:T(8,128)(2,1)S(1)}, u32[]{:S(2)}, u32[]{:S(2)}) collective-permute-start(bf16[640,640]{1,0:T(8,128)(2,1)} %get-tuple-element.22), channel_id=1, source_target_pairs={{0,1},{1,2},{2,3},{3,4},{4,5},{5,6},{6,7},{8,9},{9,10},{10,11},{11... | collective-permute-start | bytes 2457608 | tf_op jit(solution)/shard_map/ppermute | solution.py:22
  9.0 2.9 %turn.1 = (bf16[640,640]{1,0:T(8,128)(2,1)}, bf16[640,640]{1,0:T(8,128)(2,1)}) custom-call(bf16[640,640]{1,0:T(8,128)(2,1)} %get-tuple-element.20.masked, bf16[640,640]{1,0:T(8,128)(2,1)} %bitcast.13), custom_call_target="tpu_custom_call" | custom-call | bytes 3276800 | tf_op jit(solution)/shard_map/turn/pallas_call | solution.py:88
  11.9 4.5 %all-to-all-start = ((bf16[4,160,640]{2,1,0:T(8,128)(2,1)}), bf16[4,160,640]{2,1,0:T(8,128)(2,1)}, u32[]{:S(2)}, u32[]{:S(2)}) async-start(bf16[4,160,640]{2,1,0:T(8,128)(2,1)} %bitcast.15), calls=%async_computation | async-start | bytes 1638400 | tf_op jit(solution)/shard_map/all_to_all | solution.py:309
  17.7 0.0 collective-permute-done.refs_1_
  17.8 0.0 copy-start.6
  17.8 0.0 collective-permute-done.1.refs_3_
  17.8 0.9 copy-done.6
  18.7 0.3 copy-done.7
  18.9 4.4 %energy_blocks.1 = (bf16[160,640]{1,0:T(8,128)(2,1)}, bf16[160,640]{1,0:T(8,128)(2,1)}, bf16[160,640]{1,0:T(8,128)(2,1)}, bf16[160,640]{1,0:T(8,128)(2,1)}) custom-call(s32[1]{0:T(128)S(6)} %copy.10.sizes, f32[1]{0:T(128)S(6)} %copy.8.particle, f32[1]{0:T(128)S(6)} %copy.9.hole, bf16[640,640]{1,0:T(8,128)(2,1)} %get-tuple-element.21.refs_0_, ...), custom_call_target="tpu_custom_call" | custom-call | flops 1048576000 | bytes 4096000 | tf_op jit(solution)/shard_map/energy_blocks/pallas_call | solution.py:127
  23.4 2.1 %collective-permute-start.5 = (bf16[160,640]{1,0:T(8,128)(2,1)}, bf16[160,640]{1,0:T(8,128)(2,1)S(1)}, u32[]{:S(2)}, u32[]{:S(2)}) collective-permute-start(bf16[160,640]{1,0:T(8,128)(2,1)} %get-tuple-element.23.refs_0_), channel_id=1, source_target_pairs={{0,8},{8,16},{16,24},{24,0},{1,9},{9,17},{17,25},{25,1},{2,10},{10... | collective-permute-start | bytes 614408 | tf_op jit(solution)/shard_map/ppermute | solution.py:27
  25.5 1.3 %collective-permute-start.6 = (bf16[160,640]{1,0:T(8,128)(2,1)}, bf16[160,640]{1,0:T(8,128)(2,1)S(1)}, u32[]{:S(2)}, u32[]{:S(2)}) collective-permute-start(bf16[160,640]{1,0:T(8,128)(2,1)} %get-tuple-element.23.refs_0_), channel_id=1, source_target_pairs={{0,24},{8,0},{16,8},{24,16},{1,25},{9,1},{17,9},{25,17},{2,26},{10... | collective-permute-start | bytes 614408 | tf_op jit(solution)/shard_map/ppermute | solution.py:27
  26.8 2.2 %collective-permute-start.7 = (bf16[160,640]{1,0:T(8,128)(2,1)}, bf16[160,640]{1,0:T(8,128)(2,1)S(1)}, u32[]{:S(2)}, u32[]{:S(2)}) collective-permute-start(bf16[160,640]{1,0:T(8,128)(2,1)} %get-tuple-element.23.refs_0_), channel_id=1, source_target_pairs={{0,16},{8,24},{16,0},{24,8},{1,17},{9,25},{17,1},{25,9},{2,18},{10... | collective-permute-start | bytes 614408 | tf_op jit(solution)/shard_map/ppermute | solution.py:27
  29.0 1.5 %collective-permute-start.2 = (bf16[160,640]{1,0:T(8,128)(2,1)}, bf16[160,640]{1,0:T(8,128)(2,1)S(1)}, u32[]{:S(2)}, u32[]{:S(2)}) collective-permute-start(bf16[160,640]{1,0:T(8,128)(2,1)} %get-tuple-element.24), channel_id=1, source_target_pairs={{0,32},{32,64},{64,96},{96,0},{1,33},{33,65},{65,97},{97,1},{2,34}... | collective-permute-start | bytes 614408 | tf_op jit(solution)/shard_map/ppermute | solution.py:27
  30.5 2.7 %collective-permute-start.3 = (bf16[160,640]{1,0:T(8,128)(2,1)}, bf16[160,640]{1,0:T(8,128)(2,1)S(1)}, u32[]{:S(2)}, u32[]{:S(2)}) collective-permute-start(bf16[160,640]{1,0:T(8,128)(2,1)} %get-tuple-element.25), channel_id=1, source_target_pairs={{0,64},{32,96},{64,0},{96,32},{1,65},{33,97},{65,1},{97,33},{2,66}... | collective-permute-start | bytes 614408 | tf_op jit(solution)/shard_map/ppermute | solution.py:27
  33.2 1.8 %collective-permute-done.5.refs_4_ = bf16[160,640]{1,0:T(8,128)(2,1)S(1)} collective-permute-done((bf16[160,640]{1,0:T(8,128)(2,1)}, bf16[160,640]{1,0:T(8,128)(2,1)S(1)}, u32[]{:S(2)}, u32[]{:S(2)}) %collective-permute-start.5) | collective-permute-done | bytes 204832 | tf_op jit(solution)/shard_map/ppermute | solution.py:27
  35.0 2.8 %collective-permute-start.4 = (bf16[160,640]{1,0:T(8,128)(2,1)}, bf16[160,640]{1,0:T(8,128)(2,1)S(1)}, u32[]{:S(2)}, u32[]{:S(2)}) collective-permute-start(bf16[160,640]{1,0:T(8,128)(2,1)} %get-tuple-element.26), channel_id=1, source_target_pairs={{0,96},{32,0},{64,32},{96,64},{1,97},{33,1},{65,33},{97,65},{2,98}... | collective-permute-start | bytes 614408 | tf_op jit(solution)/shard_map/ppermute | solution.py:27
  37.8 0.0 all-to-all-done.refs_8_.refs_2_
  37.8 0.0 collective-permute-done.6.refs_6_
  37.8 0.0 collective-permute-start.10
  37.8 1.1 collective-permute-done.7.refs_0_
  38.9 2.8 %collective-permute-start.11 = (bf16[4,160,640]{2,1,0:T(8,128)(2,1)}, bf16[4,160,640]{2,1,0:T(8,128)(2,1)S(1)}, u32[]{:S(2)}, u32[]{:S(2)}) collective-permute-start(bf16[4,160,640]{2,1,0:T(8,128)(2,1)} %all-to-all-done.refs_8_.refs_2_), channel_id=1, source_target_pairs={{0,96},{32,0},{64,32},{96,64},{1,97},{33,1},{65,33},{97,65},{2,98}... | collective-permute-start | bytes 2457608 | tf_op jit(solution)/shard_map/ppermute | solution.py:27
  41.7 0.0 collective-permute-done.2.refs_1_
  41.7 2.1 %collective-permute-done.3.refs_2_ = bf16[160,640]{1,0:T(8,128)(2,1)S(1)} collective-permute-done((bf16[160,640]{1,0:T(8,128)(2,1)}, bf16[160,640]{1,0:T(8,128)(2,1)S(1)}, u32[]{:S(2)}, u32[]{:S(2)}) %collective-permute-start.3) | collective-permute-done | bytes 204832 | tf_op jit(solution)/shard_map/ppermute | solution.py:27
  43.8 0.0 collective-permute-done.4.refs_3_
  43.8 0.9 pad_maximum_fusion
  44.8 0.4 collective-permute-start.8
  45.2 2.8 %collective-permute-start.9 = (bf16[3,160,640]{2,1,0:T(8,128)(2,1)}, bf16[3,160,640]{2,1,0:T(8,128)(2,1)S(1)}, u32[]{:S(2)}, u32[]{:S(2)}) collective-permute-start(bf16[3,160,640]{2,1,0:T(8,128)(2,1)} %pad_maximum_fusion), channel_id=1, source_target_pairs={{0,24},{8,0},{16,8},{24,16},{1,25},{9,1},{17,9},{25,17},{2,26},{10... | collective-permute-start | bytes 1843208 | tf_op jit(solution)/shard_map/ppermute | solution.py:27
  48.0 13.3 %collective-permute-done.10.refs_9_.refs_3_ = bf16[4,160,640]{2,1,0:T(8,128)(2,1)S(1)} collective-permute-done((bf16[4,160,640]{2,1,0:T(8,128)(2,1)}, bf16[4,160,640]{2,1,0:T(8,128)(2,1)S(1)}, u32[]{:S(2)}, u32[]{:S(2)}) %collective-permute-start.10) | collective-permute-done | bytes 819232 | tf_op jit(solution)/shard_map/ppermute | solution.py:27
  61.3 0.1 collective-permute-start.12
  61.4 0.0 collective-permute-done.11.refs_10_.refs_4_
  61.4 1.0 slice.9
  62.4 3.1 %collective-permute-start.13 = (bf16[2,160,640]{2,1,0:T(8,128)(2,1)}, bf16[2,160,640]{2,1,0:T(8,128)(2,1)S(1)}, u32[]{:S(2)}, u32[]{:S(2)}) collective-permute-start(bf16[2,160,640]{2,1,0:T(8,128)(2,1)} %slice.9), channel_id=1, source_target_pairs={{0,96},{32,0},{64,32},{96,64},{1,97},{33,1},{65,33},{97,65},{2,98}... | collective-permute-start | bytes 1228808 | tf_op jit(solution)/shard_map/ppermute | solution.py:27
  65.5 0.9 copy-done.8
  66.4 0.0 collective-permute-done.9.refs_7_
  66.4 0.3 collective-permute-start.14
  66.7 0.6 copy-done.9
  67.2 0.1 dynamic-slice_bitcast_fusion
  67.3 0.1 copy.7.rates
  67.4 6.6 %collective-permute-done.12.refs_11_.refs_5_ = bf16[2,160,640]{2,1,0:T(8,128)(2,1)S(1)} collective-permute-done((bf16[2,160,640]{2,1,0:T(8,128)(2,1)S(1)}, bf16[2,160,640]{2,1,0:T(8,128)(2,1)S(1)}, u32[]{:S(2)}, u32[]{:S(2)}) %collective-permute-start.12) | collective-permute-done | bytes 409632 | tf_op jit(solution)/shard_map/ppermute | solution.py:27
  74.0 0.4 collective-permute-done.13.refs_12_.refs_6_
  74.5 0.8 copy-done.1
  75.2 13.3 %convolve_near.1.near = f32[4,640,160]{2,1,0:T(8,128)} custom-call(bf16[160,640]{1,0:T(8,128)(2,1)S(1)} %copy-done.3, bf16[160,640]{1,0:T(8,128)(2,1)S(1)} %collective-permute-done.2.refs_1_, bf16[160,640]{1,0:T(8,128)(2,1)S(1)} %collective-permute-done.3.refs_2_, bf16[160,640]{1,0:T(8,128)(2,1)S(1)} %collective-permute-done.4.refs_3_, ...), custom_call_target="tpu_custom_call" | custom-call | flops 3276800000 | bytes 5734400 | tf_op jit(solution)/shard_map/convolve_near/pallas_call | solution.py:231
  88.6 1.0 copy-done.2
  89.6 8.4 %convolve_far.1 = bf16[16,40,640]{2,1,0:T(8,128)(2,1)} custom-call(s32[1]{0:T(128)S(6)} %copy.10.sizes, f32[160,1]{1,0:T(8,128)S(1)} %copy.7.rates, f32[4,640,160]{2,1,0:T(8,128)} %convolve_near.1.near, bf16[160,640]{1,0:T(8,128)(2,1)S(1)} %collective-permute-done.7.refs_0_, bf16[3,160,640]{2,1,0:T(8,128)(2,1)S(1)} %collective-permute-done.14.refs_1_, ...), custom_call_target="tpu_custom_call" | custom-call | flops 1179648000 | bytes 6144000 | tf_op jit(solution)/shard_map/convolve_far/pallas_call | solution.py:254
  98.0 20.1 %all_to_all.10.packets = bf16[16,40,640]{2,1,0:T(8,128)(2,1)} all-to-all(bf16[16,40,640]{2,1,0:T(8,128)(2,1)} %convolve_far.1), channel_id=1, replica_groups=mesh['tx'=4,'ty'=4,'sector'=8] {'tx','ty'}, dimensions={0} | all-to-all | bytes 1638400 | tf_op jit(solution)/shard_map/all_to_all | solution.py:344
  118.1 2.4 %assemble.1 = bf16[640,640]{1,0:T(8,128)(2,1)} custom-call(bf16[16,40,640]{2,1,0:T(8,128)(2,1)} %all_to_all.10.packets), custom_call_target="tpu_custom_call" | custom-call | tf_op jit(solution)/shard_map/assemble/pallas_call | solution.py:287
  (16 shorter events, 0.1 us)
Async XLA Ops:
  0.0 67.2 %copy-start = (f32[1,640]{1,0:T(1,128)S(1)}, f32[1,640]{1,0:T(1,128)}, u32[]{:S(2)}) copy-start(f32[1,640]{1,0:T(1,128)} %param.8) | copy-start | bytes 7684
  4.7 13.1 %collective-permute-start = (bf16[640,640]{1,0:T(8,128)(2,1)}, bf16[640,640]{1,0:T(8,128)(2,1)S(1)}, u32[]{:S(2)}, u32[]{:S(2)}) collective-permute-start(bf16[640,640]{1,0:T(8,128)(2,1)} %get-tuple-element.20.masked), channel_id=1, source_target_pairs={{1,0},{2,1},{3,2},{4,3},{5,4},{6,5},{7,6},{9,8},{10,9},{11,10},{12... | collective-permute-start | bytes 2457608 | tf_op jit(solution)/shard_map/ppermute | solution.py:22
  5.9 11.8 %collective-permute-start.1 = (bf16[640,640]{1,0:T(8,128)(2,1)}, bf16[640,640]{1,0:T(8,128)(2,1)S(1)}, u32[]{:S(2)}, u32[]{:S(2)}) collective-permute-start(bf16[640,640]{1,0:T(8,128)(2,1)} %get-tuple-element.22), channel_id=1, source_target_pairs={{0,1},{1,2},{2,3},{3,4},{4,5},{5,6},{6,7},{8,9},{9,10},{10,11},{11... | collective-permute-start | bytes 2457608 | tf_op jit(solution)/shard_map/ppermute | solution.py:22
  11.9 25.9 %all-to-all-start = ((bf16[4,160,640]{2,1,0:T(8,128)(2,1)}), bf16[4,160,640]{2,1,0:T(8,128)(2,1)}, u32[]{:S(2)}, u32[]{:S(2)}) async-start(bf16[4,160,640]{2,1,0:T(8,128)(2,1)} %bitcast.15), calls=%async_computation | async-start | bytes 1638400 | tf_op jit(solution)/shard_map/all_to_all | solution.py:309
  17.8 0.9 copy-start.6
  17.8 1.2 copy-start.7
  23.4 51.9 %copy-start.3 = (bf16[160,640]{1,0:T(8,128)(2,1)S(1)}, bf16[160,640]{1,0:T(8,128)(2,1)}, u32[]{:S(2)}) copy-start(bf16[160,640]{1,0:T(8,128)(2,1)} %get-tuple-element.23.refs_0_) | copy-start | bytes 614404
  23.4 11.7 %collective-permute-start.5 = (bf16[160,640]{1,0:T(8,128)(2,1)}, bf16[160,640]{1,0:T(8,128)(2,1)S(1)}, u32[]{:S(2)}, u32[]{:S(2)}) collective-permute-start(bf16[160,640]{1,0:T(8,128)(2,1)} %get-tuple-element.23.refs_0_), channel_id=1, source_target_pairs={{0,8},{8,16},{16,24},{24,0},{1,9},{9,17},{17,25},{25,1},{2,10},{10... | collective-permute-start | bytes 614408 | tf_op jit(solution)/shard_map/ppermute | solution.py:27
  25.5 12.3 %collective-permute-start.6 = (bf16[160,640]{1,0:T(8,128)(2,1)}, bf16[160,640]{1,0:T(8,128)(2,1)S(1)}, u32[]{:S(2)}, u32[]{:S(2)}) collective-permute-start(bf16[160,640]{1,0:T(8,128)(2,1)} %get-tuple-element.23.refs_0_), channel_id=1, source_target_pairs={{0,24},{8,0},{16,8},{24,16},{1,25},{9,1},{17,9},{25,17},{2,26},{10... | collective-permute-start | bytes 614408 | tf_op jit(solution)/shard_map/ppermute | solution.py:27
  26.8 12.2 %collective-permute-start.7 = (bf16[160,640]{1,0:T(8,128)(2,1)}, bf16[160,640]{1,0:T(8,128)(2,1)S(1)}, u32[]{:S(2)}, u32[]{:S(2)}) collective-permute-start(bf16[160,640]{1,0:T(8,128)(2,1)} %get-tuple-element.23.refs_0_), channel_id=1, source_target_pairs={{0,16},{8,24},{16,0},{24,8},{1,17},{9,25},{17,1},{25,9},{2,18},{10... | collective-permute-start | bytes 614408 | tf_op jit(solution)/shard_map/ppermute | solution.py:27
  29.0 12.7 %collective-permute-start.2 = (bf16[160,640]{1,0:T(8,128)(2,1)}, bf16[160,640]{1,0:T(8,128)(2,1)S(1)}, u32[]{:S(2)}, u32[]{:S(2)}) collective-permute-start(bf16[160,640]{1,0:T(8,128)(2,1)} %get-tuple-element.24), channel_id=1, source_target_pairs={{0,32},{32,64},{64,96},{96,0},{1,33},{33,65},{65,97},{97,1},{2,34}... | collective-permute-start | bytes 614408 | tf_op jit(solution)/shard_map/ppermute | solution.py:27
  30.5 13.3 %collective-permute-start.3 = (bf16[160,640]{1,0:T(8,128)(2,1)}, bf16[160,640]{1,0:T(8,128)(2,1)S(1)}, u32[]{:S(2)}, u32[]{:S(2)}) collective-permute-start(bf16[160,640]{1,0:T(8,128)(2,1)} %get-tuple-element.25), channel_id=1, source_target_pairs={{0,64},{32,96},{64,0},{96,32},{1,65},{33,97},{65,1},{97,33},{2,66}... | collective-permute-start | bytes 614408 | tf_op jit(solution)/shard_map/ppermute | solution.py:27
  35.0 8.8 %collective-permute-start.4 = (bf16[160,640]{1,0:T(8,128)(2,1)}, bf16[160,640]{1,0:T(8,128)(2,1)S(1)}, u32[]{:S(2)}, u32[]{:S(2)}) collective-permute-start(bf16[160,640]{1,0:T(8,128)(2,1)} %get-tuple-element.26), channel_id=1, source_target_pairs={{0,96},{32,0},{64,32},{96,64},{1,97},{33,1},{65,33},{97,65},{2,98}... | collective-permute-start | bytes 614408 | tf_op jit(solution)/shard_map/ppermute | solution.py:27
  37.8 23.5 %collective-permute-start.10 = (bf16[4,160,640]{2,1,0:T(8,128)(2,1)}, bf16[4,160,640]{2,1,0:T(8,128)(2,1)S(1)}, u32[]{:S(2)}, u32[]{:S(2)}) collective-permute-start(bf16[4,160,640]{2,1,0:T(8,128)(2,1)} %all-to-all-done.refs_8_.refs_2_), channel_id=1, source_target_pairs={{0,32},{32,64},{64,96},{96,0},{1,33},{33,65},{65,97},{97,1},{2,34}... | collective-permute-start | bytes 2457608 | tf_op jit(solution)/shard_map/ppermute | solution.py:27
  38.9 22.5 %collective-permute-start.11 = (bf16[4,160,640]{2,1,0:T(8,128)(2,1)}, bf16[4,160,640]{2,1,0:T(8,128)(2,1)S(1)}, u32[]{:S(2)}, u32[]{:S(2)}) collective-permute-start(bf16[4,160,640]{2,1,0:T(8,128)(2,1)} %all-to-all-done.refs_8_.refs_2_), channel_id=1, source_target_pairs={{0,96},{32,0},{64,32},{96,64},{1,97},{33,1},{65,33},{97,65},{2,98}... | collective-permute-start | bytes 2457608 | tf_op jit(solution)/shard_map/ppermute | solution.py:27
  44.8 20.8 %collective-permute-start.8 = (bf16[3,160,640]{2,1,0:T(8,128)(2,1)}, bf16[3,160,640]{2,1,0:T(8,128)(2,1)S(1)}, u32[]{:S(2)}, u32[]{:S(2)}) collective-permute-start(bf16[3,160,640]{2,1,0:T(8,128)(2,1)} %pad_maximum_fusion), channel_id=1, source_target_pairs={{0,8},{8,16},{16,24},{24,0},{1,9},{9,17},{17,25},{25,1},{2,10},{10... | collective-permute-start | bytes 1843208 | tf_op jit(solution)/shard_map/ppermute | solution.py:27
  45.2 21.2 %collective-permute-start.9 = (bf16[3,160,640]{2,1,0:T(8,128)(2,1)}, bf16[3,160,640]{2,1,0:T(8,128)(2,1)S(1)}, u32[]{:S(2)}, u32[]{:S(2)}) collective-permute-start(bf16[3,160,640]{2,1,0:T(8,128)(2,1)} %pad_maximum_fusion), channel_id=1, source_target_pairs={{0,24},{8,0},{16,8},{24,16},{1,25},{9,1},{17,9},{25,17},{2,26},{10... | collective-permute-start | bytes 1843208 | tf_op jit(solution)/shard_map/ppermute | solution.py:27
  61.3 4.2 %copy-start.4 = (bf16[4,160,640]{2,1,0:T(8,128)(2,1)}, bf16[4,160,640]{2,1,0:T(8,128)(2,1)S(1)}, u32[]{:S(2)}) copy-start(bf16[4,160,640]{2,1,0:T(8,128)(2,1)S(1)} %collective-permute-done.10.refs_9_.refs_3_) | copy-start | bytes 2457604
  61.3 12.7 %collective-permute-start.12 = (bf16[2,160,640]{2,1,0:T(8,128)(2,1)S(1)}, bf16[2,160,640]{2,1,0:T(8,128)(2,1)S(1)}, u32[]{:S(2)}, u32[]{:S(2)}) collective-permute-start(bf16[2,160,640]{2,1,0:T(8,128)(2,1)S(1)} %slice.8), channel_id=1, source_target_pairs={{0,32},{32,64},{64,96},{96,0},{1,33},{33,65},{65,97},{97,1},{2,34}... | collective-permute-start | bytes 1228808 | tf_op jit(solution)/shard_map/ppermute | solution.py:27
  61.4 4.9 %copy-start.5 = (bf16[4,160,640]{2,1,0:T(8,128)(2,1)}, bf16[4,160,640]{2,1,0:T(8,128)(2,1)S(1)}, u32[]{:S(2)}) copy-start(bf16[4,160,640]{2,1,0:T(8,128)(2,1)S(1)} %collective-permute-done.11.refs_10_.refs_4_) | copy-start | bytes 2457604
  62.4 12.1 %collective-permute-start.13 = (bf16[2,160,640]{2,1,0:T(8,128)(2,1)}, bf16[2,160,640]{2,1,0:T(8,128)(2,1)S(1)}, u32[]{:S(2)}, u32[]{:S(2)}) collective-permute-start(bf16[2,160,640]{2,1,0:T(8,128)(2,1)} %slice.9), channel_id=1, source_target_pairs={{0,96},{32,0},{64,32},{96,64},{1,97},{33,1},{65,33},{97,65},{2,98}... | collective-permute-start | bytes 1228808 | tf_op jit(solution)/shard_map/ppermute | solution.py:27
  65.5 0.9 copy-start.8
  66.4 0.8 copy-start.9
  66.4 22.2 %collective-permute-start.14 = (bf16[3,160,640]{2,1,0:T(8,128)(2,1)}, bf16[3,160,640]{2,1,0:T(8,128)(2,1)S(1)}, u32[]{:S(2)}, u32[]{:S(2)}) collective-permute-start(bf16[3,160,640]{2,1,0:T(8,128)(2,1)} %pad_maximum_fusion), channel_id=1, source_target_pairs={{0,16},{8,24},{16,0},{24,8},{1,17},{9,25},{17,1},{25,9},{2,18},{10... | collective-permute-start | bytes 1843208 | tf_op jit(solution)/shard_map/ppermute | solution.py:27
  74.5 0.8 copy-start.1
  88.6 1.0 copy-start.2

commit v5 on v4

--- a/solution.py
+++ b/solution.py
@@ -51,7 +51,7 @@
     return jnp.dot(a, b, preferred_element_type=jnp.float32)
 
 
-def raise_kernel(sizes, prop, operator, masked, upward):
+def prepare_kernel(sizes, prop, operator, masked, upward, turned, flipped):
     inner = prop[...].astype(jnp.float32)
     inner = jnp.where(live(inner.shape, sizes[0]), inner, 0.0).astype(jnp.bfloat16)
     masked[...] = inner
@@ -60,39 +60,23 @@
     upward[...] = lax.dot_general(raised, r, NT, preferred_element_type=jnp.float32).astype(
         jnp.bfloat16
     )
-
-
-def raise_terms(sizes, prop, operator):
+    turned[...] = inner.T
+    flipped[...] = r.T
+
+
+def prepare(sizes, prop, operator):
     states = prop.shape[0]
     square = jax.ShapeDtypeStruct((states, states), jnp.bfloat16)
     return pl.pallas_call(
-        raise_kernel,
-        out_shape=(square, square),
+        prepare_kernel,
+        out_shape=(square,) * 4,
         in_specs=[SMEM, VMEM, VMEM],
-        out_specs=(VMEM, VMEM),
+        out_specs=(VMEM,) * 4,
         cost_estimate=pl.CostEstimate(
-            flops=4 * states**3, bytes_accessed=8 * states**2, transcendentals=0
+            flops=4 * states**3, bytes_accessed=12 * states**2, transcendentals=0
         ),
-        name="raise_terms",
+        name="prepare",
     )(sizes, prop, operator)
-
-
-def turn_kernel(masked, operator, turned, flipped):
-    turned[...] = masked[...].T
-    flipped[...] = operator[...].T
-
-
-def turn(masked, operator):
-    states = masked.shape[0]
-    square = jax.ShapeDtypeStruct((states, states), jnp.bfloat16)
-    return pl.pallas_call(
-        turn_kernel,
-        out_shape=(square, square),
-        in_specs=[VMEM, VMEM],
-        out_specs=(VMEM, VMEM),
-        cost_estimate=pl.CostEstimate(flops=0, bytes_accessed=8 * states**2, transcendentals=0),
-        name="turn",
-    )(masked, operator)
 
 
 def energy_kernel(sizes, particle, hole, *refs):
@@ -149,8 +133,10 @@
         if kind == "e":
             copies.append((part, e_all.at[slot, around(here_x, offset, n)]))
         elif kind == "rest":
+            tall = part.shape[1]
+            room = e_all.at[slot, :, pl.ds(offset * tall, tall)]
             for d in range(1, n):
-                copies.append((part.at[d - 1], e_all.at[slot, around(here_x, -d, n)]))
+                copies.append((part.at[d - 1], room.at[around(here_x, -d, n)]))
         else:
             some = part.shape[0]
             start = pad + around(here_x, offset, n) * n + slot * some
@@ -163,48 +149,64 @@
     return moves
 
 
+def products(e_all, g_all, slot, source, n, rows):
+    for v in range(n * n):
+        lane, first = v % n, v // n
+        left = e_all[slot, : n - first].reshape((n - first) * rows, -1)
+        right = g_all[v - source + n - 1]
+        yield lane, first, lax.dot_general(left, right, NT, preferred_element_type=jnp.float32)
+
+
+def source_of(slot, n):
+    return lax.rem(lax.axis_index("ty") + slot + slot // 2, n)
+
+
 def near_kernel(plan, n, *refs):
     parts = refs[: len(plan)]
     total, e_all, g_all, sems = refs[len(plan) :]
     rows = total.shape[2]
     moves = placed(parts, plan, n, e_all, g_all, n - 1, sems)
     g_all[: n - 1] = jnp.zeros((n - 1, *g_all.shape[1:]), jnp.bfloat16)
-    here_y = lax.axis_index("ty")
+    far = n - 1 + n * around(lax.axis_index("tx"), n // 2, n)
+    g_all[pl.ds(far, n)] = jnp.zeros((n, *g_all.shape[1:]), jnp.bfloat16)
     for move in moves:
         move.wait()
-
     for slot in range(n - 1):
-        source = lax.rem(here_y + slot + slot // 2, n)
-        for v in range(n * n):
-            lane, first = v % n, v // n
-            left = e_all[slot, : n - first].reshape((n - first) * rows, -1)
-            right = g_all[v - source + n - 1]
-            product = lax.dot_general(left, right, NT, preferred_element_type=jnp.float32)
+        for lane, first, product in products(e_all, g_all, slot, source_of(slot, n), n, rows):
             if slot == 0 and first == 0:
                 total[lane] = product
             else:
                 total[lane, first * rows :, :] += product
 
 
-def far_kernel(plan, n, step_size, sizes, rates, near, *refs):
+def far_kernel(plan, late, n, step_size, sizes, rates, near, *refs):
     parts = refs[: len(plan)]
     out, e_all, g_all, total, sems = refs[len(plan) :]
     rows = total.shape[2]
     moves = placed(parts, plan, n, e_all, g_all, n - 1, sems)
     g_all[: n - 1] = jnp.zeros((n - 1, *g_all.shape[1:]), jnp.bfloat16)
     here_x, here_y, size = lax.axis_index("tx"), lax.axis_index("ty"), sizes[0]
-    source = lax.rem(here_y + n // 2, n)
-    for move in moves:
+    for move in moves[:-late]:
         move.wait()
-    for v in range(n * n):
-        lane, first = v % n, v // n
-        left = e_all[0, : n - first].reshape((n - first) * rows, -1)
-        right = g_all[v - source + n - 1]
-        product = lax.dot_general(left, right, NT, preferred_element_type=jnp.float32)
+    for lane, first, product in products(
+        e_all, g_all, n - 1, lax.rem(here_y + n // 2, n), n, rows
+    ):
         if first == 0:
-            total[lane] = near[lane] + product
+            total[lane, : n * rows] = near[lane] + product
         else:
-            total[lane, first * rows :, :] += product
+            total[lane, first * rows : n * rows] += product
+    for move in moves[-late:]:
+        move.wait()
+    far = around(here_x, n // 2, n)
+    for slot in range(n - 1):
+        left = e_all[slot].reshape(n * rows, -1)
+        for k in range(n):
+            v = source_of(slot, n) + k
+            right = g_all[n - 1 + n * far + k]
+            top = pl.multiple_of((far + v // n) * rows, 32)
+            total[lax.rem(v, n), pl.ds(top, n * rows)] += lax.dot_general(
+                left, right, NT, preferred_element_type=jnp.float32
+            )
 
     quarter = rows // n
     scale = step_size * step_size
@@ -248,24 +250,26 @@
     )(*parts)
 
 
-def convolve_far(entries, near, sizes, rates, n, step_size):
-    plan, parts = [e[:3] for e in entries], [e[3] for e in entries]
+def convolve_far(entries, late_entries, near, sizes, rates, n, step_size):
+    plan = [e[:3] for e in entries + late_entries]
+    parts = [e[3] for e in entries + late_entries]
+    late = copies_of([e[:3] for e in late_entries], n)
     rows, states = parts[0].shape
     return pl.pallas_call(
-        functools.partial(far_kernel, plan, n, step_size),
+        functools.partial(far_kernel, plan, late, n, step_size),
         out_shape=jax.ShapeDtypeStruct((n * n, rows // n, states), jnp.bfloat16),
         in_specs=[SMEM, VMEM, VMEM] + [HBM] * len(parts),
         out_specs=VMEM,
         scratch_shapes=[
-            pltpu.VMEM((1, n, rows, states), jnp.bfloat16),
+            pltpu.VMEM((n, n, rows, states), jnp.bfloat16),
             pltpu.VMEM((n * n + n - 1, rows, states), jnp.bfloat16),
-            pltpu.VMEM((n, n * rows, rows), jnp.float32),
+            pltpu.VMEM((n, 2 * n * rows, rows), jnp.float32),
             pltpu.SemaphoreType.DMA((copies_of(plan, n),)),
         ],
         compiler_params=pltpu.CompilerParams(vmem_limit_bytes=52 * MIB),
         cost_estimate=pl.CostEstimate(
-            flops=72 * rows * rows * states,
-            bytes_accessed=60 * rows * states,
+            flops=130 * rows * rows * states,
+            bytes_accessed=80 * rows * states,
             transcendentals=0,
         ),
         name="convolve_far",
@@ -301,11 +305,9 @@
     here_x = lax.axis_index("tx")
     operator = rising_op[0]
 
-    masked, upward = raise_terms(sector_sizes, propagator[0, 0], operator)
+    masked, upward, turned, flipped = prepare(sector_sizes, propagator[0, 0], operator)
     below = shifted(upward, "sector", 1)
     above = shifted(masked, "sector", -1)
-
-    turned, flipped = turn(masked, operator)
     columns = lax.all_to_all(turned.reshape(n, rows, states), "ty", 0, 0, tiled=True)
 
     own, *away = energy_blocks(
@@ -314,33 +316,33 @@
     crossed = {d: ring(away[d - 1], "tx", d) for d in (2, 1, 3)}
     crossed = [crossed[d] for d in range(1, n)]
     down, up, across = (ring(own, "ty", d) for d in (1, -1, 2))
-    crossed, down, up, across = lax.optimization_barrier((crossed, down, up, across))
 
     previous_g, next_g, far_first, far_second = relay_gather(columns, "tx")
 
     rest = jnp.stack(crossed)
+    half = rows // 2
     rest_down, rest_up = ring(rest, "ty", 1), ring(rest, "ty", -1)
-    rest_late = tied(rest, rest_down, rest_up)
-    rest_across = ring(rest_late, "ty", 2)
-
-    entries_g = [
-        ("g", 0, 0, columns),
-        ("g", -1, 0, previous_g),
-        ("g", 1, 0, next_g),
-        ("g", 2, 0, far_first),
-        ("g", 2, 1, far_second),
-    ]
-    entries_near = (
+    across_first = ring(rest_down[:, :half], "ty", 1)
+    across_second = ring(rest_up[:, half:], "ty", -1)
+
+    near_g = [("g", 0, 0, columns), ("g", -1, 0, previous_g), ("g", 1, 0, next_g)]
+    far_g = [("g", 2, 0, far_first), ("g", 2, 1, far_second)]
+    near_e = (
         [("e", 0, 0, own)]
         + [("e", -d, 0, crossed[d - 1]) for d in range(1, n)]
-        + [("e", 0, 2, down), ("rest", None, 2, rest_down)]
-        + [("e", 0, 1, up), ("rest", None, 1, rest_up)]
-        + entries_g
-    )
-    entries_far = [("e", 0, 0, across), ("rest", None, 0, rest_across)] + entries_g
+        + [("e", 0, 2, down), ("rest", 0, 2, rest_down)]
+        + [("e", 0, 1, up), ("rest", 0, 1, rest_up)]
+    )
+    far_e = [
+        ("e", 0, 3, across),
+        ("rest", 0, 3, across_first),
+        ("rest", 1, 3, across_second),
+    ]
     rates = lax.dynamic_slice_in_dim(energies[0], here_x * rows, rows, 0)[:, None]
-    near = convolve_near(entries_near, n)
-    packets = convolve_far(entries_far, near, sector_sizes, rates, n, step_size)
+    near = convolve_near(near_e + near_g, n)
+    packets = convolve_far(
+        far_e + near_g + far_g, near_e, near, sector_sizes, rates, n, step_size
+    )
     packets = lax.all_to_all(packets, ("tx", "ty"), 0, 0, tiled=True)
     return assemble(packets, n)[None, None]
 

time: 121 us -> 119 us (0.983)
  the two profiles are of different devices: /device:TPU:0 before, /device:TPU:32 now
where the time goes in v5:
time: 119 us
  Pallas kernels  37.6 us (32%)
  starting transfers between devices  32.1 us (27%)
  waiting for transfers between devices  21.5 us (18%)
  blocking collectives  19.2 us (16%)
  local copies, waits for them, and re-layouts  5.43 us (5%)
  between operations  2.15 us (2%)
    ppermute x14, starting transfers between devices, ring(): lax.ppermute(block, axis, [(i, (i + distance) % n) for i in range(n)])  23.3 us
    all_to_all x1, blocking collectives, per_device(): packets = lax.all_to_all(packets, ('tx', 'ty'), 0, 0, tiled=True)  19.2 us
    ppermute x14, waiting for transfers between devices, ring(): lax.ppermute(block, axis, [(i, (i + distance) % n) for i in range(n)])  15.8 us
    pallas_call x1, Pallas kernels, convolve_near(): pl.pallas_call(functools.partial(near_kernel, plan, n), out_shape=jax.Sha...  14 us
    pallas_call x1, Pallas kernels, convolve_far(): pl.pallas_call(functools.partial(far_kernel, plan, late, n, step_size), o...  12.4 us
    ppermute x2, waiting for transfers between devices, shifted(): return lax.ppermute(block, axis, route)  5.69 us
    all_to_all x1, starting transfers between devices, per_device(): lax.all_to_all(turned.reshape(n, rows, states), 'ty', 0, 0, tiled=True)  4.47 us
    pallas_call x1, Pallas kernels, prepare(): pl.pallas_call(prepare_kernel, out_shape=(square,) * 4, in_specs=[SMEM, V...  4.45 us
  transfers between devices with their start and end apart: 17, of which 5 were waited for; matrix products, arithmetic and copies ran while one was open for 4% of the time, Pallas kernels for 16%

profile of v5, /device:TPU:32, one launch (start us, length us, event | category | flops | bytes accessed | tf_op | source)
XLA Modules:
  0.0 118.9 jit_solution(1971653386508131199)
XLA Ops:
  0.7 4.5 %prepare.1 = (bf16[640,640]{1,0:T(8,128)(2,1)}, bf16[640,640]{1,0:T(8,128)(2,1)}, bf16[640,640]{1,0:T(8,128)(2,1)}, bf16[640,640]{1,0:T(8,128)(2,1)}) custom-call(s32[1]{0:T(128)S(6)} %copy.10.sizes, bf16[640,640]{1,0:T(8,128)(2,1)} %bitcast.13, bf16[640,640]{1,0:T(8,128)(2,1)} %bitcast.14), custom_call_target="tpu_custom_call" | custom-call | flops 1048576000 | bytes 4915200 | tf_op jit(solution)/shard_map/prepare/pallas_call | solution.py:70
  5.1 1.9 %collective-permute-start = (bf16[640,640]{1,0:T(8,128)(2,1)}, bf16[640,640]{1,0:T(8,128)(2,1)S(1)}, u32[]{:S(2)}, u32[]{:S(2)}) collective-permute-start(bf16[640,640]{1,0:T(8,128)(2,1)} %get-tuple-element.14), channel_id=1, source_target_pairs={{1,0},{2,1},{3,2},{4,3},{5,4},{6,5},{7,6},{9,8},{10,9},{11,10},{12... | collective-permute-start | bytes 2457608 | tf_op jit(solution)/shard_map/ppermute | solution.py:22
  7.0 2.4 %collective-permute-start.1 = (bf16[640,640]{1,0:T(8,128)(2,1)}, bf16[640,640]{1,0:T(8,128)(2,1)S(1)}, u32[]{:S(2)}, u32[]{:S(2)}) collective-permute-start(bf16[640,640]{1,0:T(8,128)(2,1)} %get-tuple-element.15), channel_id=1, source_target_pairs={{0,1},{1,2},{2,3},{3,4},{4,5},{5,6},{6,7},{8,9},{9,10},{10,11},{11... | collective-permute-start | bytes 2457608 | tf_op jit(solution)/shard_map/ppermute | solution.py:22
  9.4 4.5 %all-to-all-start = ((bf16[4,160,640]{2,1,0:T(8,128)(2,1)}), bf16[4,160,640]{2,1,0:T(8,128)(2,1)S(1)}, u32[]{:S(2)}, u32[]{:S(2)}) async-start(bf16[4,160,640]{2,1,0:T(8,128)(2,1)} %bitcast.12), calls=%async_computation | async-start | bytes 1638400 | tf_op jit(solution)/shard_map/all_to_all | solution.py:311
  15.2 2.0 %collective-permute-done.refs_1_ = bf16[640,640]{1,0:T(8,128)(2,1)S(1)} collective-permute-done((bf16[640,640]{1,0:T(8,128)(2,1)}, bf16[640,640]{1,0:T(8,128)(2,1)S(1)}, u32[]{:S(2)}, u32[]{:S(2)}) %collective-permute-start) | collective-permute-done | bytes 819232 | tf_op jit(solution)/shard_map/ppermute | solution.py:22
  17.2 3.7 %collective-permute-done.1.refs_3_ = bf16[640,640]{1,0:T(8,128)(2,1)S(1)} collective-permute-done((bf16[640,640]{1,0:T(8,128)(2,1)}, bf16[640,640]{1,0:T(8,128)(2,1)S(1)}, u32[]{:S(2)}, u32[]{:S(2)}) %collective-permute-start.1) | collective-permute-done | bytes 819232 | tf_op jit(solution)/shard_map/ppermute | solution.py:22
  20.9 0.9 copy-done.7
  21.8 4.4 %energy_blocks.1 = (bf16[160,640]{1,0:T(8,128)(2,1)}, bf16[160,640]{1,0:T(8,128)(2,1)}, bf16[160,640]{1,0:T(8,128)(2,1)}, bf16[160,640]{1,0:T(8,128)(2,1)}) custom-call(s32[1]{0:T(128)S(6)} %copy.10.sizes, f32[1]{0:T(128)S(6)} %copy.8.particle, f32[1]{0:T(128)S(6)} %copy.9.hole, bf16[640,640]{1,0:T(8,128)(2,1)} %get-tuple-element.13.refs_0_, ...), custom_call_target="tpu_custom_call" | custom-call | flops 1048576000 | bytes 4096000 | tf_op jit(solution)/shard_map/energy_blocks/pallas_call | solution.py:111
  26.2 1.5 %collective-permute-start.2 = (bf16[160,640]{1,0:T(8,128)(2,1)}, bf16[160,640]{1,0:T(8,128)(2,1)S(1)}, u32[]{:S(2)}, u32[]{:S(2)}) collective-permute-start(bf16[160,640]{1,0:T(8,128)(2,1)} %get-tuple-element.17), channel_id=1, source_target_pairs={{0,32},{32,64},{64,96},{96,0},{1,33},{33,65},{65,97},{97,1},{2,34}... | collective-permute-start | bytes 614408 | tf_op jit(solution)/shard_map/ppermute | solution.py:27
  27.8 2.7 %collective-permute-start.3 = (bf16[160,640]{1,0:T(8,128)(2,1)}, bf16[160,640]{1,0:T(8,128)(2,1)S(1)}, u32[]{:S(2)}, u32[]{:S(2)}) collective-permute-start(bf16[160,640]{1,0:T(8,128)(2,1)} %get-tuple-element.18), channel_id=1, source_target_pairs={{0,64},{32,96},{64,0},{96,32},{1,65},{33,97},{65,1},{97,33},{2,66}... | collective-permute-start | bytes 614408 | tf_op jit(solution)/shard_map/ppermute | solution.py:27
  30.5 1.4 %collective-permute-start.4 = (bf16[160,640]{1,0:T(8,128)(2,1)}, bf16[160,640]{1,0:T(8,128)(2,1)S(1)}, u32[]{:S(2)}, u32[]{:S(2)}) collective-permute-start(bf16[160,640]{1,0:T(8,128)(2,1)} %get-tuple-element.19), channel_id=1, source_target_pairs={{0,96},{32,0},{64,32},{96,64},{1,97},{33,1},{65,33},{97,65},{2,98}... | collective-permute-start | bytes 614408 | tf_op jit(solution)/shard_map/ppermute | solution.py:27
  32.0 0.0 all-to-all-done.refs_8_.refs_3_
  32.0 0.1 collective-permute-start.10
  32.0 2.0 %collective-permute-start.9 = (bf16[4,160,640]{2,1,0:T(8,128)(2,1)S(1)}, bf16[4,160,640]{2,1,0:T(8,128)(2,1)}, u32[]{:S(2)}, u32[]{:S(2)}) collective-permute-start(bf16[4,160,640]{2,1,0:T(8,128)(2,1)S(1)} %all-to-all-done.refs_8_.refs_3_), channel_id=1, source_target_pairs={{0,32},{32,64},{64,96},{96,0},{1,33},{33,65},{65,97},{97,1},{2,34}... | collective-permute-start | bytes 2457608 | tf_op jit(solution)/shard_map/ppermute | solution.py:27
  34.0 0.8 collective-permute-done.2.refs_1_.refs_9_
  34.8 6.4 %collective-permute-done.3.refs_2_.refs_10_ = bf16[160,640]{1,0:T(8,128)(2,1)S(1)} collective-permute-done((bf16[160,640]{1,0:T(8,128)(2,1)}, bf16[160,640]{1,0:T(8,128)(2,1)S(1)}, u32[]{:S(2)}, u32[]{:S(2)}) %collective-permute-start.3) | collective-permute-done | bytes 204832 | tf_op jit(solution)/shard_map/ppermute | solution.py:27
  41.1 0.0 collective-permute-done.4.refs_3_.refs_11_
  41.1 0.9 pad_maximum_fusion
  42.0 3.0 %collective-permute-start.8 = (bf16[3,160,640]{2,1,0:T(8,128)(2,1)}, bf16[3,160,640]{2,1,0:T(8,128)(2,1)}, u32[]{:S(2)}, u32[]{:S(2)}) collective-permute-start(bf16[3,160,640]{2,1,0:T(8,128)(2,1)} %pad_maximum_fusion), channel_id=1, source_target_pairs={{0,24},{8,0},{16,8},{24,16},{1,25},{9,1},{17,9},{25,17},{2,26},{10... | collective-permute-start | bytes 1843208 | tf_op jit(solution)/shard_map/ppermute | solution.py:27
  45.0 0.0 collective-permute-start.6
  45.1 3.2 %collective-permute-start.7 = (bf16[160,640]{1,0:T(8,128)(2,1)}, bf16[160,640]{1,0:T(8,128)(2,1)S(1)}, u32[]{:S(2)}, u32[]{:S(2)}) collective-permute-start(bf16[160,640]{1,0:T(8,128)(2,1)} %get-tuple-element.16.refs_0_.refs_8_), channel_id=1, source_target_pairs={{0,24},{8,0},{16,8},{24,16},{1,25},{9,1},{17,9},{25,17},{2,26},{10... | collective-permute-start | bytes 614408 | tf_op jit(solution)/shard_map/ppermute | solution.py:27
  48.3 8.6 %collective-permute-done.10.refs_10_.refs_5_ = bf16[4,160,640]{2,1,0:T(8,128)(2,1)S(1)} collective-permute-done((bf16[4,160,640]{2,1,0:T(8,128)(2,1)S(1)}, bf16[4,160,640]{2,1,0:T(8,128)(2,1)S(1)}, u32[]{:S(2)}, u32[]{:S(2)}) %collective-permute-start.10) | collective-permute-done | bytes 819232 | tf_op jit(solution)/shard_map/ppermute | solution.py:27
  56.9 1.6 %collective-permute-start.5 = (bf16[160,640]{1,0:T(8,128)(2,1)}, bf16[160,640]{1,0:T(8,128)(2,1)S(1)}, u32[]{:S(2)}, u32[]{:S(2)}) collective-permute-start(bf16[160,640]{1,0:T(8,128)(2,1)} %get-tuple-element.16.refs_0_.refs_8_), channel_id=1, source_target_pairs={{0,8},{8,16},{16,24},{24,0},{1,9},{9,17},{17,25},{25,1},{2,10},{10... | collective-permute-start | bytes 614408 | tf_op jit(solution)/shard_map/ppermute | solution.py:27
  58.5 0.8 slice.19
  59.3 0.0 collective-permute-done.9.refs_9_.refs_4_
  59.3 2.7 %collective-permute-start.15 = (bf16[2,160,640]{2,1,0:T(8,128)(2,1)}, bf16[2,160,640]{2,1,0:T(8,128)(2,1)}, u32[]{:S(2)}, u32[]{:S(2)}) collective-permute-start(bf16[2,160,640]{2,1,0:T(8,128)(2,1)} %slice.19), channel_id=1, source_target_pairs={{0,96},{32,0},{64,32},{96,64},{1,97},{33,1},{65,33},{97,65},{2,98}... | collective-permute-start | bytes 1228808 | tf_op jit(solution)/shard_map/ppermute | solution.py:27
  62.0 1.8 %slice.18 = bf16[2,160,640]{2,1,0:T(8,128)(2,1)} slice(bf16[4,160,640]{2,1,0:T(8,128)(2,1)} %collective-permute-done.9.refs_9_.refs_4_), slice={[0:2], [0:160], [0:640]} | slice | bytes 819200 | tf_op jit(solution)/shard_map/slice | solution.py:41
  63.7 0.0 collective-permute-done.8.refs_7_.refs_15_
  63.7 0.0 collective-permute-start.14
  63.8 0.1 dynamic-slice_bitcast_fusion
  63.8 0.1 copy.7.rates
  64.0 1.0 slice.17
  65.0 0.0 collective-permute-done.6.refs_5_.refs_13_
  65.0 3.0 %collective-permute-start.11 = (bf16[160,640]{1,0:T(8,128)(2,1)S(1)}, bf16[160,640]{1,0:T(8,128)(2,1)S(1)}, u32[]{:S(2)}, u32[]{:S(2)}) collective-permute-start(bf16[160,640]{1,0:T(8,128)(2,1)S(1)} %copy-done.2), channel_id=1, source_target_pairs={{0,16},{8,24},{16,0},{24,8},{1,17},{9,25},{17,1},{25,9},{2,18},{10... | collective-permute-start | bytes 614408 | tf_op jit(solution)/shard_map/ppermute | solution.py:27
  68.0 0.0 collective-permute-done.7.refs_6_.refs_14_
  68.0 1.4 %collective-permute-start.13 = (bf16[3,80,640]{2,1,0:T(8,128)(2,1)S(1)}, bf16[3,80,640]{2,1,0:T(8,128)(2,1)S(1)}, u32[]{:S(2)}, u32[]{:S(2)}) collective-permute-start(bf16[3,80,640]{2,1,0:T(8,128)(2,1)S(1)} %slice.17), channel_id=1, source_target_pairs={{0,24},{8,0},{16,8},{24,16},{1,25},{9,1},{17,9},{25,17},{2,26},{10... | collective-permute-start | bytes 921608 | tf_op jit(solution)/shard_map/ppermute | solution.py:27
  69.4 0.0 collective-permute-done.5.refs_4_.refs_12_
  69.4 0.7 collective-permute-start.12
  70.1 14.0 %convolve_near.1.near = f32[4,640,160]{2,1,0:T(8,128)} custom-call(bf16[160,640]{1,0:T(8,128)(2,1)S(1)} %copy-done.2, bf16[160,640]{1,0:T(8,128)(2,1)S(1)} %collective-permute-done.2.refs_1_.refs_9_, bf16[160,640]{1,0:T(8,128)(2,1)S(1)} %collective-permute-done.3.refs_2_.refs_10_, bf16[160,640]{1,0:T(8,128)(2,1)S(1)} %collective-permute-done.4.refs_3_.refs_11_, ...), custom_call_target="tpu_custom_call" | custom-call | flops 3276800000 | bytes 5734400 | tf_op jit(solution)/shard_map/convolve_near/pallas_call | solution.py:233
  84.1 0.0 collective-permute-done.11.refs_0_
  84.2 0.0 collective-permute-done.15.refs_7_
  84.2 0.0 collective-permute-done.14.refs_6_
  84.2 0.0 collective-permute-done.13.refs_2_
  84.2 0.0 collective-permute-done.12.refs_1_
  84.2 0.7 copy-done.5
  84.9 12.4 %convolve_far.1 = bf16[16,40,640]{2,1,0:T(8,128)(2,1)} custom-call(s32[1]{0:T(128)S(6)} %copy.10.sizes, f32[160,1]{1,0:T(8,128)S(1)} %copy.7.rates, f32[4,640,160]{2,1,0:T(8,128)} %convolve_near.1.near, bf16[160,640]{1,0:T(8,128)(2,1)S(1)} %collective-permute-done.11.refs_0_, bf16[3,80,640]{2,1,0:T(8,128)(2,1)S(1)} %collective-permute-done.12.refs_1_, ...), custom_call_target="tpu_custom_call" | custom-call | flops 2129920000 | bytes 8192000 | tf_op jit(solution)/shard_map/convolve_far/pallas_call | solution.py:258
  97.3 19.2 %all_to_all.10.packets = bf16[16,40,640]{2,1,0:T(8,128)(2,1)} all-to-all(bf16[16,40,640]{2,1,0:T(8,128)(2,1)} %convolve_far.1), channel_id=1, replica_groups=mesh['tx'=4,'ty'=4,'sector'=8] {'tx','ty'}, dimensions={0} | all-to-all | bytes 1638400 | tf_op jit(solution)/shard_map/all_to_all | solution.py:346
  116.5 2.4 %assemble.1 = bf16[640,640]{1,0:T(8,128)(2,1)} custom-call(bf16[16,40,640]{2,1,0:T(8,128)(2,1)} %all_to_all.10.packets), custom_call_target="tpu_custom_call" | custom-call | tf_op jit(solution)/shard_map/assemble/pallas_call | solution.py:291
  (15 shorter events, 0.1 us)
Async XLA Ops:
  0.0 63.8 %copy-start = (f32[1,640]{1,0:T(1,128)S(1)}, f32[1,640]{1,0:T(1,128)}, u32[]{:S(2)}) copy-start(f32[1,640]{1,0:T(1,128)} %param.8) | copy-start | bytes 7684
  5.1 12.1 %collective-permute-start = (bf16[640,640]{1,0:T(8,128)(2,1)}, bf16[640,640]{1,0:T(8,128)(2,1)S(1)}, u32[]{:S(2)}, u32[]{:S(2)}) collective-permute-start(bf16[640,640]{1,0:T(8,128)(2,1)} %get-tuple-element.14), channel_id=1, source_target_pairs={{1,0},{2,1},{3,2},{4,3},{5,4},{6,5},{7,6},{9,8},{10,9},{11,10},{12... | collective-permute-start | bytes 2457608 | tf_op jit(solution)/shard_map/ppermute | solution.py:22
  7.0 13.9 %collective-permute-start.1 = (bf16[640,640]{1,0:T(8,128)(2,1)}, bf16[640,640]{1,0:T(8,128)(2,1)S(1)}, u32[]{:S(2)}, u32[]{:S(2)}) collective-permute-start(bf16[640,640]{1,0:T(8,128)(2,1)} %get-tuple-element.15), channel_id=1, source_target_pairs={{0,1},{1,2},{2,3},{3,4},{4,5},{5,6},{6,7},{8,9},{9,10},{10,11},{11... | collective-permute-start | bytes 2457608 | tf_op jit(solution)/shard_map/ppermute | solution.py:22
  9.4 22.5 %all-to-all-start = ((bf16[4,160,640]{2,1,0:T(8,128)(2,1)}), bf16[4,160,640]{2,1,0:T(8,128)(2,1)S(1)}, u32[]{:S(2)}, u32[]{:S(2)}) async-start(bf16[4,160,640]{2,1,0:T(8,128)(2,1)} %bitcast.12), calls=%async_computation | async-start | bytes 1638400 | tf_op jit(solution)/shard_map/all_to_all | solution.py:311
  17.2 3.7 %copy-start.6 = (bf16[640,640]{1,0:T(8,128)(2,1)}, bf16[640,640]{1,0:T(8,128)(2,1)S(1)}, u32[]{:S(2)}) copy-start(bf16[640,640]{1,0:T(8,128)(2,1)S(1)} %collective-permute-done.refs_1_) | copy-start | bytes 2457604
  20.9 0.9 copy-start.7
  26.2 38.7 %copy-start.2 = (bf16[160,640]{1,0:T(8,128)(2,1)S(1)}, bf16[160,640]{1,0:T(8,128)(2,1)}, u32[]{:S(2)}) copy-start(bf16[160,640]{1,0:T(8,128)(2,1)} %get-tuple-element.16.refs_0_.refs_8_) | copy-start | bytes 614404
  26.2 8.5 %collective-permute-start.2 = (bf16[160,640]{1,0:T(8,128)(2,1)}, bf16[160,640]{1,0:T(8,128)(2,1)S(1)}, u32[]{:S(2)}, u32[]{:S(2)}) collective-permute-start(bf16[160,640]{1,0:T(8,128)(2,1)} %get-tuple-element.17), channel_id=1, source_target_pairs={{0,32},{32,64},{64,96},{96,0},{1,33},{33,65},{65,97},{97,1},{2,34}... | collective-permute-start | bytes 614408 | tf_op jit(solution)/shard_map/ppermute | solution.py:27
  27.8 13.3 %collective-permute-start.3 = (bf16[160,640]{1,0:T(8,128)(2,1)}, bf16[160,640]{1,0:T(8,128)(2,1)S(1)}, u32[]{:S(2)}, u32[]{:S(2)}) collective-permute-start(bf16[160,640]{1,0:T(8,128)(2,1)} %get-tuple-element.18), channel_id=1, source_target_pairs={{0,64},{32,96},{64,0},{96,32},{1,65},{33,97},{65,1},{97,33},{2,66}... | collective-permute-start | bytes 614408 | tf_op jit(solution)/shard_map/ppermute | solution.py:27
  30.5 10.6 %collective-permute-start.4 = (bf16[160,640]{1,0:T(8,128)(2,1)}, bf16[160,640]{1,0:T(8,128)(2,1)S(1)}, u32[]{:S(2)}, u32[]{:S(2)}) collective-permute-start(bf16[160,640]{1,0:T(8,128)(2,1)} %get-tuple-element.19), channel_id=1, source_target_pairs={{0,96},{32,0},{64,32},{96,64},{1,97},{33,1},{65,33},{97,65},{2,98}... | collective-permute-start | bytes 614408 | tf_op jit(solution)/shard_map/ppermute | solution.py:27
  32.0 38.2 %copy-start.3 = (bf16[4,160,640]{2,1,0:T(8,128)(2,1)}, bf16[4,160,640]{2,1,0:T(8,128)(2,1)S(1)}, u32[]{:S(2)}) copy-start(bf16[4,160,640]{2,1,0:T(8,128)(2,1)S(1)} %all-to-all-done.refs_8_.refs_3_) | copy-start | bytes 2457604
  32.0 24.9 %collective-permute-start.10 = (bf16[4,160,640]{2,1,0:T(8,128)(2,1)S(1)}, bf16[4,160,640]{2,1,0:T(8,128)(2,1)S(1)}, u32[]{:S(2)}, u32[]{:S(2)}) collective-permute-start(bf16[4,160,640]{2,1,0:T(8,128)(2,1)S(1)} %all-to-all-done.refs_8_.refs_3_), channel_id=1, source_target_pairs={{0,96},{32,0},{64,32},{96,64},{1,97},{33,1},{65,33},{97,65},{2,98}... | collective-permute-start | bytes 2457608 | tf_op jit(solution)/shard_map/ppermute | solution.py:27
  32.0 27.2 %collective-permute-start.9 = (bf16[4,160,640]{2,1,0:T(8,128)(2,1)S(1)}, bf16[4,160,640]{2,1,0:T(8,128)(2,1)}, u32[]{:S(2)}, u32[]{:S(2)}) collective-permute-start(bf16[4,160,640]{2,1,0:T(8,128)(2,1)S(1)} %all-to-all-done.refs_8_.refs_3_), channel_id=1, source_target_pairs={{0,32},{32,64},{64,96},{96,0},{1,33},{33,65},{65,97},{97,1},{2,34}... | collective-permute-start | bytes 2457608 | tf_op jit(solution)/shard_map/ppermute | solution.py:27
  42.0 21.7 %collective-permute-start.8 = (bf16[3,160,640]{2,1,0:T(8,128)(2,1)}, bf16[3,160,640]{2,1,0:T(8,128)(2,1)}, u32[]{:S(2)}, u32[]{:S(2)}) collective-permute-start(bf16[3,160,640]{2,1,0:T(8,128)(2,1)} %pad_maximum_fusion), channel_id=1, source_target_pairs={{0,24},{8,0},{16,8},{24,16},{1,25},{9,1},{17,9},{25,17},{2,26},{10... | collective-permute-start | bytes 1843208 | tf_op jit(solution)/shard_map/ppermute | solution.py:27
  45.0 19.9 %collective-permute-start.6 = (bf16[3,160,640]{2,1,0:T(8,128)(2,1)}, bf16[3,160,640]{2,1,0:T(8,128)(2,1)S(1)}, u32[]{:S(2)}, u32[]{:S(2)}) collective-permute-start(bf16[3,160,640]{2,1,0:T(8,128)(2,1)} %pad_maximum_fusion), channel_id=1, source_target_pairs={{0,8},{8,16},{16,24},{24,0},{1,9},{9,17},{17,25},{25,1},{2,10},{10... | collective-permute-start | bytes 1843208 | tf_op jit(solution)/shard_map/ppermute | solution.py:27
  45.1 23.0 %collective-permute-start.7 = (bf16[160,640]{1,0:T(8,128)(2,1)}, bf16[160,640]{1,0:T(8,128)(2,1)S(1)}, u32[]{:S(2)}, u32[]{:S(2)}) collective-permute-start(bf16[160,640]{1,0:T(8,128)(2,1)} %get-tuple-element.16.refs_0_.refs_8_), channel_id=1, source_target_pairs={{0,24},{8,0},{16,8},{24,16},{1,25},{9,1},{17,9},{25,17},{2,26},{10... | collective-permute-start | bytes 614408 | tf_op jit(solution)/shard_map/ppermute | solution.py:27
  56.9 6.9 %copy-start.4 = (bf16[4,160,640]{2,1,0:T(8,128)(2,1)}, bf16[4,160,640]{2,1,0:T(8,128)(2,1)S(1)}, u32[]{:S(2)}) copy-start(bf16[4,160,640]{2,1,0:T(8,128)(2,1)S(1)} %collective-permute-done.10.refs_10_.refs_5_) | copy-start | bytes 2457604
  56.9 12.5 %collective-permute-start.5 = (bf16[160,640]{1,0:T(8,128)(2,1)}, bf16[160,640]{1,0:T(8,128)(2,1)S(1)}, u32[]{:S(2)}, u32[]{:S(2)}) collective-permute-start(bf16[160,640]{1,0:T(8,128)(2,1)} %get-tuple-element.16.refs_0_.refs_8_), channel_id=1, source_target_pairs={{0,8},{8,16},{16,24},{24,0},{1,9},{9,17},{17,25},{25,1},{2,10},{10... | collective-permute-start | bytes 614408 | tf_op jit(solution)/shard_map/ppermute | solution.py:27
  59.3 24.9 %collective-permute-start.15 = (bf16[2,160,640]{2,1,0:T(8,128)(2,1)}, bf16[2,160,640]{2,1,0:T(8,128)(2,1)}, u32[]{:S(2)}, u32[]{:S(2)}) collective-permute-start(bf16[2,160,640]{2,1,0:T(8,128)(2,1)} %slice.19), channel_id=1, source_target_pairs={{0,96},{32,0},{64,32},{96,64},{1,97},{33,1},{65,33},{97,65},{2,98}... | collective-permute-start | bytes 1228808 | tf_op jit(solution)/shard_map/ppermute | solution.py:27
  63.7 20.4 %collective-permute-start.14 = (bf16[2,160,640]{2,1,0:T(8,128)(2,1)}, bf16[2,160,640]{2,1,0:T(8,128)(2,1)}, u32[]{:S(2)}, u32[]{:S(2)}) collective-permute-start(bf16[2,160,640]{2,1,0:T(8,128)(2,1)} %slice.18), channel_id=1, source_target_pairs={{0,32},{32,64},{64,96},{96,0},{1,33},{33,65},{65,97},{97,1},{2,34}... | collective-permute-start | bytes 1228808 | tf_op jit(solution)/shard_map/ppermute | solution.py:27
  65.0 19.1 %copy-start.1 = (bf16[3,160,640]{2,1,0:T(8,128)(2,1)}, bf16[3,160,640]{2,1,0:T(8,128)(2,1)S(1)}, u32[]{:S(2)}) copy-start(bf16[3,160,640]{2,1,0:T(8,128)(2,1)S(1)} %collective-permute-done.6.refs_5_.refs_13_) | copy-start | bytes 1843204
  65.0 19.1 %collective-permute-start.11 = (bf16[160,640]{1,0:T(8,128)(2,1)S(1)}, bf16[160,640]{1,0:T(8,128)(2,1)S(1)}, u32[]{:S(2)}, u32[]{:S(2)}) collective-permute-start(bf16[160,640]{1,0:T(8,128)(2,1)S(1)} %copy-done.2), channel_id=1, source_target_pairs={{0,16},{8,24},{16,0},{24,8},{1,17},{9,25},{17,1},{25,9},{2,18},{10... | collective-permute-start | bytes 614408 | tf_op jit(solution)/shard_map/ppermute | solution.py:27
  68.0 16.2 %collective-permute-start.13 = (bf16[3,80,640]{2,1,0:T(8,128)(2,1)S(1)}, bf16[3,80,640]{2,1,0:T(8,128)(2,1)S(1)}, u32[]{:S(2)}, u32[]{:S(2)}) collective-permute-start(bf16[3,80,640]{2,1,0:T(8,128)(2,1)S(1)} %slice.17), channel_id=1, source_target_pairs={{0,24},{8,0},{16,8},{24,16},{1,25},{9,1},{17,9},{25,17},{2,26},{10... | collective-permute-start | bytes 921608 | tf_op jit(solution)/shard_map/ppermute | solution.py:27
  69.4 14.8 %collective-permute-start.12 = (bf16[3,80,640]{2,1,0:T(8,128)(2,1)S(1)}, bf16[3,80,640]{2,1,0:T(8,128)(2,1)S(1)}, u32[]{:S(2)}, u32[]{:S(2)}) collective-permute-start(bf16[3,80,640]{2,1,0:T(8,128)(2,1)S(1)} %slice.16), channel_id=1, source_target_pairs={{0,8},{8,16},{16,24},{24,0},{1,9},{9,17},{17,25},{25,1},{2,10},{10... | collective-permute-start | bytes 921608 | tf_op jit(solution)/shard_map/ppermute | solution.py:27
  84.2 0.7 copy-start.5

commit v6 on v5

v6 whole, which is shorter than its diff:
```python
import functools

import jax
import jax.numpy as jnp
import numpy as np
from jax import lax
from jax.experimental import pallas as pl
from jax.experimental.pallas import tpu as pltpu
from jax.sharding import Mesh
from jax.sharding import PartitionSpec as P

MIB = 1024 * 1024
VMEM = pl.BlockSpec(memory_space=pltpu.VMEM)
SMEM = pl.BlockSpec(memory_space=pltpu.SMEM)
HBM = pl.BlockSpec(memory_space=pltpu.HBM)
NT = (((1,), (1,)), ((), ()))


def shifted(block, axis, distance):
    devices = range(lax.axis_size(axis))
    route = [(i - distance, i) for i in devices if i - distance in devices]
    return lax.ppermute(block, axis, route)


def ring(block, axis, distance):
    n = lax.axis_size(axis)
    return lax.ppermute(block, axis, [(i, (i + distance) % n) for i in range(n)])


def tied(value, *others):
    return lax.optimization_barrier((value, *others))[0]


def spread(block, axis):
    return [(-d, ring(block, axis, d)) for d in (1, -1, 2)]


def live(shape, size, first_row=0):
    row = lax.broadcasted_iota(jnp.int32, shape, 0) + first_row
    column = lax.broadcasted_iota(jnp.int32, shape, 1)
    return (row < size) & (column < size)


def dot(a, b):
    return jnp.dot(a, b, preferred_element_type=jnp.float32)


def prepare_kernel(sizes, prop, operator, masked, upward, turned, flipped):
    inner = prop[...].astype(jnp.float32)
    inner = jnp.where(live(inner.shape, sizes[0]), inner, 0.0).astype(jnp.bfloat16)
    masked[...] = inner
    r = operator[...]
    raised = dot(r, inner).astype(jnp.bfloat16)
    upward[...] = lax.dot_general(raised, r, NT, preferred_element_type=jnp.float32).astype(
        jnp.bfloat16
    )
    turned[...] = inner.T
    flipped[...] = r.T


def prepare(sizes, prop, operator):
    states = prop.shape[0]
    square = jax.ShapeDtypeStruct((states, states), jnp.bfloat16)
    return pl.pallas_call(
        prepare_kernel,
        out_shape=(square,) * 4,
        in_specs=[SMEM, VMEM, VMEM],
        out_specs=(VMEM,) * 4,
        cost_estimate=pl.CostEstimate(
            flops=4 * states**3, bytes_accessed=12 * states**2, transcendentals=0
        ),
        name="prepare",
    )(sizes, prop, operator)


def energy_kernel(sizes, particle, hole, *refs):
    sources, (*outs,), copies, sems = refs[:4], refs[4:-5], refs[-5:-1], refs[-1]
    moves = [
        pltpu.make_async_copy(src, dst, sems.at[i])
        for i, (src, dst) in enumerate(zip(sources, copies))
    ]
    for move in moves:
        move.start()
    n = len(outs)
    rows = outs[0].shape[0]
    here_x = lax.axis_index("tx")
    for move in moves:
        move.wait()
    flipped, above, operator, below = copies
    inner = above[...]
    r = operator[...]
    for d in (2, 1, 3, 0):
        first = pl.multiple_of(lax.rem(here_x + d, n) * rows, 32)
        lowered = dot(flipped[pl.ds(first, rows), :], inner).astype(jnp.bfloat16)
        downward = dot(lowered, r)
        raised = below[pl.ds(first, rows), :].astype(jnp.float32)
        both = particle[0] * raised + hole[0] * downward
        kept = live(both.shape, sizes[0], first)
        outs[d][...] = jnp.where(kept, both, 0.0).astype(jnp.bfloat16)


def energy_blocks(sizes, particle, hole, above, below, operator, flipped, n):
    states = above.shape[0]
    block = jax.ShapeDtypeStruct((states // n, states), jnp.bfloat16)
    return pl.pallas_call(
        energy_kernel,
        out_shape=(block,) * n,
        in_specs=[SMEM] * 3 + [HBM] * 4,
        out_specs=(VMEM,) * n,
        scratch_shapes=[pltpu.VMEM((states, states), jnp.bfloat16)] * 4
        + [pltpu.SemaphoreType.DMA((4,))],
        cost_estimate=pl.CostEstimate(
            flops=4 * states**3, bytes_accessed=10 * states**2, transcendentals=0
        ),
        name="energy_blocks",
    )(sizes, particle, hole, flipped, above, operator, below)


def around(here, offset, n):
    return lax.rem(here + offset + n, n)


def convolve_kernel(plan, n, step_size, sizes, rates, *refs):
    parts = refs[: len(plan)]
    out, e_all, g_all, total, sems = refs[len(plan) :]
    rows, states = g_all.shape[1], e_all.shape[1] // (n * n + 1)
    here_x, here_y, size = lax.axis_index("tx"), lax.axis_index("ty"), sizes[0]
    copies_e, copies_g = [], []

    def lag_room(x, y, top, tall):
        slot = n * n - 1 - (n * around(here_x, x, n) + around(here_y, y, n))
        left = pl.multiple_of(slot * states, 128)
        return e_all.at[pl.ds(top, tall), pl.ds(left, states)]

    for part, (kind, across, step) in zip(parts, plan):
        if kind == "e":
            copies_e.append((part, lag_room(across, step, 0, rows)))
        elif kind == "all":
            tall = part.shape[1]
            for d in range(n):
                copies_e.append((part.at[d], lag_room(-d, step, across * tall, tall)))
        else:
            first = around(here_x, step, n) * (n // 2)
            for k in range(2):
                room = g_all.at[pl.ds(first, n // 2), :, pl.ds(k * states, states)]
                copies_g.append((part.at[:, k], room))
    moves = [
        pltpu.make_async_copy(src, dst, sems.at[i])
        for i, (src, dst) in enumerate(copies_e + copies_g)
    ]
    for move in moves:
        move.start()
    e_all[:, n * n * states :] = jnp.zeros((rows, states), jnp.bfloat16)
    for move in moves:
        move.wait()

    for u in range(0, n * n, 2):
        right = g_all[u // 2]
        for first in range(0, n * n - u, n):
            lags = range(first, min(first + n, n * n - u))
            left = jnp.concatenate(
                [
                    e_all[:, (n * n - 1 - lag) * states : (n * n + 1 - lag) * states]
                    for lag in lags
                ],
                axis=0,
            )
            product = lax.dot_general(left, right, NT, preferred_element_type=jnp.float32)
            where = slice((u + lags[0]) * rows, (u + lags[-1] + 1) * rows)
            if u == 0:
                total[where] = product
            else:
                total[where] += product

    quarter = rows // n
    scale = step_size * step_size
    for b in range(n):
        row = lax.broadcasted_iota(jnp.int32, (quarter, rows), 0) + b * quarter
        column = lax.broadcasted_iota(jnp.int32, (quarter, rows), 1)
        starts = (row == column) & (here_x == here_y) & (row + here_x * rows < size)
        rate = rates[b * quarter : (b + 1) * quarter]
        decay = jnp.broadcast_to(jnp.exp(-step_size * rate), (quarter, rows))
        for t in range(n * n):
            term = scale * total[t * rows + b * quarter : t * rows + (b + 1) * quarter]
            fresh = (jnp.where(starts, 1.0, 0.0) if t == 0 else decay * fresh) - term
            out[t, :, b * rows : (b + 1) * rows] = fresh.astype(jnp.bfloat16)


def convolve(entries, sizes, rates, n, step_size):
    plan, parts = [e[:3] for e in entries], [e[3] for e in entries]
    rows, states = parts[0].shape
    copies = sum({"e": 1, "all": n, "g": 2}[kind] for kind, *_ in plan)
    return pl.pallas_call(
        functools.partial(convolve_kernel, plan, n, step_size),
        out_shape=jax.ShapeDtypeStruct((n * n, rows // n, states), jnp.bfloat16),
        in_specs=[SMEM, VMEM] + [HBM] * len(parts),
        out_specs=VMEM,
        scratch_shapes=[
            pltpu.VMEM((rows, (n * n + 1) * states), jnp.bfloat16),
            pltpu.VMEM((n * n // 2, rows, 2 * states), jnp.bfloat16),
            pltpu.VMEM((n * n * rows, rows), jnp.float32),
            pltpu.SemaphoreType.DMA((copies,)),
        ],
        compiler_params=pltpu.CompilerParams(vmem_limit_bytes=52 * MIB),
        cost_estimate=pl.CostEstimate(
            flops=n * n * (n * n + 1) * rows * rows * states,
            bytes_accessed=4 * n * n * rows * states,
            transcendentals=0,
        ),
        name="convolve",
    )(sizes, rates, *parts)


def assemble_kernel(n, packets, out):
    quarter, states = packets.shape[1:]
    rows = states // n
    for x in range(n):
        for b in range(n):
            out[x * rows + b * quarter : x * rows + (b + 1) * quarter, :] = jnp.concatenate(
                [packets[x * n + y, :, b * rows : (b + 1) * rows] for y in range(n)], axis=1
            )


def assemble(packets, n):
    states = packets.shape[2]
    return pl.pallas_call(
        functools.partial(assemble_kernel, n),
        out_shape=jax.ShapeDtypeStruct((states, states), jnp.bfloat16),
        in_specs=[VMEM],
        out_specs=VMEM,
        name="assemble",
    )(packets)


def per_device(propagator, rising_op, energies, hyb_particle, hyb_hole, sector_sizes):
    states = propagator.shape[2]
    n = lax.axis_size("tx")
    step_size = 1.0 / (n * n)
    rows = states // n
    here_x = lax.axis_index("tx")
    operator = rising_op[0]

    masked, upward, turned, flipped = prepare(sector_sizes, propagator[0, 0], operator)
    below = shifted(upward, "sector", 1)
    above = shifted(masked, "sector", -1)
    columns = lax.all_to_all(turned.reshape(n, rows, states), "ty", 0, 0, tiled=True)

    own, *away = energy_blocks(
        sector_sizes, hyb_particle, hyb_hole, above, below, operator, flipped, n
    )
    away, columns = lax.optimization_barrier((away, columns))
    crossed = {d: ring(away[d - 1], "tx", d) for d in (2, 1, 3)}
    crossed = [crossed[d] for d in range(1, n)]
    gathered = [(0, columns)] + [(-d, ring(columns, "tx", d)) for d in (1, -1, 2)]

    lines = jnp.stack([own] + crossed)
    half = rows // 2
    down, up = ring(lines, "ty", 1), ring(lines, "ty", -1)
    down, up, *nearest = lax.optimization_barrier((down, up, gathered[1][1], gathered[2][1]))
    gathered[1:3] = [(gathered[1][0], nearest[0]), (gathered[2][0], nearest[1])]
    across_first = ring(down[:, :half], "ty", 1)
    across_second = ring(up[:, half:], "ty", -1)

    entries = (
        [("e", 0, 0, own)]
        + [("e", -d, 0, crossed[d - 1]) for d in range(1, n)]
        + [("all", 0, -1, down), ("all", 0, 1, up)]
        + [("all", 0, 2, across_first), ("all", 1, 2, across_second)]
        + [("g", 0, step, g.reshape(n // 2, 2, rows, states)) for step, g in gathered]
    )
    rates = lax.dynamic_slice_in_dim(energies[0], here_x * rows, rows, 0)[:, None]
    packets = convolve(entries, sector_sizes, rates, n, step_size)
    packets = lax.all_to_all(packets, ("tx", "ty"), 0, 0, tiled=True)
    return assemble(packets, n)[None, None]


def solution(mesh):
    n = round(mesh.shape["tm"] ** 0.5)
    split = Mesh(
        np.asarray(mesh.devices).reshape(n, n, mesh.shape["sector"]), ("tx", "ty", "sector")
    )
    times = ("tx", "ty")
    placed = (
        P("sector", times, None, None),
        P("sector", None, None),
        P("sector", None),
        P(times),
        P(times),
        P("sector"),
    )
    return jax.shard_map(
        per_device,
        mesh=split,
        in_specs=placed,
        out_specs=P("sector", times, None, None),
        check_vma=False,
    )
```

time: 119 us -> 111 us (0.933); the launches traced: 119 us -> 110 us
  waiting for transfers between devices: 21.5 us -> 39.4 us
  Pallas kernels: 37.6 us -> 23.2 us
  starting transfers between devices: 32.1 us -> 23.5 us
  local copies, waits for them, and re-layouts: 5.43 us -> 1.98 us
    ppermute x14 -> x10, waiting for transfers between devices: 15.8 us -> 32.3 us  [ring(): lax.ppermute(block, axis, [(i, (i + distance) % n) for i in range(n)])]
    pallas_call x2 -> x1, Pallas kernels: 26.4 us -> 12 us  [convolve(): pl.pallas_call(functools.partial(convolve_kernel, plan, n, step_size), ou...]
    ppermute x14 -> x10, starting transfers between devices: 23.3 us -> 14.7 us  [ring(): lax.ppermute(block, axis, [(i, (i + distance) % n) for i in range(n)])]
    slice x4 -> x2, local copies, waits for them, and re-layouts: 3.62 us -> 0.07 us  [the longest x1 0.04 us: per_device(): across_second = ring(up[:, half:], 'ty', -1)]
    all_to_all x1, waiting for transfers between devices: 0.01 us -> 1.44 us  [per_device(): lax.all_to_all(turned.reshape(n, rows, states), 'ty', 0, 0, tiled=True)]
  transfers between devices with their start and end apart: 17 -> 13, of which waited for: 5 -> 9; matrix products, arithmetic and copies ran while one was open for 4% -> 1% of each run, Pallas kernels for 16% -> 4%
where the time goes in v6:
time: 111 us; the launch traced here: 110 us
  waiting for transfers between devices  39.4 us (35%)
  starting transfers between devices  23.5 us (21%)
  Pallas kernels  23.2 us (21%)
  blocking collectives  18.5 us (17%)
  between operations  2.06 us (2%)
  local copies, waits for them, and re-layouts  1.98 us (2%)
    ppermute x10, waiting for transfers between devices, ring(): lax.ppermute(block, axis, [(i, (i + distance) % n) for i in range(n)])  32.3 us
    all_to_all x1, blocking collectives, per_device(): packets = lax.all_to_all(packets, ('tx', 'ty'), 0, 0, tiled=True)  18.5 us
    ppermute x10, starting transfers between devices, ring(): lax.ppermute(block, axis, [(i, (i + distance) % n) for i in range(n)])  14.7 us
    pallas_call x1, Pallas kernels, convolve(): pl.pallas_call(functools.partial(convolve_kernel, plan, n, step_size), ou...  12 us
    ppermute x2, waiting for transfers between devices, shifted(): return lax.ppermute(block, axis, route)  5.69 us
    all_to_all x1, starting transfers between devices, per_device(): lax.all_to_all(turned.reshape(n, rows, states), 'ty', 0, 0, tiled=True)  4.47 us
    pallas_call x1, Pallas kernels, prepare(): pl.pallas_call(prepare_kernel, out_shape=(square,) * 4, in_specs=[SMEM, V...  4.45 us
    pallas_call x1, Pallas kernels, energy_blocks(): pl.pallas_call(energy_kernel, out_shape=(block,) * n, in_specs=[SMEM] * 3...  4.42 us
  transfers between devices with their start and end apart: 13, of which 9 were waited for; matrix products, arithmetic and copies ran while one was open for 1% of the time, Pallas kernels for 4%

profile of v6, /device:TPU:32, one launch (start us, length us, event | category | flops | bytes accessed | tf_op | source)
XLA Modules:
  0.0 109.7 jit_solution(11777937740882939265)
XLA Ops:
  0.0 0.0 copy-start
  0.7 4.4 %prepare.1 = (bf16[640,640]{1,0:T(8,128)(2,1)}, bf16[640,640]{1,0:T(8,128)(2,1)}, bf16[640,640]{1,0:T(8,128)(2,1)}, bf16[640,640]{1,0:T(8,128)(2,1)}) custom-call(s32[1]{0:T(128)S(6)} %copy.10.sizes, bf16[640,640]{1,0:T(8,128)(2,1)} %bitcast.20, bf16[640,640]{1,0:T(8,128)(2,1)} %bitcast.21), custom_call_target="tpu_custom_call" | custom-call | flops 1048576000 | bytes 4915200 | tf_op jit(solution)/shard_map/prepare/pallas_call | solution.py:64
  5.1 1.9 %collective-permute-start = (bf16[640,640]{1,0:T(8,128)(2,1)}, bf16[640,640]{1,0:T(8,128)(2,1)S(1)}, u32[]{:S(2)}, u32[]{:S(2)}) collective-permute-start(bf16[640,640]{1,0:T(8,128)(2,1)} %get-tuple-element.22), channel_id=1, source_target_pairs={{1,0},{2,1},{3,2},{4,3},{5,4},{6,5},{7,6},{9,8},{10,9},{11,10},{12... | collective-permute-start | bytes 2457608 | tf_op jit(solution)/shard_map/ppermute | solution.py:22
  7.0 2.4 %collective-permute-start.1 = (bf16[640,640]{1,0:T(8,128)(2,1)}, bf16[640,640]{1,0:T(8,128)(2,1)S(1)}, u32[]{:S(2)}, u32[]{:S(2)}) collective-permute-start(bf16[640,640]{1,0:T(8,128)(2,1)} %get-tuple-element.23), channel_id=1, source_target_pairs={{0,1},{1,2},{2,3},{3,4},{4,5},{5,6},{6,7},{8,9},{9,10},{10,11},{11... | collective-permute-start | bytes 2457608 | tf_op jit(solution)/shard_map/ppermute | solution.py:22
  9.4 4.5 %all-to-all-start = ((bf16[4,160,640]{2,1,0:T(8,128)(2,1)}), bf16[4,160,640]{2,1,0:T(8,128)(2,1)S(1)}, u32[]{:S(2)}, u32[]{:S(2)}) async-start(bf16[4,160,640]{2,1,0:T(8,128)(2,1)} %bitcast.19), calls=%async_computation | async-start | bytes 1638400 | tf_op jit(solution)/shard_map/all_to_all | solution.py:246
  15.2 2.0 %collective-permute-done.refs_1_ = bf16[640,640]{1,0:T(8,128)(2,1)S(1)} collective-permute-done((bf16[640,640]{1,0:T(8,128)(2,1)}, bf16[640,640]{1,0:T(8,128)(2,1)S(1)}, u32[]{:S(2)}, u32[]{:S(2)}) %collective-permute-start) | collective-permute-done | bytes 819232 | tf_op jit(solution)/shard_map/ppermute | solution.py:22
  17.2 0.0 copy-start.7
  17.2 3.7 %collective-permute-done.1.refs_3_ = bf16[640,640]{1,0:T(8,128)(2,1)S(1)} collective-permute-done((bf16[640,640]{1,0:T(8,128)(2,1)}, bf16[640,640]{1,0:T(8,128)(2,1)S(1)}, u32[]{:S(2)}, u32[]{:S(2)}) %collective-permute-start.1) | collective-permute-done | bytes 819232 | tf_op jit(solution)/shard_map/ppermute | solution.py:22
  20.9 0.0 copy-start.8
  20.9 0.0 copy-done.7
  20.9 0.9 copy-done.8
  21.8 4.4 %energy_blocks.1 = (bf16[160,640]{1,0:T(8,128)(2,1)}, bf16[160,640]{1,0:T(8,128)(2,1)}, bf16[160,640]{1,0:T(8,128)(2,1)}, bf16[160,640]{1,0:T(8,128)(2,1)}) custom-call(s32[1]{0:T(128)S(6)} %copy.10.sizes, f32[1]{0:T(128)S(6)} %copy.8.particle, f32[1]{0:T(128)S(6)} %copy.9.hole, bf16[640,640]{1,0:T(8,128)(2,1)} %get-tuple-element.21.refs_0_, ...), custom_call_target="tpu_custom_call" | custom-call | flops 1048576000 | bytes 4096000 | tf_op jit(solution)/shard_map/energy_blocks/pallas_call | solution.py:105
  26.2 1.4 %all-to-all-done = bf16[4,160,640]{2,1,0:T(8,128)(2,1)S(1)} async-done(((bf16[4,160,640]{2,1,0:T(8,128)(2,1)}), bf16[4,160,640]{2,1,0:T(8,128)(2,1)S(1)}, u32[]{:S(2)}, u32[]{:S(2)}) %all-to-all-start) | async-done | bytes 819232 | tf_op jit(solution)/shard_map/all_to_all | solution.py:246
  27.7 0.0 copy-start.2
  27.7 1.5 %collective-permute-start.2 = (bf16[160,640]{1,0:T(8,128)(2,1)}, bf16[160,640]{1,0:T(8,128)(2,1)S(1)}, u32[]{:S(2)}, u32[]{:S(2)}) collective-permute-start(bf16[160,640]{1,0:T(8,128)(2,1)} %get-tuple-element.29), channel_id=1, source_target_pairs={{0,32},{32,64},{64,96},{96,0},{1,33},{33,65},{65,97},{97,1},{2,34}... | collective-permute-start | bytes 614408 | tf_op jit(solution)/shard_map/ppermute | solution.py:27
  29.2 2.7 %collective-permute-start.3 = (bf16[160,640]{1,0:T(8,128)(2,1)}, bf16[160,640]{1,0:T(8,128)(2,1)S(1)}, u32[]{:S(2)}, u32[]{:S(2)}) collective-permute-start(bf16[160,640]{1,0:T(8,128)(2,1)} %get-tuple-element.30), channel_id=1, source_target_pairs={{0,64},{32,96},{64,0},{96,32},{1,65},{33,97},{65,1},{97,33},{2,66}... | collective-permute-start | bytes 614408 | tf_op jit(solution)/shard_map/ppermute | solution.py:27
  31.9 1.4 %collective-permute-start.4 = (bf16[160,640]{1,0:T(8,128)(2,1)}, bf16[160,640]{1,0:T(8,128)(2,1)S(1)}, u32[]{:S(2)}, u32[]{:S(2)}) collective-permute-start(bf16[160,640]{1,0:T(8,128)(2,1)} %get-tuple-element.31), channel_id=1, source_target_pairs={{0,96},{32,0},{64,32},{96,64},{1,97},{33,1},{65,33},{97,65},{2,98}... | collective-permute-start | bytes 614408 | tf_op jit(solution)/shard_map/ppermute | solution.py:27
  33.3 0.0 collective-permute-start.8
  33.4 2.0 %collective-permute-start.7 = (bf16[4,160,640]{2,1,0:T(8,128)(2,1)S(1)}, bf16[4,160,640]{2,1,0:T(8,128)(2,1)S(1)}, u32[]{:S(2)}, u32[]{:S(2)}) collective-permute-start(bf16[4,160,640]{2,1,0:T(8,128)(2,1)S(1)} %all-to-all-done), channel_id=1, source_target_pairs={{0,32},{32,64},{64,96},{96,0},{1,33},{33,65},{65,97},{97,1},{2,34}... | collective-permute-start | bytes 2457608 | tf_op jit(solution)/shard_map/ppermute | solution.py:27
  35.4 0.8 collective-permute-done.2.refs_1_
  36.2 6.2 %collective-permute-done.3.refs_2_ = bf16[160,640]{1,0:T(8,128)(2,1)S(1)} collective-permute-done((bf16[160,640]{1,0:T(8,128)(2,1)}, bf16[160,640]{1,0:T(8,128)(2,1)S(1)}, u32[]{:S(2)}, u32[]{:S(2)}) %collective-permute-start.3) | collective-permute-done | bytes 204832 | tf_op jit(solution)/shard_map/ppermute | solution.py:27
  42.4 0.0 collective-permute-done.4.refs_3_
  42.4 1.1 pad_maximum_fusion
  43.5 1.8 %collective-permute-start.6 = (bf16[4,160,640]{2,1,0:T(8,128)(2,1)S(1)}, bf16[4,160,640]{2,1,0:T(8,128)(2,1)S(1)}, u32[]{:S(2)}, u32[]{:S(2)}) collective-permute-start(bf16[4,160,640]{2,1,0:T(8,128)(2,1)S(1)} %pad_maximum_fusion), channel_id=1, source_target_pairs={{0,24},{8,0},{16,8},{24,16},{1,25},{9,1},{17,9},{25,17},{2,26},{10... | collective-permute-start | bytes 2457608 | tf_op jit(solution)/shard_map/ppermute | solution.py:27
  45.3 0.3 collective-permute-start.5
  45.6 0.0 copy-done.2
  45.6 2.9 %collective-permute-start.11 = (bf16[4,160,640]{2,1,0:T(8,128)(2,1)S(1)}, bf16[4,160,640]{2,1,0:T(8,128)(2,1)}, u32[]{:S(2)}, u32[]{:S(2)}) collective-permute-start(bf16[4,160,640]{2,1,0:T(8,128)(2,1)S(1)} %all-to-all-done), channel_id=1, source_target_pairs={{0,64},{32,96},{64,0},{96,32},{1,65},{33,97},{65,1},{97,33},{2,66}... | collective-permute-start | bytes 2457608 | tf_op jit(solution)/shard_map/ppermute | solution.py:27
  48.5 11.4 %collective-permute-done.8 = bf16[4,160,640]{2,1,0:T(8,128)(2,1)S(1)} collective-permute-done((bf16[4,160,640]{2,1,0:T(8,128)(2,1)S(1)}, bf16[4,160,640]{2,1,0:T(8,128)(2,1)S(1)}, u32[]{:S(2)}, u32[]{:S(2)}) %collective-permute-start.8) | collective-permute-done | bytes 819232 | tf_op jit(solution)/shard_map/ppermute | solution.py:27
  59.9 0.0 collective-permute-done.7
  59.9 2.3 %collective-permute-done.6.refs_5_ = bf16[4,160,640]{2,1,0:T(8,128)(2,1)S(1)} collective-permute-done((bf16[4,160,640]{2,1,0:T(8,128)(2,1)S(1)}, bf16[4,160,640]{2,1,0:T(8,128)(2,1)S(1)}, u32[]{:S(2)}, u32[]{:S(2)}) %collective-permute-start.6) | collective-permute-done | bytes 819232 | tf_op jit(solution)/shard_map/ppermute | solution.py:27
  62.2 1.6 %collective-permute-done.5.refs_4_ = bf16[4,160,640]{2,1,0:T(8,128)(2,1)S(1)} collective-permute-done((bf16[4,160,640]{2,1,0:T(8,128)(2,1)S(1)}, bf16[4,160,640]{2,1,0:T(8,128)(2,1)S(1)}, u32[]{:S(2)}, u32[]{:S(2)}) %collective-permute-start.5) | collective-permute-done | bytes 819232 | tf_op jit(solution)/shard_map/ppermute | solution.py:27
  63.8 0.0 copy-done.3
  63.8 0.0 copy-start.1
  63.9 0.8 copy-done.4
  64.7 0.5 collective-permute-start.10
  65.2 1.5 %collective-permute-start.9 = (bf16[4,80,640]{2,1,0:T(8,128)(2,1)S(1)}, bf16[4,80,640]{2,1,0:T(8,128)(2,1)S(1)}, u32[]{:S(2)}, u32[]{:S(2)}) collective-permute-start(bf16[4,80,640]{2,1,0:T(8,128)(2,1)S(1)} %slice.6), channel_id=1, source_target_pairs={{0,8},{8,16},{16,24},{24,0},{1,9},{9,17},{17,25},{25,1},{2,10},{10... | collective-permute-start | bytes 1228808 | tf_op jit(solution)/shard_map/ppermute | solution.py:27
  66.7 0.0 copy-done.5
  66.7 0.0 copy-done.6
  66.7 0.0 copy-done
  66.7 0.1 dynamic-slice_bitcast_fusion
  66.8 0.1 copy.7.rates
  66.9 9.9 %collective-permute-done.11 = bf16[4,160,640]{2,1,0:T(8,128)(2,1)} collective-permute-done((bf16[4,160,640]{2,1,0:T(8,128)(2,1)S(1)}, bf16[4,160,640]{2,1,0:T(8,128)(2,1)}, u32[]{:S(2)}, u32[]{:S(2)}) %collective-permute-start.11) | collective-permute-done | bytes 819232 | tf_op jit(solution)/shard_map/ppermute | solution.py:27
  76.8 0.0 collective-permute-done.10.refs_7_
  76.8 0.0 collective-permute-done.9.refs_6_
  76.8 0.0 copy-done.1
  76.8 12.0 %convolve.1 = bf16[16,40,640]{2,1,0:T(8,128)(2,1)} custom-call(s32[1]{0:T(128)S(6)} %copy.10.sizes, f32[160,1]{1,0:T(8,128)S(1)} %copy.7.rates, bf16[160,640]{1,0:T(8,128)(2,1)S(1)} %copy-done.1, bf16[160,640]{1,0:T(8,128)(2,1)S(1)} %collective-permute-done.2.refs_1_, bf16[160,640]{1,0:T(8,128)(2,1)S(1)} %collective-permute-done.3.refs_2_, ...), custom_call_target="tpu_custom_call" | custom-call | flops 4456448000 | bytes 6553600 | tf_op jit(solution)/shard_map/convolve/pallas_call | solution.py:193
  88.8 18.5 %all_to_all.10.packets = bf16[16,40,640]{2,1,0:T(8,128)(2,1)} all-to-all(bf16[16,40,640]{2,1,0:T(8,128)(2,1)} %convolve.1), channel_id=1, replica_groups=mesh['tx'=4,'ty'=4,'sector'=8] {'tx','ty'}, dimensions={0} | all-to-all | bytes 1638400 | tf_op jit(solution)/shard_map/all_to_all | solution.py:273
  107.3 2.4 %assemble.1 = bf16[640,640]{1,0:T(8,128)(2,1)} custom-call(bf16[16,40,640]{2,1,0:T(8,128)(2,1)} %all_to_all.10.packets), custom_call_target="tpu_custom_call" | custom-call | tf_op jit(solution)/shard_map/assemble/pallas_call | solution.py:226
  (6 shorter events, 0.1 us)
Async XLA Ops:
  0.0 66.7 %copy-start = (f32[1,640]{1,0:T(1,128)S(1)}, f32[1,640]{1,0:T(1,128)}, u32[]{:S(2)}) copy-start(f32[1,640]{1,0:T(1,128)} %param.8) | copy-start | bytes 7684
  5.1 12.1 %collective-permute-start = (bf16[640,640]{1,0:T(8,128)(2,1)}, bf16[640,640]{1,0:T(8,128)(2,1)S(1)}, u32[]{:S(2)}, u32[]{:S(2)}) collective-permute-start(bf16[640,640]{1,0:T(8,128)(2,1)} %get-tuple-element.22), channel_id=1, source_target_pairs={{1,0},{2,1},{3,2},{4,3},{5,4},{6,5},{7,6},{9,8},{10,9},{11,10},{12... | collective-permute-start | bytes 2457608 | tf_op jit(solution)/shard_map/ppermute | solution.py:22
  7.0 13.9 %collective-permute-start.1 = (bf16[640,640]{1,0:T(8,128)(2,1)}, bf16[640,640]{1,0:T(8,128)(2,1)S(1)}, u32[]{:S(2)}, u32[]{:S(2)}) collective-permute-start(bf16[640,640]{1,0:T(8,128)(2,1)} %get-tuple-element.23), channel_id=1, source_target_pairs={{0,1},{1,2},{2,3},{3,4},{4,5},{5,6},{6,7},{8,9},{9,10},{10,11},{11... | collective-permute-start | bytes 2457608 | tf_op jit(solution)/shard_map/ppermute | solution.py:22
  9.4 18.2 %all-to-all-start = ((bf16[4,160,640]{2,1,0:T(8,128)(2,1)}), bf16[4,160,640]{2,1,0:T(8,128)(2,1)S(1)}, u32[]{:S(2)}, u32[]{:S(2)}) async-start(bf16[4,160,640]{2,1,0:T(8,128)(2,1)} %bitcast.19), calls=%async_computation | async-start | bytes 1638400 | tf_op jit(solution)/shard_map/all_to_all | solution.py:246
  17.2 3.7 %copy-start.7 = (bf16[640,640]{1,0:T(8,128)(2,1)}, bf16[640,640]{1,0:T(8,128)(2,1)S(1)}, u32[]{:S(2)}) copy-start(bf16[640,640]{1,0:T(8,128)(2,1)S(1)} %collective-permute-done.refs_1_) | copy-start | bytes 2457604
  20.9 0.9 copy-start.8
  27.7 17.9 %copy-start.2 = (bf16[4,160,640]{2,1,0:T(8,128)(2,1)}, bf16[4,160,640]{2,1,0:T(8,128)(2,1)S(1)}, u32[]{:S(2)}) copy-start(bf16[4,160,640]{2,1,0:T(8,128)(2,1)S(1)} %all-to-all-done) | copy-start | bytes 2457604
  27.7 8.5 %collective-permute-start.2 = (bf16[160,640]{1,0:T(8,128)(2,1)}, bf16[160,640]{1,0:T(8,128)(2,1)S(1)}, u32[]{:S(2)}, u32[]{:S(2)}) collective-permute-start(bf16[160,640]{1,0:T(8,128)(2,1)} %get-tuple-element.29), channel_id=1, source_target_pairs={{0,32},{32,64},{64,96},{96,0},{1,33},{33,65},{65,97},{97,1},{2,34}... | collective-permute-start | bytes 614408 | tf_op jit(solution)/shard_map/ppermute | solution.py:27
  29.2 13.3 %collective-permute-start.3 = (bf16[160,640]{1,0:T(8,128)(2,1)}, bf16[160,640]{1,0:T(8,128)(2,1)S(1)}, u32[]{:S(2)}, u32[]{:S(2)}) collective-permute-start(bf16[160,640]{1,0:T(8,128)(2,1)} %get-tuple-element.30), channel_id=1, source_target_pairs={{0,64},{32,96},{64,0},{96,32},{1,65},{33,97},{65,1},{97,33},{2,66}... | collective-permute-start | bytes 614408 | tf_op jit(solution)/shard_map/ppermute | solution.py:27
  31.9 10.6 %collective-permute-start.4 = (bf16[160,640]{1,0:T(8,128)(2,1)}, bf16[160,640]{1,0:T(8,128)(2,1)S(1)}, u32[]{:S(2)}, u32[]{:S(2)}) collective-permute-start(bf16[160,640]{1,0:T(8,128)(2,1)} %get-tuple-element.31), channel_id=1, source_target_pairs={{0,96},{32,0},{64,32},{96,64},{1,97},{33,1},{65,33},{97,65},{2,98}... | collective-permute-start | bytes 614408 | tf_op jit(solution)/shard_map/ppermute | solution.py:27
  33.3 26.5 %collective-permute-start.8 = (bf16[4,160,640]{2,1,0:T(8,128)(2,1)S(1)}, bf16[4,160,640]{2,1,0:T(8,128)(2,1)S(1)}, u32[]{:S(2)}, u32[]{:S(2)}) collective-permute-start(bf16[4,160,640]{2,1,0:T(8,128)(2,1)S(1)} %all-to-all-done), channel_id=1, source_target_pairs={{0,96},{32,0},{64,32},{96,64},{1,97},{33,1},{65,33},{97,65},{2,98}... | collective-permute-start | bytes 2457608 | tf_op jit(solution)/shard_map/ppermute | solution.py:27
  33.4 26.5 %collective-permute-start.7 = (bf16[4,160,640]{2,1,0:T(8,128)(2,1)S(1)}, bf16[4,160,640]{2,1,0:T(8,128)(2,1)S(1)}, u32[]{:S(2)}, u32[]{:S(2)}) collective-permute-start(bf16[4,160,640]{2,1,0:T(8,128)(2,1)S(1)} %all-to-all-done), channel_id=1, source_target_pairs={{0,32},{32,64},{64,96},{96,0},{1,33},{33,65},{65,97},{97,1},{2,34}... | collective-permute-start | bytes 2457608 | tf_op jit(solution)/shard_map/ppermute | solution.py:27
  43.5 18.7 %collective-permute-start.6 = (bf16[4,160,640]{2,1,0:T(8,128)(2,1)S(1)}, bf16[4,160,640]{2,1,0:T(8,128)(2,1)S(1)}, u32[]{:S(2)}, u32[]{:S(2)}) collective-permute-start(bf16[4,160,640]{2,1,0:T(8,128)(2,1)S(1)} %pad_maximum_fusion), channel_id=1, source_target_pairs={{0,24},{8,0},{16,8},{24,16},{1,25},{9,1},{17,9},{25,17},{2,26},{10... | collective-permute-start | bytes 2457608 | tf_op jit(solution)/shard_map/ppermute | solution.py:27
  45.3 18.5 %collective-permute-start.5 = (bf16[4,160,640]{2,1,0:T(8,128)(2,1)S(1)}, bf16[4,160,640]{2,1,0:T(8,128)(2,1)S(1)}, u32[]{:S(2)}, u32[]{:S(2)}) collective-permute-start(bf16[4,160,640]{2,1,0:T(8,128)(2,1)S(1)} %pad_maximum_fusion), channel_id=1, source_target_pairs={{0,8},{8,16},{16,24},{24,0},{1,9},{9,17},{17,25},{25,1},{2,10},{10... | collective-permute-start | bytes 2457608 | tf_op jit(solution)/shard_map/ppermute | solution.py:27
  45.6 31.2 %collective-permute-start.11 = (bf16[4,160,640]{2,1,0:T(8,128)(2,1)S(1)}, bf16[4,160,640]{2,1,0:T(8,128)(2,1)}, u32[]{:S(2)}, u32[]{:S(2)}) collective-permute-start(bf16[4,160,640]{2,1,0:T(8,128)(2,1)S(1)} %all-to-all-done), channel_id=1, source_target_pairs={{0,64},{32,96},{64,0},{96,32},{1,65},{33,97},{65,1},{97,33},{2,66}... | collective-permute-start | bytes 2457608 | tf_op jit(solution)/shard_map/ppermute | solution.py:27
  59.9 6.8 %copy-start.5 = (bf16[4,160,640]{2,1,0:T(8,128)(2,1)}, bf16[4,160,640]{2,1,0:T(8,128)(2,1)S(1)}, u32[]{:S(2)}) copy-start(bf16[4,160,640]{2,1,0:T(8,128)(2,1)S(1)} %collective-permute-done.8) | copy-start | bytes 2457604
  59.9 6.8 %copy-start.6 = (bf16[4,160,640]{2,1,0:T(8,128)(2,1)}, bf16[4,160,640]{2,1,0:T(8,128)(2,1)S(1)}, u32[]{:S(2)}) copy-start(bf16[4,160,640]{2,1,0:T(8,128)(2,1)S(1)} %collective-permute-done.7) | copy-start | bytes 2457604
  62.2 1.7 %copy-start.3 = (bf16[4,160,640]{2,1,0:T(8,128)(2,1)}, bf16[4,160,640]{2,1,0:T(8,128)(2,1)S(1)}, u32[]{:S(2)}) copy-start(bf16[4,160,640]{2,1,0:T(8,128)(2,1)S(1)} %collective-permute-done.6.refs_5_) | copy-start | bytes 2457604
  63.8 0.9 copy-start.4
  63.8 13.0 %copy-start.1 = (bf16[160,640]{1,0:T(8,128)(2,1)S(1)}, bf16[160,640]{1,0:T(8,128)(2,1)}, u32[]{:S(2)}) copy-start(bf16[160,640]{1,0:T(8,128)(2,1)} %get-tuple-element.24.refs_0_) | copy-start | bytes 614404
  64.7 12.1 %collective-permute-start.10 = (bf16[4,80,640]{2,1,0:T(8,128)(2,1)S(1)}, bf16[4,80,640]{2,1,0:T(8,128)(2,1)S(1)}, u32[]{:S(2)}, u32[]{:S(2)}) collective-permute-start(bf16[4,80,640]{2,1,0:T(8,128)(2,1)S(1)} %slice.7), channel_id=1, source_target_pairs={{0,24},{8,0},{16,8},{24,16},{1,25},{9,1},{17,9},{25,17},{2,26},{10... | collective-permute-start | bytes 1228808 | tf_op jit(solution)/shard_map/ppermute | solution.py:27
  65.2 11.6 %collective-permute-start.9 = (bf16[4,80,640]{2,1,0:T(8,128)(2,1)S(1)}, bf16[4,80,640]{2,1,0:T(8,128)(2,1)S(1)}, u32[]{:S(2)}, u32[]{:S(2)}) collective-permute-start(bf16[4,80,640]{2,1,0:T(8,128)(2,1)S(1)} %slice.6), channel_id=1, source_target_pairs={{0,8},{8,16},{16,24},{24,0},{1,9},{9,17},{17,25},{25,1},{2,10},{10... | collective-permute-start | bytes 1228808 | tf_op jit(solution)/shard_map/ppermute | solution.py:27

commit v7 on v6

--- a/solution.py
+++ b/solution.py
@@ -27,12 +27,24 @@
     return lax.ppermute(block, axis, [(i, (i + distance) % n) for i in range(n)])
 
 
-def tied(value, *others):
-    return lax.optimization_barrier((value, *others))[0]
-
-
-def spread(block, axis):
-    return [(-d, ring(block, axis, d)) for d in (1, -1, 2)]
+def turn_sign():
+    return 1 - 2 * lax.rem(lax.axis_index("sector"), 2)
+
+
+def turned_ring(block, axis, distance):
+    n, sectors = lax.axis_size(axis), lax.axis_size("sector")
+    route = []
+    for i in range(n):
+        for s in range(sectors):
+            step = distance if s % 2 == 0 else -distance
+            route.append((i * sectors + s, (i + step) % n * sectors + s))
+    return lax.ppermute(block, (axis, "sector"), route)
+
+
+def ring_gather(block, axis):
+    before = turned_ring(block, axis, 1)
+    after = turned_ring(block, axis, -1)
+    return [(0, block), (-1, before), (1, after), (2, turned_ring(before, axis, 1))]
 
 
 def live(shape, size, first_row=0):
@@ -45,7 +57,10 @@
     return jnp.dot(a, b, preferred_element_type=jnp.float32)
 
 
-def prepare_kernel(sizes, prop, operator, masked, upward, turned, flipped):
+def prepare_kernel(sizes, prop, operator, masked, upward, flipped, *refs):
+    *turned, staged = refs
+    n = len(turned)
+    rows = turned[0].shape[0]
     inner = prop[...].astype(jnp.float32)
     inner = jnp.where(live(inner.shape, sizes[0]), inner, 0.0).astype(jnp.bfloat16)
     masked[...] = inner
@@ -54,18 +69,24 @@
     upward[...] = lax.dot_general(raised, r, NT, preferred_element_type=jnp.float32).astype(
         jnp.bfloat16
     )
-    turned[...] = inner.T
+    staged[...] = inner.T
+    here_y = lax.axis_index("ty")
+    for d in range(n):
+        first = pl.multiple_of(lax.rem(here_y + d, n) * rows, 32)
+        turned[d][...] = staged[pl.ds(first, rows), :]
     flipped[...] = r.T
 
 
-def prepare(sizes, prop, operator):
+def prepare(sizes, prop, operator, n):
     states = prop.shape[0]
     square = jax.ShapeDtypeStruct((states, states), jnp.bfloat16)
+    block = jax.ShapeDtypeStruct((states // n, states), jnp.bfloat16)
     return pl.pallas_call(
         prepare_kernel,
-        out_shape=(square,) * 4,
+        out_shape=(square,) * 3 + (block,) * n,
         in_specs=[SMEM, VMEM, VMEM],
-        out_specs=(VMEM,) * 4,
+        out_specs=(VMEM,) * (3 + n),
+        scratch_shapes=[pltpu.VMEM((states, states), jnp.bfloat16)],
         cost_estimate=pl.CostEstimate(
             flops=4 * states**3, bytes_accessed=12 * states**2, transcendentals=0
         ),
@@ -125,25 +146,18 @@
     out, e_all, g_all, total, sems = refs[len(plan) :]
     rows, states = g_all.shape[1], e_all.shape[1] // (n * n + 1)
     here_x, here_y, size = lax.axis_index("tx"), lax.axis_index("ty"), sizes[0]
+    sign = turn_sign()
     copies_e, copies_g = [], []
-
-    def lag_room(x, y, top, tall):
-        slot = n * n - 1 - (n * around(here_x, x, n) + around(here_y, y, n))
-        left = pl.multiple_of(slot * states, 128)
-        return e_all.at[pl.ds(top, tall), pl.ds(left, states)]
-
-    for part, (kind, across, step) in zip(parts, plan):
-        if kind == "e":
-            copies_e.append((part, lag_room(across, step, 0, rows)))
-        elif kind == "all":
-            tall = part.shape[1]
-            for d in range(n):
-                copies_e.append((part.at[d], lag_room(-d, step, across * tall, tall)))
-        else:
-            first = around(here_x, step, n) * (n // 2)
-            for k in range(2):
-                room = g_all.at[pl.ds(first, n // 2), :, pl.ds(k * states, states)]
-                copies_g.append((part.at[:, k], room))
+    for part, (kind, step) in zip(parts, plan):
+        for d in range(n):
+            if kind == "e":
+                lag = n * around(here_x, -d, n) + around(here_y, sign * step, n)
+                left = pl.multiple_of((n * n - 1 - lag) * states, 128)
+                copies_e.append((part.at[d], e_all.at[:, pl.ds(left, states)]))
+            else:
+                u = n * around(here_x, sign * step, n) + around(here_y, -d, n)
+                left = pl.multiple_of(lax.rem(u, 2) * states, 128)
+                copies_g.append((part.at[d], g_all.at[u // 2, :, pl.ds(left, states)]))
     moves = [
         pltpu.make_async_copy(src, dst, sems.at[i])
         for i, (src, dst) in enumerate(copies_e + copies_g)
@@ -187,9 +201,9 @@
 
 
 def convolve(entries, sizes, rates, n, step_size):
-    plan, parts = [e[:3] for e in entries], [e[3] for e in entries]
-    rows, states = parts[0].shape
-    copies = sum({"e": 1, "all": n, "g": 2}[kind] for kind, *_ in plan)
+    plan, parts = [e[:2] for e in entries], [e[2] for e in entries]
+    _, rows, states = parts[0].shape
+    copies = n * len(parts)
     return pl.pallas_call(
         functools.partial(convolve_kernel, plan, n, step_size),
         out_shape=jax.ShapeDtypeStruct((n * n, rows // n, states), jnp.bfloat16),
@@ -240,34 +254,22 @@
     here_x = lax.axis_index("tx")
     operator = rising_op[0]
 
-    masked, upward, turned, flipped = prepare(sector_sizes, propagator[0, 0], operator)
+    masked, upward, flipped, own_g, *away_g = prepare(
+        sector_sizes, propagator[0, 0], operator, n
+    )
     below = shifted(upward, "sector", 1)
     above = shifted(masked, "sector", -1)
-    columns = lax.all_to_all(turned.reshape(n, rows, states), "ty", 0, 0, tiled=True)
-
-    own, *away = energy_blocks(
+    crossed_g = {d: ring(away_g[d - 1], "ty", d) for d in (2, 1, 3)}
+    columns = jnp.stack([own_g] + [crossed_g[d] for d in range(1, n)])
+
+    own_e, *away_e = energy_blocks(
         sector_sizes, hyb_particle, hyb_hole, above, below, operator, flipped, n
     )
-    away, columns = lax.optimization_barrier((away, columns))
-    crossed = {d: ring(away[d - 1], "tx", d) for d in (2, 1, 3)}
-    crossed = [crossed[d] for d in range(1, n)]
-    gathered = [(0, columns)] + [(-d, ring(columns, "tx", d)) for d in (1, -1, 2)]
-
-    lines = jnp.stack([own] + crossed)
-    half = rows // 2
-    down, up = ring(lines, "ty", 1), ring(lines, "ty", -1)
-    down, up, *nearest = lax.optimization_barrier((down, up, gathered[1][1], gathered[2][1]))
-    gathered[1:3] = [(gathered[1][0], nearest[0]), (gathered[2][0], nearest[1])]
-    across_first = ring(down[:, :half], "ty", 1)
-    across_second = ring(up[:, half:], "ty", -1)
-
-    entries = (
-        [("e", 0, 0, own)]
-        + [("e", -d, 0, crossed[d - 1]) for d in range(1, n)]
-        + [("all", 0, -1, down), ("all", 0, 1, up)]
-        + [("all", 0, 2, across_first), ("all", 1, 2, across_second)]
-        + [("g", 0, step, g.reshape(n // 2, 2, rows, states)) for step, g in gathered]
-    )
+    crossed_e = {d: ring(away_e[d - 1], "tx", d) for d in (2, 1, 3)}
+    lines = jnp.stack([own_e] + [crossed_e[d] for d in range(1, n)])
+
+    entries = [("g", step, part) for step, part in ring_gather(columns, "tx")]
+    entries = [("e", step, part) for step, part in ring_gather(lines, "ty")] + entries
     rates = lax.dynamic_slice_in_dim(energies[0], here_x * rows, rows, 0)[:, None]
     packets = convolve(entries, sector_sizes, rates, n, step_size)
     packets = lax.all_to_all(packets, ("tx", "ty"), 0, 0, tiled=True)

time: 111 us -> 107 us (0.964)
  waiting for transfers between devices: 39.4 us -> 41.8 us
  blocking collectives: 18.5 us -> 16.2 us
  starting transfers between devices: 23.5 us -> 22.2 us
    ppermute x0 -> x6, waiting for transfers between devices: none -> 29.3 us  [turned_ring(): return lax.ppermute(block, (axis, 'sector'), route)]
    ppermute x10 -> x6, waiting for transfers between devices: 32.3 us -> 8.22 us  [ring(): lax.ppermute(block, axis, [(i, (i + distance) % n) for i in range(n)])]
    ppermute x0 -> x6, starting transfers between devices: none -> 6.31 us  [turned_ring(): return lax.ppermute(block, (axis, 'sector'), route)]
    all_to_all x1 -> x0, starting transfers between devices: 4.47 us -> none  [per_device(): lax.all_to_all(turned.reshape(n, rows, states), 'ty', 0, 0, tiled=True)]
    ppermute x10 -> x6, starting transfers between devices: 14.7 us -> 11.6 us  [ring(): lax.ppermute(block, axis, [(i, (i + distance) % n) for i in range(n)])]
    all_to_all x1, blocking collectives: 18.5 us -> 16.2 us  [per_device(): packets = lax.all_to_all(packets, ('tx', 'ty'), 0, 0, tiled=True)]
    all_to_all x1 -> x0, waiting for transfers between devices: 1.44 us -> none  [per_device(): lax.all_to_all(turned.reshape(n, rows, states), 'ty', 0, 0, tiled=True)]
    ppermute x2, waiting for transfers between devices: 5.69 us -> 4.26 us  [shifted(): return lax.ppermute(block, axis, route)]
  transfers between devices with their start and end apart: 13 -> 14, of which waited for: 9 -> 9; matrix products, arithmetic and copies ran while one was open for 1% -> 0% of each run, Pallas kernels for 4% -> 4%
where the time goes in v7:
time: 107 us; the launch traced here: 106 us
  waiting for transfers between devices  41.8 us (39%)
  Pallas kernels  22.7 us (21%)
  starting transfers between devices  22.2 us (21%)
  blocking collectives  16.2 us (15%)
  between operations  2.06 us (2%)
  local copies, waits for them, and re-layouts  1.16 us (1%)
    ppermute x6, waiting for transfers between devices, turned_ring(): return lax.ppermute(block, (axis, 'sector'), route)  29.3 us
    all_to_all x1, blocking collectives, per_device(): packets = lax.all_to_all(packets, ('tx', 'ty'), 0, 0, tiled=True)  16.2 us
    ppermute x6, starting transfers between devices, ring(): lax.ppermute(block, axis, [(i, (i + distance) % n) for i in range(n)])  11.6 us
    pallas_call x1, Pallas kernels, convolve(): pl.pallas_call(functools.partial(convolve_kernel, plan, n, step_size), ou...  11.2 us
    ppermute x6, waiting for transfers between devices, ring(): lax.ppermute(block, axis, [(i, (i + distance) % n) for i in range(n)])  8.22 us
    ppermute x6, starting transfers between devices, turned_ring(): return lax.ppermute(block, (axis, 'sector'), route)  6.31 us
    pallas_call x1, Pallas kernels, prepare(): pl.pallas_call(prepare_kernel, out_shape=(square,) * 3 + (block,) * n, in...  4.59 us
    pallas_call x1, Pallas kernels, energy_blocks(): pl.pallas_call(energy_kernel, out_shape=(block,) * n, in_specs=[SMEM] * 3...  4.44 us
  transfers between devices with their start and end apart: 14, of which 9 were waited for; matrix products, arithmetic and copies ran while one was open for 0% of the time, Pallas kernels for 4%

profile of v7, /device:TPU:32, one launch (start us, length us, event | category | flops | bytes accessed | tf_op | source)
XLA Modules:
  0.0 106.4 jit_solution(5000906229652981596)
XLA Ops:
  0.0 0.0 copy-start
  0.7 4.6 %prepare.1 = (bf16[640,640]{1,0:T(8,128)(2,1)}, bf16[640,640]{1,0:T(8,128)(2,1)}, bf16[640,640]{1,0:T(8,128)(2,1)}, bf16[160,640]{1,0:T(8,128)(2,1)}, bf16[160,6...) custom-call(s32[1]{0:T(128)S(6)} %copy.10.sizes, bf16[640,640]{1,0:T(8,128)(2,1)} %bitcast.21, ...), custom_call_target="tpu_custom_call" | custom-call | flops 1048576000 | bytes 4915200 | tf_op jit(solution)/shard_map/prepare/pallas_call | solution.py:84
  5.3 1.9 %collective-permute-start = (bf16[640,640]{1,0:T(8,128)(2,1)}, bf16[640,640]{1,0:T(8,128)(2,1)S(1)}, u32[]{:S(2)}, u32[]{:S(2)}) collective-permute-start(bf16[640,640]{1,0:T(8,128)(2,1)} %get-tuple-element.17), channel_id=1, source_target_pairs={{1,0},{2,1},{3,2},{4,3},{5,4},{6,5},{7,6},{9,8},{10,9},{11,10},{12... | collective-permute-start | bytes 2457608 | tf_op jit(solution)/shard_map/ppermute | solution.py:22
  7.2 2.4 %collective-permute-start.1 = (bf16[640,640]{1,0:T(8,128)(2,1)}, bf16[640,640]{1,0:T(8,128)(2,1)S(1)}, u32[]{:S(2)}, u32[]{:S(2)}) collective-permute-start(bf16[640,640]{1,0:T(8,128)(2,1)} %get-tuple-element.18), channel_id=1, source_target_pairs={{0,1},{1,2},{2,3},{3,4},{4,5},{5,6},{6,7},{8,9},{9,10},{10,11},{11... | collective-permute-start | bytes 2457608 | tf_op jit(solution)/shard_map/ppermute | solution.py:22
  9.6 1.6 %collective-permute-start.8 = (bf16[160,640]{1,0:T(8,128)(2,1)}, bf16[160,640]{1,0:T(8,128)(2,1)S(1)}, u32[]{:S(2)}, u32[]{:S(2)}) collective-permute-start(bf16[160,640]{1,0:T(8,128)(2,1)} %get-tuple-element.24), channel_id=1, source_target_pairs={{0,8},{8,16},{16,24},{24,0},{1,9},{9,17},{17,25},{25,1},{2,10},{10... | collective-permute-start | bytes 614408 | tf_op jit(solution)/shard_map/ppermute | solution.py:27
  11.2 2.9 %collective-permute-start.9 = (bf16[160,640]{1,0:T(8,128)(2,1)}, bf16[160,640]{1,0:T(8,128)(2,1)S(1)}, u32[]{:S(2)}, u32[]{:S(2)}) collective-permute-start(bf16[160,640]{1,0:T(8,128)(2,1)} %get-tuple-element.25), channel_id=1, source_target_pairs={{0,16},{8,24},{16,0},{24,8},{1,17},{9,25},{17,1},{25,9},{2,18},{10... | collective-permute-start | bytes 614408 | tf_op jit(solution)/shard_map/ppermute | solution.py:27
  14.1 1.3 %collective-permute-start.10 = (bf16[160,640]{1,0:T(8,128)(2,1)}, bf16[160,640]{1,0:T(8,128)(2,1)S(1)}, u32[]{:S(2)}, u32[]{:S(2)}) collective-permute-start(bf16[160,640]{1,0:T(8,128)(2,1)} %get-tuple-element.26), channel_id=1, source_target_pairs={{0,24},{8,0},{16,8},{24,16},{1,25},{9,1},{17,9},{25,17},{2,26},{10... | collective-permute-start | bytes 614408 | tf_op jit(solution)/shard_map/ppermute | solution.py:27
  16.8 0.5 collective-permute-done.refs_1_
  17.3 3.7 %collective-permute-done.1.refs_3_ = bf16[640,640]{1,0:T(8,128)(2,1)S(1)} collective-permute-done((bf16[640,640]{1,0:T(8,128)(2,1)}, bf16[640,640]{1,0:T(8,128)(2,1)S(1)}, u32[]{:S(2)}, u32[]{:S(2)}) %collective-permute-start.1) | collective-permute-done | bytes 819232 | tf_op jit(solution)/shard_map/ppermute | solution.py:22
  21.0 0.0 copy-done.6
  21.0 0.9 copy-done.7
  22.0 4.4 %energy_blocks.1 = (bf16[160,640]{1,0:T(8,128)(2,1)}, bf16[160,640]{1,0:T(8,128)(2,1)}, bf16[160,640]{1,0:T(8,128)(2,1)}, bf16[160,640]{1,0:T(8,128)(2,1)}) custom-call(s32[1]{0:T(128)S(6)} %copy.10.sizes, f32[1]{0:T(128)S(6)} %copy.8.particle, f32[1]{0:T(128)S(6)} %copy.9.hole, bf16[640,640]{1,0:T(8,128)(2,1)} %get-tuple-element.16.refs_0_, ...), custom_call_target="tpu_custom_call" | custom-call | flops 1048576000 | bytes 4096000 | tf_op jit(solution)/shard_map/energy_blocks/pallas_call | solution.py:126
  26.4 1.5 %collective-permute-start.2 = (bf16[160,640]{1,0:T(8,128)(2,1)}, bf16[160,640]{1,0:T(8,128)(2,1)S(1)}, u32[]{:S(2)}, u32[]{:S(2)}) collective-permute-start(bf16[160,640]{1,0:T(8,128)(2,1)} %get-tuple-element.20), channel_id=1, source_target_pairs={{0,32},{32,64},{64,96},{96,0},{1,33},{33,65},{65,97},{97,1},{2,34}... | collective-permute-start | bytes 614408 | tf_op jit(solution)/shard_map/ppermute | solution.py:27
  28.0 2.7 %collective-permute-start.3 = (bf16[160,640]{1,0:T(8,128)(2,1)}, bf16[160,640]{1,0:T(8,128)(2,1)S(1)}, u32[]{:S(2)}, u32[]{:S(2)}) collective-permute-start(bf16[160,640]{1,0:T(8,128)(2,1)} %get-tuple-element.21), channel_id=1, source_target_pairs={{0,64},{32,96},{64,0},{96,32},{1,65},{33,97},{65,1},{97,33},{2,66}... | collective-permute-start | bytes 614408 | tf_op jit(solution)/shard_map/ppermute | solution.py:27
  30.7 0.0 collective-permute-done.8
  30.7 1.5 %collective-permute-start.4 = (bf16[160,640]{1,0:T(8,128)(2,1)}, bf16[160,640]{1,0:T(8,128)(2,1)S(1)}, u32[]{:S(2)}, u32[]{:S(2)}) collective-permute-start(bf16[160,640]{1,0:T(8,128)(2,1)} %get-tuple-element.22), channel_id=1, source_target_pairs={{0,96},{32,0},{64,32},{96,64},{1,97},{33,1},{65,33},{97,65},{2,98}... | collective-permute-start | bytes 614408 | tf_op jit(solution)/shard_map/ppermute | solution.py:27
  32.2 0.0 collective-permute-done.9
  32.2 0.0 collective-permute-done.10
  32.2 0.0 copy-done.2
  32.2 0.0 copy-start.3
  32.2 0.1 pad_maximum_fusion.1.refs_4_
  32.3 0.0 copy-start.1
  32.3 0.6 collective-permute-start.11
  33.0 2.0 %collective-permute-done.2 = bf16[160,640]{1,0:T(8,128)(2,1)S(1)} collective-permute-done((bf16[160,640]{1,0:T(8,128)(2,1)}, bf16[160,640]{1,0:T(8,128)(2,1)S(1)}, u32[]{:S(2)}, u32[]{:S(2)}) %collective-permute-start.2) | collective-permute-done | bytes 204832 | tf_op jit(solution)/shard_map/ppermute | solution.py:27
  35.0 5.1 %collective-permute-done.3 = bf16[160,640]{1,0:T(8,128)(2,1)S(1)} collective-permute-done((bf16[160,640]{1,0:T(8,128)(2,1)}, bf16[160,640]{1,0:T(8,128)(2,1)S(1)}, u32[]{:S(2)}, u32[]{:S(2)}) %collective-permute-start.3) | collective-permute-done | bytes 204832 | tf_op jit(solution)/shard_map/ppermute | solution.py:27
  40.0 1.2 %collective-permute-done.4 = bf16[160,640]{1,0:T(8,128)(2,1)S(1)} collective-permute-done((bf16[160,640]{1,0:T(8,128)(2,1)}, bf16[160,640]{1,0:T(8,128)(2,1)S(1)}, u32[]{:S(2)}, u32[]{:S(2)}) %collective-permute-start.4) | collective-permute-done | bytes 204832 | tf_op jit(solution)/shard_map/ppermute | solution.py:27
  41.2 0.0 copy-done.3
  41.2 0.1 pad_maximum_fusion.refs_0_
  41.3 1.6 %collective-permute-start.5 = (bf16[4,160,640]{2,1,0:T(8,128)(2,1)S(1)}, bf16[4,160,640]{2,1,0:T(8,128)(2,1)S(1)}, u32[]{:S(2)}, u32[]{:S(2)}) collective-permute-start(bf16[4,160,640]{2,1,0:T(8,128)(2,1)S(1)} %pad_maximum_fusion.refs_0_), channel_id=1, source_target_pairs={{0,8},{1,25},{2,10},{3,27},{4,12},{5,29},{6,14},{7,31},{8,16},{9,1... | collective-permute-start | bytes 2457608 | tf_op jit(solution)/shard_map/ppermute | solution.py:41
  43.0 0.0 copy-done.1
  43.0 1.6 %collective-permute-start.12 = (bf16[4,160,640]{2,1,0:T(8,128)(2,1)S(1)}, bf16[4,160,640]{2,1,0:T(8,128)(2,1)}, u32[]{:S(2)}, u32[]{:S(2)}) collective-permute-start(bf16[4,160,640]{2,1,0:T(8,128)(2,1)S(1)} %pad_maximum_fusion.1.refs_4_), channel_id=1, source_target_pairs={{0,96},{1,33},{2,98},{3,35},{4,100},{5,37},{6,102},{7,39},{32,0},{... | collective-permute-start | bytes 2457608 | tf_op jit(solution)/shard_map/ppermute | solution.py:41
  44.5 1.7 %collective-permute-start.6 = (bf16[4,160,640]{2,1,0:T(8,128)(2,1)S(1)}, bf16[4,160,640]{2,1,0:T(8,128)(2,1)}, u32[]{:S(2)}, u32[]{:S(2)}) collective-permute-start(bf16[4,160,640]{2,1,0:T(8,128)(2,1)S(1)} %pad_maximum_fusion.refs_0_), channel_id=1, source_target_pairs={{0,24},{1,9},{2,26},{3,11},{4,28},{5,13},{6,30},{7,15},{8,0},{9,17... | collective-permute-start | bytes 2457608 | tf_op jit(solution)/shard_map/ppermute | solution.py:41
  46.2 5.6 %collective-permute-done.11.refs_5_ = bf16[4,160,640]{2,1,0:T(8,128)(2,1)S(1)} collective-permute-done((bf16[4,160,640]{2,1,0:T(8,128)(2,1)S(1)}, bf16[4,160,640]{2,1,0:T(8,128)(2,1)S(1)}, u32[]{:S(2)}, u32[]{:S(2)}) %collective-permute-start.11) | collective-permute-done | bytes 819232 | tf_op jit(solution)/shard_map/ppermute | solution.py:41
  51.8 0.0 collective-permute-start.13
  51.8 11.1 %collective-permute-done.5.refs_1_ = bf16[4,160,640]{2,1,0:T(8,128)(2,1)S(1)} collective-permute-done((bf16[4,160,640]{2,1,0:T(8,128)(2,1)S(1)}, bf16[4,160,640]{2,1,0:T(8,128)(2,1)S(1)}, u32[]{:S(2)}, u32[]{:S(2)}) %collective-permute-start.5) | collective-permute-done | bytes 819232 | tf_op jit(solution)/shard_map/ppermute | solution.py:41
  62.9 0.8 collective-permute-start.7
  63.7 0.0 copy-done
  63.7 0.1 dynamic-slice_bitcast_fusion
  63.7 0.1 copy.7.rates
  63.9 0.0 collective-permute-done.12.refs_6_
  63.9 2.5 %collective-permute-done.13.refs_7_ = bf16[4,160,640]{2,1,0:T(8,128)(2,1)} collective-permute-done((bf16[4,160,640]{2,1,0:T(8,128)(2,1)S(1)}, bf16[4,160,640]{2,1,0:T(8,128)(2,1)}, u32[]{:S(2)}, u32[]{:S(2)}) %collective-permute-start.13) | collective-permute-done | bytes 819232 | tf_op jit(solution)/shard_map/ppermute | solution.py:41
  66.4 0.0 collective-permute-done.6.refs_2_
  66.4 10.2 %collective-permute-done.7.refs_3_ = bf16[4,160,640]{2,1,0:T(8,128)(2,1)} collective-permute-done((bf16[4,160,640]{2,1,0:T(8,128)(2,1)S(1)}, bf16[4,160,640]{2,1,0:T(8,128)(2,1)}, u32[]{:S(2)}, u32[]{:S(2)}) %collective-permute-start.7) | collective-permute-done | bytes 819232 | tf_op jit(solution)/shard_map/ppermute | solution.py:41
  76.5 0.0 copy-done.4
  76.5 0.0 copy-done.5
  76.5 11.2 %convolve.1 = bf16[16,40,640]{2,1,0:T(8,128)(2,1)S(1)} custom-call(s32[1]{0:T(128)S(6)} %copy.10.sizes, f32[160,1]{1,0:T(8,128)S(1)} %copy.7.rates, bf16[4,160,640]{2,1,0:T(8,128)(2,1)S(1)} %pad_maximum_fusion.refs_0_, bf16[4,160,640]{2,1,0:T(8,128)(2,1)} %copy-done.5, bf16[4,160,640]{2,1,0:T(8,128)(2,1)} %collective-permute-done.6.refs_2_, ...), custom_call_target="tpu_custom_call" | custom-call | flops 4456448000 | bytes 6553600 | tf_op jit(solution)/shard_map/convolve/pallas_call | solution.py:207
  87.8 16.2 %all_to_all.5.packets = bf16[16,40,640]{2,1,0:T(8,128)(2,1)} all-to-all(bf16[16,40,640]{2,1,0:T(8,128)(2,1)S(1)} %convolve.1), channel_id=1, replica_groups=mesh['tx'=4,'ty'=4,'sector'=8] {'tx','ty'}, dimensions={0} | all-to-all | bytes 1638400 | tf_op jit(solution)/shard_map/all_to_all | solution.py:275
  104.0 2.4 %assemble.1 = bf16[640,640]{1,0:T(8,128)(2,1)} custom-call(bf16[16,40,640]{2,1,0:T(8,128)(2,1)} %all_to_all.5.packets), custom_call_target="tpu_custom_call" | custom-call | tf_op jit(solution)/shard_map/assemble/pallas_call | solution.py:240
  (5 shorter events, 0.0 us)
Async XLA Ops:
  0.0 63.7 %copy-start = (f32[1,640]{1,0:T(1,128)S(1)}, f32[1,640]{1,0:T(1,128)}, u32[]{:S(2)}) copy-start(f32[1,640]{1,0:T(1,128)} %param.8) | copy-start | bytes 7684
  5.3 12.1 %collective-permute-start = (bf16[640,640]{1,0:T(8,128)(2,1)}, bf16[640,640]{1,0:T(8,128)(2,1)S(1)}, u32[]{:S(2)}, u32[]{:S(2)}) collective-permute-start(bf16[640,640]{1,0:T(8,128)(2,1)} %get-tuple-element.17), channel_id=1, source_target_pairs={{1,0},{2,1},{3,2},{4,3},{5,4},{6,5},{7,6},{9,8},{10,9},{11,10},{12... | collective-permute-start | bytes 2457608 | tf_op jit(solution)/shard_map/ppermute | solution.py:22
  7.2 13.9 %collective-permute-start.1 = (bf16[640,640]{1,0:T(8,128)(2,1)}, bf16[640,640]{1,0:T(8,128)(2,1)S(1)}, u32[]{:S(2)}, u32[]{:S(2)}) collective-permute-start(bf16[640,640]{1,0:T(8,128)(2,1)} %get-tuple-element.18), channel_id=1, source_target_pairs={{0,1},{1,2},{2,3},{3,4},{4,5},{5,6},{6,7},{8,9},{9,10},{10,11},{11... | collective-permute-start | bytes 2457608 | tf_op jit(solution)/shard_map/ppermute | solution.py:22
  9.6 21.1 %collective-permute-start.8 = (bf16[160,640]{1,0:T(8,128)(2,1)}, bf16[160,640]{1,0:T(8,128)(2,1)S(1)}, u32[]{:S(2)}, u32[]{:S(2)}) collective-permute-start(bf16[160,640]{1,0:T(8,128)(2,1)} %get-tuple-element.24), channel_id=1, source_target_pairs={{0,8},{8,16},{16,24},{24,0},{1,9},{9,17},{17,25},{25,1},{2,10},{10... | collective-permute-start | bytes 614408 | tf_op jit(solution)/shard_map/ppermute | solution.py:27
  11.2 20.9 %collective-permute-start.9 = (bf16[160,640]{1,0:T(8,128)(2,1)}, bf16[160,640]{1,0:T(8,128)(2,1)S(1)}, u32[]{:S(2)}, u32[]{:S(2)}) collective-permute-start(bf16[160,640]{1,0:T(8,128)(2,1)} %get-tuple-element.25), channel_id=1, source_target_pairs={{0,16},{8,24},{16,0},{24,8},{1,17},{9,25},{17,1},{25,9},{2,18},{10... | collective-permute-start | bytes 614408 | tf_op jit(solution)/shard_map/ppermute | solution.py:27
  14.1 18.0 %collective-permute-start.10 = (bf16[160,640]{1,0:T(8,128)(2,1)}, bf16[160,640]{1,0:T(8,128)(2,1)S(1)}, u32[]{:S(2)}, u32[]{:S(2)}) collective-permute-start(bf16[160,640]{1,0:T(8,128)(2,1)} %get-tuple-element.26), channel_id=1, source_target_pairs={{0,24},{8,0},{16,8},{24,16},{1,25},{9,1},{17,9},{25,17},{2,26},{10... | collective-permute-start | bytes 614408 | tf_op jit(solution)/shard_map/ppermute | solution.py:27
  17.3 3.7 %copy-start.6 = (bf16[640,640]{1,0:T(8,128)(2,1)}, bf16[640,640]{1,0:T(8,128)(2,1)S(1)}, u32[]{:S(2)}) copy-start(bf16[640,640]{1,0:T(8,128)(2,1)S(1)} %collective-permute-done.refs_1_) | copy-start | bytes 2457604
  21.0 0.9 copy-start.7
  22.0 10.2 %copy-start.2 = (bf16[160,640]{1,0:T(8,128)(2,1)S(1)}, bf16[160,640]{1,0:T(8,128)(2,1)}, u32[]{:S(2)}) copy-start(bf16[160,640]{1,0:T(8,128)(2,1)} %get-tuple-element.23) | copy-start | bytes 614404
  26.4 8.5 %collective-permute-start.2 = (bf16[160,640]{1,0:T(8,128)(2,1)}, bf16[160,640]{1,0:T(8,128)(2,1)S(1)}, u32[]{:S(2)}, u32[]{:S(2)}) collective-permute-start(bf16[160,640]{1,0:T(8,128)(2,1)} %get-tuple-element.20), channel_id=1, source_target_pairs={{0,32},{32,64},{64,96},{96,0},{1,33},{33,65},{65,97},{97,1},{2,34}... | collective-permute-start | bytes 614408 | tf_op jit(solution)/shard_map/ppermute | solution.py:27
  28.0 12.0 %collective-permute-start.3 = (bf16[160,640]{1,0:T(8,128)(2,1)}, bf16[160,640]{1,0:T(8,128)(2,1)S(1)}, u32[]{:S(2)}, u32[]{:S(2)}) collective-permute-start(bf16[160,640]{1,0:T(8,128)(2,1)} %get-tuple-element.21), channel_id=1, source_target_pairs={{0,64},{32,96},{64,0},{96,32},{1,65},{33,97},{65,1},{97,33},{2,66}... | collective-permute-start | bytes 614408 | tf_op jit(solution)/shard_map/ppermute | solution.py:27
  30.7 10.5 %collective-permute-start.4 = (bf16[160,640]{1,0:T(8,128)(2,1)}, bf16[160,640]{1,0:T(8,128)(2,1)S(1)}, u32[]{:S(2)}, u32[]{:S(2)}) collective-permute-start(bf16[160,640]{1,0:T(8,128)(2,1)} %get-tuple-element.22), channel_id=1, source_target_pairs={{0,96},{32,0},{64,32},{96,64},{1,97},{33,1},{65,33},{97,65},{2,98}... | collective-permute-start | bytes 614408 | tf_op jit(solution)/shard_map/ppermute | solution.py:27
  32.2 9.0 %copy-start.3 = (bf16[160,640]{1,0:T(8,128)(2,1)S(1)}, bf16[160,640]{1,0:T(8,128)(2,1)}, u32[]{:S(2)}) copy-start(bf16[160,640]{1,0:T(8,128)(2,1)} %get-tuple-element.19) | copy-start | bytes 614404
  32.3 10.7 %copy-start.1 = (bf16[4,160,640]{2,1,0:T(8,128)(2,1)}, bf16[4,160,640]{2,1,0:T(8,128)(2,1)S(1)}, u32[]{:S(2)}) copy-start(bf16[4,160,640]{2,1,0:T(8,128)(2,1)S(1)} %pad_maximum_fusion.1.refs_4_) | copy-start | bytes 2457604
  32.3 19.4 %collective-permute-start.11 = (bf16[4,160,640]{2,1,0:T(8,128)(2,1)S(1)}, bf16[4,160,640]{2,1,0:T(8,128)(2,1)S(1)}, u32[]{:S(2)}, u32[]{:S(2)}) collective-permute-start(bf16[4,160,640]{2,1,0:T(8,128)(2,1)S(1)} %pad_maximum_fusion.1.refs_4_), channel_id=1, source_target_pairs={{0,32},{1,97},{2,34},{3,99},{4,36},{5,101},{6,38},{7,103},{32,64},... | collective-permute-start | bytes 2457608 | tf_op jit(solution)/shard_map/ppermute | solution.py:41
  41.3 21.6 %collective-permute-start.5 = (bf16[4,160,640]{2,1,0:T(8,128)(2,1)S(1)}, bf16[4,160,640]{2,1,0:T(8,128)(2,1)S(1)}, u32[]{:S(2)}, u32[]{:S(2)}) collective-permute-start(bf16[4,160,640]{2,1,0:T(8,128)(2,1)S(1)} %pad_maximum_fusion.refs_0_), channel_id=1, source_target_pairs={{0,8},{1,25},{2,10},{3,27},{4,12},{5,29},{6,14},{7,31},{8,16},{9,1... | collective-permute-start | bytes 2457608 | tf_op jit(solution)/shard_map/ppermute | solution.py:41
  43.0 20.9 %collective-permute-start.12 = (bf16[4,160,640]{2,1,0:T(8,128)(2,1)S(1)}, bf16[4,160,640]{2,1,0:T(8,128)(2,1)}, u32[]{:S(2)}, u32[]{:S(2)}) collective-permute-start(bf16[4,160,640]{2,1,0:T(8,128)(2,1)S(1)} %pad_maximum_fusion.1.refs_4_), channel_id=1, source_target_pairs={{0,96},{1,33},{2,98},{3,35},{4,100},{5,37},{6,102},{7,39},{32,0},{... | collective-permute-start | bytes 2457608 | tf_op jit(solution)/shard_map/ppermute | solution.py:41
  44.5 21.8 %collective-permute-start.6 = (bf16[4,160,640]{2,1,0:T(8,128)(2,1)S(1)}, bf16[4,160,640]{2,1,0:T(8,128)(2,1)}, u32[]{:S(2)}, u32[]{:S(2)}) collective-permute-start(bf16[4,160,640]{2,1,0:T(8,128)(2,1)S(1)} %pad_maximum_fusion.refs_0_), channel_id=1, source_target_pairs={{0,24},{1,9},{2,26},{3,11},{4,28},{5,13},{6,30},{7,15},{8,0},{9,17... | collective-permute-start | bytes 2457608 | tf_op jit(solution)/shard_map/ppermute | solution.py:41
  51.8 24.8 %copy-start.4 = (bf16[4,160,640]{2,1,0:T(8,128)(2,1)}, bf16[4,160,640]{2,1,0:T(8,128)(2,1)S(1)}, u32[]{:S(2)}) copy-start(bf16[4,160,640]{2,1,0:T(8,128)(2,1)S(1)} %collective-permute-done.11.refs_5_) | copy-start | bytes 2457604
  51.8 14.6 %collective-permute-start.13 = (bf16[4,160,640]{2,1,0:T(8,128)(2,1)S(1)}, bf16[4,160,640]{2,1,0:T(8,128)(2,1)}, u32[]{:S(2)}, u32[]{:S(2)}) collective-permute-start(bf16[4,160,640]{2,1,0:T(8,128)(2,1)S(1)} %collective-permute-done.11.refs_5_), channel_id=1, source_target_pairs={{0,32},{1,97},{2,34},{3,99},{4,36},{5,101},{6,38},{7,103},{32,64},... | collective-permute-start | bytes 2457608 | tf_op jit(solution)/shard_map/ppermute | solution.py:41
  62.9 13.7 %copy-start.5 = (bf16[4,160,640]{2,1,0:T(8,128)(2,1)}, bf16[4,160,640]{2,1,0:T(8,128)(2,1)S(1)}, u32[]{:S(2)}) copy-start(bf16[4,160,640]{2,1,0:T(8,128)(2,1)S(1)} %collective-permute-done.5.refs_1_) | copy-start | bytes 2457604
  62.9 13.7 %collective-permute-start.7 = (bf16[4,160,640]{2,1,0:T(8,128)(2,1)S(1)}, bf16[4,160,640]{2,1,0:T(8,128)(2,1)}, u32[]{:S(2)}, u32[]{:S(2)}) collective-permute-start(bf16[4,160,640]{2,1,0:T(8,128)(2,1)S(1)} %collective-permute-done.5.refs_1_), channel_id=1, source_target_pairs={{0,8},{1,25},{2,10},{3,27},{4,12},{5,29},{6,14},{7,31},{8,16},{9,1... | collective-permute-start | bytes 2457608 | tf_op jit(solution)/shard_map/ppermute | solution.py:41

commit v8 on v7

--- a/solution.py
+++ b/solution.py
@@ -27,6 +27,10 @@
     return lax.ppermute(block, axis, [(i, (i + distance) % n) for i in range(n)])
 
 
+def tied(value, *others):
+    return lax.optimization_barrier((value, *others))[0]
+
+
 def turn_sign():
     return 1 - 2 * lax.rem(lax.axis_index("sector"), 2)
 
@@ -39,12 +43,6 @@
             step = distance if s % 2 == 0 else -distance
             route.append((i * sectors + s, (i + step) % n * sectors + s))
     return lax.ppermute(block, (axis, "sector"), route)
-
-
-def ring_gather(block, axis):
-    before = turned_ring(block, axis, 1)
-    after = turned_ring(block, axis, -1)
-    return [(0, block), (-1, before), (1, after), (2, turned_ring(before, axis, 1))]
 
 
 def live(shape, size, first_row=0):
@@ -133,6 +131,7 @@
         cost_estimate=pl.CostEstimate(
             flops=4 * states**3, bytes_accessed=10 * states**2, transcendentals=0
         ),
+        compiler_params=pltpu.CompilerParams(vmem_limit_bytes=56 * MIB),
         name="energy_blocks",
     )(sizes, particle, hole, flipped, above, operator, below)
 
@@ -228,20 +227,20 @@
 def assemble_kernel(n, packets, out):
     quarter, states = packets.shape[1:]
     rows = states // n
-    for x in range(n):
-        for b in range(n):
-            out[x * rows + b * quarter : x * rows + (b + 1) * quarter, :] = jnp.concatenate(
-                [packets[x * n + y, :, b * rows : (b + 1) * rows] for y in range(n)], axis=1
-            )
+    for b in range(n):
+        out[b * quarter : (b + 1) * quarter, :] = jnp.concatenate(
+            [packets[y, :, b * rows : (b + 1) * rows] for y in range(n)], axis=1
+        )
 
 
 def assemble(packets, n):
-    states = packets.shape[2]
+    quarter, states = packets.shape[1:]
     return pl.pallas_call(
         functools.partial(assemble_kernel, n),
         out_shape=jax.ShapeDtypeStruct((states, states), jnp.bfloat16),
-        in_specs=[VMEM],
-        out_specs=VMEM,
+        grid=(n,),
+        in_specs=[pl.BlockSpec((n, quarter, states), lambda x: (x, 0, 0))],
+        out_specs=pl.BlockSpec((states // n, states), lambda x: (x, 0)),
         name="assemble",
     )(packets)
 
@@ -268,8 +267,20 @@
     crossed_e = {d: ring(away_e[d - 1], "tx", d) for d in (2, 1, 3)}
     lines = jnp.stack([own_e] + [crossed_e[d] for d in range(1, n)])
 
-    entries = [("g", step, part) for step, part in ring_gather(columns, "tx")]
-    entries = [("e", step, part) for step, part in ring_gather(lines, "ty")] + entries
+    before_g = turned_ring(columns, "tx", 1)
+    before_e = turned_ring(lines, "ty", 1)
+    after_g = turned_ring(tied(columns, lines), "tx", -1)
+    after_e = turned_ring(tied(lines, before_g), "ty", -1)
+    far_g = turned_ring(before_g, "tx", 1)
+    far_e = turned_ring(before_e, "ty", 1)
+    entries = [
+        (kind, step, part)
+        for kind, parts in (
+            ("e", (lines, before_e, after_e, far_e)),
+            ("g", (columns, before_g, after_g, far_g)),
+        )
+        for step, part in zip((0, -1, 1, 2), parts)
+    ]
     rates = lax.dynamic_slice_in_dim(energies[0], here_x * rows, rows, 0)[:, None]
     packets = convolve(entries, sector_sizes, rates, n, step_size)
     packets = lax.all_to_all(packets, ("tx", "ty"), 0, 0, tiled=True)

time: 107 us -> 107 us (level)
  waiting for transfers between devices: 41.8 us -> 35.9 us
  starting transfers between devices: 22.2 us -> 24.9 us
  blocking collectives: 16.2 us -> 17.8 us
  Pallas kernels: 22.7 us -> 23.9 us
    ppermute x6, waiting for transfers between devices: 29.3 us -> 23.4 us  [turned_ring(): return lax.ppermute(block, (axis, 'sector'), route)]
    ppermute x6, starting transfers between devices: 6.31 us -> 8.98 us  [turned_ring(): return lax.ppermute(block, (axis, 'sector'), route)]
    all_to_all x1, blocking collectives: 16.2 us -> 17.8 us  [per_device(): packets = lax.all_to_all(packets, ('tx', 'ty'), 0, 0, tiled=True)]
    pallas_call x1, Pallas kernels: 2.41 us -> 3.53 us  [assemble(): pl.pallas_call(functools.partial(assemble_kernel, n), out_shape=jax.Shape...]
  transfers between devices with their start and end apart: 14 -> 14, of which waited for: 9 -> 8; matrix products, arithmetic and copies ran while one was open for 0% -> 0% of each run, Pallas kernels for 4% -> 4%
where the time goes in v8:
time: 107 us; the launch traced here: 106 us
  waiting for transfers between devices  35.9 us (34%)
  starting transfers between devices  24.9 us (23%)
  Pallas kernels  23.9 us (22%)
  blocking collectives  17.8 us (17%)
  between operations  2.07 us (2%)
  local copies, waits for them, and re-layouts  1.16 us (1%)
    ppermute x6, waiting for transfers between devices, turned_ring(): return lax.ppermute(block, (axis, 'sector'), route)  23.4 us
    all_to_all x1, blocking collectives, per_device(): packets = lax.all_to_all(packets, ('tx', 'ty'), 0, 0, tiled=True)  17.8 us
    ppermute x6, starting transfers between devices, ring(): lax.ppermute(block, axis, [(i, (i + distance) % n) for i in range(n)])  11.6 us
    pallas_call x1, Pallas kernels, convolve(): pl.pallas_call(functools.partial(convolve_kernel, plan, n, step_size), ou...  11.4 us
    ppermute x6, starting transfers between devices, turned_ring(): return lax.ppermute(block, (axis, 'sector'), route)  8.98 us
    ppermute x6, waiting for transfers between devices, ring(): lax.ppermute(block, axis, [(i, (i + distance) % n) for i in range(n)])  8.22 us
    pallas_call x1, Pallas kernels, prepare(): pl.pallas_call(prepare_kernel, out_shape=(square,) * 3 + (block,) * n, in...  4.59 us
    pallas_call x1, Pallas kernels, energy_blocks(): pl.pallas_call(energy_kernel, out_shape=(block,) * n, in_specs=[SMEM] * 3...  4.44 us
  transfers between devices with their start and end apart: 14, of which 8 were waited for; matrix products, arithmetic and copies ran while one was open for 0% of the time, Pallas kernels for 4%

profile of v8, /device:TPU:32, one launch (start us, length us, event | category | flops | bytes accessed | tf_op | source)
XLA Modules:
  0.0 106.1 jit_solution(3819748989102402788)
XLA Ops:
  0.0 0.0 copy-start
  0.7 4.6 %prepare.1 = (bf16[640,640]{1,0:T(8,128)(2,1)}, bf16[640,640]{1,0:T(8,128)(2,1)}, bf16[640,640]{1,0:T(8,128)(2,1)}, bf16[160,640]{1,0:T(8,128)(2,1)}, bf16[160,6...) custom-call(s32[1]{0:T(128)S(6)} %copy.10.sizes, bf16[640,640]{1,0:T(8,128)(2,1)} %bitcast.21, ...), custom_call_target="tpu_custom_call" | custom-call | flops 1048576000 | bytes 4915200 | tf_op jit(solution)/shard_map/prepare/pallas_call | solution.py:82
  5.3 1.9 %collective-permute-start = (bf16[640,640]{1,0:T(8,128)(2,1)}, bf16[640,640]{1,0:T(8,128)(2,1)S(1)}, u32[]{:S(2)}, u32[]{:S(2)}) collective-permute-start(bf16[640,640]{1,0:T(8,128)(2,1)} %get-tuple-element.19), channel_id=1, source_target_pairs={{1,0},{2,1},{3,2},{4,3},{5,4},{6,5},{7,6},{9,8},{10,9},{11,10},{12... | collective-permute-start | bytes 2457608 | tf_op jit(solution)/shard_map/ppermute | solution.py:22
  7.2 2.4 %collective-permute-start.1 = (bf16[640,640]{1,0:T(8,128)(2,1)}, bf16[640,640]{1,0:T(8,128)(2,1)S(1)}, u32[]{:S(2)}, u32[]{:S(2)}) collective-permute-start(bf16[640,640]{1,0:T(8,128)(2,1)} %get-tuple-element.20), channel_id=1, source_target_pairs={{0,1},{1,2},{2,3},{3,4},{4,5},{5,6},{6,7},{8,9},{9,10},{10,11},{11... | collective-permute-start | bytes 2457608 | tf_op jit(solution)/shard_map/ppermute | solution.py:22
  9.6 1.6 %collective-permute-start.6 = (bf16[160,640]{1,0:T(8,128)(2,1)}, bf16[160,640]{1,0:T(8,128)(2,1)S(1)}, u32[]{:S(2)}, u32[]{:S(2)}) collective-permute-start(bf16[160,640]{1,0:T(8,128)(2,1)} %get-tuple-element.26), channel_id=1, source_target_pairs={{0,8},{8,16},{16,24},{24,0},{1,9},{9,17},{17,25},{25,1},{2,10},{10... | collective-permute-start | bytes 614408 | tf_op jit(solution)/shard_map/ppermute | solution.py:27
  11.2 2.9 %collective-permute-start.7 = (bf16[160,640]{1,0:T(8,128)(2,1)}, bf16[160,640]{1,0:T(8,128)(2,1)S(1)}, u32[]{:S(2)}, u32[]{:S(2)}) collective-permute-start(bf16[160,640]{1,0:T(8,128)(2,1)} %get-tuple-element.27), channel_id=1, source_target_pairs={{0,16},{8,24},{16,0},{24,8},{1,17},{9,25},{17,1},{25,9},{2,18},{10... | collective-permute-start | bytes 614408 | tf_op jit(solution)/shard_map/ppermute | solution.py:27
  14.1 1.3 %collective-permute-start.8 = (bf16[160,640]{1,0:T(8,128)(2,1)}, bf16[160,640]{1,0:T(8,128)(2,1)S(1)}, u32[]{:S(2)}, u32[]{:S(2)}) collective-permute-start(bf16[160,640]{1,0:T(8,128)(2,1)} %get-tuple-element.28), channel_id=1, source_target_pairs={{0,24},{8,0},{16,8},{24,16},{1,25},{9,1},{17,9},{25,17},{2,26},{10... | collective-permute-start | bytes 614408 | tf_op jit(solution)/shard_map/ppermute | solution.py:27
  16.8 0.5 collective-permute-done.refs_1_
  17.3 3.7 %collective-permute-done.1.refs_3_ = bf16[640,640]{1,0:T(8,128)(2,1)S(1)} collective-permute-done((bf16[640,640]{1,0:T(8,128)(2,1)}, bf16[640,640]{1,0:T(8,128)(2,1)S(1)}, u32[]{:S(2)}, u32[]{:S(2)}) %collective-permute-start.1) | collective-permute-done | bytes 819232 | tf_op jit(solution)/shard_map/ppermute | solution.py:22
  21.0 0.0 copy-done.6
  21.0 0.9 copy-done.7
  22.0 4.4 %energy_blocks.1 = (bf16[160,640]{1,0:T(8,128)(2,1)}, bf16[160,640]{1,0:T(8,128)(2,1)}, bf16[160,640]{1,0:T(8,128)(2,1)}, bf16[160,640]{1,0:T(8,128)(2,1)}) custom-call(s32[1]{0:T(128)S(6)} %copy.10.sizes, f32[1]{0:T(128)S(6)} %copy.8.particle, f32[1]{0:T(128)S(6)} %copy.9.hole, bf16[640,640]{1,0:T(8,128)(2,1)} %get-tuple-element.18.refs_0_, ...), custom_call_target="tpu_custom_call" | custom-call | flops 1048576000 | bytes 4096000 | tf_op jit(solution)/shard_map/energy_blocks/pallas_call | solution.py:124
  26.4 1.5 %collective-permute-start.2 = (bf16[160,640]{1,0:T(8,128)(2,1)}, bf16[160,640]{1,0:T(8,128)(2,1)S(1)}, u32[]{:S(2)}, u32[]{:S(2)}) collective-permute-start(bf16[160,640]{1,0:T(8,128)(2,1)} %get-tuple-element.22), channel_id=1, source_target_pairs={{0,32},{32,64},{64,96},{96,0},{1,33},{33,65},{65,97},{97,1},{2,34}... | collective-permute-start | bytes 614408 | tf_op jit(solution)/shard_map/ppermute | solution.py:27
  28.0 2.7 %collective-permute-start.3 = (bf16[160,640]{1,0:T(8,128)(2,1)}, bf16[160,640]{1,0:T(8,128)(2,1)S(1)}, u32[]{:S(2)}, u32[]{:S(2)}) collective-permute-start(bf16[160,640]{1,0:T(8,128)(2,1)} %get-tuple-element.23), channel_id=1, source_target_pairs={{0,64},{32,96},{64,0},{96,32},{1,65},{33,97},{65,1},{97,33},{2,66}... | collective-permute-start | bytes 614408 | tf_op jit(solution)/shard_map/ppermute | solution.py:27
  30.7 0.0 collective-permute-done.6
  30.7 1.5 %collective-permute-start.4 = (bf16[160,640]{1,0:T(8,128)(2,1)}, bf16[160,640]{1,0:T(8,128)(2,1)S(1)}, u32[]{:S(2)}, u32[]{:S(2)}) collective-permute-start(bf16[160,640]{1,0:T(8,128)(2,1)} %get-tuple-element.24), channel_id=1, source_target_pairs={{0,96},{32,0},{64,32},{96,64},{1,97},{33,1},{65,33},{97,65},{2,98}... | collective-permute-start | bytes 614408 | tf_op jit(solution)/shard_map/ppermute | solution.py:27
  32.2 0.0 collective-permute-done.7
  32.2 0.0 collective-permute-done.8
  32.2 0.0 copy-done.2
  32.2 0.0 copy-start.3
  32.2 0.1 pad_maximum_fusion.1.refs_4_
  32.3 0.0 copy-start.1
  32.3 0.6 collective-permute-start.9
  33.0 2.0 %collective-permute-done.2 = bf16[160,640]{1,0:T(8,128)(2,1)S(1)} collective-permute-done((bf16[160,640]{1,0:T(8,128)(2,1)}, bf16[160,640]{1,0:T(8,128)(2,1)S(1)}, u32[]{:S(2)}, u32[]{:S(2)}) %collective-permute-start.2) | collective-permute-done | bytes 204832 | tf_op jit(solution)/shard_map/ppermute | solution.py:27
  35.0 5.1 %collective-permute-done.3 = bf16[160,640]{1,0:T(8,128)(2,1)S(1)} collective-permute-done((bf16[160,640]{1,0:T(8,128)(2,1)}, bf16[160,640]{1,0:T(8,128)(2,1)S(1)}, u32[]{:S(2)}, u32[]{:S(2)}) %collective-permute-start.3) | collective-permute-done | bytes 204832 | tf_op jit(solution)/shard_map/ppermute | solution.py:27
  40.0 1.2 %collective-permute-done.4 = bf16[160,640]{1,0:T(8,128)(2,1)S(1)} collective-permute-done((bf16[160,640]{1,0:T(8,128)(2,1)}, bf16[160,640]{1,0:T(8,128)(2,1)S(1)}, u32[]{:S(2)}, u32[]{:S(2)}) %collective-permute-start.4) | collective-permute-done | bytes 204832 | tf_op jit(solution)/shard_map/ppermute | solution.py:27
  41.2 0.0 copy-done.3
  41.2 0.1 pad_maximum_fusion.refs_0_
  41.3 1.6 %collective-permute-start.5 = (bf16[4,160,640]{2,1,0:T(8,128)(2,1)S(1)}, bf16[4,160,640]{2,1,0:T(8,128)(2,1)S(1)}, u32[]{:S(2)}, u32[]{:S(2)}) collective-permute-start(bf16[4,160,640]{2,1,0:T(8,128)(2,1)S(1)} %pad_maximum_fusion.refs_0_), channel_id=1, source_target_pairs={{0,8},{1,25},{2,10},{3,27},{4,12},{5,29},{6,14},{7,31},{8,16},{9,1... | collective-permute-start | bytes 2457608 | tf_op jit(solution)/shard_map/ppermute | solution.py:45
  43.0 5.7 %collective-permute-done.9.refs_5_ = bf16[4,160,640]{2,1,0:T(8,128)(2,1)S(1)} collective-permute-done((bf16[4,160,640]{2,1,0:T(8,128)(2,1)S(1)}, bf16[4,160,640]{2,1,0:T(8,128)(2,1)S(1)}, u32[]{:S(2)}, u32[]{:S(2)}) %collective-permute-start.9) | collective-permute-done | bytes 819232 | tf_op jit(solution)/shard_map/ppermute | solution.py:45
  48.7 3.0 %collective-permute-start.10 = (bf16[4,160,640]{2,1,0:T(8,128)(2,1)S(1)}, bf16[4,160,640]{2,1,0:T(8,128)(2,1)}, u32[]{:S(2)}, u32[]{:S(2)}) collective-permute-start(bf16[4,160,640]{2,1,0:T(8,128)(2,1)S(1)} %pad_maximum_fusion.refs_0_), channel_id=1, source_target_pairs={{0,24},{1,9},{2,26},{3,11},{4,28},{5,13},{6,30},{7,15},{8,0},{9,17... | collective-permute-start | bytes 2457608 | tf_op jit(solution)/shard_map/ppermute | solution.py:45
  51.7 0.0 collective-permute-start.13
  51.7 0.0 copy-done.1
  51.7 3.2 %collective-permute-start.12 = (bf16[4,160,640]{2,1,0:T(8,128)(2,1)S(1)}, bf16[4,160,640]{2,1,0:T(8,128)(2,1)}, u32[]{:S(2)}, u32[]{:S(2)}) collective-permute-start(bf16[4,160,640]{2,1,0:T(8,128)(2,1)S(1)} %pad_maximum_fusion.1.refs_4_), channel_id=1, source_target_pairs={{0,96},{1,33},{2,98},{3,35},{4,100},{5,37},{6,102},{7,39},{32,0},{... | collective-permute-start | bytes 2457608 | tf_op jit(solution)/shard_map/ppermute | solution.py:45
  55.0 2.6 %collective-permute-done.5.refs_1_ = bf16[4,160,640]{2,1,0:T(8,128)(2,1)S(1)} collective-permute-done((bf16[4,160,640]{2,1,0:T(8,128)(2,1)S(1)}, bf16[4,160,640]{2,1,0:T(8,128)(2,1)S(1)}, u32[]{:S(2)}, u32[]{:S(2)}) %collective-permute-start.5) | collective-permute-done | bytes 819232 | tf_op jit(solution)/shard_map/ppermute | solution.py:45
  57.5 0.4 collective-permute-start.11
  58.0 0.0 copy-done
  58.0 0.1 dynamic-slice_bitcast_fusion
  58.0 0.1 copy.7.rates
  58.2 15.1 %collective-permute-done.13.refs_7_ = bf16[4,160,640]{2,1,0:T(8,128)(2,1)} collective-permute-done((bf16[4,160,640]{2,1,0:T(8,128)(2,1)S(1)}, bf16[4,160,640]{2,1,0:T(8,128)(2,1)}, u32[]{:S(2)}, u32[]{:S(2)}) %collective-permute-start.13) | collective-permute-done | bytes 819232 | tf_op jit(solution)/shard_map/ppermute | solution.py:45
  73.3 0.0 collective-permute-done.10.refs_2_
  73.3 0.0 collective-permute-done.12.refs_6_
  73.3 0.0 collective-permute-done.11.refs_3_
  73.3 0.0 copy-done.4
  73.3 0.0 copy-done.5
  73.3 11.4 %convolve.1 = bf16[16,40,640]{2,1,0:T(8,128)(2,1)S(1)} custom-call(s32[1]{0:T(128)S(6)} %copy.10.sizes, f32[160,1]{1,0:T(8,128)S(1)} %copy.7.rates, bf16[4,160,640]{2,1,0:T(8,128)(2,1)S(1)} %pad_maximum_fusion.refs_0_, bf16[4,160,640]{2,1,0:T(8,128)(2,1)} %copy-done.5, bf16[4,160,640]{2,1,0:T(8,128)(2,1)} %collective-permute-done.10.refs_2_, ...), custom_call_target="tpu_custom_call" | custom-call | flops 4456448000 | bytes 6553600 | tf_op jit(solution)/shard_map/convolve/pallas_call | solution.py:206
  84.7 17.8 %all_to_all.5.packets = bf16[16,40,640]{2,1,0:T(8,128)(2,1)} all-to-all(bf16[16,40,640]{2,1,0:T(8,128)(2,1)S(1)} %convolve.1), channel_id=1, replica_groups=mesh['tx'=4,'ty'=4,'sector'=8] {'tx','ty'}, dimensions={0} | all-to-all | bytes 1638400 | tf_op jit(solution)/shard_map/all_to_all | solution.py:286
  102.5 3.5 %assemble.1 = bf16[640,640]{1,0:T(8,128)(2,1)} custom-call(bf16[16,40,640]{2,1,0:T(8,128)(2,1)} %all_to_all.5.packets), custom_call_target="tpu_custom_call" | custom-call | tf_op jit(solution)/shard_map/assemble/pallas_call | solution.py:238
  (5 shorter events, 0.0 us)
Async XLA Ops:
  0.0 58.0 %copy-start = (f32[1,640]{1,0:T(1,128)S(1)}, f32[1,640]{1,0:T(1,128)}, u32[]{:S(2)}) copy-start(f32[1,640]{1,0:T(1,128)} %param.8) | copy-start | bytes 7684
  5.3 12.1 %collective-permute-start = (bf16[640,640]{1,0:T(8,128)(2,1)}, bf16[640,640]{1,0:T(8,128)(2,1)S(1)}, u32[]{:S(2)}, u32[]{:S(2)}) collective-permute-start(bf16[640,640]{1,0:T(8,128)(2,1)} %get-tuple-element.19), channel_id=1, source_target_pairs={{1,0},{2,1},{3,2},{4,3},{5,4},{6,5},{7,6},{9,8},{10,9},{11,10},{12... | collective-permute-start | bytes 2457608 | tf_op jit(solution)/shard_map/ppermute | solution.py:22
  7.2 13.9 %collective-permute-start.1 = (bf16[640,640]{1,0:T(8,128)(2,1)}, bf16[640,640]{1,0:T(8,128)(2,1)S(1)}, u32[]{:S(2)}, u32[]{:S(2)}) collective-permute-start(bf16[640,640]{1,0:T(8,128)(2,1)} %get-tuple-element.20), channel_id=1, source_target_pairs={{0,1},{1,2},{2,3},{3,4},{4,5},{5,6},{6,7},{8,9},{9,10},{10,11},{11... | collective-permute-start | bytes 2457608 | tf_op jit(solution)/shard_map/ppermute | solution.py:22
  9.6 21.1 %collective-permute-start.6 = (bf16[160,640]{1,0:T(8,128)(2,1)}, bf16[160,640]{1,0:T(8,128)(2,1)S(1)}, u32[]{:S(2)}, u32[]{:S(2)}) collective-permute-start(bf16[160,640]{1,0:T(8,128)(2,1)} %get-tuple-element.26), channel_id=1, source_target_pairs={{0,8},{8,16},{16,24},{24,0},{1,9},{9,17},{17,25},{25,1},{2,10},{10... | collective-permute-start | bytes 614408 | tf_op jit(solution)/shard_map/ppermute | solution.py:27
  11.2 20.9 %collective-permute-start.7 = (bf16[160,640]{1,0:T(8,128)(2,1)}, bf16[160,640]{1,0:T(8,128)(2,1)S(1)}, u32[]{:S(2)}, u32[]{:S(2)}) collective-permute-start(bf16[160,640]{1,0:T(8,128)(2,1)} %get-tuple-element.27), channel_id=1, source_target_pairs={{0,16},{8,24},{16,0},{24,8},{1,17},{9,25},{17,1},{25,9},{2,18},{10... | collective-permute-start | bytes 614408 | tf_op jit(solution)/shard_map/ppermute | solution.py:27
  14.1 18.0 %collective-permute-start.8 = (bf16[160,640]{1,0:T(8,128)(2,1)}, bf16[160,640]{1,0:T(8,128)(2,1)S(1)}, u32[]{:S(2)}, u32[]{:S(2)}) collective-permute-start(bf16[160,640]{1,0:T(8,128)(2,1)} %get-tuple-element.28), channel_id=1, source_target_pairs={{0,24},{8,0},{16,8},{24,16},{1,25},{9,1},{17,9},{25,17},{2,26},{10... | collective-permute-start | bytes 614408 | tf_op jit(solution)/shard_map/ppermute | solution.py:27
  17.3 3.7 %copy-start.6 = (bf16[640,640]{1,0:T(8,128)(2,1)}, bf16[640,640]{1,0:T(8,128)(2,1)S(1)}, u32[]{:S(2)}) copy-start(bf16[640,640]{1,0:T(8,128)(2,1)S(1)} %collective-permute-done.refs_1_) | copy-start | bytes 2457604
  21.0 0.9 copy-start.7
  22.0 10.2 %copy-start.2 = (bf16[160,640]{1,0:T(8,128)(2,1)S(1)}, bf16[160,640]{1,0:T(8,128)(2,1)}, u32[]{:S(2)}) copy-start(bf16[160,640]{1,0:T(8,128)(2,1)} %get-tuple-element.25) | copy-start | bytes 614404
  26.4 8.5 %collective-permute-start.2 = (bf16[160,640]{1,0:T(8,128)(2,1)}, bf16[160,640]{1,0:T(8,128)(2,1)S(1)}, u32[]{:S(2)}, u32[]{:S(2)}) collective-permute-start(bf16[160,640]{1,0:T(8,128)(2,1)} %get-tuple-element.22), channel_id=1, source_target_pairs={{0,32},{32,64},{64,96},{96,0},{1,33},{33,65},{65,97},{97,1},{2,34}... | collective-permute-start | bytes 614408 | tf_op jit(solution)/shard_map/ppermute | solution.py:27
  28.0 12.0 %collective-permute-start.3 = (bf16[160,640]{1,0:T(8,128)(2,1)}, bf16[160,640]{1,0:T(8,128)(2,1)S(1)}, u32[]{:S(2)}, u32[]{:S(2)}) collective-permute-start(bf16[160,640]{1,0:T(8,128)(2,1)} %get-tuple-element.23), channel_id=1, source_target_pairs={{0,64},{32,96},{64,0},{96,32},{1,65},{33,97},{65,1},{97,33},{2,66}... | collective-permute-start | bytes 614408 | tf_op jit(solution)/shard_map/ppermute | solution.py:27
  30.7 10.5 %collective-permute-start.4 = (bf16[160,640]{1,0:T(8,128)(2,1)}, bf16[160,640]{1,0:T(8,128)(2,1)S(1)}, u32[]{:S(2)}, u32[]{:S(2)}) collective-permute-start(bf16[160,640]{1,0:T(8,128)(2,1)} %get-tuple-element.24), channel_id=1, source_target_pairs={{0,96},{32,0},{64,32},{96,64},{1,97},{33,1},{65,33},{97,65},{2,98}... | collective-permute-start | bytes 614408 | tf_op jit(solution)/shard_map/ppermute | solution.py:27
  32.2 9.0 %copy-start.3 = (bf16[160,640]{1,0:T(8,128)(2,1)S(1)}, bf16[160,640]{1,0:T(8,128)(2,1)}, u32[]{:S(2)}) copy-start(bf16[160,640]{1,0:T(8,128)(2,1)} %get-tuple-element.21) | copy-start | bytes 614404
  32.3 19.4 %copy-start.1 = (bf16[4,160,640]{2,1,0:T(8,128)(2,1)}, bf16[4,160,640]{2,1,0:T(8,128)(2,1)S(1)}, u32[]{:S(2)}) copy-start(bf16[4,160,640]{2,1,0:T(8,128)(2,1)S(1)} %pad_maximum_fusion.1.refs_4_) | copy-start | bytes 2457604
  32.3 16.4 %collective-permute-start.9 = (bf16[4,160,640]{2,1,0:T(8,128)(2,1)S(1)}, bf16[4,160,640]{2,1,0:T(8,128)(2,1)S(1)}, u32[]{:S(2)}, u32[]{:S(2)}) collective-permute-start(bf16[4,160,640]{2,1,0:T(8,128)(2,1)S(1)} %pad_maximum_fusion.1.refs_4_), channel_id=1, source_target_pairs={{0,32},{1,97},{2,34},{3,99},{4,36},{5,101},{6,38},{7,103},{32,64},... | collective-permute-start | bytes 2457608 | tf_op jit(solution)/shard_map/ppermute | solution.py:45
  41.3 16.2 %collective-permute-start.5 = (bf16[4,160,640]{2,1,0:T(8,128)(2,1)S(1)}, bf16[4,160,640]{2,1,0:T(8,128)(2,1)S(1)}, u32[]{:S(2)}, u32[]{:S(2)}) collective-permute-start(bf16[4,160,640]{2,1,0:T(8,128)(2,1)S(1)} %pad_maximum_fusion.refs_0_), channel_id=1, source_target_pairs={{0,8},{1,25},{2,10},{3,27},{4,12},{5,29},{6,14},{7,31},{8,16},{9,1... | collective-permute-start | bytes 2457608 | tf_op jit(solution)/shard_map/ppermute | solution.py:45
  48.7 24.6 %copy-start.4 = (bf16[4,160,640]{2,1,0:T(8,128)(2,1)}, bf16[4,160,640]{2,1,0:T(8,128)(2,1)S(1)}, u32[]{:S(2)}) copy-start(bf16[4,160,640]{2,1,0:T(8,128)(2,1)S(1)} %collective-permute-done.9.refs_5_) | copy-start | bytes 2457604
  48.7 24.6 %collective-permute-start.10 = (bf16[4,160,640]{2,1,0:T(8,128)(2,1)S(1)}, bf16[4,160,640]{2,1,0:T(8,128)(2,1)}, u32[]{:S(2)}, u32[]{:S(2)}) collective-permute-start(bf16[4,160,640]{2,1,0:T(8,128)(2,1)S(1)} %pad_maximum_fusion.refs_0_), channel_id=1, source_target_pairs={{0,24},{1,9},{2,26},{3,11},{4,28},{5,13},{6,30},{7,15},{8,0},{9,17... | collective-permute-start | bytes 2457608 | tf_op jit(solution)/shard_map/ppermute | solution.py:45
  51.7 21.6 %collective-permute-start.13 = (bf16[4,160,640]{2,1,0:T(8,128)(2,1)S(1)}, bf16[4,160,640]{2,1,0:T(8,128)(2,1)}, u32[]{:S(2)}, u32[]{:S(2)}) collective-permute-start(bf16[4,160,640]{2,1,0:T(8,128)(2,1)S(1)} %collective-permute-done.9.refs_5_), channel_id=1, source_target_pairs={{0,32},{1,97},{2,34},{3,99},{4,36},{5,101},{6,38},{7,103},{32,64},... | collective-permute-start | bytes 2457608 | tf_op jit(solution)/shard_map/ppermute | solution.py:45
  51.7 21.6 %collective-permute-start.12 = (bf16[4,160,640]{2,1,0:T(8,128)(2,1)S(1)}, bf16[4,160,640]{2,1,0:T(8,128)(2,1)}, u32[]{:S(2)}, u32[]{:S(2)}) collective-permute-start(bf16[4,160,640]{2,1,0:T(8,128)(2,1)S(1)} %pad_maximum_fusion.1.refs_4_), channel_id=1, source_target_pairs={{0,96},{1,33},{2,98},{3,35},{4,100},{5,37},{6,102},{7,39},{32,0},{... | collective-permute-start | bytes 2457608 | tf_op jit(solution)/shard_map/ppermute | solution.py:45
  57.5 15.8 %copy-start.5 = (bf16[4,160,640]{2,1,0:T(8,128)(2,1)}, bf16[4,160,640]{2,1,0:T(8,128)(2,1)S(1)}, u32[]{:S(2)}) copy-start(bf16[4,160,640]{2,1,0:T(8,128)(2,1)S(1)} %collective-permute-done.5.refs_1_) | copy-start | bytes 2457604
  57.5 15.8 %collective-permute-start.11 = (bf16[4,160,640]{2,1,0:T(8,128)(2,1)S(1)}, bf16[4,160,640]{2,1,0:T(8,128)(2,1)}, u32[]{:S(2)}, u32[]{:S(2)}) collective-permute-start(bf16[4,160,640]{2,1,0:T(8,128)(2,1)S(1)} %collective-permute-done.5.refs_1_), channel_id=1, source_target_pairs={{0,8},{1,25},{2,10},{3,27},{4,12},{5,29},{6,14},{7,31},{8,16},{9,1... | collective-permute-start | bytes 2457608 | tf_op jit(solution)/shard_map/ppermute | solution.py:45

commit v9 on v8

--- a/solution.py
+++ b/solution.py
@@ -148,15 +148,16 @@
     sign = turn_sign()
     copies_e, copies_g = [], []
     for part, (kind, step) in zip(parts, plan):
-        for d in range(n):
+        skipped = 1 if part.shape[0] == n - 1 else 0
+        for d in range(skipped, skipped + part.shape[0]):
             if kind == "e":
                 lag = n * around(here_x, -d, n) + around(here_y, sign * step, n)
                 left = pl.multiple_of((n * n - 1 - lag) * states, 128)
-                copies_e.append((part.at[d], e_all.at[:, pl.ds(left, states)]))
+                copies_e.append((part.at[d - skipped], e_all.at[:, pl.ds(left, states)]))
             else:
                 u = n * around(here_x, sign * step, n) + around(here_y, -d, n)
                 left = pl.multiple_of(lax.rem(u, 2) * states, 128)
-                copies_g.append((part.at[d], g_all.at[u // 2, :, pl.ds(left, states)]))
+                copies_g.append((part.at[d - skipped], g_all.at[u // 2, :, pl.ds(left, states)]))
     moves = [
         pltpu.make_async_copy(src, dst, sems.at[i])
         for i, (src, dst) in enumerate(copies_e + copies_g)
@@ -202,7 +203,7 @@
 def convolve(entries, sizes, rates, n, step_size):
     plan, parts = [e[:2] for e in entries], [e[2] for e in entries]
     _, rows, states = parts[0].shape
-    copies = n * len(parts)
+    copies = sum(part.shape[0] for part in parts)
     return pl.pallas_call(
         functools.partial(convolve_kernel, plan, n, step_size),
         out_shape=jax.ShapeDtypeStruct((n * n, rows // n, states), jnp.bfloat16),
@@ -227,20 +228,20 @@
 def assemble_kernel(n, packets, out):
     quarter, states = packets.shape[1:]
     rows = states // n
-    for b in range(n):
-        out[b * quarter : (b + 1) * quarter, :] = jnp.concatenate(
-            [packets[y, :, b * rows : (b + 1) * rows] for y in range(n)], axis=1
-        )
+    for x in range(n):
+        for b in range(n):
+            out[x * rows + b * quarter : x * rows + (b + 1) * quarter, :] = jnp.concatenate(
+                [packets[x * n + y, :, b * rows : (b + 1) * rows] for y in range(n)], axis=1
+            )
 
 
 def assemble(packets, n):
-    quarter, states = packets.shape[1:]
+    states = packets.shape[2]
     return pl.pallas_call(
         functools.partial(assemble_kernel, n),
         out_shape=jax.ShapeDtypeStruct((states, states), jnp.bfloat16),
-        grid=(n,),
-        in_specs=[pl.BlockSpec((n, quarter, states), lambda x: (x, 0, 0))],
-        out_specs=pl.BlockSpec((states // n, states), lambda x: (x, 0)),
+        in_specs=[VMEM],
+        out_specs=VMEM,
         name="assemble",
     )(packets)
 
@@ -265,17 +266,23 @@
         sector_sizes, hyb_particle, hyb_hole, above, below, operator, flipped, n
     )
     crossed_e = {d: ring(away_e[d - 1], "tx", d) for d in (2, 1, 3)}
-    lines = jnp.stack([own_e] + [crossed_e[d] for d in range(1, n)])
-
+    crossed_e = [crossed_e[d] for d in range(1, n)]
+    own_before, own_after = turned_ring(own_e, "ty", 1), turned_ring(own_e, "ty", -1)
+    columns, crossed_e, own_before, own_after = lax.optimization_barrier(
+        (columns, crossed_e, own_before, own_after)
+    )
     before_g = turned_ring(columns, "tx", 1)
+    lines = jnp.stack(crossed_e)
     before_e = turned_ring(lines, "ty", 1)
-    after_g = turned_ring(tied(columns, lines), "tx", -1)
-    after_e = turned_ring(tied(lines, before_g), "ty", -1)
+    after_g = turned_ring(columns, "tx", -1)
+    after_e = turned_ring(lines, "ty", -1)
+    own_far = turned_ring(own_before, "ty", 1)
     far_g = turned_ring(before_g, "tx", 1)
     far_e = turned_ring(before_e, "ty", 1)
     entries = [
         (kind, step, part)
         for kind, parts in (
+            ("e", (own_e[None], own_before[None], own_after[None], own_far[None])),
             ("e", (lines, before_e, after_e, far_e)),
             ("g", (columns, before_g, after_g, far_g)),
         )

time: 107 us -> 111 us (1.037)
  waiting for transfers between devices: 35.9 us -> 42.1 us
    ppermute x6 -> x9, waiting for transfers between devices: 23.4 us -> 33.3 us  [turned_ring(): return lax.ppermute(block, (axis, 'sector'), route)]
    ppermute x6, waiting for transfers between devices: 8.22 us -> 4.59 us  [ring(): lax.ppermute(block, axis, [(i, (i + distance) % n) for i in range(n)])]
    pallas_call x1, Pallas kernels: 3.53 us -> 2.41 us  [assemble(): pl.pallas_call(functools.partial(assemble_kernel, n), out_shape=jax.Shape...]
    ppermute x6 -> x9, starting transfers between devices: 8.98 us -> 8.59 us  [turned_ring(): return lax.ppermute(block, (axis, 'sector'), route)]
  transfers between devices with their start and end apart: 14 -> 17, of which waited for: 8 -> 6; matrix products, arithmetic and copies ran while one was open for 0% -> 0% of each run, Pallas kernels for 4% -> 4%
where the time goes in v9:
time: 111 us
  waiting for transfers between devices  42.1 us (38%)
  starting transfers between devices  24.5 us (22%)
  Pallas kernels  23.6 us (21%)
  blocking collectives  16.9 us (15%)
  between operations  2.1 us (2%)
  local copies, waits for them, and re-layouts  1.15 us (1%)
    ppermute x9, waiting for transfers between devices, turned_ring(): return lax.ppermute(block, (axis, 'sector'), route)  33.3 us
    all_to_all x1, blocking collectives, per_device(): packets = lax.all_to_all(packets, ('tx', 'ty'), 0, 0, tiled=True)  16.9 us
    pallas_call x1, Pallas kernels, convolve(): pl.pallas_call(functools.partial(convolve_kernel, plan, n, step_size), ou...  12.2 us
    ppermute x6, starting transfers between devices, ring(): lax.ppermute(block, axis, [(i, (i + distance) % n) for i in range(n)])  11.6 us
    ppermute x9, starting transfers between devices, turned_ring(): return lax.ppermute(block, (axis, 'sector'), route)  8.59 us
    ppermute x6, waiting for transfers between devices, ring(): lax.ppermute(block, axis, [(i, (i + distance) % n) for i in range(n)])  4.59 us
    pallas_call x1, Pallas kernels, prepare(): pl.pallas_call(prepare_kernel, out_shape=(square,) * 3 + (block,) * n, in...  4.58 us
    pallas_call x1, Pallas kernels, energy_blocks(): pl.pallas_call(energy_kernel, out_shape=(block,) * n, in_specs=[SMEM] * 3...  4.47 us
  transfers between devices with their start and end apart: 17, of which 6 were waited for; matrix products, arithmetic and copies ran while one was open for 0% of the time, Pallas kernels for 4%

profile of v9, /device:TPU:32, one launch (start us, length us, event | category | flops | bytes accessed | tf_op | source)
XLA Modules:
  0.0 110.7 jit_solution(15685855139254703360)
XLA Ops:
  0.0 0.0 copy-start
  0.7 4.6 %prepare.1 = (bf16[640,640]{1,0:T(8,128)(2,1)}, bf16[640,640]{1,0:T(8,128)(2,1)}, bf16[640,640]{1,0:T(8,128)(2,1)}, bf16[160,640]{1,0:T(8,128)(2,1)}, bf16[160,6...) custom-call(s32[1]{0:T(128)S(6)} %copy.10.sizes, bf16[640,640]{1,0:T(8,128)(2,1)} %bitcast.27, ...), custom_call_target="tpu_custom_call" | custom-call | flops 1048576000 | bytes 4915200 | tf_op jit(solution)/shard_map/prepare/pallas_call | solution.py:82
  5.2 1.9 %collective-permute-start = (bf16[640,640]{1,0:T(8,128)(2,1)}, bf16[640,640]{1,0:T(8,128)(2,1)S(1)}, u32[]{:S(2)}, u32[]{:S(2)}) collective-permute-start(bf16[640,640]{1,0:T(8,128)(2,1)} %get-tuple-element.23), channel_id=1, source_target_pairs={{1,0},{2,1},{3,2},{4,3},{5,4},{6,5},{7,6},{9,8},{10,9},{11,10},{12... | collective-permute-start | bytes 2457608 | tf_op jit(solution)/shard_map/ppermute | solution.py:22
  7.2 2.4 %collective-permute-start.1 = (bf16[640,640]{1,0:T(8,128)(2,1)}, bf16[640,640]{1,0:T(8,128)(2,1)S(1)}, u32[]{:S(2)}, u32[]{:S(2)}) collective-permute-start(bf16[640,640]{1,0:T(8,128)(2,1)} %get-tuple-element.24), channel_id=1, source_target_pairs={{0,1},{1,2},{2,3},{3,4},{4,5},{5,6},{6,7},{8,9},{9,10},{10,11},{11... | collective-permute-start | bytes 2457608 | tf_op jit(solution)/shard_map/ppermute | solution.py:22
  9.6 1.6 %collective-permute-start.2 = (bf16[160,640]{1,0:T(8,128)(2,1)}, bf16[160,640]{1,0:T(8,128)(2,1)S(1)}, u32[]{:S(2)}, u32[]{:S(2)}) collective-permute-start(bf16[160,640]{1,0:T(8,128)(2,1)} %get-tuple-element.27), channel_id=1, source_target_pairs={{0,8},{8,16},{16,24},{24,0},{1,9},{9,17},{17,25},{25,1},{2,10},{10... | collective-permute-start | bytes 614408 | tf_op jit(solution)/shard_map/ppermute | solution.py:27
  11.2 2.9 %collective-permute-start.3 = (bf16[160,640]{1,0:T(8,128)(2,1)}, bf16[160,640]{1,0:T(8,128)(2,1)S(1)}, u32[]{:S(2)}, u32[]{:S(2)}) collective-permute-start(bf16[160,640]{1,0:T(8,128)(2,1)} %get-tuple-element.28), channel_id=1, source_target_pairs={{0,16},{8,24},{16,0},{24,8},{1,17},{9,25},{17,1},{25,9},{2,18},{10... | collective-permute-start | bytes 614408 | tf_op jit(solution)/shard_map/ppermute | solution.py:27
  14.1 1.3 %collective-permute-start.4 = (bf16[160,640]{1,0:T(8,128)(2,1)}, bf16[160,640]{1,0:T(8,128)(2,1)S(1)}, u32[]{:S(2)}, u32[]{:S(2)}) collective-permute-start(bf16[160,640]{1,0:T(8,128)(2,1)} %get-tuple-element.29), channel_id=1, source_target_pairs={{0,24},{8,0},{16,8},{24,16},{1,25},{9,1},{17,9},{25,17},{2,26},{10... | collective-permute-start | bytes 614408 | tf_op jit(solution)/shard_map/ppermute | solution.py:27
  16.8 0.5 collective-permute-done.refs_1_
  17.3 3.7 %collective-permute-done.1.refs_3_ = bf16[640,640]{1,0:T(8,128)(2,1)S(1)} collective-permute-done((bf16[640,640]{1,0:T(8,128)(2,1)}, bf16[640,640]{1,0:T(8,128)(2,1)S(1)}, u32[]{:S(2)}, u32[]{:S(2)}) %collective-permute-start.1) | collective-permute-done | bytes 819232 | tf_op jit(solution)/shard_map/ppermute | solution.py:22
  21.0 0.0 copy-done.5
  21.0 0.9 copy-done.6
  22.0 4.5 %energy_blocks.1 = (bf16[160,640]{1,0:T(8,128)(2,1)}, bf16[160,640]{1,0:T(8,128)(2,1)}, bf16[160,640]{1,0:T(8,128)(2,1)}, bf16[160,640]{1,0:T(8,128)(2,1)}) custom-call(s32[1]{0:T(128)S(6)} %copy.10.sizes, f32[1]{0:T(128)S(6)} %copy.8.particle, f32[1]{0:T(128)S(6)} %copy.9.hole, bf16[640,640]{1,0:T(8,128)(2,1)} %get-tuple-element.22.refs_0_, ...), custom_call_target="tpu_custom_call" | custom-call | flops 1048576000 | bytes 4096000 | tf_op jit(solution)/shard_map/energy_blocks/pallas_call | solution.py:124
  26.5 1.5 %collective-permute-start.5 = (bf16[160,640]{1,0:T(8,128)(2,1)}, bf16[160,640]{1,0:T(8,128)(2,1)S(1)}, u32[]{:S(2)}, u32[]{:S(2)}) collective-permute-start(bf16[160,640]{1,0:T(8,128)(2,1)} %get-tuple-element.30), channel_id=1, source_target_pairs={{0,32},{32,64},{64,96},{96,0},{1,33},{33,65},{65,97},{97,1},{2,34}... | collective-permute-start | bytes 614408 | tf_op jit(solution)/shard_map/ppermute | solution.py:27
  28.0 2.7 %collective-permute-start.6 = (bf16[160,640]{1,0:T(8,128)(2,1)}, bf16[160,640]{1,0:T(8,128)(2,1)S(1)}, u32[]{:S(2)}, u32[]{:S(2)}) collective-permute-start(bf16[160,640]{1,0:T(8,128)(2,1)} %get-tuple-element.31), channel_id=1, source_target_pairs={{0,64},{32,96},{64,0},{96,32},{1,65},{33,97},{65,1},{97,33},{2,66}... | collective-permute-start | bytes 614408 | tf_op jit(solution)/shard_map/ppermute | solution.py:27
  30.7 0.0 collective-permute-done.2
  30.7 1.4 %collective-permute-start.7 = (bf16[160,640]{1,0:T(8,128)(2,1)}, bf16[160,640]{1,0:T(8,128)(2,1)S(1)}, u32[]{:S(2)}, u32[]{:S(2)}) collective-permute-start(bf16[160,640]{1,0:T(8,128)(2,1)} %get-tuple-element.32), channel_id=1, source_target_pairs={{0,96},{32,0},{64,32},{96,64},{1,97},{33,1},{65,33},{97,65},{2,98}... | collective-permute-start | bytes 614408 | tf_op jit(solution)/shard_map/ppermute | solution.py:27
  32.2 0.0 collective-permute-done.3
  32.2 3.0 %collective-permute-start.9 = (bf16[160,640]{1,0:T(8,128)(2,1)}, bf16[160,640]{1,0:T(8,128)(2,1)S(1)}, u32[]{:S(2)}, u32[]{:S(2)}) collective-permute-start(bf16[160,640]{1,0:T(8,128)(2,1)} %get-tuple-element.25), channel_id=1, source_target_pairs={{0,24},{1,9},{2,26},{3,11},{4,28},{5,13},{6,30},{7,15},{8,0},{9,17... | collective-permute-start | bytes 614408 | tf_op jit(solution)/shard_map/ppermute | solution.py:45
  35.2 0.0 collective-permute-done.4
  35.2 0.0 collective-permute-start.8
  35.2 0.0 copy-done.3
  35.2 0.1 pad_maximum_fusion.refs_8_
  35.3 0.0 copy-start.2
  35.4 0.0 collective-permute-done.5
  35.4 4.6 %collective-permute-done.6 = bf16[160,640]{1,0:T(8,128)(2,1)S(1)} collective-permute-done((bf16[160,640]{1,0:T(8,128)(2,1)}, bf16[160,640]{1,0:T(8,128)(2,1)S(1)}, u32[]{:S(2)}, u32[]{:S(2)}) %collective-permute-start.6) | collective-permute-done | bytes 204832 | tf_op jit(solution)/shard_map/ppermute | solution.py:27
  39.9 0.0 collective-permute-done.7
  39.9 0.0 collective-permute-done.9
  40.0 2.4 %collective-permute-done.8 = bf16[160,640]{1,0:T(8,128)(2,1)S(1)} collective-permute-done((bf16[160,640]{1,0:T(8,128)(2,1)}, bf16[160,640]{1,0:T(8,128)(2,1)S(1)}, u32[]{:S(2)}, u32[]{:S(2)}) %collective-permute-start.8) | collective-permute-done | bytes 204832 | tf_op jit(solution)/shard_map/ppermute | solution.py:45
  42.4 0.6 collective-permute-start.14
  43.0 0.1 pad_maximum_fusion.1.refs_4_
  43.1 0.1 collective-permute-start.11
  43.1 2.7 %collective-permute-start.15 = (bf16[4,160,640]{2,1,0:T(8,128)(2,1)S(1)}, bf16[4,160,640]{2,1,0:T(8,128)(2,1)}, u32[]{:S(2)}, u32[]{:S(2)}) collective-permute-start(bf16[4,160,640]{2,1,0:T(8,128)(2,1)S(1)} %pad_maximum_fusion.refs_8_), channel_id=1, source_target_pairs={{0,96},{1,33},{2,98},{3,35},{4,100},{5,37},{6,102},{7,39},{32,0},{... | collective-permute-start | bytes 2457608 | tf_op jit(solution)/shard_map/ppermute | solution.py:45
  45.9 17.8 %collective-permute-done.14.refs_9_ = bf16[4,160,640]{2,1,0:T(8,128)(2,1)S(1)} collective-permute-done((bf16[4,160,640]{2,1,0:T(8,128)(2,1)S(1)}, bf16[4,160,640]{2,1,0:T(8,128)(2,1)S(1)}, u32[]{:S(2)}, u32[]{:S(2)}) %collective-permute-start.14) | collective-permute-done | bytes 819232 | tf_op jit(solution)/shard_map/ppermute | solution.py:45
  63.7 0.0 collective-permute-start.16
  63.7 1.6 %collective-permute-start.12 = (bf16[3,160,640]{2,1,0:T(8,128)(2,1)S(1)}, bf16[3,160,640]{2,1,0:T(8,128)(2,1)}, u32[]{:S(2)}, u32[]{:S(2)}) collective-permute-start(bf16[3,160,640]{2,1,0:T(8,128)(2,1)S(1)} %pad_maximum_fusion.1.refs_4_), channel_id=1, source_target_pairs={{0,24},{1,9},{2,26},{3,11},{4,28},{5,13},{6,30},{7,15},{8,0},{9,17... | collective-permute-start | bytes 1843208 | tf_op jit(solution)/shard_map/ppermute | solution.py:45
  65.3 0.0 collective-permute-done.11.refs_5_
  65.3 0.4 collective-permute-start.13
  65.7 0.2 collective-permute-start.10
  65.9 0.1 dynamic-slice_bitcast_fusion
  65.9 0.1 copy.7.rates
  66.1 13.0 %collective-permute-done.10 = bf16[160,640]{1,0:T(8,128)(2,1)S(1)} collective-permute-done((bf16[160,640]{1,0:T(8,128)(2,1)S(1)}, bf16[160,640]{1,0:T(8,128)(2,1)S(1)}, u32[]{:S(2)}, u32[]{:S(2)}) %collective-permute-start.10) | collective-permute-done | bytes 204832 | tf_op jit(solution)/shard_map/ppermute | solution.py:45
  79.1 0.0 collective-permute-done.12.refs_6_
  79.1 0.0 collective-permute-done.15.refs_10_
  79.1 0.0 collective-permute-done.13.refs_7_
  79.1 0.0 collective-permute-done.16.refs_11_
  79.1 12.2 %convolve.1 = bf16[16,40,640]{2,1,0:T(8,128)(2,1)} custom-call(s32[1]{0:T(128)S(6)} %copy.10.sizes, f32[160,1]{1,0:T(8,128)S(1)} %copy.7.rates, bf16[1,160,640]{2,1,0:T(8,128)(2,1)S(1)} %bitcast.16, bf16[1,160,640]{2,1,0:T(8,128)(2,1)S(1)} %bitcast.18, bf16[1,160,640]{2,1,0:T(8,128)(2,1)S(1)} %bitcast.17, bf16[1,160,640]{2,1,0:T(8,128)(2,1)S(1)} %bitcast.19, ...), custom_call_target="tpu_custom_call" | custom-call | flops 4456448000 | bytes 6553600 | tf_op jit(solution)/shard_map/convolve/pallas_call | solution.py:207
  91.3 16.9 %all_to_all.5.packets = bf16[16,40,640]{2,1,0:T(8,128)(2,1)} all-to-all(bf16[16,40,640]{2,1,0:T(8,128)(2,1)} %convolve.1), channel_id=1, replica_groups=mesh['tx'=4,'ty'=4,'sector'=8] {'tx','ty'}, dimensions={0} | all-to-all | bytes 1638400 | tf_op jit(solution)/shard_map/all_to_all | solution.py:293
  108.2 2.4 %assemble.1 = bf16[640,640]{1,0:T(8,128)(2,1)} custom-call(bf16[16,40,640]{2,1,0:T(8,128)(2,1)} %all_to_all.5.packets), custom_call_target="tpu_custom_call" | custom-call | tf_op jit(solution)/shard_map/assemble/pallas_call | solution.py:240
  (9 shorter events, 0.0 us)
Async XLA Ops:
  0.0 65.9 %copy-start = (f32[1,640]{1,0:T(1,128)S(1)}, f32[1,640]{1,0:T(1,128)}, u32[]{:S(2)}) copy-start(f32[1,640]{1,0:T(1,128)} %param.8) | copy-start | bytes 7684
  5.2 12.1 %collective-permute-start = (bf16[640,640]{1,0:T(8,128)(2,1)}, bf16[640,640]{1,0:T(8,128)(2,1)S(1)}, u32[]{:S(2)}, u32[]{:S(2)}) collective-permute-start(bf16[640,640]{1,0:T(8,128)(2,1)} %get-tuple-element.23), channel_id=1, source_target_pairs={{1,0},{2,1},{3,2},{4,3},{5,4},{6,5},{7,6},{9,8},{10,9},{11,10},{12... | collective-permute-start | bytes 2457608 | tf_op jit(solution)/shard_map/ppermute | solution.py:22
  7.2 13.9 %collective-permute-start.1 = (bf16[640,640]{1,0:T(8,128)(2,1)}, bf16[640,640]{1,0:T(8,128)(2,1)S(1)}, u32[]{:S(2)}, u32[]{:S(2)}) collective-permute-start(bf16[640,640]{1,0:T(8,128)(2,1)} %get-tuple-element.24), channel_id=1, source_target_pairs={{0,1},{1,2},{2,3},{3,4},{4,5},{5,6},{6,7},{8,9},{9,10},{10,11},{11... | collective-permute-start | bytes 2457608 | tf_op jit(solution)/shard_map/ppermute | solution.py:22
  9.6 21.2 %collective-permute-start.2 = (bf16[160,640]{1,0:T(8,128)(2,1)}, bf16[160,640]{1,0:T(8,128)(2,1)S(1)}, u32[]{:S(2)}, u32[]{:S(2)}) collective-permute-start(bf16[160,640]{1,0:T(8,128)(2,1)} %get-tuple-element.27), channel_id=1, source_target_pairs={{0,8},{8,16},{16,24},{24,0},{1,9},{9,17},{17,25},{25,1},{2,10},{10... | collective-permute-start | bytes 614408 | tf_op jit(solution)/shard_map/ppermute | solution.py:27
  11.2 21.0 %collective-permute-start.3 = (bf16[160,640]{1,0:T(8,128)(2,1)}, bf16[160,640]{1,0:T(8,128)(2,1)S(1)}, u32[]{:S(2)}, u32[]{:S(2)}) collective-permute-start(bf16[160,640]{1,0:T(8,128)(2,1)} %get-tuple-element.28), channel_id=1, source_target_pairs={{0,16},{8,24},{16,0},{24,8},{1,17},{9,25},{17,1},{25,9},{2,18},{10... | collective-permute-start | bytes 614408 | tf_op jit(solution)/shard_map/ppermute | solution.py:27
  14.1 21.1 %collective-permute-start.4 = (bf16[160,640]{1,0:T(8,128)(2,1)}, bf16[160,640]{1,0:T(8,128)(2,1)S(1)}, u32[]{:S(2)}, u32[]{:S(2)}) collective-permute-start(bf16[160,640]{1,0:T(8,128)(2,1)} %get-tuple-element.29), channel_id=1, source_target_pairs={{0,24},{8,0},{16,8},{24,16},{1,25},{9,1},{17,9},{25,17},{2,26},{10... | collective-permute-start | bytes 614408 | tf_op jit(solution)/shard_map/ppermute | solution.py:27
  17.3 3.7 %copy-start.5 = (bf16[640,640]{1,0:T(8,128)(2,1)}, bf16[640,640]{1,0:T(8,128)(2,1)S(1)}, u32[]{:S(2)}) copy-start(bf16[640,640]{1,0:T(8,128)(2,1)S(1)} %collective-permute-done.refs_1_) | copy-start | bytes 2457604
  21.0 0.9 copy-start.6
  22.0 13.2 %copy-start.3 = (bf16[160,640]{1,0:T(8,128)(2,1)S(1)}, bf16[160,640]{1,0:T(8,128)(2,1)}, u32[]{:S(2)}) copy-start(bf16[160,640]{1,0:T(8,128)(2,1)} %get-tuple-element.26) | copy-start | bytes 614404
  26.5 8.9 %collective-permute-start.5 = (bf16[160,640]{1,0:T(8,128)(2,1)}, bf16[160,640]{1,0:T(8,128)(2,1)S(1)}, u32[]{:S(2)}, u32[]{:S(2)}) collective-permute-start(bf16[160,640]{1,0:T(8,128)(2,1)} %get-tuple-element.30), channel_id=1, source_target_pairs={{0,32},{32,64},{64,96},{96,0},{1,33},{33,65},{65,97},{97,1},{2,34}... | collective-permute-start | bytes 614408 | tf_op jit(solution)/shard_map/ppermute | solution.py:27
  28.0 11.9 %collective-permute-start.6 = (bf16[160,640]{1,0:T(8,128)(2,1)}, bf16[160,640]{1,0:T(8,128)(2,1)S(1)}, u32[]{:S(2)}, u32[]{:S(2)}) collective-permute-start(bf16[160,640]{1,0:T(8,128)(2,1)} %get-tuple-element.31), channel_id=1, source_target_pairs={{0,64},{32,96},{64,0},{96,32},{1,65},{33,97},{65,1},{97,33},{2,66}... | collective-permute-start | bytes 614408 | tf_op jit(solution)/shard_map/ppermute | solution.py:27
  30.7 9.2 %collective-permute-start.7 = (bf16[160,640]{1,0:T(8,128)(2,1)}, bf16[160,640]{1,0:T(8,128)(2,1)S(1)}, u32[]{:S(2)}, u32[]{:S(2)}) collective-permute-start(bf16[160,640]{1,0:T(8,128)(2,1)} %get-tuple-element.32), channel_id=1, source_target_pairs={{0,96},{32,0},{64,32},{96,64},{1,97},{33,1},{65,33},{97,65},{2,98}... | collective-permute-start | bytes 614408 | tf_op jit(solution)/shard_map/ppermute | solution.py:27
  32.2 7.8 %collective-permute-start.9 = (bf16[160,640]{1,0:T(8,128)(2,1)}, bf16[160,640]{1,0:T(8,128)(2,1)S(1)}, u32[]{:S(2)}, u32[]{:S(2)}) collective-permute-start(bf16[160,640]{1,0:T(8,128)(2,1)} %get-tuple-element.25), channel_id=1, source_target_pairs={{0,24},{1,9},{2,26},{3,11},{4,28},{5,13},{6,30},{7,15},{8,0},{9,17... | collective-permute-start | bytes 614408 | tf_op jit(solution)/shard_map/ppermute | solution.py:45
  35.2 7.2 %collective-permute-start.8 = (bf16[160,640]{1,0:T(8,128)(2,1)}, bf16[160,640]{1,0:T(8,128)(2,1)S(1)}, u32[]{:S(2)}, u32[]{:S(2)}) collective-permute-start(bf16[160,640]{1,0:T(8,128)(2,1)} %get-tuple-element.25), channel_id=1, source_target_pairs={{0,8},{1,25},{2,10},{3,27},{4,12},{5,29},{6,14},{7,31},{8,16},{9,1... | collective-permute-start | bytes 614408 | tf_op jit(solution)/shard_map/ppermute | solution.py:45
  35.3 43.8 %copy-start.2 = (bf16[4,160,640]{2,1,0:T(8,128)(2,1)}, bf16[4,160,640]{2,1,0:T(8,128)(2,1)S(1)}, u32[]{:S(2)}) copy-start(bf16[4,160,640]{2,1,0:T(8,128)(2,1)S(1)} %pad_maximum_fusion.refs_8_) | copy-start | bytes 2457604
  42.4 21.3 %collective-permute-start.14 = (bf16[4,160,640]{2,1,0:T(8,128)(2,1)S(1)}, bf16[4,160,640]{2,1,0:T(8,128)(2,1)S(1)}, u32[]{:S(2)}, u32[]{:S(2)}) collective-permute-start(bf16[4,160,640]{2,1,0:T(8,128)(2,1)S(1)} %pad_maximum_fusion.refs_8_), channel_id=1, source_target_pairs={{0,32},{1,97},{2,34},{3,99},{4,36},{5,101},{6,38},{7,103},{32,64},... | collective-permute-start | bytes 2457608 | tf_op jit(solution)/shard_map/ppermute | solution.py:45
  43.0 36.2 %copy-start.1 = (bf16[160,640]{1,0:T(8,128)(2,1)S(1)}, bf16[160,640]{1,0:T(8,128)(2,1)}, u32[]{:S(2)}) copy-start(bf16[160,640]{1,0:T(8,128)(2,1)} %get-tuple-element.25) | copy-start | bytes 614404
  43.1 22.3 %collective-permute-start.11 = (bf16[3,160,640]{2,1,0:T(8,128)(2,1)S(1)}, bf16[3,160,640]{2,1,0:T(8,128)(2,1)}, u32[]{:S(2)}, u32[]{:S(2)}) collective-permute-start(bf16[3,160,640]{2,1,0:T(8,128)(2,1)S(1)} %pad_maximum_fusion.1.refs_4_), channel_id=1, source_target_pairs={{0,8},{1,25},{2,10},{3,27},{4,12},{5,29},{6,14},{7,31},{8,16},{9,1... | collective-permute-start | bytes 1843208 | tf_op jit(solution)/shard_map/ppermute | solution.py:45
  43.1 35.9 %collective-permute-start.15 = (bf16[4,160,640]{2,1,0:T(8,128)(2,1)S(1)}, bf16[4,160,640]{2,1,0:T(8,128)(2,1)}, u32[]{:S(2)}, u32[]{:S(2)}) collective-permute-start(bf16[4,160,640]{2,1,0:T(8,128)(2,1)S(1)} %pad_maximum_fusion.refs_8_), channel_id=1, source_target_pairs={{0,96},{1,33},{2,98},{3,35},{4,100},{5,37},{6,102},{7,39},{32,0},{... | collective-permute-start | bytes 2457608 | tf_op jit(solution)/shard_map/ppermute | solution.py:45
  63.7 15.4 %copy-start.4 = (bf16[4,160,640]{2,1,0:T(8,128)(2,1)}, bf16[4,160,640]{2,1,0:T(8,128)(2,1)S(1)}, u32[]{:S(2)}) copy-start(bf16[4,160,640]{2,1,0:T(8,128)(2,1)S(1)} %collective-permute-done.14.refs_9_) | copy-start | bytes 2457604
  63.7 15.4 %collective-permute-start.16 = (bf16[4,160,640]{2,1,0:T(8,128)(2,1)S(1)}, bf16[4,160,640]{2,1,0:T(8,128)(2,1)}, u32[]{:S(2)}, u32[]{:S(2)}) collective-permute-start(bf16[4,160,640]{2,1,0:T(8,128)(2,1)S(1)} %collective-permute-done.14.refs_9_), channel_id=1, source_target_pairs={{0,32},{1,97},{2,34},{3,99},{4,36},{5,101},{6,38},{7,103},{32,64},... | collective-permute-start | bytes 2457608 | tf_op jit(solution)/shard_map/ppermute | solution.py:45
  63.7 15.4 %collective-permute-start.12 = (bf16[3,160,640]{2,1,0:T(8,128)(2,1)S(1)}, bf16[3,160,640]{2,1,0:T(8,128)(2,1)}, u32[]{:S(2)}, u32[]{:S(2)}) collective-permute-start(bf16[3,160,640]{2,1,0:T(8,128)(2,1)S(1)} %pad_maximum_fusion.1.refs_4_), channel_id=1, source_target_pairs={{0,24},{1,9},{2,26},{3,11},{4,28},{5,13},{6,30},{7,15},{8,0},{9,17... | collective-permute-start | bytes 1843208 | tf_op jit(solution)/shard_map/ppermute | solution.py:45
  65.3 13.8 %collective-permute-start.13 = (bf16[3,160,640]{2,1,0:T(8,128)(2,1)}, bf16[3,160,640]{2,1,0:T(8,128)(2,1)}, u32[]{:S(2)}, u32[]{:S(2)}) collective-permute-start(bf16[3,160,640]{2,1,0:T(8,128)(2,1)} %collective-permute-done.11.refs_5_), channel_id=1, source_target_pairs={{0,8},{1,25},{2,10},{3,27},{4,12},{5,29},{6,14},{7,31},{8,16},{9,1... | collective-permute-start | bytes 1843208 | tf_op jit(solution)/shard_map/ppermute | solution.py:45
  65.7 13.4 %collective-permute-start.10 = (bf16[160,640]{1,0:T(8,128)(2,1)S(1)}, bf16[160,640]{1,0:T(8,128)(2,1)S(1)}, u32[]{:S(2)}, u32[]{:S(2)}) collective-permute-start(bf16[160,640]{1,0:T(8,128)(2,1)S(1)} %collective-permute-done.8), channel_id=1, source_target_pairs={{0,8},{1,25},{2,10},{3,27},{4,12},{5,29},{6,14},{7,31},{8,16},{9,1... | collective-permute-start | bytes 614408 | tf_op jit(solution)/shard_map/ppermute | solution.py:45

commit v10 on v8

--- a/solution.py
+++ b/solution.py
@@ -103,15 +103,17 @@
     n = len(outs)
     rows = outs[0].shape[0]
     here_x = lax.axis_index("tx")
-    for move in moves:
-        move.wait()
     flipped, above, operator, below = copies
-    inner = above[...]
-    r = operator[...]
+    moves[0].wait()
+    moves[1].wait()
     for d in (2, 1, 3, 0):
         first = pl.multiple_of(lax.rem(here_x + d, n) * rows, 32)
-        lowered = dot(flipped[pl.ds(first, rows), :], inner).astype(jnp.bfloat16)
-        downward = dot(lowered, r)
+        lowered = dot(flipped[pl.ds(first, rows), :], above[...]).astype(jnp.bfloat16)
+        if d == 2:
+            moves[2].wait()
+        downward = dot(lowered, operator[...])
+        if d == 2:
+            moves[3].wait()
         raised = below[pl.ds(first, rows), :].astype(jnp.float32)
         both = particle[0] * raised + hole[0] * downward
         kept = live(both.shape, sizes[0], first)
@@ -131,7 +133,6 @@
         cost_estimate=pl.CostEstimate(
             flops=4 * states**3, bytes_accessed=10 * states**2, transcendentals=0
         ),
-        compiler_params=pltpu.CompilerParams(vmem_limit_bytes=56 * MIB),
         name="energy_blocks",
     )(sizes, particle, hole, flipped, above, operator, below)
 
@@ -227,20 +228,20 @@
 def assemble_kernel(n, packets, out):
     quarter, states = packets.shape[1:]
     rows = states // n
-    for b in range(n):
-        out[b * quarter : (b + 1) * quarter, :] = jnp.concatenate(
-            [packets[y, :, b * rows : (b + 1) * rows] for y in range(n)], axis=1
-        )
+    for x in range(n):
+        for b in range(n):
+            out[x * rows + b * quarter : x * rows + (b + 1) * quarter, :] = jnp.concatenate(
+                [packets[x * n + y, :, b * rows : (b + 1) * rows] for y in range(n)], axis=1
+            )
 
 
 def assemble(packets, n):
-    quarter, states = packets.shape[1:]
+    states = packets.shape[2]
     return pl.pallas_call(
         functools.partial(assemble_kernel, n),
         out_shape=jax.ShapeDtypeStruct((states, states), jnp.bfloat16),
-        grid=(n,),
-        in_specs=[pl.BlockSpec((n, quarter, states), lambda x: (x, 0, 0))],
-        out_specs=pl.BlockSpec((states // n, states), lambda x: (x, 0)),
+        in_specs=[VMEM],
+        out_specs=VMEM,
         name="assemble",
     )(packets)
 
@@ -268,8 +269,8 @@
     lines = jnp.stack([own_e] + [crossed_e[d] for d in range(1, n)])
 
     before_g = turned_ring(columns, "tx", 1)
+    after_g = turned_ring(columns, "tx", -1)
     before_e = turned_ring(lines, "ty", 1)
-    after_g = turned_ring(tied(columns, lines), "tx", -1)
     after_e = turned_ring(tied(lines, before_g), "ty", -1)
     far_g = turned_ring(before_g, "tx", 1)
     far_e = turned_ring(before_e, "ty", 1)

time: 107 us -> 109 us (1.019)
  blocking collectives: 17.8 us -> 20.5 us
  Pallas kernels: 23.9 us -> 22.7 us
    all_to_all x1, blocking collectives: 17.8 us -> 20.5 us  [per_device(): packets = lax.all_to_all(packets, ('tx', 'ty'), 0, 0, tiled=True)]
    pallas_call x1, Pallas kernels: 3.53 us -> 2.41 us  [assemble(): pl.pallas_call(functools.partial(assemble_kernel, n), out_shape=jax.Shape...]
  transfers between devices with their start and end apart: 14 -> 14, of which waited for: 8 -> 9; matrix products, arithmetic and copies ran while one was open for 0% -> 0% of each run, Pallas kernels for 4% -> 4%
where the time goes in v10:
time: 109 us
  waiting for transfers between devices  36.7 us (34%)
  starting transfers between devices  25.3 us (23%)
  Pallas kernels  22.7 us (21%)
  blocking collectives  20.5 us (19%)
  between operations  2.08 us (2%)
  local copies, waits for them, and re-layouts  1.16 us (1%)
    ppermute x6, waiting for transfers between devices, turned_ring(): return lax.ppermute(block, (axis, 'sector'), route)  24.3 us
    all_to_all x1, blocking collectives, per_device(): packets = lax.all_to_all(packets, ('tx', 'ty'), 0, 0, tiled=True)  20.5 us
    ppermute x6, starting transfers between devices, ring(): lax.ppermute(block, axis, [(i, (i + distance) % n) for i in range(n)])  11.6 us
    pallas_call x1, Pallas kernels, convolve(): pl.pallas_call(functools.partial(convolve_kernel, plan, n, step_size), ou...  11.4 us
    ppermute x6, starting transfers between devices, turned_ring(): return lax.ppermute(block, (axis, 'sector'), route)  9.4 us
    ppermute x6, waiting for transfers between devices, ring(): lax.ppermute(block, axis, [(i, (i + distance) % n) for i in range(n)])  8.23 us
    pallas_call x1, Pallas kernels, prepare(): pl.pallas_call(prepare_kernel, out_shape=(square,) * 3 + (block,) * n, in...  4.59 us
    pallas_call x1, Pallas kernels, energy_blocks(): pl.pallas_call(energy_kernel, out_shape=(block,) * n, in_specs=[SMEM] * 3...  4.34 us
  transfers between devices with their start and end apart: 14, of which 9 were waited for; matrix products, arithmetic and copies ran while one was open for 0% of the time, Pallas kernels for 4%

profile of v10, /device:TPU:32, one launch (start us, length us, event | category | flops | bytes accessed | tf_op | source)
XLA Modules:
  0.0 108.8 jit_solution(7834758166589785741)
XLA Ops:
  0.0 0.0 copy-start
  0.7 4.6 %prepare.1 = (bf16[640,640]{1,0:T(8,128)(2,1)}, bf16[640,640]{1,0:T(8,128)(2,1)}, bf16[640,640]{1,0:T(8,128)(2,1)}, bf16[160,640]{1,0:T(8,128)(2,1)}, bf16[160,6...) custom-call(s32[1]{0:T(128)S(6)} %copy.10.sizes, bf16[640,640]{1,0:T(8,128)(2,1)} %bitcast.21, ...), custom_call_target="tpu_custom_call" | custom-call | flops 1048576000 | bytes 4915200 | tf_op jit(solution)/shard_map/prepare/pallas_call | solution.py:82
  5.3 1.9 %collective-permute-start = (bf16[640,640]{1,0:T(8,128)(2,1)}, bf16[640,640]{1,0:T(8,128)(2,1)S(1)}, u32[]{:S(2)}, u32[]{:S(2)}) collective-permute-start(bf16[640,640]{1,0:T(8,128)(2,1)} %get-tuple-element.18), channel_id=1, source_target_pairs={{1,0},{2,1},{3,2},{4,3},{5,4},{6,5},{7,6},{9,8},{10,9},{11,10},{12... | collective-permute-start | bytes 2457608 | tf_op jit(solution)/shard_map/ppermute | solution.py:22
  7.2 2.4 %collective-permute-start.1 = (bf16[640,640]{1,0:T(8,128)(2,1)}, bf16[640,640]{1,0:T(8,128)(2,1)S(1)}, u32[]{:S(2)}, u32[]{:S(2)}) collective-permute-start(bf16[640,640]{1,0:T(8,128)(2,1)} %get-tuple-element.19), channel_id=1, source_target_pairs={{0,1},{1,2},{2,3},{3,4},{4,5},{5,6},{6,7},{8,9},{9,10},{10,11},{11... | collective-permute-start | bytes 2457608 | tf_op jit(solution)/shard_map/ppermute | solution.py:22
  9.6 1.6 %collective-permute-start.6 = (bf16[160,640]{1,0:T(8,128)(2,1)}, bf16[160,640]{1,0:T(8,128)(2,1)S(1)}, u32[]{:S(2)}, u32[]{:S(2)}) collective-permute-start(bf16[160,640]{1,0:T(8,128)(2,1)} %get-tuple-element.25), channel_id=1, source_target_pairs={{0,8},{8,16},{16,24},{24,0},{1,9},{9,17},{17,25},{25,1},{2,10},{10... | collective-permute-start | bytes 614408 | tf_op jit(solution)/shard_map/ppermute | solution.py:27
  11.2 2.9 %collective-permute-start.7 = (bf16[160,640]{1,0:T(8,128)(2,1)}, bf16[160,640]{1,0:T(8,128)(2,1)S(1)}, u32[]{:S(2)}, u32[]{:S(2)}) collective-permute-start(bf16[160,640]{1,0:T(8,128)(2,1)} %get-tuple-element.26), channel_id=1, source_target_pairs={{0,16},{8,24},{16,0},{24,8},{1,17},{9,25},{17,1},{25,9},{2,18},{10... | collective-permute-start | bytes 614408 | tf_op jit(solution)/shard_map/ppermute | solution.py:27
  14.1 1.3 %collective-permute-start.8 = (bf16[160,640]{1,0:T(8,128)(2,1)}, bf16[160,640]{1,0:T(8,128)(2,1)S(1)}, u32[]{:S(2)}, u32[]{:S(2)}) collective-permute-start(bf16[160,640]{1,0:T(8,128)(2,1)} %get-tuple-element.27), channel_id=1, source_target_pairs={{0,24},{8,0},{16,8},{24,16},{1,25},{9,1},{17,9},{25,17},{2,26},{10... | collective-permute-start | bytes 614408 | tf_op jit(solution)/shard_map/ppermute | solution.py:27
  16.8 0.5 collective-permute-done.refs_1_
  17.3 3.7 %collective-permute-done.1.refs_3_ = bf16[640,640]{1,0:T(8,128)(2,1)S(1)} collective-permute-done((bf16[640,640]{1,0:T(8,128)(2,1)}, bf16[640,640]{1,0:T(8,128)(2,1)S(1)}, u32[]{:S(2)}, u32[]{:S(2)}) %collective-permute-start.1) | collective-permute-done | bytes 819232 | tf_op jit(solution)/shard_map/ppermute | solution.py:22
  21.0 0.0 copy-done.6
  21.0 0.9 copy-done.7
  22.0 4.3 %energy_blocks.1 = (bf16[160,640]{1,0:T(8,128)(2,1)}, bf16[160,640]{1,0:T(8,128)(2,1)}, bf16[160,640]{1,0:T(8,128)(2,1)}, bf16[160,640]{1,0:T(8,128)(2,1)}) custom-call(s32[1]{0:T(128)S(6)} %copy.10.sizes, f32[1]{0:T(128)S(6)} %copy.8.particle, f32[1]{0:T(128)S(6)} %copy.9.hole, bf16[640,640]{1,0:T(8,128)(2,1)} %get-tuple-element.17.refs_0_, ...), custom_call_target="tpu_custom_call" | custom-call | flops 1048576000 | bytes 4096000 | tf_op jit(solution)/shard_map/energy_blocks/pallas_call | solution.py:126
  26.3 1.5 %collective-permute-start.2 = (bf16[160,640]{1,0:T(8,128)(2,1)}, bf16[160,640]{1,0:T(8,128)(2,1)S(1)}, u32[]{:S(2)}, u32[]{:S(2)}) collective-permute-start(bf16[160,640]{1,0:T(8,128)(2,1)} %get-tuple-element.21), channel_id=1, source_target_pairs={{0,32},{32,64},{64,96},{96,0},{1,33},{33,65},{65,97},{97,1},{2,34}... | collective-permute-start | bytes 614408 | tf_op jit(solution)/shard_map/ppermute | solution.py:27
  27.9 2.7 %collective-permute-start.3 = (bf16[160,640]{1,0:T(8,128)(2,1)}, bf16[160,640]{1,0:T(8,128)(2,1)S(1)}, u32[]{:S(2)}, u32[]{:S(2)}) collective-permute-start(bf16[160,640]{1,0:T(8,128)(2,1)} %get-tuple-element.22), channel_id=1, source_target_pairs={{0,64},{32,96},{64,0},{96,32},{1,65},{33,97},{65,1},{97,33},{2,66}... | collective-permute-start | bytes 614408 | tf_op jit(solution)/shard_map/ppermute | solution.py:27
  30.6 0.0 collective-permute-done.6
  30.6 1.5 %collective-permute-start.4 = (bf16[160,640]{1,0:T(8,128)(2,1)}, bf16[160,640]{1,0:T(8,128)(2,1)S(1)}, u32[]{:S(2)}, u32[]{:S(2)}) collective-permute-start(bf16[160,640]{1,0:T(8,128)(2,1)} %get-tuple-element.23), channel_id=1, source_target_pairs={{0,96},{32,0},{64,32},{96,64},{1,97},{33,1},{65,33},{97,65},{2,98}... | collective-permute-start | bytes 614408 | tf_op jit(solution)/shard_map/ppermute | solution.py:27
  32.1 0.0 collective-permute-done.7
  32.1 0.0 collective-permute-done.8
  32.1 0.0 copy-done.2
  32.1 0.0 copy-start.3
  32.1 0.1 pad_maximum_fusion.1.refs_4_
  32.2 0.0 copy-start.1
  32.2 0.6 collective-permute-start.9
  32.9 2.0 %collective-permute-done.2 = bf16[160,640]{1,0:T(8,128)(2,1)S(1)} collective-permute-done((bf16[160,640]{1,0:T(8,128)(2,1)}, bf16[160,640]{1,0:T(8,128)(2,1)S(1)}, u32[]{:S(2)}, u32[]{:S(2)}) %collective-permute-start.2) | collective-permute-done | bytes 204832 | tf_op jit(solution)/shard_map/ppermute | solution.py:27
  34.9 5.1 %collective-permute-done.3 = bf16[160,640]{1,0:T(8,128)(2,1)S(1)} collective-permute-done((bf16[160,640]{1,0:T(8,128)(2,1)}, bf16[160,640]{1,0:T(8,128)(2,1)S(1)}, u32[]{:S(2)}, u32[]{:S(2)}) %collective-permute-start.3) | collective-permute-done | bytes 204832 | tf_op jit(solution)/shard_map/ppermute | solution.py:27
  39.9 1.2 %collective-permute-done.4 = bf16[160,640]{1,0:T(8,128)(2,1)S(1)} collective-permute-done((bf16[160,640]{1,0:T(8,128)(2,1)}, bf16[160,640]{1,0:T(8,128)(2,1)S(1)}, u32[]{:S(2)}, u32[]{:S(2)}) %collective-permute-start.4) | collective-permute-done | bytes 204832 | tf_op jit(solution)/shard_map/ppermute | solution.py:27
  41.1 0.0 copy-done.3
  41.1 0.1 pad_maximum_fusion.refs_0_
  41.2 1.6 %collective-permute-start.5 = (bf16[4,160,640]{2,1,0:T(8,128)(2,1)S(1)}, bf16[4,160,640]{2,1,0:T(8,128)(2,1)S(1)}, u32[]{:S(2)}, u32[]{:S(2)}) collective-permute-start(bf16[4,160,640]{2,1,0:T(8,128)(2,1)S(1)} %pad_maximum_fusion.refs_0_), channel_id=1, source_target_pairs={{0,8},{1,25},{2,10},{3,27},{4,12},{5,29},{6,14},{7,31},{8,16},{9,1... | collective-permute-start | bytes 2457608 | tf_op jit(solution)/shard_map/ppermute | solution.py:45
  42.9 0.0 copy-done.1
  42.9 1.6 %collective-permute-start.12 = (bf16[4,160,640]{2,1,0:T(8,128)(2,1)S(1)}, bf16[4,160,640]{2,1,0:T(8,128)(2,1)}, u32[]{:S(2)}, u32[]{:S(2)}) collective-permute-start(bf16[4,160,640]{2,1,0:T(8,128)(2,1)S(1)} %pad_maximum_fusion.1.refs_4_), channel_id=1, source_target_pairs={{0,96},{1,33},{2,98},{3,35},{4,100},{5,37},{6,102},{7,39},{32,0},{... | collective-permute-start | bytes 2457608 | tf_op jit(solution)/shard_map/ppermute | solution.py:45
  44.4 7.2 %collective-permute-done.9.refs_5_ = bf16[4,160,640]{2,1,0:T(8,128)(2,1)S(1)} collective-permute-done((bf16[4,160,640]{2,1,0:T(8,128)(2,1)S(1)}, bf16[4,160,640]{2,1,0:T(8,128)(2,1)S(1)}, u32[]{:S(2)}, u32[]{:S(2)}) %collective-permute-start.9) | collective-permute-done | bytes 819232 | tf_op jit(solution)/shard_map/ppermute | solution.py:45
  51.7 5.3 %collective-permute-start.10 = (bf16[4,160,640]{2,1,0:T(8,128)(2,1)S(1)}, bf16[4,160,640]{2,1,0:T(8,128)(2,1)}, u32[]{:S(2)}, u32[]{:S(2)}) collective-permute-start(bf16[4,160,640]{2,1,0:T(8,128)(2,1)S(1)} %pad_maximum_fusion.refs_0_), channel_id=1, source_target_pairs={{0,24},{1,9},{2,26},{3,11},{4,28},{5,13},{6,30},{7,15},{8,0},{9,17... | collective-permute-start | bytes 2457608 | tf_op jit(solution)/shard_map/ppermute | solution.py:45
  57.0 0.0 collective-permute-start.13
  57.0 0.0 collective-permute-done.5.refs_1_
  57.0 0.3 collective-permute-start.11
  57.2 0.0 copy-done
  57.3 0.1 dynamic-slice_bitcast_fusion
  57.3 0.1 copy.7.rates
  57.5 1.7 %collective-permute-done.12.refs_6_ = bf16[4,160,640]{2,1,0:T(8,128)(2,1)} collective-permute-done((bf16[4,160,640]{2,1,0:T(8,128)(2,1)S(1)}, bf16[4,160,640]{2,1,0:T(8,128)(2,1)}, u32[]{:S(2)}, u32[]{:S(2)}) %collective-permute-start.12) | collective-permute-done | bytes 819232 | tf_op jit(solution)/shard_map/ppermute | solution.py:45
  59.2 11.4 %collective-permute-done.13.refs_7_ = bf16[4,160,640]{2,1,0:T(8,128)(2,1)} collective-permute-done((bf16[4,160,640]{2,1,0:T(8,128)(2,1)S(1)}, bf16[4,160,640]{2,1,0:T(8,128)(2,1)}, u32[]{:S(2)}, u32[]{:S(2)}) %collective-permute-start.13) | collective-permute-done | bytes 819232 | tf_op jit(solution)/shard_map/ppermute | solution.py:45
  70.6 3.9 %collective-permute-done.10.refs_2_ = bf16[4,160,640]{2,1,0:T(8,128)(2,1)} collective-permute-done((bf16[4,160,640]{2,1,0:T(8,128)(2,1)S(1)}, bf16[4,160,640]{2,1,0:T(8,128)(2,1)}, u32[]{:S(2)}, u32[]{:S(2)}) %collective-permute-start.10) | collective-permute-done | bytes 819232 | tf_op jit(solution)/shard_map/ppermute | solution.py:45
  74.5 0.0 collective-permute-done.11.refs_3_
  74.5 0.0 copy-done.4
  74.5 0.0 copy-done.5
  74.5 11.4 %convolve.1 = bf16[16,40,640]{2,1,0:T(8,128)(2,1)S(1)} custom-call(s32[1]{0:T(128)S(6)} %copy.10.sizes, f32[160,1]{1,0:T(8,128)S(1)} %copy.7.rates, bf16[4,160,640]{2,1,0:T(8,128)(2,1)S(1)} %pad_maximum_fusion.refs_0_, bf16[4,160,640]{2,1,0:T(8,128)(2,1)} %copy-done.5, bf16[4,160,640]{2,1,0:T(8,128)(2,1)} %collective-permute-done.10.refs_2_, ...), custom_call_target="tpu_custom_call" | custom-call | flops 4456448000 | bytes 6553600 | tf_op jit(solution)/shard_map/convolve/pallas_call | solution.py:207
  85.9 20.5 %all_to_all.5.packets = bf16[16,40,640]{2,1,0:T(8,128)(2,1)} all-to-all(bf16[16,40,640]{2,1,0:T(8,128)(2,1)S(1)} %convolve.1), channel_id=1, replica_groups=mesh['tx'=4,'ty'=4,'sector'=8] {'tx','ty'}, dimensions={0} | all-to-all | bytes 1638400 | tf_op jit(solution)/shard_map/all_to_all | solution.py:287
  106.4 2.4 %assemble.1 = bf16[640,640]{1,0:T(8,128)(2,1)} custom-call(bf16[16,40,640]{2,1,0:T(8,128)(2,1)} %all_to_all.5.packets), custom_call_target="tpu_custom_call" | custom-call | tf_op jit(solution)/shard_map/assemble/pallas_call | solution.py:240
  (5 shorter events, 0.0 us)
Async XLA Ops:
  0.0 57.2 %copy-start = (f32[1,640]{1,0:T(1,128)S(1)}, f32[1,640]{1,0:T(1,128)}, u32[]{:S(2)}) copy-start(f32[1,640]{1,0:T(1,128)} %param.8) | copy-start | bytes 7684
  5.3 12.1 %collective-permute-start = (bf16[640,640]{1,0:T(8,128)(2,1)}, bf16[640,640]{1,0:T(8,128)(2,1)S(1)}, u32[]{:S(2)}, u32[]{:S(2)}) collective-permute-start(bf16[640,640]{1,0:T(8,128)(2,1)} %get-tuple-element.18), channel_id=1, source_target_pairs={{1,0},{2,1},{3,2},{4,3},{5,4},{6,5},{7,6},{9,8},{10,9},{11,10},{12... | collective-permute-start | bytes 2457608 | tf_op jit(solution)/shard_map/ppermute | solution.py:22
  7.2 13.9 %collective-permute-start.1 = (bf16[640,640]{1,0:T(8,128)(2,1)}, bf16[640,640]{1,0:T(8,128)(2,1)S(1)}, u32[]{:S(2)}, u32[]{:S(2)}) collective-permute-start(bf16[640,640]{1,0:T(8,128)(2,1)} %get-tuple-element.19), channel_id=1, source_target_pairs={{0,1},{1,2},{2,3},{3,4},{4,5},{5,6},{6,7},{8,9},{9,10},{10,11},{11... | collective-permute-start | bytes 2457608 | tf_op jit(solution)/shard_map/ppermute | solution.py:22
  9.6 21.0 %collective-permute-start.6 = (bf16[160,640]{1,0:T(8,128)(2,1)}, bf16[160,640]{1,0:T(8,128)(2,1)S(1)}, u32[]{:S(2)}, u32[]{:S(2)}) collective-permute-start(bf16[160,640]{1,0:T(8,128)(2,1)} %get-tuple-element.25), channel_id=1, source_target_pairs={{0,8},{8,16},{16,24},{24,0},{1,9},{9,17},{17,25},{25,1},{2,10},{10... | collective-permute-start | bytes 614408 | tf_op jit(solution)/shard_map/ppermute | solution.py:27
  11.2 20.8 %collective-permute-start.7 = (bf16[160,640]{1,0:T(8,128)(2,1)}, bf16[160,640]{1,0:T(8,128)(2,1)S(1)}, u32[]{:S(2)}, u32[]{:S(2)}) collective-permute-start(bf16[160,640]{1,0:T(8,128)(2,1)} %get-tuple-element.26), channel_id=1, source_target_pairs={{0,16},{8,24},{16,0},{24,8},{1,17},{9,25},{17,1},{25,9},{2,18},{10... | collective-permute-start | bytes 614408 | tf_op jit(solution)/shard_map/ppermute | solution.py:27
  14.1 17.9 %collective-permute-start.8 = (bf16[160,640]{1,0:T(8,128)(2,1)}, bf16[160,640]{1,0:T(8,128)(2,1)S(1)}, u32[]{:S(2)}, u32[]{:S(2)}) collective-permute-start(bf16[160,640]{1,0:T(8,128)(2,1)} %get-tuple-element.27), channel_id=1, source_target_pairs={{0,24},{8,0},{16,8},{24,16},{1,25},{9,1},{17,9},{25,17},{2,26},{10... | collective-permute-start | bytes 614408 | tf_op jit(solution)/shard_map/ppermute | solution.py:27
  17.3 3.7 %copy-start.6 = (bf16[640,640]{1,0:T(8,128)(2,1)}, bf16[640,640]{1,0:T(8,128)(2,1)S(1)}, u32[]{:S(2)}) copy-start(bf16[640,640]{1,0:T(8,128)(2,1)S(1)} %collective-permute-done.refs_1_) | copy-start | bytes 2457604
  21.0 0.9 copy-start.7
  22.0 10.1 %copy-start.2 = (bf16[160,640]{1,0:T(8,128)(2,1)S(1)}, bf16[160,640]{1,0:T(8,128)(2,1)}, u32[]{:S(2)}) copy-start(bf16[160,640]{1,0:T(8,128)(2,1)} %get-tuple-element.24) | copy-start | bytes 614404
  26.3 8.5 %collective-permute-start.2 = (bf16[160,640]{1,0:T(8,128)(2,1)}, bf16[160,640]{1,0:T(8,128)(2,1)S(1)}, u32[]{:S(2)}, u32[]{:S(2)}) collective-permute-start(bf16[160,640]{1,0:T(8,128)(2,1)} %get-tuple-element.21), channel_id=1, source_target_pairs={{0,32},{32,64},{64,96},{96,0},{1,33},{33,65},{65,97},{97,1},{2,34}... | collective-permute-start | bytes 614408 | tf_op jit(solution)/shard_map/ppermute | solution.py:27
  27.9 12.0 %collective-permute-start.3 = (bf16[160,640]{1,0:T(8,128)(2,1)}, bf16[160,640]{1,0:T(8,128)(2,1)S(1)}, u32[]{:S(2)}, u32[]{:S(2)}) collective-permute-start(bf16[160,640]{1,0:T(8,128)(2,1)} %get-tuple-element.22), channel_id=1, source_target_pairs={{0,64},{32,96},{64,0},{96,32},{1,65},{33,97},{65,1},{97,33},{2,66}... | collective-permute-start | bytes 614408 | tf_op jit(solution)/shard_map/ppermute | solution.py:27
  30.6 10.5 %collective-permute-start.4 = (bf16[160,640]{1,0:T(8,128)(2,1)}, bf16[160,640]{1,0:T(8,128)(2,1)S(1)}, u32[]{:S(2)}, u32[]{:S(2)}) collective-permute-start(bf16[160,640]{1,0:T(8,128)(2,1)} %get-tuple-element.23), channel_id=1, source_target_pairs={{0,96},{32,0},{64,32},{96,64},{1,97},{33,1},{65,33},{97,65},{2,98}... | collective-permute-start | bytes 614408 | tf_op jit(solution)/shard_map/ppermute | solution.py:27
  32.1 9.0 %copy-start.3 = (bf16[160,640]{1,0:T(8,128)(2,1)S(1)}, bf16[160,640]{1,0:T(8,128)(2,1)}, u32[]{:S(2)}) copy-start(bf16[160,640]{1,0:T(8,128)(2,1)} %get-tuple-element.20) | copy-start | bytes 614404
  32.2 10.6 %copy-start.1 = (bf16[4,160,640]{2,1,0:T(8,128)(2,1)}, bf16[4,160,640]{2,1,0:T(8,128)(2,1)S(1)}, u32[]{:S(2)}) copy-start(bf16[4,160,640]{2,1,0:T(8,128)(2,1)S(1)} %pad_maximum_fusion.1.refs_4_) | copy-start | bytes 2457604
  32.2 19.4 %collective-permute-start.9 = (bf16[4,160,640]{2,1,0:T(8,128)(2,1)S(1)}, bf16[4,160,640]{2,1,0:T(8,128)(2,1)S(1)}, u32[]{:S(2)}, u32[]{:S(2)}) collective-permute-start(bf16[4,160,640]{2,1,0:T(8,128)(2,1)S(1)} %pad_maximum_fusion.1.refs_4_), channel_id=1, source_target_pairs={{0,32},{1,97},{2,34},{3,99},{4,36},{5,101},{6,38},{7,103},{32,64},... | collective-permute-start | bytes 2457608 | tf_op jit(solution)/shard_map/ppermute | solution.py:45
  41.2 15.7 %collective-permute-start.5 = (bf16[4,160,640]{2,1,0:T(8,128)(2,1)S(1)}, bf16[4,160,640]{2,1,0:T(8,128)(2,1)S(1)}, u32[]{:S(2)}, u32[]{:S(2)}) collective-permute-start(bf16[4,160,640]{2,1,0:T(8,128)(2,1)S(1)} %pad_maximum_fusion.refs_0_), channel_id=1, source_target_pairs={{0,8},{1,25},{2,10},{3,27},{4,12},{5,29},{6,14},{7,31},{8,16},{9,1... | collective-permute-start | bytes 2457608 | tf_op jit(solution)/shard_map/ppermute | solution.py:45
  42.9 16.3 %collective-permute-start.12 = (bf16[4,160,640]{2,1,0:T(8,128)(2,1)S(1)}, bf16[4,160,640]{2,1,0:T(8,128)(2,1)}, u32[]{:S(2)}, u32[]{:S(2)}) collective-permute-start(bf16[4,160,640]{2,1,0:T(8,128)(2,1)S(1)} %pad_maximum_fusion.1.refs_4_), channel_id=1, source_target_pairs={{0,96},{1,33},{2,98},{3,35},{4,100},{5,37},{6,102},{7,39},{32,0},{... | collective-permute-start | bytes 2457608 | tf_op jit(solution)/shard_map/ppermute | solution.py:45
  51.7 22.8 %copy-start.4 = (bf16[4,160,640]{2,1,0:T(8,128)(2,1)}, bf16[4,160,640]{2,1,0:T(8,128)(2,1)S(1)}, u32[]{:S(2)}) copy-start(bf16[4,160,640]{2,1,0:T(8,128)(2,1)S(1)} %collective-permute-done.9.refs_5_) | copy-start | bytes 2457604
  51.7 22.8 %collective-permute-start.10 = (bf16[4,160,640]{2,1,0:T(8,128)(2,1)S(1)}, bf16[4,160,640]{2,1,0:T(8,128)(2,1)}, u32[]{:S(2)}, u32[]{:S(2)}) collective-permute-start(bf16[4,160,640]{2,1,0:T(8,128)(2,1)S(1)} %pad_maximum_fusion.refs_0_), channel_id=1, source_target_pairs={{0,24},{1,9},{2,26},{3,11},{4,28},{5,13},{6,30},{7,15},{8,0},{9,17... | collective-permute-start | bytes 2457608 | tf_op jit(solution)/shard_map/ppermute | solution.py:45
  57.0 13.7 %collective-permute-start.13 = (bf16[4,160,640]{2,1,0:T(8,128)(2,1)S(1)}, bf16[4,160,640]{2,1,0:T(8,128)(2,1)}, u32[]{:S(2)}, u32[]{:S(2)}) collective-permute-start(bf16[4,160,640]{2,1,0:T(8,128)(2,1)S(1)} %collective-permute-done.9.refs_5_), channel_id=1, source_target_pairs={{0,32},{1,97},{2,34},{3,99},{4,36},{5,101},{6,38},{7,103},{32,64},... | collective-permute-start | bytes 2457608 | tf_op jit(solution)/shard_map/ppermute | solution.py:45
  57.0 17.5 %copy-start.5 = (bf16[4,160,640]{2,1,0:T(8,128)(2,1)}, bf16[4,160,640]{2,1,0:T(8,128)(2,1)S(1)}, u32[]{:S(2)}) copy-start(bf16[4,160,640]{2,1,0:T(8,128)(2,1)S(1)} %collective-permute-done.5.refs_1_) | copy-start | bytes 2457604
  57.0 17.5 %collective-permute-start.11 = (bf16[4,160,640]{2,1,0:T(8,128)(2,1)S(1)}, bf16[4,160,640]{2,1,0:T(8,128)(2,1)}, u32[]{:S(2)}, u32[]{:S(2)}) collective-permute-start(bf16[4,160,640]{2,1,0:T(8,128)(2,1)S(1)} %collective-permute-done.5.refs_1_), channel_id=1, source_target_pairs={{0,8},{1,25},{2,10},{3,27},{4,12},{5,29},{6,14},{7,31},{8,16},{9,1... | collective-permute-start | bytes 2457608 | tf_op jit(solution)/shard_map/ppermute | solution.py:45

commit v11 on v7

--- a/solution.py
+++ b/solution.py
@@ -12,6 +12,7 @@
 MIB = 1024 * 1024
 VMEM = pl.BlockSpec(memory_space=pltpu.VMEM)
 SMEM = pl.BlockSpec(memory_space=pltpu.SMEM)
+ANY = pl.BlockSpec(memory_space=pl.ANY)
 HBM = pl.BlockSpec(memory_space=pltpu.HBM)
 NT = (((1,), (1,)), ((), ()))
 
@@ -126,13 +127,14 @@
     return pl.pallas_call(
         energy_kernel,
         out_shape=(block,) * n,
-        in_specs=[SMEM] * 3 + [HBM] * 4,
+        in_specs=[SMEM] * 3 + [ANY] * 4,
         out_specs=(VMEM,) * n,
         scratch_shapes=[pltpu.VMEM((states, states), jnp.bfloat16)] * 4
         + [pltpu.SemaphoreType.DMA((4,))],
         cost_estimate=pl.CostEstimate(
             flops=4 * states**3, bytes_accessed=10 * states**2, transcendentals=0
         ),
+        compiler_params=pltpu.CompilerParams(vmem_limit_bytes=16 * MIB),
         name="energy_blocks",
     )(sizes, particle, hole, flipped, above, operator, below)
 
@@ -207,7 +209,7 @@
     return pl.pallas_call(
         functools.partial(convolve_kernel, plan, n, step_size),
         out_shape=jax.ShapeDtypeStruct((n * n, rows // n, states), jnp.bfloat16),
-        in_specs=[SMEM, VMEM] + [HBM] * len(parts),
+        in_specs=[SMEM, VMEM] + [ANY] * len(parts),
         out_specs=VMEM,
         scratch_shapes=[
             pltpu.VMEM((rows, (n * n + 1) * states), jnp.bfloat16),
@@ -215,7 +217,7 @@
             pltpu.VMEM((n * n * rows, rows), jnp.float32),
             pltpu.SemaphoreType.DMA((copies,)),
         ],
-        compiler_params=pltpu.CompilerParams(vmem_limit_bytes=52 * MIB),
+        compiler_params=pltpu.CompilerParams(vmem_limit_bytes=20 * MIB),
         cost_estimate=pl.CostEstimate(
             flops=n * n * (n * n + 1) * rows * rows * states,
             bytes_accessed=4 * n * n * rows * states,

time: 107 us -> 104 us (0.972)
  Pallas kernels: 22.7 us -> 20 us
    pallas_call x1, Pallas kernels: 4.44 us -> 2.22 us  [energy_blocks(): pl.pallas_call(energy_kernel, out_shape=(block,) * n, in_specs=[SMEM] * 3...]
  transfers between devices with their start and end apart: 14 -> 14, of which waited for: 9 -> 9; matrix products, arithmetic and copies ran while one was open for 0% -> 0% of each run, Pallas kernels for 4% -> 2%
where the time goes in v11:
time: 104 us
  waiting for transfers between devices  41.7 us (40%)
  starting transfers between devices  22.2 us (21%)
  Pallas kernels  20 us (19%)
  blocking collectives  16.2 us (16%)
  between operations  2.05 us (2%)
  local copies, waits for them, and re-layouts  1.34 us (1%)
    ppermute x6, waiting for transfers between devices, turned_ring(): return lax.ppermute(block, (axis, 'sector'), route)  29.4 us
    all_to_all x1, blocking collectives, per_device(): packets = lax.all_to_all(packets, ('tx', 'ty'), 0, 0, tiled=True)  16.2 us
    ppermute x6, starting transfers between devices, ring(): lax.ppermute(block, axis, [(i, (i + distance) % n) for i in range(n)])  11.6 us
    pallas_call x1, Pallas kernels, convolve(): pl.pallas_call(functools.partial(convolve_kernel, plan, n, step_size), ou...  10.6 us
    ppermute x6, waiting for transfers between devices, ring(): lax.ppermute(block, axis, [(i, (i + distance) % n) for i in range(n)])  8.03 us
    ppermute x6, starting transfers between devices, turned_ring(): return lax.ppermute(block, (axis, 'sector'), route)  6.29 us
    pallas_call x1, Pallas kernels, prepare(): pl.pallas_call(prepare_kernel, out_shape=(square,) * 3 + (block,) * n, in...  4.71 us
    ppermute x2, starting transfers between devices, shifted(): return lax.ppermute(block, axis, route)  4.31 us
  transfers between devices with their start and end apart: 14, of which 9 were waited for; matrix products, arithmetic and copies ran while one was open for 0% of the time, Pallas kernels for 2%

profile of v11, /device:TPU:32, one launch (start us, length us, event | category | flops | bytes accessed | tf_op | source)
XLA Modules:
  0.0 103.7 jit_solution(3984360717547899779)
XLA Ops:
  0.0 0.0 copy-start
  0.7 0.0 copy-start.1
  0.7 4.7 %prepare.1 = (bf16[640,640]{1,0:T(8,128)(2,1)}, bf16[640,640]{1,0:T(8,128)(2,1)}, bf16[640,640]{1,0:T(8,128)(2,1)}, bf16[160,640]{1,0:T(8,128)(2,1)}, bf16[160,6...) custom-call(s32[1]{0:T(128)S(6)} %copy.10.sizes, bf16[640,640]{1,0:T(8,128)(2,1)} %bitcast.23, ...), custom_call_target="tpu_custom_call" | custom-call | flops 1048576000 | bytes 4915200 | tf_op jit(solution)/shard_map/prepare/pallas_call | solution.py:85
  5.4 1.9 %collective-permute-start = (bf16[640,640]{1,0:T(8,128)(2,1)}, bf16[640,640]{1,0:T(8,128)(2,1)S(1)}, u32[]{:S(2)}, u32[]{:S(2)}) collective-permute-start(bf16[640,640]{1,0:T(8,128)(2,1)} %get-tuple-element.17), channel_id=1, source_target_pairs={{1,0},{2,1},{3,2},{4,3},{5,4},{6,5},{7,6},{9,8},{10,9},{11,10},{12... | collective-permute-start | bytes 2457608 | tf_op jit(solution)/shard_map/ppermute | solution.py:23
  7.3 2.4 %collective-permute-start.1 = (bf16[640,640]{1,0:T(8,128)(2,1)}, bf16[640,640]{1,0:T(8,128)(2,1)S(1)}, u32[]{:S(2)}, u32[]{:S(2)}) collective-permute-start(bf16[640,640]{1,0:T(8,128)(2,1)} %get-tuple-element.18), channel_id=1, source_target_pairs={{0,1},{1,2},{2,3},{3,4},{4,5},{5,6},{6,7},{8,9},{9,10},{10,11},{11... | collective-permute-start | bytes 2457608 | tf_op jit(solution)/shard_map/ppermute | solution.py:23
  9.7 1.6 %collective-permute-start.8 = (bf16[160,640]{1,0:T(8,128)(2,1)}, bf16[160,640]{1,0:T(8,128)(2,1)S(1)}, u32[]{:S(2)}, u32[]{:S(2)}) collective-permute-start(bf16[160,640]{1,0:T(8,128)(2,1)} %get-tuple-element.24), channel_id=1, source_target_pairs={{0,8},{8,16},{16,24},{24,0},{1,9},{9,17},{17,25},{25,1},{2,10},{10... | collective-permute-start | bytes 614408 | tf_op jit(solution)/shard_map/ppermute | solution.py:28
  11.4 2.9 %collective-permute-start.9 = (bf16[160,640]{1,0:T(8,128)(2,1)}, bf16[160,640]{1,0:T(8,128)(2,1)S(1)}, u32[]{:S(2)}, u32[]{:S(2)}) collective-permute-start(bf16[160,640]{1,0:T(8,128)(2,1)} %get-tuple-element.25), channel_id=1, source_target_pairs={{0,16},{8,24},{16,0},{24,8},{1,17},{9,25},{17,1},{25,9},{2,18},{10... | collective-permute-start | bytes 614408 | tf_op jit(solution)/shard_map/ppermute | solution.py:28
  14.3 1.3 %collective-permute-start.10 = (bf16[160,640]{1,0:T(8,128)(2,1)}, bf16[160,640]{1,0:T(8,128)(2,1)S(1)}, u32[]{:S(2)}, u32[]{:S(2)}) collective-permute-start(bf16[160,640]{1,0:T(8,128)(2,1)} %get-tuple-element.26), channel_id=1, source_target_pairs={{0,24},{8,0},{16,8},{24,16},{1,25},{9,1},{17,9},{25,17},{2,26},{10... | collective-permute-start | bytes 614408 | tf_op jit(solution)/shard_map/ppermute | solution.py:28
  16.9 0.6 collective-permute-done.refs_1_
  17.5 3.7 %collective-permute-done.1.refs_3_ = bf16[640,640]{1,0:T(8,128)(2,1)S(1)} collective-permute-done((bf16[640,640]{1,0:T(8,128)(2,1)}, bf16[640,640]{1,0:T(8,128)(2,1)S(1)}, u32[]{:S(2)}, u32[]{:S(2)}) %collective-permute-start.1) | collective-permute-done | bytes 819232 | tf_op jit(solution)/shard_map/ppermute | solution.py:23
  21.2 0.0 copy-done.1
  21.2 0.0 copy-start.2
  21.2 1.1 %copy-done.2 = bf16[640,640]{1,0:T(8,128)(2,1)S(1)} copy-done((bf16[640,640]{1,0:T(8,128)(2,1)S(1)}, bf16[640,640]{1,0:T(8,128)(2,1)}, u32[]{:S(2)}) %copy-start.2) | copy-done | bytes 819224
  22.3 0.0 copy-start.3
  22.3 2.2 %energy_blocks.1 = (bf16[160,640]{1,0:T(8,128)(2,1)S(1)}, bf16[160,640]{1,0:T(8,128)(2,1)S(1)}, bf16[160,640]{1,0:T(8,128)(2,1)S(1)}, bf16[160,640]{1,0:T(8,128)(2,1)S(1)}) custom-call(s32[1]{0:T(128)S(6)} %copy.10.sizes, f32[1]{0:T(128)S(6)} %copy.8.particle, f32[1]{0:T(128)S(6)} %copy.9.hole, bf16[640,640]{1,0:T(8,128)(2,1)S(1)} %copy-done.2, ...), custom_call_target="tpu_custom_call" | custom-call | flops 1048576000 | bytes 4096000 | tf_op jit(solution)/shard_map/energy_blocks/pallas_call | solution.py:127
  24.6 1.5 %collective-permute-start.2 = (bf16[160,640]{1,0:T(8,128)(2,1)S(1)}, bf16[160,640]{1,0:T(8,128)(2,1)S(1)}, u32[]{:S(2)}, u32[]{:S(2)}) collective-permute-start(bf16[160,640]{1,0:T(8,128)(2,1)S(1)} %get-tuple-element.20), channel_id=1, source_target_pairs={{0,32},{32,64},{64,96},{96,0},{1,33},{33,65},{65,97},{97,1},{2,34}... | collective-permute-start | bytes 614408 | tf_op jit(solution)/shard_map/ppermute | solution.py:28
  26.1 2.7 %collective-permute-start.3 = (bf16[160,640]{1,0:T(8,128)(2,1)S(1)}, bf16[160,640]{1,0:T(8,128)(2,1)S(1)}, u32[]{:S(2)}, u32[]{:S(2)}) collective-permute-start(bf16[160,640]{1,0:T(8,128)(2,1)S(1)} %get-tuple-element.21), channel_id=1, source_target_pairs={{0,64},{32,96},{64,0},{96,32},{1,65},{33,97},{65,1},{97,33},{2,66}... | collective-permute-start | bytes 614408 | tf_op jit(solution)/shard_map/ppermute | solution.py:28
  28.8 0.0 collective-permute-done.8
  28.8 1.4 %collective-permute-start.4 = (bf16[160,640]{1,0:T(8,128)(2,1)S(1)}, bf16[160,640]{1,0:T(8,128)(2,1)S(1)}, u32[]{:S(2)}, u32[]{:S(2)}) collective-permute-start(bf16[160,640]{1,0:T(8,128)(2,1)S(1)} %get-tuple-element.22), channel_id=1, source_target_pairs={{0,96},{32,0},{64,32},{96,64},{1,97},{33,1},{65,33},{97,65},{2,98}... | collective-permute-start | bytes 614408 | tf_op jit(solution)/shard_map/ppermute | solution.py:28
  30.3 0.0 collective-permute-done.9
  30.3 0.0 collective-permute-done.10
  30.3 0.0 copy-done.3
  30.3 0.1 pad_maximum_fusion.1.refs_4_
  30.4 0.6 collective-permute-start.11
  31.1 1.8 %collective-permute-done.2 = bf16[160,640]{1,0:T(8,128)(2,1)S(1)} collective-permute-done((bf16[160,640]{1,0:T(8,128)(2,1)S(1)}, bf16[160,640]{1,0:T(8,128)(2,1)S(1)}, u32[]{:S(2)}, u32[]{:S(2)}) %collective-permute-start.2) | collective-permute-done | bytes 204832 | tf_op jit(solution)/shard_map/ppermute | solution.py:28
  32.8 5.1 %collective-permute-done.3 = bf16[160,640]{1,0:T(8,128)(2,1)S(1)} collective-permute-done((bf16[160,640]{1,0:T(8,128)(2,1)S(1)}, bf16[160,640]{1,0:T(8,128)(2,1)S(1)}, u32[]{:S(2)}, u32[]{:S(2)}) %collective-permute-start.3) | collective-permute-done | bytes 204832 | tf_op jit(solution)/shard_map/ppermute | solution.py:28
  37.9 1.2 %collective-permute-done.4 = bf16[160,640]{1,0:T(8,128)(2,1)S(1)} collective-permute-done((bf16[160,640]{1,0:T(8,128)(2,1)S(1)}, bf16[160,640]{1,0:T(8,128)(2,1)S(1)}, u32[]{:S(2)}, u32[]{:S(2)}) %collective-permute-start.4) | collective-permute-done | bytes 204832 | tf_op jit(solution)/shard_map/ppermute | solution.py:28
  39.1 0.1 pad_maximum_fusion.refs_0_
  39.2 1.6 %collective-permute-start.5 = (bf16[4,160,640]{2,1,0:T(8,128)(2,1)S(1)}, bf16[4,160,640]{2,1,0:T(8,128)(2,1)S(1)}, u32[]{:S(2)}, u32[]{:S(2)}) collective-permute-start(bf16[4,160,640]{2,1,0:T(8,128)(2,1)S(1)} %pad_maximum_fusion.refs_0_), channel_id=1, source_target_pairs={{0,8},{1,25},{2,10},{3,27},{4,12},{5,29},{6,14},{7,31},{8,16},{9,1... | collective-permute-start | bytes 2457608 | tf_op jit(solution)/shard_map/ppermute | solution.py:42
  40.9 1.6 %collective-permute-start.12 = (bf16[4,160,640]{2,1,0:T(8,128)(2,1)S(1)}, bf16[4,160,640]{2,1,0:T(8,128)(2,1)}, u32[]{:S(2)}, u32[]{:S(2)}) collective-permute-start(bf16[4,160,640]{2,1,0:T(8,128)(2,1)S(1)} %pad_maximum_fusion.1.refs_4_), channel_id=1, source_target_pairs={{0,96},{1,33},{2,98},{3,35},{4,100},{5,37},{6,102},{7,39},{32,0},{... | collective-permute-start | bytes 2457608 | tf_op jit(solution)/shard_map/ppermute | solution.py:42
  42.4 1.7 %collective-permute-start.6 = (bf16[4,160,640]{2,1,0:T(8,128)(2,1)S(1)}, bf16[4,160,640]{2,1,0:T(8,128)(2,1)}, u32[]{:S(2)}, u32[]{:S(2)}) collective-permute-start(bf16[4,160,640]{2,1,0:T(8,128)(2,1)S(1)} %pad_maximum_fusion.refs_0_), channel_id=1, source_target_pairs={{0,24},{1,9},{2,26},{3,11},{4,28},{5,13},{6,30},{7,15},{8,0},{9,17... | collective-permute-start | bytes 2457608 | tf_op jit(solution)/shard_map/ppermute | solution.py:42
  44.1 5.6 %collective-permute-done.11.refs_5_ = bf16[4,160,640]{2,1,0:T(8,128)(2,1)S(1)} collective-permute-done((bf16[4,160,640]{2,1,0:T(8,128)(2,1)S(1)}, bf16[4,160,640]{2,1,0:T(8,128)(2,1)S(1)}, u32[]{:S(2)}, u32[]{:S(2)}) %collective-permute-start.11) | collective-permute-done | bytes 819232 | tf_op jit(solution)/shard_map/ppermute | solution.py:42
  49.7 0.0 collective-permute-start.13
  49.7 11.1 %collective-permute-done.5.refs_1_ = bf16[4,160,640]{2,1,0:T(8,128)(2,1)S(1)} collective-permute-done((bf16[4,160,640]{2,1,0:T(8,128)(2,1)S(1)}, bf16[4,160,640]{2,1,0:T(8,128)(2,1)S(1)}, u32[]{:S(2)}, u32[]{:S(2)}) %collective-permute-start.5) | collective-permute-done | bytes 819232 | tf_op jit(solution)/shard_map/ppermute | solution.py:42
  60.8 0.8 collective-permute-start.7
  61.6 0.0 copy-done
  61.6 0.1 dynamic-slice_bitcast_fusion
  61.6 0.1 copy.7.rates
  61.7 0.0 collective-permute-done.12.refs_6_
  61.8 2.5 %collective-permute-done.13.refs_7_ = bf16[4,160,640]{2,1,0:T(8,128)(2,1)} collective-permute-done((bf16[4,160,640]{2,1,0:T(8,128)(2,1)S(1)}, bf16[4,160,640]{2,1,0:T(8,128)(2,1)}, u32[]{:S(2)}, u32[]{:S(2)}) %collective-permute-start.13) | collective-permute-done | bytes 819232 | tf_op jit(solution)/shard_map/ppermute | solution.py:42
  64.3 0.0 collective-permute-done.6.refs_2_
  64.3 10.2 %collective-permute-done.7.refs_3_ = bf16[4,160,640]{2,1,0:T(8,128)(2,1)} collective-permute-done((bf16[4,160,640]{2,1,0:T(8,128)(2,1)S(1)}, bf16[4,160,640]{2,1,0:T(8,128)(2,1)}, u32[]{:S(2)}, u32[]{:S(2)}) %collective-permute-start.7) | collective-permute-done | bytes 819232 | tf_op jit(solution)/shard_map/ppermute | solution.py:42
  74.4 10.6 %convolve.1 = bf16[16,40,640]{2,1,0:T(8,128)(2,1)S(1)} custom-call(s32[1]{0:T(128)S(6)} %copy.10.sizes, f32[160,1]{1,0:T(8,128)S(1)} %copy.7.rates, bf16[4,160,640]{2,1,0:T(8,128)(2,1)S(1)} %pad_maximum_fusion.refs_0_, bf16[4,160,640]{2,1,0:T(8,128)(2,1)S(1)} %collective-permute-done.5.refs_1_, bf16[4,160,640]{2,1,0:T(8,128)(2,1)} %collective-permute-done.6.refs_2_, ...), custom_call_target="tpu_custom_call" | custom-call | flops 4456448000 | bytes 6553600 | tf_op jit(solution)/shard_map/convolve/pallas_call | solution.py:209
  85.1 16.2 %all_to_all.5.packets = bf16[16,40,640]{2,1,0:T(8,128)(2,1)} all-to-all(bf16[16,40,640]{2,1,0:T(8,128)(2,1)S(1)} %convolve.1), channel_id=1, replica_groups=mesh['tx'=4,'ty'=4,'sector'=8] {'tx','ty'}, dimensions={0} | all-to-all | bytes 1638400 | tf_op jit(solution)/shard_map/all_to_all | solution.py:277
  101.3 2.4 %assemble.1 = bf16[640,640]{1,0:T(8,128)(2,1)} custom-call(bf16[16,40,640]{2,1,0:T(8,128)(2,1)} %all_to_all.5.packets), custom_call_target="tpu_custom_call" | custom-call | tf_op jit(solution)/shard_map/assemble/pallas_call | solution.py:242
Async XLA Ops:
  0.0 61.6 %copy-start = (f32[1,640]{1,0:T(1,128)S(1)}, f32[1,640]{1,0:T(1,128)}, u32[]{:S(2)}) copy-start(f32[1,640]{1,0:T(1,128)} %param.8) | copy-start | bytes 7684
  0.7 20.5 %copy-start.1 = (bf16[1,640,640]{2,1,0:T(8,128)(2,1)S(1)}, bf16[1,640,640]{2,1,0:T(8,128)(2,1)}, u32[]{:S(2)}) copy-start(bf16[1,640,640]{2,1,0:T(8,128)(2,1)} %param.7) | copy-start | bytes 2457604
  5.4 12.1 %collective-permute-start = (bf16[640,640]{1,0:T(8,128)(2,1)}, bf16[640,640]{1,0:T(8,128)(2,1)S(1)}, u32[]{:S(2)}, u32[]{:S(2)}) collective-permute-start(bf16[640,640]{1,0:T(8,128)(2,1)} %get-tuple-element.17), channel_id=1, source_target_pairs={{1,0},{2,1},{3,2},{4,3},{5,4},{6,5},{7,6},{9,8},{10,9},{11,10},{12... | collective-permute-start | bytes 2457608 | tf_op jit(solution)/shard_map/ppermute | solution.py:23
  7.3 13.9 %collective-permute-start.1 = (bf16[640,640]{1,0:T(8,128)(2,1)}, bf16[640,640]{1,0:T(8,128)(2,1)S(1)}, u32[]{:S(2)}, u32[]{:S(2)}) collective-permute-start(bf16[640,640]{1,0:T(8,128)(2,1)} %get-tuple-element.18), channel_id=1, source_target_pairs={{0,1},{1,2},{2,3},{3,4},{4,5},{5,6},{6,7},{8,9},{9,10},{10,11},{11... | collective-permute-start | bytes 2457608 | tf_op jit(solution)/shard_map/ppermute | solution.py:23
  9.7 19.1 %collective-permute-start.8 = (bf16[160,640]{1,0:T(8,128)(2,1)}, bf16[160,640]{1,0:T(8,128)(2,1)S(1)}, u32[]{:S(2)}, u32[]{:S(2)}) collective-permute-start(bf16[160,640]{1,0:T(8,128)(2,1)} %get-tuple-element.24), channel_id=1, source_target_pairs={{0,8},{8,16},{16,24},{24,0},{1,9},{9,17},{17,25},{25,1},{2,10},{10... | collective-permute-start | bytes 614408 | tf_op jit(solution)/shard_map/ppermute | solution.py:28
  11.4 18.9 %collective-permute-start.9 = (bf16[160,640]{1,0:T(8,128)(2,1)}, bf16[160,640]{1,0:T(8,128)(2,1)S(1)}, u32[]{:S(2)}, u32[]{:S(2)}) collective-permute-start(bf16[160,640]{1,0:T(8,128)(2,1)} %get-tuple-element.25), channel_id=1, source_target_pairs={{0,16},{8,24},{16,0},{24,8},{1,17},{9,25},{17,1},{25,9},{2,18},{10... | collective-permute-start | bytes 614408 | tf_op jit(solution)/shard_map/ppermute | solution.py:28
  14.3 16.0 %collective-permute-start.10 = (bf16[160,640]{1,0:T(8,128)(2,1)}, bf16[160,640]{1,0:T(8,128)(2,1)S(1)}, u32[]{:S(2)}, u32[]{:S(2)}) collective-permute-start(bf16[160,640]{1,0:T(8,128)(2,1)} %get-tuple-element.26), channel_id=1, source_target_pairs={{0,24},{8,0},{16,8},{24,16},{1,25},{9,1},{17,9},{25,17},{2,26},{10... | collective-permute-start | bytes 614408 | tf_op jit(solution)/shard_map/ppermute | solution.py:28
  21.2 1.1 %copy-start.2 = (bf16[640,640]{1,0:T(8,128)(2,1)S(1)}, bf16[640,640]{1,0:T(8,128)(2,1)}, u32[]{:S(2)}) copy-start(bf16[640,640]{1,0:T(8,128)(2,1)} %get-tuple-element.16.refs_0_) | copy-start | bytes 2457604
  22.3 8.0 %copy-start.3 = (bf16[160,640]{1,0:T(8,128)(2,1)S(1)}, bf16[160,640]{1,0:T(8,128)(2,1)}, u32[]{:S(2)}) copy-start(bf16[160,640]{1,0:T(8,128)(2,1)} %get-tuple-element.23) | copy-start | bytes 614404
  24.6 8.3 %collective-permute-start.2 = (bf16[160,640]{1,0:T(8,128)(2,1)S(1)}, bf16[160,640]{1,0:T(8,128)(2,1)S(1)}, u32[]{:S(2)}, u32[]{:S(2)}) collective-permute-start(bf16[160,640]{1,0:T(8,128)(2,1)S(1)} %get-tuple-element.20), channel_id=1, source_target_pairs={{0,32},{32,64},{64,96},{96,0},{1,33},{33,65},{65,97},{97,1},{2,34}... | collective-permute-start | bytes 614408 | tf_op jit(solution)/shard_map/ppermute | solution.py:28
  26.1 11.8 %collective-permute-start.3 = (bf16[160,640]{1,0:T(8,128)(2,1)S(1)}, bf16[160,640]{1,0:T(8,128)(2,1)S(1)}, u32[]{:S(2)}, u32[]{:S(2)}) collective-permute-start(bf16[160,640]{1,0:T(8,128)(2,1)S(1)} %get-tuple-element.21), channel_id=1, source_target_pairs={{0,64},{32,96},{64,0},{96,32},{1,65},{33,97},{65,1},{97,33},{2,66}... | collective-permute-start | bytes 614408 | tf_op jit(solution)/shard_map/ppermute | solution.py:28
  28.8 10.3 %collective-permute-start.4 = (bf16[160,640]{1,0:T(8,128)(2,1)S(1)}, bf16[160,640]{1,0:T(8,128)(2,1)S(1)}, u32[]{:S(2)}, u32[]{:S(2)}) collective-permute-start(bf16[160,640]{1,0:T(8,128)(2,1)S(1)} %get-tuple-element.22), channel_id=1, source_target_pairs={{0,96},{32,0},{64,32},{96,64},{1,97},{33,1},{65,33},{97,65},{2,98}... | collective-permute-start | bytes 614408 | tf_op jit(solution)/shard_map/ppermute | solution.py:28
  30.4 19.3 %collective-permute-start.11 = (bf16[4,160,640]{2,1,0:T(8,128)(2,1)S(1)}, bf16[4,160,640]{2,1,0:T(8,128)(2,1)S(1)}, u32[]{:S(2)}, u32[]{:S(2)}) collective-permute-start(bf16[4,160,640]{2,1,0:T(8,128)(2,1)S(1)} %pad_maximum_fusion.1.refs_4_), channel_id=1, source_target_pairs={{0,32},{1,97},{2,34},{3,99},{4,36},{5,101},{6,38},{7,103},{32,64},... | collective-permute-start | bytes 2457608 | tf_op jit(solution)/shard_map/ppermute | solution.py:42
  39.2 21.6 %collective-permute-start.5 = (bf16[4,160,640]{2,1,0:T(8,128)(2,1)S(1)}, bf16[4,160,640]{2,1,0:T(8,128)(2,1)S(1)}, u32[]{:S(2)}, u32[]{:S(2)}) collective-permute-start(bf16[4,160,640]{2,1,0:T(8,128)(2,1)S(1)} %pad_maximum_fusion.refs_0_), channel_id=1, source_target_pairs={{0,8},{1,25},{2,10},{3,27},{4,12},{5,29},{6,14},{7,31},{8,16},{9,1... | collective-permute-start | bytes 2457608 | tf_op jit(solution)/shard_map/ppermute | solution.py:42
  40.9 20.9 %collective-permute-start.12 = (bf16[4,160,640]{2,1,0:T(8,128)(2,1)S(1)}, bf16[4,160,640]{2,1,0:T(8,128)(2,1)}, u32[]{:S(2)}, u32[]{:S(2)}) collective-permute-start(bf16[4,160,640]{2,1,0:T(8,128)(2,1)S(1)} %pad_maximum_fusion.1.refs_4_), channel_id=1, source_target_pairs={{0,96},{1,33},{2,98},{3,35},{4,100},{5,37},{6,102},{7,39},{32,0},{... | collective-permute-start | bytes 2457608 | tf_op jit(solution)/shard_map/ppermute | solution.py:42
  42.4 21.8 %collective-permute-start.6 = (bf16[4,160,640]{2,1,0:T(8,128)(2,1)S(1)}, bf16[4,160,640]{2,1,0:T(8,128)(2,1)}, u32[]{:S(2)}, u32[]{:S(2)}) collective-permute-start(bf16[4,160,640]{2,1,0:T(8,128)(2,1)S(1)} %pad_maximum_fusion.refs_0_), channel_id=1, source_target_pairs={{0,24},{1,9},{2,26},{3,11},{4,28},{5,13},{6,30},{7,15},{8,0},{9,17... | collective-permute-start | bytes 2457608 | tf_op jit(solution)/shard_map/ppermute | solution.py:42
  49.7 14.6 %collective-permute-start.13 = (bf16[4,160,640]{2,1,0:T(8,128)(2,1)S(1)}, bf16[4,160,640]{2,1,0:T(8,128)(2,1)}, u32[]{:S(2)}, u32[]{:S(2)}) collective-permute-start(bf16[4,160,640]{2,1,0:T(8,128)(2,1)S(1)} %collective-permute-done.11.refs_5_), channel_id=1, source_target_pairs={{0,32},{1,97},{2,34},{3,99},{4,36},{5,101},{6,38},{7,103},{32,64},... | collective-permute-start | bytes 2457608 | tf_op jit(solution)/shard_map/ppermute | solution.py:42
  60.8 13.7 %collective-permute-start.7 = (bf16[4,160,640]{2,1,0:T(8,128)(2,1)S(1)}, bf16[4,160,640]{2,1,0:T(8,128)(2,1)}, u32[]{:S(2)}, u32[]{:S(2)}) collective-permute-start(bf16[4,160,640]{2,1,0:T(8,128)(2,1)S(1)} %collective-permute-done.5.refs_1_), channel_id=1, source_target_pairs={{0,8},{1,25},{2,10},{3,27},{4,12},{5,29},{6,14},{7,31},{8,16},{9,1... | collective-permute-start | bytes 2457608 | tf_op jit(solution)/shard_map/ppermute | solution.py:42

commit v12 on v11

--- a/solution.py
+++ b/solution.py
@@ -13,7 +13,6 @@
 VMEM = pl.BlockSpec(memory_space=pltpu.VMEM)
 SMEM = pl.BlockSpec(memory_space=pltpu.SMEM)
 ANY = pl.BlockSpec(memory_space=pl.ANY)
-HBM = pl.BlockSpec(memory_space=pltpu.HBM)
 NT = (((1,), (1,)), ((), ()))
 
 
@@ -58,7 +57,7 @@
     return jnp.dot(a, b, preferred_element_type=jnp.float32)
 
 
-def prepare_kernel(sizes, prop, operator, masked, upward, flipped, *refs):
+def prepare_kernel(sizes, prop, operator, masked, upward, *refs):
     *turned, staged = refs
     n = len(turned)
     rows = turned[0].shape[0]
@@ -75,7 +74,6 @@
     for d in range(n):
         first = pl.multiple_of(lax.rem(here_y + d, n) * rows, 32)
         turned[d][...] = staged[pl.ds(first, rows), :]
-    flipped[...] = r.T
 
 
 def prepare(sizes, prop, operator, n):
@@ -84,9 +82,9 @@
     block = jax.ShapeDtypeStruct((states // n, states), jnp.bfloat16)
     return pl.pallas_call(
         prepare_kernel,
-        out_shape=(square,) * 3 + (block,) * n,
+        out_shape=(square,) * 2 + (block,) * n,
         in_specs=[SMEM, VMEM, VMEM],
-        out_specs=(VMEM,) * (3 + n),
+        out_specs=(VMEM,) * (2 + n),
         scratch_shapes=[pltpu.VMEM((states, states), jnp.bfloat16)],
         cost_estimate=pl.CostEstimate(
             flops=4 * states**3, bytes_accessed=12 * states**2, transcendentals=0
@@ -96,7 +94,7 @@
 
 
 def energy_kernel(sizes, particle, hole, *refs):
-    sources, (*outs,), copies, sems = refs[:4], refs[4:-5], refs[-5:-1], refs[-1]
+    sources, (*outs,), copies, lowered, sems = refs[:3], refs[3:-5], refs[-5:-2], refs[-2], refs[-1]
     moves = [
         pltpu.make_async_copy(src, dst, sems.at[i])
         for i, (src, dst) in enumerate(zip(sources, copies))
@@ -108,35 +106,36 @@
     here_x = lax.axis_index("tx")
     for move in moves:
         move.wait()
-    flipped, above, operator, below = copies
-    inner = above[...]
+    above, operator, below = copies
     r = operator[...]
+    lowered[...] = lax.dot_general(
+        r, above[...], (((0,), (0,)), ((), ())), preferred_element_type=jnp.float32
+    ).astype(jnp.bfloat16)
     for d in (2, 1, 3, 0):
         first = pl.multiple_of(lax.rem(here_x + d, n) * rows, 32)
-        lowered = dot(flipped[pl.ds(first, rows), :], inner).astype(jnp.bfloat16)
-        downward = dot(lowered, r)
+        downward = dot(lowered[pl.ds(first, rows), :], r)
         raised = below[pl.ds(first, rows), :].astype(jnp.float32)
         both = particle[0] * raised + hole[0] * downward
         kept = live(both.shape, sizes[0], first)
         outs[d][...] = jnp.where(kept, both, 0.0).astype(jnp.bfloat16)
 
 
-def energy_blocks(sizes, particle, hole, above, below, operator, flipped, n):
+def energy_blocks(sizes, particle, hole, above, below, operator, n):
     states = above.shape[0]
     block = jax.ShapeDtypeStruct((states // n, states), jnp.bfloat16)
     return pl.pallas_call(
         energy_kernel,
         out_shape=(block,) * n,
-        in_specs=[SMEM] * 3 + [ANY] * 4,
+        in_specs=[SMEM] * 3 + [ANY] * 3,
         out_specs=(VMEM,) * n,
         scratch_shapes=[pltpu.VMEM((states, states), jnp.bfloat16)] * 4
-        + [pltpu.SemaphoreType.DMA((4,))],
+        + [pltpu.SemaphoreType.DMA((3,))],
         cost_estimate=pl.CostEstimate(
-            flops=4 * states**3, bytes_accessed=10 * states**2, transcendentals=0
+            flops=4 * states**3, bytes_accessed=8 * states**2, transcendentals=0
         ),
         compiler_params=pltpu.CompilerParams(vmem_limit_bytes=16 * MIB),
         name="energy_blocks",
-    )(sizes, particle, hole, flipped, above, operator, below)
+    )(sizes, particle, hole, above, operator, below)
 
 
 def around(here, offset, n):
@@ -256,7 +255,7 @@
     here_x = lax.axis_index("tx")
     operator = rising_op[0]
 
-    masked, upward, flipped, own_g, *away_g = prepare(
+    masked, upward, own_g, *away_g = prepare(
         sector_sizes, propagator[0, 0], operator, n
     )
     below = shifted(upward, "sector", 1)
@@ -265,7 +264,7 @@
     columns = jnp.stack([own_g] + [crossed_g[d] for d in range(1, n)])
 
     own_e, *away_e = energy_blocks(
-        sector_sizes, hyb_particle, hyb_hole, above, below, operator, flipped, n
+        sector_sizes, hyb_particle, hyb_hole, above, below, operator, n
     )
     crossed_e = {d: ring(away_e[d - 1], "tx", d) for d in (2, 1, 3)}
     lines = jnp.stack([own_e] + [crossed_e[d] for d in range(1, n)])

time: 104 us -> 103 us (level)
  local copies, waits for them, and re-layouts: 1.34 us -> 0.2 us
    unnamed x8 -> x6, local copies, waits for them, and re-layouts: 1.16 us -> 0.01 us
where the time goes in v12:
time: 103 us; the launch traced here: 102 us
  waiting for transfers between devices  41.6 us (40%)
  starting transfers between devices  22.3 us (22%)
  Pallas kernels  19.9 us (19%)
  blocking collectives  16.2 us (16%)
  between operations  2.06 us (2%)
    ppermute x6, waiting for transfers between devices, turned_ring(): return lax.ppermute(block, (axis, 'sector'), route)  29.3 us
    all_to_all x1, blocking collectives, per_device(): packets = lax.all_to_all(packets, ('tx', 'ty'), 0, 0, tiled=True)  16.2 us
    ppermute x6, starting transfers between devices, ring(): lax.ppermute(block, axis, [(i, (i + distance) % n) for i in range(n)])  11.6 us
    pallas_call x1, Pallas kernels, convolve(): pl.pallas_call(functools.partial(convolve_kernel, plan, n, step_size), ou...  10.6 us
    ppermute x6, waiting for transfers between devices, ring(): lax.ppermute(block, axis, [(i, (i + distance) % n) for i in range(n)])  8.02 us
    ppermute x6, starting transfers between devices, turned_ring(): return lax.ppermute(block, (axis, 'sector'), route)  6.33 us
    pallas_call x1, Pallas kernels, prepare(): pl.pallas_call(prepare_kernel, out_shape=(square,) * 2 + (block,) * n, in...  4.48 us
    ppermute x2, starting transfers between devices, shifted(): return lax.ppermute(block, axis, route)  4.31 us
  transfers between devices with their start and end apart: 14, of which 9 were waited for; matrix products, arithmetic and copies ran while one was open for 0% of the time, Pallas kernels for 2%

profile of v12, /device:TPU:32, one launch (start us, length us, event | category | flops | bytes accessed | tf_op | source)
XLA Modules:
  0.0 102.4 jit_solution(4524558603631779452)
XLA Ops:
  0.0 0.0 copy-start
  0.7 0.0 copy-start.1
  0.7 4.5 %prepare.1 = (bf16[640,640]{1,0:T(8,128)(2,1)}, bf16[640,640]{1,0:T(8,128)(2,1)}, bf16[160,640]{1,0:T(8,128)(2,1)}, bf16[160,640]{1,0:T(8,128)(2,1)}, bf16[160,6...) custom-call(s32[1]{0:T(128)S(6)} %copy.10.sizes, bf16[640,640]{1,0:T(8,128)(2,1)} %bitcast.23, bf16[640,640]{1,0:T(8,128)(2,1)} %bitcast.14), custom_call_target="tpu_custom_call" | custom-call | flops 1048576000 | bytes 4915200 | tf_op jit(solution)/shard_map/prepare/pallas_call | solution.py:83
  5.2 1.9 %collective-permute-start = (bf16[640,640]{1,0:T(8,128)(2,1)}, bf16[640,640]{1,0:T(8,128)(2,1)S(1)}, u32[]{:S(2)}, u32[]{:S(2)}) collective-permute-start(bf16[640,640]{1,0:T(8,128)(2,1)} %get-tuple-element.15), channel_id=1, source_target_pairs={{1,0},{2,1},{3,2},{4,3},{5,4},{6,5},{7,6},{9,8},{10,9},{11,10},{12... | collective-permute-start | bytes 2457608 | tf_op jit(solution)/shard_map/ppermute | solution.py:22
  7.1 2.4 %collective-permute-start.1 = (bf16[640,640]{1,0:T(8,128)(2,1)}, bf16[640,640]{1,0:T(8,128)(2,1)S(1)}, u32[]{:S(2)}, u32[]{:S(2)}) collective-permute-start(bf16[640,640]{1,0:T(8,128)(2,1)} %get-tuple-element.16), channel_id=1, source_target_pairs={{0,1},{1,2},{2,3},{3,4},{4,5},{5,6},{6,7},{8,9},{9,10},{10,11},{11... | collective-permute-start | bytes 2457608 | tf_op jit(solution)/shard_map/ppermute | solution.py:22
  9.5 1.7 %collective-permute-start.8 = (bf16[160,640]{1,0:T(8,128)(2,1)}, bf16[160,640]{1,0:T(8,128)(2,1)S(1)}, u32[]{:S(2)}, u32[]{:S(2)}) collective-permute-start(bf16[160,640]{1,0:T(8,128)(2,1)} %get-tuple-element.22), channel_id=1, source_target_pairs={{0,8},{8,16},{16,24},{24,0},{1,9},{9,17},{17,25},{25,1},{2,10},{10... | collective-permute-start | bytes 614408 | tf_op jit(solution)/shard_map/ppermute | solution.py:27
  11.2 2.9 %collective-permute-start.9 = (bf16[160,640]{1,0:T(8,128)(2,1)}, bf16[160,640]{1,0:T(8,128)(2,1)S(1)}, u32[]{:S(2)}, u32[]{:S(2)}) collective-permute-start(bf16[160,640]{1,0:T(8,128)(2,1)} %get-tuple-element.23), channel_id=1, source_target_pairs={{0,16},{8,24},{16,0},{24,8},{1,17},{9,25},{17,1},{25,9},{2,18},{10... | collective-permute-start | bytes 614408 | tf_op jit(solution)/shard_map/ppermute | solution.py:27
  14.0 1.3 %collective-permute-start.10 = (bf16[160,640]{1,0:T(8,128)(2,1)}, bf16[160,640]{1,0:T(8,128)(2,1)S(1)}, u32[]{:S(2)}, u32[]{:S(2)}) collective-permute-start(bf16[160,640]{1,0:T(8,128)(2,1)} %get-tuple-element.24), channel_id=1, source_target_pairs={{0,24},{8,0},{16,8},{24,16},{1,25},{9,1},{17,9},{25,17},{2,26},{10... | collective-permute-start | bytes 614408 | tf_op jit(solution)/shard_map/ppermute | solution.py:27
  16.7 0.0 copy-start.2
  16.7 0.5 collective-permute-done.refs_0_
  17.2 3.7 %collective-permute-done.1.refs_2_ = bf16[640,640]{1,0:T(8,128)(2,1)S(1)} collective-permute-done((bf16[640,640]{1,0:T(8,128)(2,1)}, bf16[640,640]{1,0:T(8,128)(2,1)S(1)}, u32[]{:S(2)}, u32[]{:S(2)}) %collective-permute-start.1) | collective-permute-done | bytes 819232 | tf_op jit(solution)/shard_map/ppermute | solution.py:22
  20.9 0.0 copy-done.1
  21.0 2.3 %energy_blocks.1 = (bf16[160,640]{1,0:T(8,128)(2,1)S(1)}, bf16[160,640]{1,0:T(8,128)(2,1)S(1)}, bf16[160,640]{1,0:T(8,128)(2,1)S(1)}, bf16[160,640]{1,0:T(8,128)(2,1)S(1)}) custom-call(s32[1]{0:T(128)S(6)} %copy.10.sizes, f32[1]{0:T(128)S(6)} %copy.8.particle, f32[1]{0:T(128)S(6)} %copy.9.hole, bf16[640,640]{1,0:T(8,128)(2,1)S(1)} %collective-permute-done.refs_0_, ...), custom_call_target="tpu_custom_call" | custom-call | flops 1048576000 | bytes 3276800 | tf_op jit(solution)/shard_map/energy_blocks/pallas_call | solution.py:126
  23.3 1.6 %collective-permute-start.2 = (bf16[160,640]{1,0:T(8,128)(2,1)S(1)}, bf16[160,640]{1,0:T(8,128)(2,1)S(1)}, u32[]{:S(2)}, u32[]{:S(2)}) collective-permute-start(bf16[160,640]{1,0:T(8,128)(2,1)S(1)} %get-tuple-element.18), channel_id=1, source_target_pairs={{0,32},{32,64},{64,96},{96,0},{1,33},{33,65},{65,97},{97,1},{2,34}... | collective-permute-start | bytes 614408 | tf_op jit(solution)/shard_map/ppermute | solution.py:27
  24.9 2.7 %collective-permute-start.3 = (bf16[160,640]{1,0:T(8,128)(2,1)S(1)}, bf16[160,640]{1,0:T(8,128)(2,1)S(1)}, u32[]{:S(2)}, u32[]{:S(2)}) collective-permute-start(bf16[160,640]{1,0:T(8,128)(2,1)S(1)} %get-tuple-element.19), channel_id=1, source_target_pairs={{0,64},{32,96},{64,0},{96,32},{1,65},{33,97},{65,1},{97,33},{2,66}... | collective-permute-start | bytes 614408 | tf_op jit(solution)/shard_map/ppermute | solution.py:27
  27.6 0.0 collective-permute-done.8
  27.6 1.4 %collective-permute-start.4 = (bf16[160,640]{1,0:T(8,128)(2,1)S(1)}, bf16[160,640]{1,0:T(8,128)(2,1)S(1)}, u32[]{:S(2)}, u32[]{:S(2)}) collective-permute-start(bf16[160,640]{1,0:T(8,128)(2,1)S(1)} %get-tuple-element.20), channel_id=1, source_target_pairs={{0,96},{32,0},{64,32},{96,64},{1,97},{33,1},{65,33},{97,65},{2,98}... | collective-permute-start | bytes 614408 | tf_op jit(solution)/shard_map/ppermute | solution.py:27
  29.0 0.0 collective-permute-done.9
  29.0 0.0 collective-permute-done.10
  29.0 0.0 copy-done.2
  29.0 0.1 pad_maximum_fusion.1.refs_4_
  29.2 0.7 collective-permute-start.11
  29.8 1.8 %collective-permute-done.2 = bf16[160,640]{1,0:T(8,128)(2,1)S(1)} collective-permute-done((bf16[160,640]{1,0:T(8,128)(2,1)S(1)}, bf16[160,640]{1,0:T(8,128)(2,1)S(1)}, u32[]{:S(2)}, u32[]{:S(2)}) %collective-permute-start.2) | collective-permute-done | bytes 204832 | tf_op jit(solution)/shard_map/ppermute | solution.py:27
  31.6 5.1 %collective-permute-done.3 = bf16[160,640]{1,0:T(8,128)(2,1)S(1)} collective-permute-done((bf16[160,640]{1,0:T(8,128)(2,1)S(1)}, bf16[160,640]{1,0:T(8,128)(2,1)S(1)}, u32[]{:S(2)}, u32[]{:S(2)}) %collective-permute-start.3) | collective-permute-done | bytes 204832 | tf_op jit(solution)/shard_map/ppermute | solution.py:27
  36.7 1.1 %collective-permute-done.4 = bf16[160,640]{1,0:T(8,128)(2,1)S(1)} collective-permute-done((bf16[160,640]{1,0:T(8,128)(2,1)S(1)}, bf16[160,640]{1,0:T(8,128)(2,1)S(1)}, u32[]{:S(2)}, u32[]{:S(2)}) %collective-permute-start.4) | collective-permute-done | bytes 204832 | tf_op jit(solution)/shard_map/ppermute | solution.py:27
  37.8 0.1 pad_maximum_fusion.refs_0_
  38.0 1.7 %collective-permute-start.5 = (bf16[4,160,640]{2,1,0:T(8,128)(2,1)S(1)}, bf16[4,160,640]{2,1,0:T(8,128)(2,1)S(1)}, u32[]{:S(2)}, u32[]{:S(2)}) collective-permute-start(bf16[4,160,640]{2,1,0:T(8,128)(2,1)S(1)} %pad_maximum_fusion.refs_0_), channel_id=1, source_target_pairs={{0,8},{1,25},{2,10},{3,27},{4,12},{5,29},{6,14},{7,31},{8,16},{9,1... | collective-permute-start | bytes 2457608 | tf_op jit(solution)/shard_map/ppermute | solution.py:41
  39.6 1.6 %collective-permute-start.12 = (bf16[4,160,640]{2,1,0:T(8,128)(2,1)S(1)}, bf16[4,160,640]{2,1,0:T(8,128)(2,1)}, u32[]{:S(2)}, u32[]{:S(2)}) collective-permute-start(bf16[4,160,640]{2,1,0:T(8,128)(2,1)S(1)} %pad_maximum_fusion.1.refs_4_), channel_id=1, source_target_pairs={{0,96},{1,33},{2,98},{3,35},{4,100},{5,37},{6,102},{7,39},{32,0},{... | collective-permute-start | bytes 2457608 | tf_op jit(solution)/shard_map/ppermute | solution.py:41
  41.2 1.6 %collective-permute-start.6 = (bf16[4,160,640]{2,1,0:T(8,128)(2,1)S(1)}, bf16[4,160,640]{2,1,0:T(8,128)(2,1)}, u32[]{:S(2)}, u32[]{:S(2)}) collective-permute-start(bf16[4,160,640]{2,1,0:T(8,128)(2,1)S(1)} %pad_maximum_fusion.refs_0_), channel_id=1, source_target_pairs={{0,24},{1,9},{2,26},{3,11},{4,28},{5,13},{6,30},{7,15},{8,0},{9,17... | collective-permute-start | bytes 2457608 | tf_op jit(solution)/shard_map/ppermute | solution.py:41
  42.8 5.6 %collective-permute-done.11.refs_5_ = bf16[4,160,640]{2,1,0:T(8,128)(2,1)S(1)} collective-permute-done((bf16[4,160,640]{2,1,0:T(8,128)(2,1)S(1)}, bf16[4,160,640]{2,1,0:T(8,128)(2,1)S(1)}, u32[]{:S(2)}, u32[]{:S(2)}) %collective-permute-start.11) | collective-permute-done | bytes 819232 | tf_op jit(solution)/shard_map/ppermute | solution.py:41
  48.5 0.0 collective-permute-start.13
  48.5 11.0 %collective-permute-done.5.refs_1_ = bf16[4,160,640]{2,1,0:T(8,128)(2,1)S(1)} collective-permute-done((bf16[4,160,640]{2,1,0:T(8,128)(2,1)S(1)}, bf16[4,160,640]{2,1,0:T(8,128)(2,1)S(1)}, u32[]{:S(2)}, u32[]{:S(2)}) %collective-permute-start.5) | collective-permute-done | bytes 819232 | tf_op jit(solution)/shard_map/ppermute | solution.py:41
  59.5 0.8 collective-permute-start.7
  60.3 0.0 copy-done
  60.3 0.1 dynamic-slice_bitcast_fusion
  60.4 0.1 copy.7.rates
  60.5 0.0 collective-permute-done.12.refs_6_
  60.5 2.5 %collective-permute-done.13.refs_7_ = bf16[4,160,640]{2,1,0:T(8,128)(2,1)} collective-permute-done((bf16[4,160,640]{2,1,0:T(8,128)(2,1)S(1)}, bf16[4,160,640]{2,1,0:T(8,128)(2,1)}, u32[]{:S(2)}, u32[]{:S(2)}) %collective-permute-start.13) | collective-permute-done | bytes 819232 | tf_op jit(solution)/shard_map/ppermute | solution.py:41
  63.0 0.0 collective-permute-done.6.refs_2_
  63.0 10.1 %collective-permute-done.7.refs_3_ = bf16[4,160,640]{2,1,0:T(8,128)(2,1)} collective-permute-done((bf16[4,160,640]{2,1,0:T(8,128)(2,1)S(1)}, bf16[4,160,640]{2,1,0:T(8,128)(2,1)}, u32[]{:S(2)}, u32[]{:S(2)}) %collective-permute-start.7) | collective-permute-done | bytes 819232 | tf_op jit(solution)/shard_map/ppermute | solution.py:41
  73.2 10.6 %convolve.1 = bf16[16,40,640]{2,1,0:T(8,128)(2,1)S(1)} custom-call(s32[1]{0:T(128)S(6)} %copy.10.sizes, f32[160,1]{1,0:T(8,128)S(1)} %copy.7.rates, bf16[4,160,640]{2,1,0:T(8,128)(2,1)S(1)} %pad_maximum_fusion.refs_0_, bf16[4,160,640]{2,1,0:T(8,128)(2,1)S(1)} %collective-permute-done.5.refs_1_, bf16[4,160,640]{2,1,0:T(8,128)(2,1)} %collective-permute-done.6.refs_2_, ...), custom_call_target="tpu_custom_call" | custom-call | flops 4456448000 | bytes 6553600 | tf_op jit(solution)/shard_map/convolve/pallas_call | solution.py:208
  83.8 16.2 %all_to_all.5.packets = bf16[16,40,640]{2,1,0:T(8,128)(2,1)} all-to-all(bf16[16,40,640]{2,1,0:T(8,128)(2,1)S(1)} %convolve.1), channel_id=1, replica_groups=mesh['tx'=4,'ty'=4,'sector'=8] {'tx','ty'}, dimensions={0} | all-to-all | bytes 1638400 | tf_op jit(solution)/shard_map/all_to_all | solution.py:276
  100.0 2.4 %assemble.1 = bf16[640,640]{1,0:T(8,128)(2,1)} custom-call(bf16[16,40,640]{2,1,0:T(8,128)(2,1)} %all_to_all.5.packets), custom_call_target="tpu_custom_call" | custom-call | tf_op jit(solution)/shard_map/assemble/pallas_call | solution.py:241
Async XLA Ops:
  0.0 60.3 %copy-start = (f32[1,640]{1,0:T(1,128)S(1)}, f32[1,640]{1,0:T(1,128)}, u32[]{:S(2)}) copy-start(f32[1,640]{1,0:T(1,128)} %param.8) | copy-start | bytes 7684
  0.7 20.3 %copy-start.1 = (bf16[1,640,640]{2,1,0:T(8,128)(2,1)S(1)}, bf16[1,640,640]{2,1,0:T(8,128)(2,1)}, u32[]{:S(2)}) copy-start(bf16[1,640,640]{2,1,0:T(8,128)(2,1)} %param.7) | copy-start | bytes 2457604
  5.2 12.1 %collective-permute-start = (bf16[640,640]{1,0:T(8,128)(2,1)}, bf16[640,640]{1,0:T(8,128)(2,1)S(1)}, u32[]{:S(2)}, u32[]{:S(2)}) collective-permute-start(bf16[640,640]{1,0:T(8,128)(2,1)} %get-tuple-element.15), channel_id=1, source_target_pairs={{1,0},{2,1},{3,2},{4,3},{5,4},{6,5},{7,6},{9,8},{10,9},{11,10},{12... | collective-permute-start | bytes 2457608 | tf_op jit(solution)/shard_map/ppermute | solution.py:22
  7.1 13.9 %collective-permute-start.1 = (bf16[640,640]{1,0:T(8,128)(2,1)}, bf16[640,640]{1,0:T(8,128)(2,1)S(1)}, u32[]{:S(2)}, u32[]{:S(2)}) collective-permute-start(bf16[640,640]{1,0:T(8,128)(2,1)} %get-tuple-element.16), channel_id=1, source_target_pairs={{0,1},{1,2},{2,3},{3,4},{4,5},{5,6},{6,7},{8,9},{9,10},{10,11},{11... | collective-permute-start | bytes 2457608 | tf_op jit(solution)/shard_map/ppermute | solution.py:22
  9.5 18.1 %collective-permute-start.8 = (bf16[160,640]{1,0:T(8,128)(2,1)}, bf16[160,640]{1,0:T(8,128)(2,1)S(1)}, u32[]{:S(2)}, u32[]{:S(2)}) collective-permute-start(bf16[160,640]{1,0:T(8,128)(2,1)} %get-tuple-element.22), channel_id=1, source_target_pairs={{0,8},{8,16},{16,24},{24,0},{1,9},{9,17},{17,25},{25,1},{2,10},{10... | collective-permute-start | bytes 614408 | tf_op jit(solution)/shard_map/ppermute | solution.py:27
  11.2 17.9 %collective-permute-start.9 = (bf16[160,640]{1,0:T(8,128)(2,1)}, bf16[160,640]{1,0:T(8,128)(2,1)S(1)}, u32[]{:S(2)}, u32[]{:S(2)}) collective-permute-start(bf16[160,640]{1,0:T(8,128)(2,1)} %get-tuple-element.23), channel_id=1, source_target_pairs={{0,16},{8,24},{16,0},{24,8},{1,17},{9,25},{17,1},{25,9},{2,18},{10... | collective-permute-start | bytes 614408 | tf_op jit(solution)/shard_map/ppermute | solution.py:27
  14.0 15.0 %collective-permute-start.10 = (bf16[160,640]{1,0:T(8,128)(2,1)}, bf16[160,640]{1,0:T(8,128)(2,1)S(1)}, u32[]{:S(2)}, u32[]{:S(2)}) collective-permute-start(bf16[160,640]{1,0:T(8,128)(2,1)} %get-tuple-element.24), channel_id=1, source_target_pairs={{0,24},{8,0},{16,8},{24,16},{1,25},{9,1},{17,9},{25,17},{2,26},{10... | collective-permute-start | bytes 614408 | tf_op jit(solution)/shard_map/ppermute | solution.py:27
  16.7 12.3 %copy-start.2 = (bf16[160,640]{1,0:T(8,128)(2,1)S(1)}, bf16[160,640]{1,0:T(8,128)(2,1)}, u32[]{:S(2)}) copy-start(bf16[160,640]{1,0:T(8,128)(2,1)} %get-tuple-element.21) | copy-start | bytes 614404
  23.3 8.3 %collective-permute-start.2 = (bf16[160,640]{1,0:T(8,128)(2,1)S(1)}, bf16[160,640]{1,0:T(8,128)(2,1)S(1)}, u32[]{:S(2)}, u32[]{:S(2)}) collective-permute-start(bf16[160,640]{1,0:T(8,128)(2,1)S(1)} %get-tuple-element.18), channel_id=1, source_target_pairs={{0,32},{32,64},{64,96},{96,0},{1,33},{33,65},{65,97},{97,1},{2,34}... | collective-permute-start | bytes 614408 | tf_op jit(solution)/shard_map/ppermute | solution.py:27
  24.9 11.8 %collective-permute-start.3 = (bf16[160,640]{1,0:T(8,128)(2,1)S(1)}, bf16[160,640]{1,0:T(8,128)(2,1)S(1)}, u32[]{:S(2)}, u32[]{:S(2)}) collective-permute-start(bf16[160,640]{1,0:T(8,128)(2,1)S(1)} %get-tuple-element.19), channel_id=1, source_target_pairs={{0,64},{32,96},{64,0},{96,32},{1,65},{33,97},{65,1},{97,33},{2,66}... | collective-permute-start | bytes 614408 | tf_op jit(solution)/shard_map/ppermute | solution.py:27
  27.6 10.2 %collective-permute-start.4 = (bf16[160,640]{1,0:T(8,128)(2,1)S(1)}, bf16[160,640]{1,0:T(8,128)(2,1)S(1)}, u32[]{:S(2)}, u32[]{:S(2)}) collective-permute-start(bf16[160,640]{1,0:T(8,128)(2,1)S(1)} %get-tuple-element.20), channel_id=1, source_target_pairs={{0,96},{32,0},{64,32},{96,64},{1,97},{33,1},{65,33},{97,65},{2,98}... | collective-permute-start | bytes 614408 | tf_op jit(solution)/shard_map/ppermute | solution.py:27
  29.2 19.3 %collective-permute-start.11 = (bf16[4,160,640]{2,1,0:T(8,128)(2,1)S(1)}, bf16[4,160,640]{2,1,0:T(8,128)(2,1)S(1)}, u32[]{:S(2)}, u32[]{:S(2)}) collective-permute-start(bf16[4,160,640]{2,1,0:T(8,128)(2,1)S(1)} %pad_maximum_fusion.1.refs_4_), channel_id=1, source_target_pairs={{0,32},{1,97},{2,34},{3,99},{4,36},{5,101},{6,38},{7,103},{32,64},... | collective-permute-start | bytes 2457608 | tf_op jit(solution)/shard_map/ppermute | solution.py:41
  38.0 21.5 %collective-permute-start.5 = (bf16[4,160,640]{2,1,0:T(8,128)(2,1)S(1)}, bf16[4,160,640]{2,1,0:T(8,128)(2,1)S(1)}, u32[]{:S(2)}, u32[]{:S(2)}) collective-permute-start(bf16[4,160,640]{2,1,0:T(8,128)(2,1)S(1)} %pad_maximum_fusion.refs_0_), channel_id=1, source_target_pairs={{0,8},{1,25},{2,10},{3,27},{4,12},{5,29},{6,14},{7,31},{8,16},{9,1... | collective-permute-start | bytes 2457608 | tf_op jit(solution)/shard_map/ppermute | solution.py:41
  39.6 20.9 %collective-permute-start.12 = (bf16[4,160,640]{2,1,0:T(8,128)(2,1)S(1)}, bf16[4,160,640]{2,1,0:T(8,128)(2,1)}, u32[]{:S(2)}, u32[]{:S(2)}) collective-permute-start(bf16[4,160,640]{2,1,0:T(8,128)(2,1)S(1)} %pad_maximum_fusion.1.refs_4_), channel_id=1, source_target_pairs={{0,96},{1,33},{2,98},{3,35},{4,100},{5,37},{6,102},{7,39},{32,0},{... | collective-permute-start | bytes 2457608 | tf_op jit(solution)/shard_map/ppermute | solution.py:41
  41.2 21.8 %collective-permute-start.6 = (bf16[4,160,640]{2,1,0:T(8,128)(2,1)S(1)}, bf16[4,160,640]{2,1,0:T(8,128)(2,1)}, u32[]{:S(2)}, u32[]{:S(2)}) collective-permute-start(bf16[4,160,640]{2,1,0:T(8,128)(2,1)S(1)} %pad_maximum_fusion.refs_0_), channel_id=1, source_target_pairs={{0,24},{1,9},{2,26},{3,11},{4,28},{5,13},{6,30},{7,15},{8,0},{9,17... | collective-permute-start | bytes 2457608 | tf_op jit(solution)/shard_map/ppermute | solution.py:41
  48.5 14.6 %collective-permute-start.13 = (bf16[4,160,640]{2,1,0:T(8,128)(2,1)S(1)}, bf16[4,160,640]{2,1,0:T(8,128)(2,1)}, u32[]{:S(2)}, u32[]{:S(2)}) collective-permute-start(bf16[4,160,640]{2,1,0:T(8,128)(2,1)S(1)} %collective-permute-done.11.refs_5_), channel_id=1, source_target_pairs={{0,32},{1,97},{2,34},{3,99},{4,36},{5,101},{6,38},{7,103},{32,64},... | collective-permute-start | bytes 2457608 | tf_op jit(solution)/shard_map/ppermute | solution.py:41
  59.5 13.7 %collective-permute-start.7 = (bf16[4,160,640]{2,1,0:T(8,128)(2,1)S(1)}, bf16[4,160,640]{2,1,0:T(8,128)(2,1)}, u32[]{:S(2)}, u32[]{:S(2)}) collective-permute-start(bf16[4,160,640]{2,1,0:T(8,128)(2,1)S(1)} %collective-permute-done.5.refs_1_), channel_id=1, source_target_pairs={{0,8},{1,25},{2,10},{3,27},{4,12},{5,29},{6,14},{7,31},{8,16},{9,1... | collective-permute-start | bytes 2457608 | tf_op jit(solution)/shard_map/ppermute | solution.py:41

commit v13 on v12

--- a/solution.py
+++ b/solution.py
@@ -39,12 +39,6 @@
             step = distance if s % 2 == 0 else -distance
             route.append((i * sectors + s, (i + step) % n * sectors + s))
     return lax.ppermute(block, (axis, "sector"), route)
-
-
-def ring_gather(block, axis):
-    before = turned_ring(block, axis, 1)
-    after = turned_ring(block, axis, -1)
-    return [(0, block), (-1, before), (1, after), (2, turned_ring(before, axis, 1))]
 
 
 def live(shape, size, first_row=0):
@@ -149,16 +143,17 @@
     here_x, here_y, size = lax.axis_index("tx"), lax.axis_index("ty"), sizes[0]
     sign = turn_sign()
     copies_e, copies_g = [], []
-    for part, (kind, step) in zip(parts, plan):
-        for d in range(n):
+    for part, (kind, step, crossed) in zip(parts, plan):
+        for k in range(part.shape[0]):
+            d = crossed + k
             if kind == "e":
                 lag = n * around(here_x, -d, n) + around(here_y, sign * step, n)
                 left = pl.multiple_of((n * n - 1 - lag) * states, 128)
-                copies_e.append((part.at[d], e_all.at[:, pl.ds(left, states)]))
+                copies_e.append((part.at[k], e_all.at[:, pl.ds(left, states)]))
             else:
                 u = n * around(here_x, sign * step, n) + around(here_y, -d, n)
                 left = pl.multiple_of(lax.rem(u, 2) * states, 128)
-                copies_g.append((part.at[d], g_all.at[u // 2, :, pl.ds(left, states)]))
+                copies_g.append((part.at[k], g_all.at[u // 2, :, pl.ds(left, states)]))
     moves = [
         pltpu.make_async_copy(src, dst, sems.at[i])
         for i, (src, dst) in enumerate(copies_e + copies_g)
@@ -202,9 +197,9 @@
 
 
 def convolve(entries, sizes, rates, n, step_size):
-    plan, parts = [e[:2] for e in entries], [e[2] for e in entries]
+    plan, parts = [e[:3] for e in entries], [e[3] for e in entries]
     _, rows, states = parts[0].shape
-    copies = n * len(parts)
+    copies = sum(part.shape[0] for part in parts)
     return pl.pallas_call(
         functools.partial(convolve_kernel, plan, n, step_size),
         out_shape=jax.ShapeDtypeStruct((n * n, rows // n, states), jnp.bfloat16),
@@ -267,10 +262,23 @@
         sector_sizes, hyb_particle, hyb_hole, above, below, operator, n
     )
     crossed_e = {d: ring(away_e[d - 1], "tx", d) for d in (2, 1, 3)}
-    lines = jnp.stack([own_e] + [crossed_e[d] for d in range(1, n)])
-
-    entries = [("g", step, part) for step, part in ring_gather(columns, "tx")]
-    entries = [("e", step, part) for step, part in ring_gather(lines, "ty")] + entries
+    before_g = turned_ring(columns, "tx", 1)
+    after_g = turned_ring(columns, "tx", -1)
+    far_g = turned_ring(before_g, "tx", 1)
+
+    blocks = [own_e] + [crossed_e[d] for d in range(1, n)]
+    halves = [jnp.stack(blocks[: n // 2]), jnp.stack(blocks[n // 2 :])]
+    before_e = [turned_ring(half, "ty", 1) for half in halves]
+    lines = jnp.stack(blocks)
+    after_e = turned_ring(lines, "ty", -1)
+    far_e = [turned_ring(half, "ty", 1) for half in before_e]
+    entries = [("e", 0, 0, lines), ("e", 1, 0, after_e)]
+    for k in range(2):
+        entries += [("e", -1, k * n // 2, before_e[k]), ("e", 2, k * n // 2, far_e[k])]
+    entries += [
+        ("g", step, 0, part)
+        for step, part in zip((0, -1, 1, 2), (columns, before_g, after_g, far_g))
+    ]
     rates = lax.dynamic_slice_in_dim(energies[0], here_x * rows, rows, 0)[:, None]
     packets = convolve(entries, sector_sizes, rates, n, step_size)
     packets = lax.all_to_all(packets, ("tx", "ty"), 0, 0, tiled=True)

time: 103 us -> 109 us (1.058)
  starting transfers between devices: 22.3 us -> 29 us
  waiting for transfers between devices: 41.6 us -> 40.4 us
  other arithmetic: 0.25 us -> 1.35 us
    ppermute x6, waiting for transfers between devices: 8.02 us -> 23.8 us  [ring(): lax.ppermute(block, axis, [(i, (i + distance) % n) for i in range(n)])]
    ppermute x6 -> x8, waiting for transfers between devices: 29.3 us -> 16.5 us  [turned_ring(): return lax.ppermute(block, (axis, 'sector'), route)]
    ppermute x6 -> x8, starting transfers between devices: 6.33 us -> 13.4 us  [turned_ring(): return lax.ppermute(block, (axis, 'sector'), route)]
    ppermute x2, waiting for transfers between devices: 4.25 us -> 0.01 us  [shifted(): return lax.ppermute(block, axis, route)]
  transfers between devices with their start and end apart: 14 -> 16, of which waited for: 9 -> 8; matrix products, arithmetic and copies ran while one was open for 0% -> 1% of each run, Pallas kernels for 2% -> 2%
where the time goes in v13:
time: 109 us
  waiting for transfers between devices  40.4 us (37%)
  starting transfers between devices  29 us (27%)
  Pallas kernels  19.7 us (18%)
  blocking collectives  16.2 us (15%)
  between operations  2.08 us (2%)
  other arithmetic  1.35 us (1%)
    ppermute x6, waiting for transfers between devices, ring(): lax.ppermute(block, axis, [(i, (i + distance) % n) for i in range(n)])  23.8 us
    ppermute x8, waiting for transfers between devices, turned_ring(): return lax.ppermute(block, (axis, 'sector'), route)  16.5 us
    all_to_all x1, blocking collectives, per_device(): packets = lax.all_to_all(packets, ('tx', 'ty'), 0, 0, tiled=True)  16.2 us
    ppermute x8, starting transfers between devices, turned_ring(): return lax.ppermute(block, (axis, 'sector'), route)  13.4 us
    ppermute x6, starting transfers between devices, ring(): lax.ppermute(block, axis, [(i, (i + distance) % n) for i in range(n)])  11.3 us
    pallas_call x1, Pallas kernels, convolve(): pl.pallas_call(functools.partial(convolve_kernel, plan, n, step_size), ou...  10.5 us
    pallas_call x1, Pallas kernels, prepare(): pl.pallas_call(prepare_kernel, out_shape=(square,) * 2 + (block,) * n, in...  4.41 us
    ppermute x2, starting transfers between devices, shifted(): return lax.ppermute(block, axis, route)  4.31 us
  transfers between devices with their start and end apart: 16, of which 8 were waited for; matrix products, arithmetic and copies ran while one was open for 1% of the time, Pallas kernels for 2%

profile of v13, /device:TPU:32, one launch (start us, length us, event | category | flops | bytes accessed | tf_op | source)
XLA Modules:
  0.0 109.0 jit_solution(11103160298233416783)
XLA Ops:
  0.0 0.0 copy-start
  0.7 4.4 %prepare.1 = (bf16[640,640]{1,0:T(8,128)(2,1)}, bf16[640,640]{1,0:T(8,128)(2,1)}, bf16[160,640]{1,0:T(8,128)(2,1)}, bf16[160,640]{1,0:T(8,128)(2,1)}, bf16[160,6...) custom-call(s32[1]{0:T(128)S(6)} %copy.10.sizes, bf16[640,640]{1,0:T(8,128)(2,1)} %bitcast.27, bf16[640,640]{1,0:T(8,128)(2,1)} %bitcast.15), custom_call_target="tpu_custom_call" | custom-call | flops 1048576000 | bytes 4915200 | tf_op jit(solution)/shard_map/prepare/pallas_call | solution.py:77
  5.1 1.9 %collective-permute-start = (bf16[640,640]{1,0:T(8,128)(2,1)}, bf16[640,640]{1,0:T(8,128)(2,1)S(1)}, u32[]{:S(2)}, u32[]{:S(2)}) collective-permute-start(bf16[640,640]{1,0:T(8,128)(2,1)} %get-tuple-element.15), channel_id=1, source_target_pairs={{1,0},{2,1},{3,2},{4,3},{5,4},{6,5},{7,6},{9,8},{10,9},{11,10},{12... | collective-permute-start | bytes 2457608 | tf_op jit(solution)/shard_map/ppermute | solution.py:22
  7.0 2.4 %collective-permute-start.1 = (bf16[640,640]{1,0:T(8,128)(2,1)}, bf16[640,640]{1,0:T(8,128)(2,1)S(1)}, u32[]{:S(2)}, u32[]{:S(2)}) collective-permute-start(bf16[640,640]{1,0:T(8,128)(2,1)} %get-tuple-element.16), channel_id=1, source_target_pairs={{0,1},{1,2},{2,3},{3,4},{4,5},{5,6},{6,7},{8,9},{9,10},{10,11},{11... | collective-permute-start | bytes 2457608 | tf_op jit(solution)/shard_map/ppermute | solution.py:22
  9.4 1.6 %collective-permute-start.10 = (bf16[160,640]{1,0:T(8,128)(2,1)}, bf16[160,640]{1,0:T(8,128)(2,1)S(1)}, u32[]{:S(2)}, u32[]{:S(2)}) collective-permute-start(bf16[160,640]{1,0:T(8,128)(2,1)} %get-tuple-element.22), channel_id=1, source_target_pairs={{0,8},{8,16},{16,24},{24,0},{1,9},{9,17},{17,25},{25,1},{2,10},{10... | collective-permute-start | bytes 614408 | tf_op jit(solution)/shard_map/ppermute | solution.py:27
  11.1 2.9 %collective-permute-start.11 = (bf16[160,640]{1,0:T(8,128)(2,1)}, bf16[160,640]{1,0:T(8,128)(2,1)S(1)}, u32[]{:S(2)}, u32[]{:S(2)}) collective-permute-start(bf16[160,640]{1,0:T(8,128)(2,1)} %get-tuple-element.23), channel_id=1, source_target_pairs={{0,16},{8,24},{16,0},{24,8},{1,17},{9,25},{17,1},{25,9},{2,18},{10... | collective-permute-start | bytes 614408 | tf_op jit(solution)/shard_map/ppermute | solution.py:27
  14.0 1.3 %collective-permute-start.12 = (bf16[160,640]{1,0:T(8,128)(2,1)}, bf16[160,640]{1,0:T(8,128)(2,1)S(1)}, u32[]{:S(2)}, u32[]{:S(2)}) collective-permute-start(bf16[160,640]{1,0:T(8,128)(2,1)} %get-tuple-element.24), channel_id=1, source_target_pairs={{0,24},{8,0},{16,8},{24,16},{1,25},{9,1},{17,9},{25,17},{2,26},{10... | collective-permute-start | bytes 614408 | tf_op jit(solution)/shard_map/ppermute | solution.py:27
  15.3 3.0 %collective-permute-done.10 = bf16[160,640]{1,0:T(8,128)(2,1)S(1)} collective-permute-done((bf16[160,640]{1,0:T(8,128)(2,1)}, bf16[160,640]{1,0:T(8,128)(2,1)S(1)}, u32[]{:S(2)}, u32[]{:S(2)}) %collective-permute-start.10) | collective-permute-done | bytes 204832 | tf_op jit(solution)/shard_map/ppermute | solution.py:27
  18.3 5.7 %collective-permute-done.11 = bf16[160,640]{1,0:T(8,128)(2,1)S(1)} collective-permute-done((bf16[160,640]{1,0:T(8,128)(2,1)}, bf16[160,640]{1,0:T(8,128)(2,1)S(1)}, u32[]{:S(2)}, u32[]{:S(2)}) %collective-permute-start.11) | collective-permute-done | bytes 204832 | tf_op jit(solution)/shard_map/ppermute | solution.py:27
  24.0 0.0 collective-permute-done.12
  24.0 0.0 copy-start.1
  24.0 1.1 %pad_maximum_fusion.1.refs_6_ = bf16[4,160,640]{2,1,0:T(8,128)(2,1)S(1)} fusion(bf16[1,160,640]{2,1,0:T(8,128)(2,1)S(1)} %bitcast.26, bf16[1,160,640]{2,1,0:T(8,128)(2,1)S(1)} %bitcast.25, bf16[1,160,640]{2,1,0:T(8,128)(2,1)S(1)} %bitcast.24, bf16[1,160,640]{2,1,0:T(8,128)(2,1)} %bitcast.23), kind=kLoop, calls=%fused_computation.1 | loop fusion | flops 1228800 | bytes 1638400 | tf_op jit(solution)/shard_map/stack | solution.py:259
  25.1 1.6 %collective-permute-start.13 = (bf16[4,160,640]{2,1,0:T(8,128)(2,1)S(1)}, bf16[4,160,640]{2,1,0:T(8,128)(2,1)S(1)}, u32[]{:S(2)}, u32[]{:S(2)}) collective-permute-start(bf16[4,160,640]{2,1,0:T(8,128)(2,1)S(1)} %pad_maximum_fusion.1.refs_6_), channel_id=1, source_target_pairs={{0,32},{1,97},{2,34},{3,99},{4,36},{5,101},{6,38},{7,103},{32,64},... | collective-permute-start | bytes 2457608 | tf_op jit(solution)/shard_map/ppermute | solution.py:41
  28.0 0.0 collective-permute-done.refs_0_
  28.0 0.0 collective-permute-done.1.refs_2_
  28.0 0.0 copy-done.1
  28.0 2.3 %energy_blocks.1 = (bf16[160,640]{1,0:T(8,128)(2,1)S(1)}, bf16[160,640]{1,0:T(8,128)(2,1)S(1)}, bf16[160,640]{1,0:T(8,128)(2,1)S(1)}, bf16[160,640]{1,0:T(8,128)(2,1)S(1)}) custom-call(s32[1]{0:T(128)S(6)} %copy.10.sizes, f32[1]{0:T(128)S(6)} %copy.8.particle, f32[1]{0:T(128)S(6)} %copy.9.hole, bf16[640,640]{1,0:T(8,128)(2,1)S(1)} %collective-permute-done.refs_0_, ...), custom_call_target="tpu_custom_call" | custom-call | flops 1048576000 | bytes 3276800 | tf_op jit(solution)/shard_map/energy_blocks/pallas_call | solution.py:120
  30.4 1.6 %collective-permute-start.2 = (bf16[160,640]{1,0:T(8,128)(2,1)S(1)}, bf16[160,640]{1,0:T(8,128)(2,1)S(1)}, u32[]{:S(2)}, u32[]{:S(2)}) collective-permute-start(bf16[160,640]{1,0:T(8,128)(2,1)S(1)} %get-tuple-element.18), channel_id=1, source_target_pairs={{0,32},{32,64},{64,96},{96,0},{1,33},{33,65},{65,97},{97,1},{2,34}... | collective-permute-start | bytes 614408 | tf_op jit(solution)/shard_map/ppermute | solution.py:27
  31.9 1.7 %collective-permute-start.3 = (bf16[160,640]{1,0:T(8,128)(2,1)S(1)}, bf16[160,640]{1,0:T(8,128)(2,1)S(1)}, u32[]{:S(2)}, u32[]{:S(2)}) collective-permute-start(bf16[160,640]{1,0:T(8,128)(2,1)S(1)} %get-tuple-element.19), channel_id=1, source_target_pairs={{0,64},{32,96},{64,0},{96,32},{1,65},{33,97},{65,1},{97,33},{2,66}... | collective-permute-start | bytes 614408 | tf_op jit(solution)/shard_map/ppermute | solution.py:27
  33.6 2.2 %collective-permute-start.4 = (bf16[160,640]{1,0:T(8,128)(2,1)S(1)}, bf16[160,640]{1,0:T(8,128)(2,1)S(1)}, u32[]{:S(2)}, u32[]{:S(2)}) collective-permute-start(bf16[160,640]{1,0:T(8,128)(2,1)S(1)} %get-tuple-element.20), channel_id=1, source_target_pairs={{0,96},{32,0},{64,32},{96,64},{1,97},{33,1},{65,33},{97,65},{2,98}... | collective-permute-start | bytes 614408 | tf_op jit(solution)/shard_map/ppermute | solution.py:27
  35.8 0.2 collective-permute-start.14
  36.0 12.4 %collective-permute-done.2 = bf16[160,640]{1,0:T(8,128)(2,1)S(1)} collective-permute-done((bf16[160,640]{1,0:T(8,128)(2,1)S(1)}, bf16[160,640]{1,0:T(8,128)(2,1)S(1)}, u32[]{:S(2)}, u32[]{:S(2)}) %collective-permute-start.2) | collective-permute-done | bytes 204832 | tf_op jit(solution)/shard_map/ppermute | solution.py:27
  48.5 2.3 %collective-permute-start.6 = (bf16[2,160,640]{2,1,0:T(8,128)(2,1)S(1)}, bf16[2,160,640]{2,1,0:T(8,128)(2,1)}, u32[]{:S(2)}, u32[]{:S(2)}) collective-permute-start(bf16[2,160,640]{2,1,0:T(8,128)(2,1)S(1)} %pad_maximum_fusion.2), channel_id=1, source_target_pairs={{0,8},{1,25},{2,10},{3,27},{4,12},{5,29},{6,14},{7,31},{8,16},{9,1... | collective-permute-start | bytes 1228808 | tf_op jit(solution)/shard_map/ppermute | solution.py:41
  50.8 2.8 %collective-permute-done.3 = bf16[160,640]{1,0:T(8,128)(2,1)S(1)} collective-permute-done((bf16[160,640]{1,0:T(8,128)(2,1)S(1)}, bf16[160,640]{1,0:T(8,128)(2,1)S(1)}, u32[]{:S(2)}, u32[]{:S(2)}) %collective-permute-start.3) | collective-permute-done | bytes 204832 | tf_op jit(solution)/shard_map/ppermute | solution.py:27
  53.5 0.0 collective-permute-done.4
  53.6 2.3 %collective-permute-start.8 = (bf16[2,160,640]{2,1,0:T(8,128)(2,1)S(1)}, bf16[2,160,640]{2,1,0:T(8,128)(2,1)}, u32[]{:S(2)}, u32[]{:S(2)}) collective-permute-start(bf16[2,160,640]{2,1,0:T(8,128)(2,1)S(1)} %pad_maximum_fusion.3), channel_id=1, source_target_pairs={{0,8},{1,25},{2,10},{3,27},{4,12},{5,29},{6,14},{7,31},{8,16},{9,1... | collective-permute-start | bytes 1228808 | tf_op jit(solution)/shard_map/ppermute | solution.py:41
  55.9 0.0 collective-permute-done.13.refs_7_
  55.9 0.0 collective-permute-start.15
  55.9 0.1 pad_maximum_fusion.refs_0_
  56.0 1.8 %collective-permute-start.5 = (bf16[4,160,640]{2,1,0:T(8,128)(2,1)S(1)}, bf16[4,160,640]{2,1,0:T(8,128)(2,1)}, u32[]{:S(2)}, u32[]{:S(2)}) collective-permute-start(bf16[4,160,640]{2,1,0:T(8,128)(2,1)S(1)} %pad_maximum_fusion.refs_0_), channel_id=1, source_target_pairs={{0,24},{1,9},{2,26},{3,11},{4,28},{5,13},{6,30},{7,15},{8,0},{9,17... | collective-permute-start | bytes 2457608 | tf_op jit(solution)/shard_map/ppermute | solution.py:41
  57.9 0.9 collective-permute-done.6.refs_2_
  58.8 2.6 %collective-permute-start.7 = (bf16[2,160,640]{2,1,0:T(8,128)(2,1)}, bf16[2,160,640]{2,1,0:T(8,128)(2,1)}, u32[]{:S(2)}, u32[]{:S(2)}) collective-permute-start(bf16[2,160,640]{2,1,0:T(8,128)(2,1)} %collective-permute-done.6.refs_2_), channel_id=1, source_target_pairs={{0,8},{1,25},{2,10},{3,27},{4,12},{5,29},{6,14},{7,31},{8,16},{9,1... | collective-permute-start | bytes 1228808 | tf_op jit(solution)/shard_map/ppermute | solution.py:41
  61.4 6.2 %collective-permute-done.8.refs_4_ = bf16[2,160,640]{2,1,0:T(8,128)(2,1)} collective-permute-done((bf16[2,160,640]{2,1,0:T(8,128)(2,1)S(1)}, bf16[2,160,640]{2,1,0:T(8,128)(2,1)}, u32[]{:S(2)}, u32[]{:S(2)}) %collective-permute-start.8) | collective-permute-done | bytes 409632 | tf_op jit(solution)/shard_map/ppermute | solution.py:41
  67.6 2.6 %collective-permute-start.9 = (bf16[2,160,640]{2,1,0:T(8,128)(2,1)}, bf16[2,160,640]{2,1,0:T(8,128)(2,1)}, u32[]{:S(2)}, u32[]{:S(2)}) collective-permute-start(bf16[2,160,640]{2,1,0:T(8,128)(2,1)} %collective-permute-done.8.refs_4_), channel_id=1, source_target_pairs={{0,8},{1,25},{2,10},{3,27},{4,12},{5,29},{6,14},{7,31},{8,16},{9,1... | collective-permute-start | bytes 1228808 | tf_op jit(solution)/shard_map/ppermute | solution.py:41
  70.1 0.0 copy-done
  70.1 0.1 dynamic-slice_bitcast_fusion
  70.2 0.1 copy.7.rates
  70.3 0.0 collective-permute-done.14.refs_8_
  70.3 0.0 collective-permute-done.15.refs_9_
  70.4 5.0 %collective-permute-done.7.refs_3_ = bf16[2,160,640]{2,1,0:T(8,128)(2,1)} collective-permute-done((bf16[2,160,640]{2,1,0:T(8,128)(2,1)}, bf16[2,160,640]{2,1,0:T(8,128)(2,1)}, u32[]{:S(2)}, u32[]{:S(2)}) %collective-permute-start.7) | collective-permute-done | bytes 409632 | tf_op jit(solution)/shard_map/ppermute | solution.py:41
  75.4 4.4 %collective-permute-done.9.refs_5_ = bf16[2,160,640]{2,1,0:T(8,128)(2,1)} collective-permute-done((bf16[2,160,640]{2,1,0:T(8,128)(2,1)}, bf16[2,160,640]{2,1,0:T(8,128)(2,1)}, u32[]{:S(2)}, u32[]{:S(2)}) %collective-permute-start.9) | collective-permute-done | bytes 409632 | tf_op jit(solution)/shard_map/ppermute | solution.py:41
  79.8 0.0 collective-permute-done.5.refs_1_
  79.8 10.5 %convolve.1 = bf16[16,40,640]{2,1,0:T(8,128)(2,1)S(1)} custom-call(s32[1]{0:T(128)S(6)} %copy.10.sizes, f32[160,1]{1,0:T(8,128)S(1)} %copy.7.rates, bf16[4,160,640]{2,1,0:T(8,128)(2,1)S(1)} %pad_maximum_fusion.refs_0_, bf16[4,160,640]{2,1,0:T(8,128)(2,1)} %collective-permute-done.5.refs_1_, bf16[2,160,640]{2,1,0:T(8,128)(2,1)} %collective-permute-done.6.refs_2_, ...), custom_call_target="tpu_custom_call" | custom-call | flops 4456448000 | bytes 6553600 | tf_op jit(solution)/shard_map/convolve/pallas_call | solution.py:203
  90.3 16.2 %all_to_all.5.packets = bf16[16,40,640]{2,1,0:T(8,128)(2,1)} all-to-all(bf16[16,40,640]{2,1,0:T(8,128)(2,1)S(1)} %convolve.1), channel_id=1, replica_groups=mesh['tx'=4,'ty'=4,'sector'=8] {'tx','ty'}, dimensions={0} | all-to-all | bytes 1638400 | tf_op jit(solution)/shard_map/all_to_all | solution.py:284
  106.5 2.4 %assemble.1 = bf16[640,640]{1,0:T(8,128)(2,1)} custom-call(bf16[16,40,640]{2,1,0:T(8,128)(2,1)} %all_to_all.5.packets), custom_call_target="tpu_custom_call" | custom-call | tf_op jit(solution)/shard_map/assemble/pallas_call | solution.py:236
  (2 shorter events, 0.1 us)
Async XLA Ops:
  0.0 70.1 %copy-start = (f32[1,640]{1,0:T(1,128)S(1)}, f32[1,640]{1,0:T(1,128)}, u32[]{:S(2)}) copy-start(f32[1,640]{1,0:T(1,128)} %param.8) | copy-start | bytes 7684
  5.1 22.9 %collective-permute-start = (bf16[640,640]{1,0:T(8,128)(2,1)}, bf16[640,640]{1,0:T(8,128)(2,1)S(1)}, u32[]{:S(2)}, u32[]{:S(2)}) collective-permute-start(bf16[640,640]{1,0:T(8,128)(2,1)} %get-tuple-element.15), channel_id=1, source_target_pairs={{1,0},{2,1},{3,2},{4,3},{5,4},{6,5},{7,6},{9,8},{10,9},{11,10},{12... | collective-permute-start | bytes 2457608 | tf_op jit(solution)/shard_map/ppermute | solution.py:22
  7.0 21.0 %collective-permute-start.1 = (bf16[640,640]{1,0:T(8,128)(2,1)}, bf16[640,640]{1,0:T(8,128)(2,1)S(1)}, u32[]{:S(2)}, u32[]{:S(2)}) collective-permute-start(bf16[640,640]{1,0:T(8,128)(2,1)} %get-tuple-element.16), channel_id=1, source_target_pairs={{0,1},{1,2},{2,3},{3,4},{4,5},{5,6},{6,7},{8,9},{9,10},{10,11},{11... | collective-permute-start | bytes 2457608 | tf_op jit(solution)/shard_map/ppermute | solution.py:22
  9.4 8.9 %collective-permute-start.10 = (bf16[160,640]{1,0:T(8,128)(2,1)}, bf16[160,640]{1,0:T(8,128)(2,1)S(1)}, u32[]{:S(2)}, u32[]{:S(2)}) collective-permute-start(bf16[160,640]{1,0:T(8,128)(2,1)} %get-tuple-element.22), channel_id=1, source_target_pairs={{0,8},{8,16},{16,24},{24,0},{1,9},{9,17},{17,25},{25,1},{2,10},{10... | collective-permute-start | bytes 614408 | tf_op jit(solution)/shard_map/ppermute | solution.py:27
  11.1 12.9 %collective-permute-start.11 = (bf16[160,640]{1,0:T(8,128)(2,1)}, bf16[160,640]{1,0:T(8,128)(2,1)S(1)}, u32[]{:S(2)}, u32[]{:S(2)}) collective-permute-start(bf16[160,640]{1,0:T(8,128)(2,1)} %get-tuple-element.23), channel_id=1, source_target_pairs={{0,16},{8,24},{16,0},{24,8},{1,17},{9,25},{17,1},{25,9},{2,18},{10... | collective-permute-start | bytes 614408 | tf_op jit(solution)/shard_map/ppermute | solution.py:27
  14.0 10.0 %collective-permute-start.12 = (bf16[160,640]{1,0:T(8,128)(2,1)}, bf16[160,640]{1,0:T(8,128)(2,1)S(1)}, u32[]{:S(2)}, u32[]{:S(2)}) collective-permute-start(bf16[160,640]{1,0:T(8,128)(2,1)} %get-tuple-element.24), channel_id=1, source_target_pairs={{0,24},{8,0},{16,8},{24,16},{1,25},{9,1},{17,9},{25,17},{2,26},{10... | collective-permute-start | bytes 614408 | tf_op jit(solution)/shard_map/ppermute | solution.py:27
  24.0 4.0 %copy-start.1 = (bf16[1,640,640]{2,1,0:T(8,128)(2,1)S(1)}, bf16[1,640,640]{2,1,0:T(8,128)(2,1)}, u32[]{:S(2)}) copy-start(bf16[1,640,640]{2,1,0:T(8,128)(2,1)} %param.7) | copy-start | bytes 2457604
  25.1 30.8 %collective-permute-start.13 = (bf16[4,160,640]{2,1,0:T(8,128)(2,1)S(1)}, bf16[4,160,640]{2,1,0:T(8,128)(2,1)S(1)}, u32[]{:S(2)}, u32[]{:S(2)}) collective-permute-start(bf16[4,160,640]{2,1,0:T(8,128)(2,1)S(1)} %pad_maximum_fusion.1.refs_6_), channel_id=1, source_target_pairs={{0,32},{1,97},{2,34},{3,99},{4,36},{5,101},{6,38},{7,103},{32,64},... | collective-permute-start | bytes 2457608 | tf_op jit(solution)/shard_map/ppermute | solution.py:41
  30.4 18.1 %collective-permute-start.2 = (bf16[160,640]{1,0:T(8,128)(2,1)S(1)}, bf16[160,640]{1,0:T(8,128)(2,1)S(1)}, u32[]{:S(2)}, u32[]{:S(2)}) collective-permute-start(bf16[160,640]{1,0:T(8,128)(2,1)S(1)} %get-tuple-element.18), channel_id=1, source_target_pairs={{0,32},{32,64},{64,96},{96,0},{1,33},{33,65},{65,97},{97,1},{2,34}... | collective-permute-start | bytes 614408 | tf_op jit(solution)/shard_map/ppermute | solution.py:27
  31.9 21.6 %collective-permute-start.3 = (bf16[160,640]{1,0:T(8,128)(2,1)S(1)}, bf16[160,640]{1,0:T(8,128)(2,1)S(1)}, u32[]{:S(2)}, u32[]{:S(2)}) collective-permute-start(bf16[160,640]{1,0:T(8,128)(2,1)S(1)} %get-tuple-element.19), channel_id=1, source_target_pairs={{0,64},{32,96},{64,0},{96,32},{1,65},{33,97},{65,1},{97,33},{2,66}... | collective-permute-start | bytes 614408 | tf_op jit(solution)/shard_map/ppermute | solution.py:27
  33.6 19.9 %collective-permute-start.4 = (bf16[160,640]{1,0:T(8,128)(2,1)S(1)}, bf16[160,640]{1,0:T(8,128)(2,1)S(1)}, u32[]{:S(2)}, u32[]{:S(2)}) collective-permute-start(bf16[160,640]{1,0:T(8,128)(2,1)S(1)} %get-tuple-element.20), channel_id=1, source_target_pairs={{0,96},{32,0},{64,32},{96,64},{1,97},{33,1},{65,33},{97,65},{2,98}... | collective-permute-start | bytes 614408 | tf_op jit(solution)/shard_map/ppermute | solution.py:27
  35.8 34.6 %collective-permute-start.14 = (bf16[4,160,640]{2,1,0:T(8,128)(2,1)S(1)}, bf16[4,160,640]{2,1,0:T(8,128)(2,1)S(1)}, u32[]{:S(2)}, u32[]{:S(2)}) collective-permute-start(bf16[4,160,640]{2,1,0:T(8,128)(2,1)S(1)} %pad_maximum_fusion.1.refs_6_), channel_id=1, source_target_pairs={{0,96},{1,33},{2,98},{3,35},{4,100},{5,37},{6,102},{7,39},{32,0},{... | collective-permute-start | bytes 2457608 | tf_op jit(solution)/shard_map/ppermute | solution.py:41
  48.5 10.3 %collective-permute-start.6 = (bf16[2,160,640]{2,1,0:T(8,128)(2,1)S(1)}, bf16[2,160,640]{2,1,0:T(8,128)(2,1)}, u32[]{:S(2)}, u32[]{:S(2)}) collective-permute-start(bf16[2,160,640]{2,1,0:T(8,128)(2,1)S(1)} %pad_maximum_fusion.2), channel_id=1, source_target_pairs={{0,8},{1,25},{2,10},{3,27},{4,12},{5,29},{6,14},{7,31},{8,16},{9,1... | collective-permute-start | bytes 1228808 | tf_op jit(solution)/shard_map/ppermute | solution.py:41
  53.6 14.0 %collective-permute-start.8 = (bf16[2,160,640]{2,1,0:T(8,128)(2,1)S(1)}, bf16[2,160,640]{2,1,0:T(8,128)(2,1)}, u32[]{:S(2)}, u32[]{:S(2)}) collective-permute-start(bf16[2,160,640]{2,1,0:T(8,128)(2,1)S(1)} %pad_maximum_fusion.3), channel_id=1, source_target_pairs={{0,8},{1,25},{2,10},{3,27},{4,12},{5,29},{6,14},{7,31},{8,16},{9,1... | collective-permute-start | bytes 1228808 | tf_op jit(solution)/shard_map/ppermute | solution.py:41
  55.9 14.5 %collective-permute-start.15 = (bf16[4,160,640]{2,1,0:T(8,128)(2,1)S(1)}, bf16[4,160,640]{2,1,0:T(8,128)(2,1)}, u32[]{:S(2)}, u32[]{:S(2)}) collective-permute-start(bf16[4,160,640]{2,1,0:T(8,128)(2,1)S(1)} %collective-permute-done.13.refs_7_), channel_id=1, source_target_pairs={{0,32},{1,97},{2,34},{3,99},{4,36},{5,101},{6,38},{7,103},{32,64},... | collective-permute-start | bytes 2457608 | tf_op jit(solution)/shard_map/ppermute | solution.py:41
  56.0 23.7 %collective-permute-start.5 = (bf16[4,160,640]{2,1,0:T(8,128)(2,1)S(1)}, bf16[4,160,640]{2,1,0:T(8,128)(2,1)}, u32[]{:S(2)}, u32[]{:S(2)}) collective-permute-start(bf16[4,160,640]{2,1,0:T(8,128)(2,1)S(1)} %pad_maximum_fusion.refs_0_), channel_id=1, source_target_pairs={{0,24},{1,9},{2,26},{3,11},{4,28},{5,13},{6,30},{7,15},{8,0},{9,17... | collective-permute-start | bytes 2457608 | tf_op jit(solution)/shard_map/ppermute | solution.py:41
  58.8 16.6 %collective-permute-start.7 = (bf16[2,160,640]{2,1,0:T(8,128)(2,1)}, bf16[2,160,640]{2,1,0:T(8,128)(2,1)}, u32[]{:S(2)}, u32[]{:S(2)}) collective-permute-start(bf16[2,160,640]{2,1,0:T(8,128)(2,1)} %collective-permute-done.6.refs_2_), channel_id=1, source_target_pairs={{0,8},{1,25},{2,10},{3,27},{4,12},{5,29},{6,14},{7,31},{8,16},{9,1... | collective-permute-start | bytes 1228808 | tf_op jit(solution)/shard_map/ppermute | solution.py:41
  67.6 12.2 %collective-permute-start.9 = (bf16[2,160,640]{2,1,0:T(8,128)(2,1)}, bf16[2,160,640]{2,1,0:T(8,128)(2,1)}, u32[]{:S(2)}, u32[]{:S(2)}) collective-permute-start(bf16[2,160,640]{2,1,0:T(8,128)(2,1)} %collective-permute-done.8.refs_4_), channel_id=1, source_target_pairs={{0,8},{1,25},{2,10},{3,27},{4,12},{5,29},{6,14},{7,31},{8,16},{9,1... | collective-permute-start | bytes 1228808 | tf_op jit(solution)/shard_map/ppermute | solution.py:41

commit v14 on v13

--- a/solution.py
+++ b/solution.py
@@ -256,29 +256,20 @@
     below = shifted(upward, "sector", 1)
     above = shifted(masked, "sector", -1)
     crossed_g = {d: ring(away_g[d - 1], "ty", d) for d in (2, 1, 3)}
-    columns = jnp.stack([own_g] + [crossed_g[d] for d in range(1, n)])
-
     own_e, *away_e = energy_blocks(
         sector_sizes, hyb_particle, hyb_hole, above, below, operator, n
     )
     crossed_e = {d: ring(away_e[d - 1], "tx", d) for d in (2, 1, 3)}
-    before_g = turned_ring(columns, "tx", 1)
-    after_g = turned_ring(columns, "tx", -1)
-    far_g = turned_ring(before_g, "tx", 1)
-
-    blocks = [own_e] + [crossed_e[d] for d in range(1, n)]
-    halves = [jnp.stack(blocks[: n // 2]), jnp.stack(blocks[n // 2 :])]
-    before_e = [turned_ring(half, "ty", 1) for half in halves]
-    lines = jnp.stack(blocks)
-    after_e = turned_ring(lines, "ty", -1)
-    far_e = [turned_ring(half, "ty", 1) for half in before_e]
-    entries = [("e", 0, 0, lines), ("e", 1, 0, after_e)]
-    for k in range(2):
-        entries += [("e", -1, k * n // 2, before_e[k]), ("e", 2, k * n // 2, far_e[k])]
-    entries += [
-        ("g", step, 0, part)
-        for step, part in zip((0, -1, 1, 2), (columns, before_g, after_g, far_g))
-    ]
+    entries = []
+    for kind, axis, own, crossed in (("e", "ty", own_e, crossed_e), ("g", "tx", own_g, crossed_g)):
+        blocks = [own] + [crossed[d] for d in range(1, n)]
+        whole = jnp.stack(blocks)
+        after = turned_ring(whole, axis, -1)
+        entries += [(kind, 0, 0, whole), (kind, 1, 0, after)]
+        for k in (0, n // 2):
+            before = turned_ring(jnp.stack(blocks[k : k + n // 2]), axis, 1)
+            far = turned_ring(before, axis, 1)
+            entries += [(kind, -1, k, before), (kind, 2, k, far)]
     rates = lax.dynamic_slice_in_dim(energies[0], here_x * rows, rows, 0)[:, None]
     packets = convolve(entries, sector_sizes, rates, n, step_size)
     packets = lax.all_to_all(packets, ("tx", "ty"), 0, 0, tiled=True)

time: 109 us -> 110 us (level)
  starting transfers between devices: 29 us -> 24.2 us
  waiting for transfers between devices: 40.4 us -> 43.5 us
  local copies, waits for them, and re-layouts: 0.19 us -> 2.97 us
    ppermute x8 -> x10, waiting for transfers between devices: 16.5 us -> 25.2 us  [turned_ring(): return lax.ppermute(block, (axis, 'sector'), route)]
    ppermute x6, waiting for transfers between devices: 23.8 us -> 18.3 us  [ring(): lax.ppermute(block, axis, [(i, (i + distance) % n) for i in range(n)])]
    ppermute x8 -> x10, starting transfers between devices: 13.4 us -> 9.2 us  [turned_ring(): return lax.ppermute(block, (axis, 'sector'), route)]
    unnamed x4 -> x14, local copies, waits for them, and re-layouts: 0.01 us -> 2.79 us
  transfers between devices with their start and end apart: 16 -> 18, of which waited for: 8 -> 8; matrix products, arithmetic and copies ran while one was open for 1% -> 1% of each run, Pallas kernels for 2% -> 2%
where the time goes in v14:
time: 110 us
  waiting for transfers between devices  43.5 us (40%)
  starting transfers between devices  24.2 us (22%)
  Pallas kernels  19.6 us (18%)
  blocking collectives  15.8 us (14%)
  local copies, waits for them, and re-layouts  2.97 us (3%)
  between operations  2.13 us (2%)
  other arithmetic  1.37 us (1%)
    ppermute x10, waiting for transfers between devices, turned_ring(): return lax.ppermute(block, (axis, 'sector'), route)  25.2 us
    ppermute x6, waiting for transfers between devices, ring(): lax.ppermute(block, axis, [(i, (i + distance) % n) for i in range(n)])  18.3 us
    all_to_all x1, blocking collectives, per_device(): packets = lax.all_to_all(packets, ('tx', 'ty'), 0, 0, tiled=True)  15.8 us
    ppermute x6, starting transfers between devices, ring(): lax.ppermute(block, axis, [(i, (i + distance) % n) for i in range(n)])  10.6 us
    pallas_call x1, Pallas kernels, convolve(): pl.pallas_call(functools.partial(convolve_kernel, plan, n, step_size), ou...  10.4 us
    ppermute x10, starting transfers between devices, turned_ring(): return lax.ppermute(block, (axis, 'sector'), route)  9.2 us
    ppermute x2, starting transfers between devices, shifted(): return lax.ppermute(block, axis, route)  4.45 us
    pallas_call x1, Pallas kernels, prepare(): pl.pallas_call(prepare_kernel, out_shape=(square,) * 2 + (block,) * n, in...  4.42 us
  transfers between devices with their start and end apart: 18, of which 8 were waited for; matrix products, arithmetic and copies ran while one was open for 1% of the time, Pallas kernels for 2%

profile of v14, /device:TPU:32, one launch (start us, length us, event | category | flops | bytes accessed | tf_op | source)
XLA Modules:
  0.0 109.6 jit_solution(1777514558191347788)
XLA Ops:
  0.7 4.4 %prepare.1 = (bf16[640,640]{1,0:T(8,128)(2,1)}, bf16[640,640]{1,0:T(8,128)(2,1)}, bf16[160,640]{1,0:T(8,128)(2,1)}, bf16[160,640]{1,0:T(8,128)(2,1)}, bf16[160,6...) custom-call(s32[1]{0:T(128)S(6)} %copy.10.sizes, bf16[640,640]{1,0:T(8,128)(2,1)} %bitcast.31, bf16[640,640]{1,0:T(8,128)(2,1)} %bitcast.15), custom_call_target="tpu_custom_call" | custom-call | flops 1048576000 | bytes 4915200 | tf_op jit(solution)/shard_map/prepare/pallas_call | solution.py:77
  5.1 2.0 %collective-permute-start = (bf16[640,640]{1,0:T(8,128)(2,1)}, bf16[640,640]{1,0:T(8,128)(2,1)S(1)}, u32[]{:S(2)}, u32[]{:S(2)}) collective-permute-start(bf16[640,640]{1,0:T(8,128)(2,1)} %get-tuple-element.15), channel_id=1, source_target_pairs={{1,0},{2,1},{3,2},{4,3},{5,4},{6,5},{7,6},{9,8},{10,9},{11,10},{12... | collective-permute-start | bytes 2457608 | tf_op jit(solution)/shard_map/ppermute | solution.py:22
  7.1 2.4 %collective-permute-start.1 = (bf16[640,640]{1,0:T(8,128)(2,1)}, bf16[640,640]{1,0:T(8,128)(2,1)S(1)}, u32[]{:S(2)}, u32[]{:S(2)}) collective-permute-start(bf16[640,640]{1,0:T(8,128)(2,1)} %get-tuple-element.16), channel_id=1, source_target_pairs={{0,1},{1,2},{2,3},{3,4},{4,5},{5,6},{6,7},{8,9},{9,10},{10,11},{11... | collective-permute-start | bytes 2457608 | tf_op jit(solution)/shard_map/ppermute | solution.py:22
  9.6 1.6 %collective-permute-start.10 = (bf16[160,640]{1,0:T(8,128)(2,1)}, bf16[160,640]{1,0:T(8,128)(2,1)S(1)}, u32[]{:S(2)}, u32[]{:S(2)}) collective-permute-start(bf16[160,640]{1,0:T(8,128)(2,1)} %get-tuple-element.22), channel_id=1, source_target_pairs={{0,8},{8,16},{16,24},{24,0},{1,9},{9,17},{17,25},{25,1},{2,10},{10... | collective-permute-start | bytes 614408 | tf_op jit(solution)/shard_map/ppermute | solution.py:27
  11.2 2.9 %collective-permute-start.11 = (bf16[160,640]{1,0:T(8,128)(2,1)}, bf16[160,640]{1,0:T(8,128)(2,1)S(1)}, u32[]{:S(2)}, u32[]{:S(2)}) collective-permute-start(bf16[160,640]{1,0:T(8,128)(2,1)} %get-tuple-element.23), channel_id=1, source_target_pairs={{0,16},{8,24},{16,0},{24,8},{1,17},{9,25},{17,1},{25,9},{2,18},{10... | collective-permute-start | bytes 614408 | tf_op jit(solution)/shard_map/ppermute | solution.py:27
  14.1 1.3 %collective-permute-start.12 = (bf16[160,640]{1,0:T(8,128)(2,1)}, bf16[160,640]{1,0:T(8,128)(2,1)S(1)}, u32[]{:S(2)}, u32[]{:S(2)}) collective-permute-start(bf16[160,640]{1,0:T(8,128)(2,1)} %get-tuple-element.24), channel_id=1, source_target_pairs={{0,24},{8,0},{16,8},{24,16},{1,25},{9,1},{17,9},{25,17},{2,26},{10... | collective-permute-start | bytes 614408 | tf_op jit(solution)/shard_map/ppermute | solution.py:27
  15.4 3.0 %collective-permute-done.10 = bf16[160,640]{1,0:T(8,128)(2,1)S(1)} collective-permute-done((bf16[160,640]{1,0:T(8,128)(2,1)}, bf16[160,640]{1,0:T(8,128)(2,1)S(1)}, u32[]{:S(2)}, u32[]{:S(2)}) %collective-permute-start.10) | collective-permute-done | bytes 204832 | tf_op jit(solution)/shard_map/ppermute | solution.py:27
  18.4 1.0 pad_maximum_fusion.4
  19.4 1.5 %collective-permute-start.14 = (bf16[2,160,640]{2,1,0:T(8,128)(2,1)S(1)}, bf16[2,160,640]{2,1,0:T(8,128)(2,1)S(1)}, u32[]{:S(2)}, u32[]{:S(2)}) collective-permute-start(bf16[2,160,640]{2,1,0:T(8,128)(2,1)S(1)} %pad_maximum_fusion.4), channel_id=1, source_target_pairs={{0,32},{1,97},{2,34},{3,99},{4,36},{5,101},{6,38},{7,103},{32,64},... | collective-permute-start | bytes 1228808 | tf_op jit(solution)/shard_map/ppermute | solution.py:41
  22.2 0.0 collective-permute-done.refs_0_
  22.2 0.0 collective-permute-done.1.refs_2_
  22.3 2.3 %energy_blocks.1 = (bf16[160,640]{1,0:T(8,128)(2,1)S(1)}, bf16[160,640]{1,0:T(8,128)(2,1)S(1)}, bf16[160,640]{1,0:T(8,128)(2,1)S(1)}, bf16[160,640]{1,0:T(8,128)(2,1)S(1)}) custom-call(s32[1]{0:T(128)S(6)} %copy.10.sizes, f32[1]{0:T(128)S(6)} %copy.8.particle, f32[1]{0:T(128)S(6)} %copy.9.hole, bf16[640,640]{1,0:T(8,128)(2,1)S(1)} %collective-permute-done.refs_0_, ...), custom_call_target="tpu_custom_call" | custom-call | flops 1048576000 | bytes 3276800 | tf_op jit(solution)/shard_map/energy_blocks/pallas_call | solution.py:120
  24.6 1.6 %collective-permute-start.2 = (bf16[160,640]{1,0:T(8,128)(2,1)S(1)}, bf16[160,640]{1,0:T(8,128)(2,1)S(1)}, u32[]{:S(2)}, u32[]{:S(2)}) collective-permute-start(bf16[160,640]{1,0:T(8,128)(2,1)S(1)} %get-tuple-element.18), channel_id=1, source_target_pairs={{0,32},{32,64},{64,96},{96,0},{1,33},{33,65},{65,97},{97,1},{2,34}... | collective-permute-start | bytes 614408 | tf_op jit(solution)/shard_map/ppermute | solution.py:27
  26.2 0.0 collective-permute-done.11
  26.2 0.0 collective-permute-done.12
  26.3 1.3 %collective-permute-start.16 = (bf16[2,160,640]{2,1,0:T(8,128)(2,1)S(1)}, bf16[2,160,640]{2,1,0:T(8,128)(2,1)}, u32[]{:S(2)}, u32[]{:S(2)}) collective-permute-start(bf16[2,160,640]{2,1,0:T(8,128)(2,1)S(1)} %pad_maximum_fusion.5), channel_id=1, source_target_pairs={{0,32},{1,97},{2,34},{3,99},{4,36},{5,101},{6,38},{7,103},{32,64},... | collective-permute-start | bytes 1228808 | tf_op jit(solution)/shard_map/ppermute | solution.py:41
  27.5 2.0 %collective-permute-start.3 = (bf16[160,640]{1,0:T(8,128)(2,1)S(1)}, bf16[160,640]{1,0:T(8,128)(2,1)S(1)}, u32[]{:S(2)}, u32[]{:S(2)}) collective-permute-start(bf16[160,640]{1,0:T(8,128)(2,1)S(1)} %get-tuple-element.19), channel_id=1, source_target_pairs={{0,64},{32,96},{64,0},{96,32},{1,65},{33,97},{65,1},{97,33},{2,66}... | collective-permute-start | bytes 614408 | tf_op jit(solution)/shard_map/ppermute | solution.py:27
  29.5 1.2 %collective-permute-start.4 = (bf16[160,640]{1,0:T(8,128)(2,1)S(1)}, bf16[160,640]{1,0:T(8,128)(2,1)S(1)}, u32[]{:S(2)}, u32[]{:S(2)}) collective-permute-start(bf16[160,640]{1,0:T(8,128)(2,1)S(1)} %get-tuple-element.20), channel_id=1, source_target_pairs={{0,96},{32,0},{64,32},{96,64},{1,97},{33,1},{65,33},{97,65},{2,98}... | collective-permute-start | bytes 614408 | tf_op jit(solution)/shard_map/ppermute | solution.py:27
  30.7 0.1 pad_maximum_fusion.1.refs_6_
  30.8 0.0 collective-permute-done.14.refs_8_
  30.8 0.0 copy-start.2
  30.8 1.0 collective-permute-start.13
  31.9 1.7 %collective-permute-done.2 = bf16[160,640]{1,0:T(8,128)(2,1)S(1)} collective-permute-done((bf16[160,640]{1,0:T(8,128)(2,1)S(1)}, bf16[160,640]{1,0:T(8,128)(2,1)S(1)}, u32[]{:S(2)}, u32[]{:S(2)}) %collective-permute-start.2) | collective-permute-done | bytes 204832 | tf_op jit(solution)/shard_map/ppermute | solution.py:27
  33.6 0.5 collective-permute-start.15
  34.2 13.6 %collective-permute-done.3 = bf16[160,640]{1,0:T(8,128)(2,1)S(1)} collective-permute-done((bf16[160,640]{1,0:T(8,128)(2,1)S(1)}, bf16[160,640]{1,0:T(8,128)(2,1)S(1)}, u32[]{:S(2)}, u32[]{:S(2)}) %collective-permute-start.3) | collective-permute-done | bytes 204832 | tf_op jit(solution)/shard_map/ppermute | solution.py:27
  47.8 0.1 collective-permute-start.6
  47.9 0.0 collective-permute-done.4
  47.9 0.1 pad_maximum_fusion.refs_0_
  48.1 0.1 collective-permute-start.8
  48.2 0.0 collective-permute-done.16.refs_10_
  48.2 3.2 %collective-permute-start.5 = (bf16[4,160,640]{2,1,0:T(8,128)(2,1)S(1)}, bf16[4,160,640]{2,1,0:T(8,128)(2,1)S(1)}, u32[]{:S(2)}, u32[]{:S(2)}) collective-permute-start(bf16[4,160,640]{2,1,0:T(8,128)(2,1)S(1)} %pad_maximum_fusion.refs_0_), channel_id=1, source_target_pairs={{0,24},{1,9},{2,26},{3,11},{4,28},{5,13},{6,30},{7,15},{8,0},{9,17... | collective-permute-start | bytes 2457608 | tf_op jit(solution)/shard_map/ppermute | solution.py:41
  51.4 4.0 %collective-permute-done.15.refs_9_ = bf16[2,160,640]{2,1,0:T(8,128)(2,1)S(1)} collective-permute-done((bf16[2,160,640]{2,1,0:T(8,128)(2,1)S(1)}, bf16[2,160,640]{2,1,0:T(8,128)(2,1)S(1)}, u32[]{:S(2)}, u32[]{:S(2)}) %collective-permute-start.15) | collective-permute-done | bytes 409632 | tf_op jit(solution)/shard_map/ppermute | solution.py:41
  55.4 0.8 copy-done.4
  56.2 0.0 collective-permute-start.17
  56.2 3.0 %collective-permute-done.6.refs_2_ = bf16[2,160,640]{2,1,0:T(8,128)(2,1)} collective-permute-done((bf16[2,160,640]{2,1,0:T(8,128)(2,1)S(1)}, bf16[2,160,640]{2,1,0:T(8,128)(2,1)}, u32[]{:S(2)}, u32[]{:S(2)}) %collective-permute-start.6) | collective-permute-done | bytes 409632 | tf_op jit(solution)/shard_map/ppermute | solution.py:41
  59.2 1.2 %collective-permute-start.7 = (bf16[2,160,640]{2,1,0:T(8,128)(2,1)}, bf16[2,160,640]{2,1,0:T(8,128)(2,1)}, u32[]{:S(2)}, u32[]{:S(2)}) collective-permute-start(bf16[2,160,640]{2,1,0:T(8,128)(2,1)} %collective-permute-done.6.refs_2_), channel_id=1, source_target_pairs={{0,8},{1,25},{2,10},{3,27},{4,12},{5,29},{6,14},{7,31},{8,16},{9,1... | collective-permute-start | bytes 1228808 | tf_op jit(solution)/shard_map/ppermute | solution.py:41
  60.3 7.6 %collective-permute-done.8.refs_4_ = bf16[2,160,640]{2,1,0:T(8,128)(2,1)} collective-permute-done((bf16[2,160,640]{2,1,0:T(8,128)(2,1)S(1)}, bf16[2,160,640]{2,1,0:T(8,128)(2,1)}, u32[]{:S(2)}, u32[]{:S(2)}) %collective-permute-start.8) | collective-permute-done | bytes 409632 | tf_op jit(solution)/shard_map/ppermute | solution.py:41
  68.0 0.3 collective-permute-start.9
  68.2 0.1 dynamic-slice_bitcast_fusion
  68.3 0.1 copy.7.rates
  68.4 0.0 collective-permute-done.13.refs_7_
  68.4 6.2 %collective-permute-done.7.refs_3_ = bf16[2,160,640]{2,1,0:T(8,128)(2,1)} collective-permute-done((bf16[2,160,640]{2,1,0:T(8,128)(2,1)}, bf16[2,160,640]{2,1,0:T(8,128)(2,1)}, u32[]{:S(2)}, u32[]{:S(2)}) %collective-permute-start.7) | collective-permute-done | bytes 409632 | tf_op jit(solution)/shard_map/ppermute | solution.py:41
  74.6 4.4 %collective-permute-done.9.refs_5_ = bf16[2,160,640]{2,1,0:T(8,128)(2,1)} collective-permute-done((bf16[2,160,640]{2,1,0:T(8,128)(2,1)}, bf16[2,160,640]{2,1,0:T(8,128)(2,1)}, u32[]{:S(2)}, u32[]{:S(2)}) %collective-permute-start.9) | collective-permute-done | bytes 409632 | tf_op jit(solution)/shard_map/ppermute | solution.py:41
  79.0 1.0 copy-done.3
  80.0 1.0 copy-done.5
  81.0 10.4 %convolve.1 = bf16[16,40,640]{2,1,0:T(8,128)(2,1)S(1)} custom-call(s32[1]{0:T(128)S(6)} %copy.10.sizes, f32[160,1]{1,0:T(8,128)S(1)} %copy.7.rates, bf16[4,160,640]{2,1,0:T(8,128)(2,1)S(1)} %pad_maximum_fusion.refs_0_, bf16[4,160,640]{2,1,0:T(8,128)(2,1)S(1)} %collective-permute-done.5.refs_1_, bf16[2,160,640]{2,1,0:T(8,128)(2,1)} %collective-permute-done.6.refs_2_, ...), custom_call_target="tpu_custom_call" | custom-call | flops 4456448000 | bytes 6553600 | tf_op jit(solution)/shard_map/convolve/pallas_call | solution.py:203
  91.4 15.8 %all_to_all.5.packets = bf16[16,40,640]{2,1,0:T(8,128)(2,1)} all-to-all(bf16[16,40,640]{2,1,0:T(8,128)(2,1)S(1)} %convolve.1), channel_id=1, replica_groups=mesh['tx'=4,'ty'=4,'sector'=8] {'tx','ty'}, dimensions={0} | all-to-all | bytes 1638400 | tf_op jit(solution)/shard_map/all_to_all | solution.py:275
  107.2 2.4 %assemble.1 = bf16[640,640]{1,0:T(8,128)(2,1)} custom-call(bf16[16,40,640]{2,1,0:T(8,128)(2,1)} %all_to_all.5.packets), custom_call_target="tpu_custom_call" | custom-call | tf_op jit(solution)/shard_map/assemble/pallas_call | solution.py:236
  (15 shorter events, 0.2 us)
Async XLA Ops:
  0.0 68.2 %copy-start = (f32[1,640]{1,0:T(1,128)S(1)}, f32[1,640]{1,0:T(1,128)}, u32[]{:S(2)}) copy-start(f32[1,640]{1,0:T(1,128)} %param.8) | copy-start | bytes 7684
  5.1 17.2 %copy-start.1 = (bf16[1,640,640]{2,1,0:T(8,128)(2,1)S(1)}, bf16[1,640,640]{2,1,0:T(8,128)(2,1)}, u32[]{:S(2)}) copy-start(bf16[1,640,640]{2,1,0:T(8,128)(2,1)} %param.7) | copy-start | bytes 2457604
  5.1 17.1 %collective-permute-start = (bf16[640,640]{1,0:T(8,128)(2,1)}, bf16[640,640]{1,0:T(8,128)(2,1)S(1)}, u32[]{:S(2)}, u32[]{:S(2)}) collective-permute-start(bf16[640,640]{1,0:T(8,128)(2,1)} %get-tuple-element.15), channel_id=1, source_target_pairs={{1,0},{2,1},{3,2},{4,3},{5,4},{6,5},{7,6},{9,8},{10,9},{11,10},{12... | collective-permute-start | bytes 2457608 | tf_op jit(solution)/shard_map/ppermute | solution.py:22
  7.1 15.1 %collective-permute-start.1 = (bf16[640,640]{1,0:T(8,128)(2,1)}, bf16[640,640]{1,0:T(8,128)(2,1)S(1)}, u32[]{:S(2)}, u32[]{:S(2)}) collective-permute-start(bf16[640,640]{1,0:T(8,128)(2,1)} %get-tuple-element.16), channel_id=1, source_target_pairs={{0,1},{1,2},{2,3},{3,4},{4,5},{5,6},{6,7},{8,9},{9,10},{10,11},{11... | collective-permute-start | bytes 2457608 | tf_op jit(solution)/shard_map/ppermute | solution.py:22
  9.6 8.9 %collective-permute-start.10 = (bf16[160,640]{1,0:T(8,128)(2,1)}, bf16[160,640]{1,0:T(8,128)(2,1)S(1)}, u32[]{:S(2)}, u32[]{:S(2)}) collective-permute-start(bf16[160,640]{1,0:T(8,128)(2,1)} %get-tuple-element.22), channel_id=1, source_target_pairs={{0,8},{8,16},{16,24},{24,0},{1,9},{9,17},{17,25},{25,1},{2,10},{10... | collective-permute-start | bytes 614408 | tf_op jit(solution)/shard_map/ppermute | solution.py:27
  11.2 15.0 %collective-permute-start.11 = (bf16[160,640]{1,0:T(8,128)(2,1)}, bf16[160,640]{1,0:T(8,128)(2,1)S(1)}, u32[]{:S(2)}, u32[]{:S(2)}) collective-permute-start(bf16[160,640]{1,0:T(8,128)(2,1)} %get-tuple-element.23), channel_id=1, source_target_pairs={{0,16},{8,24},{16,0},{24,8},{1,17},{9,25},{17,1},{25,9},{2,18},{10... | collective-permute-start | bytes 614408 | tf_op jit(solution)/shard_map/ppermute | solution.py:27
  14.1 12.1 %collective-permute-start.12 = (bf16[160,640]{1,0:T(8,128)(2,1)}, bf16[160,640]{1,0:T(8,128)(2,1)S(1)}, u32[]{:S(2)}, u32[]{:S(2)}) collective-permute-start(bf16[160,640]{1,0:T(8,128)(2,1)} %get-tuple-element.24), channel_id=1, source_target_pairs={{0,24},{8,0},{16,8},{24,16},{1,25},{9,1},{17,9},{25,17},{2,26},{10... | collective-permute-start | bytes 614408 | tf_op jit(solution)/shard_map/ppermute | solution.py:27
  19.4 11.4 %collective-permute-start.14 = (bf16[2,160,640]{2,1,0:T(8,128)(2,1)S(1)}, bf16[2,160,640]{2,1,0:T(8,128)(2,1)S(1)}, u32[]{:S(2)}, u32[]{:S(2)}) collective-permute-start(bf16[2,160,640]{2,1,0:T(8,128)(2,1)S(1)} %pad_maximum_fusion.4), channel_id=1, source_target_pairs={{0,32},{1,97},{2,34},{3,99},{4,36},{5,101},{6,38},{7,103},{32,64},... | collective-permute-start | bytes 1228808 | tf_op jit(solution)/shard_map/ppermute | solution.py:41
  24.6 9.0 %collective-permute-start.2 = (bf16[160,640]{1,0:T(8,128)(2,1)S(1)}, bf16[160,640]{1,0:T(8,128)(2,1)S(1)}, u32[]{:S(2)}, u32[]{:S(2)}) collective-permute-start(bf16[160,640]{1,0:T(8,128)(2,1)S(1)} %get-tuple-element.18), channel_id=1, source_target_pairs={{0,32},{32,64},{64,96},{96,0},{1,33},{33,65},{65,97},{97,1},{2,34}... | collective-permute-start | bytes 614408 | tf_op jit(solution)/shard_map/ppermute | solution.py:27
  26.2 4.5 %copy-start.6 = (bf16[160,640]{1,0:T(8,128)(2,1)S(1)}, bf16[160,640]{1,0:T(8,128)(2,1)}, u32[]{:S(2)}) copy-start(bf16[160,640]{1,0:T(8,128)(2,1)} %get-tuple-element.21) | copy-start | bytes 614404
  26.3 21.9 %collective-permute-start.16 = (bf16[2,160,640]{2,1,0:T(8,128)(2,1)S(1)}, bf16[2,160,640]{2,1,0:T(8,128)(2,1)}, u32[]{:S(2)}, u32[]{:S(2)}) collective-permute-start(bf16[2,160,640]{2,1,0:T(8,128)(2,1)S(1)} %pad_maximum_fusion.5), channel_id=1, source_target_pairs={{0,32},{1,97},{2,34},{3,99},{4,36},{5,101},{6,38},{7,103},{32,64},... | collective-permute-start | bytes 1228808 | tf_op jit(solution)/shard_map/ppermute | solution.py:41
  27.5 20.2 %collective-permute-start.3 = (bf16[160,640]{1,0:T(8,128)(2,1)S(1)}, bf16[160,640]{1,0:T(8,128)(2,1)S(1)}, u32[]{:S(2)}, u32[]{:S(2)}) collective-permute-start(bf16[160,640]{1,0:T(8,128)(2,1)S(1)} %get-tuple-element.19), channel_id=1, source_target_pairs={{0,64},{32,96},{64,0},{96,32},{1,65},{33,97},{65,1},{97,33},{2,66}... | collective-permute-start | bytes 614408 | tf_op jit(solution)/shard_map/ppermute | solution.py:27
  29.5 18.4 %collective-permute-start.4 = (bf16[160,640]{1,0:T(8,128)(2,1)S(1)}, bf16[160,640]{1,0:T(8,128)(2,1)S(1)}, u32[]{:S(2)}, u32[]{:S(2)}) collective-permute-start(bf16[160,640]{1,0:T(8,128)(2,1)S(1)} %get-tuple-element.20), channel_id=1, source_target_pairs={{0,96},{32,0},{64,32},{96,64},{1,97},{33,1},{65,33},{97,65},{2,98}... | collective-permute-start | bytes 614408 | tf_op jit(solution)/shard_map/ppermute | solution.py:27
  30.8 3.3 %copy-start.2 = (bf16[2,160,640]{2,1,0:T(8,128)(2,1)}, bf16[2,160,640]{2,1,0:T(8,128)(2,1)S(1)}, u32[]{:S(2)}) copy-start(bf16[2,160,640]{2,1,0:T(8,128)(2,1)S(1)} %collective-permute-done.14.refs_8_) | copy-start | bytes 1228804
  30.8 37.6 %collective-permute-start.13 = (bf16[4,160,640]{2,1,0:T(8,128)(2,1)S(1)}, bf16[4,160,640]{2,1,0:T(8,128)(2,1)S(1)}, u32[]{:S(2)}, u32[]{:S(2)}) collective-permute-start(bf16[4,160,640]{2,1,0:T(8,128)(2,1)S(1)} %pad_maximum_fusion.1.refs_6_), channel_id=1, source_target_pairs={{0,96},{1,33},{2,98},{3,35},{4,100},{5,37},{6,102},{7,39},{32,0},{... | collective-permute-start | bytes 2457608 | tf_op jit(solution)/shard_map/ppermute | solution.py:41
  33.6 21.9 %collective-permute-start.15 = (bf16[2,160,640]{2,1,0:T(8,128)(2,1)S(1)}, bf16[2,160,640]{2,1,0:T(8,128)(2,1)S(1)}, u32[]{:S(2)}, u32[]{:S(2)}) collective-permute-start(bf16[2,160,640]{2,1,0:T(8,128)(2,1)S(1)} %collective-permute-done.14.refs_8_), channel_id=1, source_target_pairs={{0,32},{1,97},{2,34},{3,99},{4,36},{5,101},{6,38},{7,103},{32,64},... | collective-permute-start | bytes 1228808 | tf_op jit(solution)/shard_map/ppermute | solution.py:41
  47.8 11.4 %collective-permute-start.6 = (bf16[2,160,640]{2,1,0:T(8,128)(2,1)S(1)}, bf16[2,160,640]{2,1,0:T(8,128)(2,1)}, u32[]{:S(2)}, u32[]{:S(2)}) collective-permute-start(bf16[2,160,640]{2,1,0:T(8,128)(2,1)S(1)} %pad_maximum_fusion.2), channel_id=1, source_target_pairs={{0,8},{1,25},{2,10},{3,27},{4,12},{5,29},{6,14},{7,31},{8,16},{9,1... | collective-permute-start | bytes 1228808 | tf_op jit(solution)/shard_map/ppermute | solution.py:41
  48.1 19.9 %collective-permute-start.8 = (bf16[2,160,640]{2,1,0:T(8,128)(2,1)S(1)}, bf16[2,160,640]{2,1,0:T(8,128)(2,1)}, u32[]{:S(2)}, u32[]{:S(2)}) collective-permute-start(bf16[2,160,640]{2,1,0:T(8,128)(2,1)S(1)} %pad_maximum_fusion.3), channel_id=1, source_target_pairs={{0,8},{1,25},{2,10},{3,27},{4,12},{5,29},{6,14},{7,31},{8,16},{9,1... | collective-permute-start | bytes 1228808 | tf_op jit(solution)/shard_map/ppermute | solution.py:41
  48.2 30.8 %collective-permute-start.5 = (bf16[4,160,640]{2,1,0:T(8,128)(2,1)S(1)}, bf16[4,160,640]{2,1,0:T(8,128)(2,1)S(1)}, u32[]{:S(2)}, u32[]{:S(2)}) collective-permute-start(bf16[4,160,640]{2,1,0:T(8,128)(2,1)S(1)} %pad_maximum_fusion.refs_0_), channel_id=1, source_target_pairs={{0,24},{1,9},{2,26},{3,11},{4,28},{5,13},{6,30},{7,15},{8,0},{9,17... | collective-permute-start | bytes 2457608 | tf_op jit(solution)/shard_map/ppermute | solution.py:41
  55.4 0.8 copy-start.4
  56.2 12.2 %collective-permute-start.17 = (bf16[2,160,640]{2,1,0:T(8,128)(2,1)}, bf16[2,160,640]{2,1,0:T(8,128)(2,1)}, u32[]{:S(2)}, u32[]{:S(2)}) collective-permute-start(bf16[2,160,640]{2,1,0:T(8,128)(2,1)} %collective-permute-done.16.refs_10_), channel_id=1, source_target_pairs={{0,32},{1,97},{2,34},{3,99},{4,36},{5,101},{6,38},{7,103},{32,64},... | collective-permute-start | bytes 1228808 | tf_op jit(solution)/shard_map/ppermute | solution.py:41
  59.2 15.4 %collective-permute-start.7 = (bf16[2,160,640]{2,1,0:T(8,128)(2,1)}, bf16[2,160,640]{2,1,0:T(8,128)(2,1)}, u32[]{:S(2)}, u32[]{:S(2)}) collective-permute-start(bf16[2,160,640]{2,1,0:T(8,128)(2,1)} %collective-permute-done.6.refs_2_), channel_id=1, source_target_pairs={{0,8},{1,25},{2,10},{3,27},{4,12},{5,29},{6,14},{7,31},{8,16},{9,1... | collective-permute-start | bytes 1228808 | tf_op jit(solution)/shard_map/ppermute | solution.py:41
  68.0 11.0 %collective-permute-start.9 = (bf16[2,160,640]{2,1,0:T(8,128)(2,1)}, bf16[2,160,640]{2,1,0:T(8,128)(2,1)}, u32[]{:S(2)}, u32[]{:S(2)}) collective-permute-start(bf16[2,160,640]{2,1,0:T(8,128)(2,1)} %collective-permute-done.8.refs_4_), channel_id=1, source_target_pairs={{0,8},{1,25},{2,10},{3,27},{4,12},{5,29},{6,14},{7,31},{8,16},{9,1... | collective-permute-start | bytes 1228808 | tf_op jit(solution)/shard_map/ppermute | solution.py:41
  79.0 1.0 copy-start.3
  80.0 1.0 copy-start.5

commit v15 on v12

--- a/solution.py
+++ b/solution.py
@@ -57,10 +57,7 @@
     return jnp.dot(a, b, preferred_element_type=jnp.float32)
 
 
-def prepare_kernel(sizes, prop, operator, masked, upward, *refs):
-    *turned, staged = refs
-    n = len(turned)
-    rows = turned[0].shape[0]
+def raise_kernel(sizes, prop, operator, masked, upward):
     inner = prop[...].astype(jnp.float32)
     inner = jnp.where(live(inner.shape, sizes[0]), inner, 0.0).astype(jnp.bfloat16)
     masked[...] = inner
@@ -69,28 +66,51 @@
     upward[...] = lax.dot_general(raised, r, NT, preferred_element_type=jnp.float32).astype(
         jnp.bfloat16
     )
-    staged[...] = inner.T
+
+
+def raise_terms(sizes, prop, operator):
+    states = prop.shape[0]
+    square = jax.ShapeDtypeStruct((states, states), jnp.bfloat16)
+    return pl.pallas_call(
+        raise_kernel,
+        out_shape=(square,) * 2,
+        in_specs=[SMEM, VMEM, VMEM],
+        out_specs=(VMEM,) * 2,
+        cost_estimate=pl.CostEstimate(
+            flops=4 * states**3, bytes_accessed=8 * states**2, transcendentals=0
+        ),
+        name="raise_terms",
+    )(sizes, prop, operator)
+
+
+def turn_kernel(masked, *refs):
+    *turned, staged, copied, sem = refs
+    move = pltpu.make_async_copy(masked, copied, sem.at[0])
+    move.start()
+    move.wait()
+    n = len(turned)
+    rows = turned[0].shape[0]
+    staged[...] = copied[...].T
     here_y = lax.axis_index("ty")
     for d in range(n):
         first = pl.multiple_of(lax.rem(here_y + d, n) * rows, 32)
         turned[d][...] = staged[pl.ds(first, rows), :]
 
 
-def prepare(sizes, prop, operator, n):
-    states = prop.shape[0]
-    square = jax.ShapeDtypeStruct((states, states), jnp.bfloat16)
+def turn_blocks(masked, n):
+    states = masked.shape[0]
     block = jax.ShapeDtypeStruct((states // n, states), jnp.bfloat16)
     return pl.pallas_call(
-        prepare_kernel,
-        out_shape=(square,) * 2 + (block,) * n,
-        in_specs=[SMEM, VMEM, VMEM],
-        out_specs=(VMEM,) * (2 + n),
-        scratch_shapes=[pltpu.VMEM((states, states), jnp.bfloat16)],
-        cost_estimate=pl.CostEstimate(
-            flops=4 * states**3, bytes_accessed=12 * states**2, transcendentals=0
-        ),
-        name="prepare",
-    )(sizes, prop, operator)
+        turn_kernel,
+        out_shape=(block,) * n,
+        in_specs=[ANY],
+        out_specs=(VMEM,) * n,
+        scratch_shapes=[pltpu.VMEM((states, states), jnp.bfloat16)] * 2
+        + [pltpu.SemaphoreType.DMA((1,))],
+        cost_estimate=pl.CostEstimate(flops=0, bytes_accessed=4 * states**2, transcendentals=0),
+        compiler_params=pltpu.CompilerParams(vmem_limit_bytes=16 * MIB),
+        name="turn_blocks",
+    )(masked)
 
 
 def energy_kernel(sizes, particle, hole, *refs):
@@ -255,11 +275,10 @@
     here_x = lax.axis_index("tx")
     operator = rising_op[0]
 
-    masked, upward, own_g, *away_g = prepare(
-        sector_sizes, propagator[0, 0], operator, n
-    )
+    masked, upward = raise_terms(sector_sizes, propagator[0, 0], operator)
     below = shifted(upward, "sector", 1)
     above = shifted(masked, "sector", -1)
+    own_g, *away_g = turn_blocks(masked, n)
     crossed_g = {d: ring(away_g[d - 1], "ty", d) for d in (2, 1, 3)}
     columns = jnp.stack([own_g] + [crossed_g[d] for d in range(1, n)])
 

time: 103 us -> 105 us (1.019)
  waiting for transfers between devices: 41.6 us -> 30.9 us
  blocking collectives: 16.2 us -> 23.1 us
  starting transfers between devices: 22.3 us -> 27 us
  local copies, waits for them, and re-layouts: 0.2 us -> 1.34 us
    all_to_all x1, blocking collectives: 16.2 us -> 23.1 us  [per_device(): packets = lax.all_to_all(packets, ('tx', 'ty'), 0, 0, tiled=True)]
    ppermute x6, waiting for transfers between devices: 29.3 us -> 22.7 us  [turned_ring(): return lax.ppermute(block, (axis, 'sector'), route)]
    ppermute x6, starting transfers between devices: 6.33 us -> 9.86 us  [turned_ring(): return lax.ppermute(block, (axis, 'sector'), route)]
    ppermute x2, waiting for transfers between devices: 4.25 us -> 1.33 us  [shifted(): return lax.ppermute(block, axis, route)]
    ppermute x2, starting transfers between devices: 4.31 us -> 5.55 us  [shifted(): return lax.ppermute(block, axis, route)]
    ppermute x6, waiting for transfers between devices: 8.02 us -> 6.86 us  [ring(): lax.ppermute(block, axis, [(i, (i + distance) % n) for i in range(n)])]
    unnamed x6, local copies, waits for them, and re-layouts: 0.01 us -> 1.16 us
    pallas_call x1 -> x2, Pallas kernels: 4.48 us -> 4.5 us  [the longest x1 4.04 us: raise_terms(): pl.pallas_call(raise_kernel, out_shape=(square,) * 2, in_specs=[SMEM, VME...]
  transfers between devices with their start and end apart: 14 -> 14, of which waited for: 9 -> 9; matrix products, arithmetic and copies ran while one was open for 0% -> 0% of each run, Pallas kernels for 2% -> 3%
where the time goes in v15:
time: 105 us
  waiting for transfers between devices  30.9 us (29%)
  starting transfers between devices  27 us (26%)
  blocking collectives  23.1 us (22%)
  Pallas kernels  19.9 us (19%)
  between operations  2.06 us (2%)
  local copies, waits for them, and re-layouts  1.34 us (1%)
    all_to_all x1, blocking collectives, per_device(): packets = lax.all_to_all(packets, ('tx', 'ty'), 0, 0, tiled=True)  23.1 us
    ppermute x6, waiting for transfers between devices, turned_ring(): return lax.ppermute(block, (axis, 'sector'), route)  22.7 us
    ppermute x6, starting transfers between devices, ring(): lax.ppermute(block, axis, [(i, (i + distance) % n) for i in range(n)])  11.6 us
    pallas_call x1, Pallas kernels, convolve(): pl.pallas_call(functools.partial(convolve_kernel, plan, n, step_size), ou...  10.6 us
    ppermute x6, starting transfers between devices, turned_ring(): return lax.ppermute(block, (axis, 'sector'), route)  9.86 us
    ppermute x6, waiting for transfers between devices, ring(): lax.ppermute(block, axis, [(i, (i + distance) % n) for i in range(n)])  6.86 us
    ppermute x2, starting transfers between devices, shifted(): return lax.ppermute(block, axis, route)  5.55 us
    pallas_call x1, Pallas kernels, raise_terms(): pl.pallas_call(raise_kernel, out_shape=(square,) * 2, in_specs=[SMEM, VME...  4.04 us
  transfers between devices with their start and end apart: 14, of which 9 were waited for; matrix products, arithmetic and copies ran while one was open for 0% of the time, Pallas kernels for 3%

profile of v15, /device:TPU:32, one launch (start us, length us, event | category | flops | bytes accessed | tf_op | source)
XLA Modules:
  0.0 104.6 jit_solution(11878581083198392422)
XLA Ops:
  0.0 0.0 copy-start
  0.7 0.0 copy-start.2
  0.7 4.0 %raise_terms.1 = (bf16[640,640]{1,0:T(8,128)(2,1)}, bf16[640,640]{1,0:T(8,128)(2,1)}) custom-call(s32[1]{0:T(128)S(6)} %copy.10.sizes, bf16[640,640]{1,0:T(8,128)(2,1)} %bitcast.23, bf16[640,640]{1,0:T(8,128)(2,1)} %bitcast.15), custom_call_target="tpu_custom_call" | custom-call | flops 1048576000 | bytes 3276800 | tf_op jit(solution)/shard_map/raise_terms/pallas_call | solution.py:74
  4.7 1.9 %collective-permute-start.1 = (bf16[640,640]{1,0:T(8,128)(2,1)}, bf16[640,640]{1,0:T(8,128)(2,1)S(1)}, u32[]{:S(2)}, u32[]{:S(2)}) collective-permute-start(bf16[640,640]{1,0:T(8,128)(2,1)} %get-tuple-element.16), channel_id=1, source_target_pairs={{0,1},{1,2},{2,3},{3,4},{4,5},{5,6},{6,7},{8,9},{9,10},{10,11},{11... | collective-permute-start | bytes 2457608 | tf_op jit(solution)/shard_map/ppermute | solution.py:22
  6.6 3.6 %collective-permute-start = (bf16[640,640]{1,0:T(8,128)(2,1)}, bf16[640,640]{1,0:T(8,128)(2,1)S(1)}, u32[]{:S(2)}, u32[]{:S(2)}) collective-permute-start(bf16[640,640]{1,0:T(8,128)(2,1)} %get-tuple-element.15.masked), channel_id=1, source_target_pairs={{1,0},{2,1},{3,2},{4,3},{5,4},{6,5},{7,6},{9,8},{10,9},{11,10},{12... | collective-permute-start | bytes 2457608 | tf_op jit(solution)/shard_map/ppermute | solution.py:22
  10.3 0.0 copy-start.1
  10.3 1.1 %copy-done.1 = bf16[640,640]{1,0:T(8,128)(2,1)S(1)} copy-done((bf16[640,640]{1,0:T(8,128)(2,1)S(1)}, bf16[640,640]{1,0:T(8,128)(2,1)}, u32[]{:S(2)}) %copy-start.1) | copy-done | bytes 819224
  11.4 0.5 turn_blocks.1
  11.9 1.6 %collective-permute-start.8 = (bf16[160,640]{1,0:T(8,128)(2,1)S(1)}, bf16[160,640]{1,0:T(8,128)(2,1)S(1)}, u32[]{:S(2)}, u32[]{:S(2)}) collective-permute-start(bf16[160,640]{1,0:T(8,128)(2,1)S(1)} %get-tuple-element.22), channel_id=1, source_target_pairs={{0,8},{8,16},{16,24},{24,0},{1,9},{9,17},{17,25},{25,1},{2,10},{10... | collective-permute-start | bytes 614408 | tf_op jit(solution)/shard_map/ppermute | solution.py:27
  13.6 2.9 %collective-permute-start.9 = (bf16[160,640]{1,0:T(8,128)(2,1)S(1)}, bf16[160,640]{1,0:T(8,128)(2,1)S(1)}, u32[]{:S(2)}, u32[]{:S(2)}) collective-permute-start(bf16[160,640]{1,0:T(8,128)(2,1)S(1)} %get-tuple-element.23), channel_id=1, source_target_pairs={{0,16},{8,24},{16,0},{24,8},{1,17},{9,25},{17,1},{25,9},{2,18},{10... | collective-permute-start | bytes 614408 | tf_op jit(solution)/shard_map/ppermute | solution.py:27
  16.5 1.3 %collective-permute-start.10 = (bf16[160,640]{1,0:T(8,128)(2,1)S(1)}, bf16[160,640]{1,0:T(8,128)(2,1)S(1)}, u32[]{:S(2)}, u32[]{:S(2)}) collective-permute-start(bf16[160,640]{1,0:T(8,128)(2,1)S(1)} %get-tuple-element.24), channel_id=1, source_target_pairs={{0,24},{8,0},{16,8},{24,16},{1,25},{9,1},{17,9},{25,17},{2,26},{10... | collective-permute-start | bytes 614408 | tf_op jit(solution)/shard_map/ppermute | solution.py:27
  19.1 0.0 collective-permute-done.1.refs_2_
  19.1 1.3 %collective-permute-done.refs_0_ = bf16[640,640]{1,0:T(8,128)(2,1)S(1)} collective-permute-done((bf16[640,640]{1,0:T(8,128)(2,1)}, bf16[640,640]{1,0:T(8,128)(2,1)S(1)}, u32[]{:S(2)}, u32[]{:S(2)}) %collective-permute-start) | collective-permute-done | bytes 819232 | tf_op jit(solution)/shard_map/ppermute | solution.py:22
  20.4 0.0 copy-done.2
  20.4 2.3 %energy_blocks.1 = (bf16[160,640]{1,0:T(8,128)(2,1)S(1)}, bf16[160,640]{1,0:T(8,128)(2,1)S(1)}, bf16[160,640]{1,0:T(8,128)(2,1)S(1)}, bf16[160,640]{1,0:T(8,128)(2,1)S(1)}) custom-call(s32[1]{0:T(128)S(6)} %copy.10.sizes, f32[1]{0:T(128)S(6)} %copy.8.particle, f32[1]{0:T(128)S(6)} %copy.9.hole, bf16[640,640]{1,0:T(8,128)(2,1)S(1)} %collective-permute-done.refs_0_, ...), custom_call_target="tpu_custom_call" | custom-call | flops 1048576000 | bytes 3276800 | tf_op jit(solution)/shard_map/energy_blocks/pallas_call | solution.py:146
  22.8 1.6 %collective-permute-start.2 = (bf16[160,640]{1,0:T(8,128)(2,1)S(1)}, bf16[160,640]{1,0:T(8,128)(2,1)S(1)}, u32[]{:S(2)}, u32[]{:S(2)}) collective-permute-start(bf16[160,640]{1,0:T(8,128)(2,1)S(1)} %get-tuple-element.18), channel_id=1, source_target_pairs={{0,32},{32,64},{64,96},{96,0},{1,33},{33,65},{65,97},{97,1},{2,34}... | collective-permute-start | bytes 614408 | tf_op jit(solution)/shard_map/ppermute | solution.py:27
  24.3 2.7 %collective-permute-start.3 = (bf16[160,640]{1,0:T(8,128)(2,1)S(1)}, bf16[160,640]{1,0:T(8,128)(2,1)S(1)}, u32[]{:S(2)}, u32[]{:S(2)}) collective-permute-start(bf16[160,640]{1,0:T(8,128)(2,1)S(1)} %get-tuple-element.19), channel_id=1, source_target_pairs={{0,64},{32,96},{64,0},{96,32},{1,65},{33,97},{65,1},{97,33},{2,66}... | collective-permute-start | bytes 614408 | tf_op jit(solution)/shard_map/ppermute | solution.py:27
  27.1 0.0 collective-permute-done.8
  27.1 1.4 %collective-permute-start.4 = (bf16[160,640]{1,0:T(8,128)(2,1)S(1)}, bf16[160,640]{1,0:T(8,128)(2,1)S(1)}, u32[]{:S(2)}, u32[]{:S(2)}) collective-permute-start(bf16[160,640]{1,0:T(8,128)(2,1)S(1)} %get-tuple-element.20), channel_id=1, source_target_pairs={{0,96},{32,0},{64,32},{96,64},{1,97},{33,1},{65,33},{97,65},{2,98}... | collective-permute-start | bytes 614408 | tf_op jit(solution)/shard_map/ppermute | solution.py:27
  28.5 0.0 collective-permute-done.9
  28.5 0.0 collective-permute-done.10
  28.5 0.1 pad_maximum_fusion.1.refs_4_
  28.6 0.7 collective-permute-start.11
  29.3 1.2 %collective-permute-done.2 = bf16[160,640]{1,0:T(8,128)(2,1)S(1)} collective-permute-done((bf16[160,640]{1,0:T(8,128)(2,1)S(1)}, bf16[160,640]{1,0:T(8,128)(2,1)S(1)}, u32[]{:S(2)}, u32[]{:S(2)}) %collective-permute-start.2) | collective-permute-done | bytes 204832 | tf_op jit(solution)/shard_map/ppermute | solution.py:27
  30.5 5.5 %collective-permute-done.3 = bf16[160,640]{1,0:T(8,128)(2,1)S(1)} collective-permute-done((bf16[160,640]{1,0:T(8,128)(2,1)S(1)}, bf16[160,640]{1,0:T(8,128)(2,1)S(1)}, u32[]{:S(2)}, u32[]{:S(2)}) %collective-permute-start.3) | collective-permute-done | bytes 204832 | tf_op jit(solution)/shard_map/ppermute | solution.py:27
  36.0 0.1 collective-permute-done.4
  36.2 0.1 pad_maximum_fusion.refs_0_
  36.3 1.6 %collective-permute-start.5 = (bf16[4,160,640]{2,1,0:T(8,128)(2,1)S(1)}, bf16[4,160,640]{2,1,0:T(8,128)(2,1)S(1)}, u32[]{:S(2)}, u32[]{:S(2)}) collective-permute-start(bf16[4,160,640]{2,1,0:T(8,128)(2,1)S(1)} %pad_maximum_fusion.refs_0_), channel_id=1, source_target_pairs={{0,8},{1,25},{2,10},{3,27},{4,12},{5,29},{6,14},{7,31},{8,16},{9,1... | collective-permute-start | bytes 2457608 | tf_op jit(solution)/shard_map/ppermute | solution.py:41
  37.9 3.7 %collective-permute-start.12 = (bf16[4,160,640]{2,1,0:T(8,128)(2,1)S(1)}, bf16[4,160,640]{2,1,0:T(8,128)(2,1)}, u32[]{:S(2)}, u32[]{:S(2)}) collective-permute-start(bf16[4,160,640]{2,1,0:T(8,128)(2,1)S(1)} %pad_maximum_fusion.1.refs_4_), channel_id=1, source_target_pairs={{0,96},{1,33},{2,98},{3,35},{4,100},{5,37},{6,102},{7,39},{32,0},{... | collective-permute-start | bytes 2457608 | tf_op jit(solution)/shard_map/ppermute | solution.py:41
  41.6 1.7 %collective-permute-start.6 = (bf16[4,160,640]{2,1,0:T(8,128)(2,1)S(1)}, bf16[4,160,640]{2,1,0:T(8,128)(2,1)}, u32[]{:S(2)}, u32[]{:S(2)}) collective-permute-start(bf16[4,160,640]{2,1,0:T(8,128)(2,1)S(1)} %pad_maximum_fusion.refs_0_), channel_id=1, source_target_pairs={{0,24},{1,9},{2,26},{3,11},{4,28},{5,13},{6,30},{7,15},{8,0},{9,17... | collective-permute-start | bytes 2457608 | tf_op jit(solution)/shard_map/ppermute | solution.py:41
  43.3 2.5 %collective-permute-done.11.refs_5_ = bf16[4,160,640]{2,1,0:T(8,128)(2,1)S(1)} collective-permute-done((bf16[4,160,640]{2,1,0:T(8,128)(2,1)S(1)}, bf16[4,160,640]{2,1,0:T(8,128)(2,1)S(1)}, u32[]{:S(2)}, u32[]{:S(2)}) %collective-permute-start.11) | collective-permute-done | bytes 819232 | tf_op jit(solution)/shard_map/ppermute | solution.py:41
  45.8 0.2 collective-permute-start.13
  46.0 7.9 %collective-permute-done.5.refs_1_ = bf16[4,160,640]{2,1,0:T(8,128)(2,1)S(1)} collective-permute-done((bf16[4,160,640]{2,1,0:T(8,128)(2,1)S(1)}, bf16[4,160,640]{2,1,0:T(8,128)(2,1)S(1)}, u32[]{:S(2)}, u32[]{:S(2)}) %collective-permute-start.5) | collective-permute-done | bytes 819232 | tf_op jit(solution)/shard_map/ppermute | solution.py:41
  53.9 2.0 %collective-permute-start.7 = (bf16[4,160,640]{2,1,0:T(8,128)(2,1)S(1)}, bf16[4,160,640]{2,1,0:T(8,128)(2,1)}, u32[]{:S(2)}, u32[]{:S(2)}) collective-permute-start(bf16[4,160,640]{2,1,0:T(8,128)(2,1)S(1)} %collective-permute-done.5.refs_1_), channel_id=1, source_target_pairs={{0,8},{1,25},{2,10},{3,27},{4,12},{5,29},{6,14},{7,31},{8,16},{9,1... | collective-permute-start | bytes 2457608 | tf_op jit(solution)/shard_map/ppermute | solution.py:41
  55.9 0.0 copy-done
  55.9 0.1 dynamic-slice_bitcast_fusion
  56.0 0.1 copy.7.rates
  56.1 0.6 collective-permute-done.12.refs_6_
  56.7 6.6 %collective-permute-done.13.refs_7_ = bf16[4,160,640]{2,1,0:T(8,128)(2,1)} collective-permute-done((bf16[4,160,640]{2,1,0:T(8,128)(2,1)S(1)}, bf16[4,160,640]{2,1,0:T(8,128)(2,1)}, u32[]{:S(2)}, u32[]{:S(2)}) %collective-permute-start.13) | collective-permute-done | bytes 819232 | tf_op jit(solution)/shard_map/ppermute | solution.py:41
  63.3 0.0 collective-permute-done.6.refs_2_
  63.3 5.0 %collective-permute-done.7.refs_3_ = bf16[4,160,640]{2,1,0:T(8,128)(2,1)} collective-permute-done((bf16[4,160,640]{2,1,0:T(8,128)(2,1)S(1)}, bf16[4,160,640]{2,1,0:T(8,128)(2,1)}, u32[]{:S(2)}, u32[]{:S(2)}) %collective-permute-start.7) | collective-permute-done | bytes 819232 | tf_op jit(solution)/shard_map/ppermute | solution.py:41
  68.4 10.6 %convolve.1 = bf16[16,40,640]{2,1,0:T(8,128)(2,1)S(1)} custom-call(s32[1]{0:T(128)S(6)} %copy.10.sizes, f32[160,1]{1,0:T(8,128)S(1)} %copy.7.rates, bf16[4,160,640]{2,1,0:T(8,128)(2,1)S(1)} %pad_maximum_fusion.refs_0_, bf16[4,160,640]{2,1,0:T(8,128)(2,1)S(1)} %collective-permute-done.5.refs_1_, bf16[4,160,640]{2,1,0:T(8,128)(2,1)} %collective-permute-done.6.refs_2_, ...), custom_call_target="tpu_custom_call" | custom-call | flops 4456448000 | bytes 6553600 | tf_op jit(solution)/shard_map/convolve/pallas_call | solution.py:228
  79.0 23.1 %all_to_all.5.packets = bf16[16,40,640]{2,1,0:T(8,128)(2,1)} all-to-all(bf16[16,40,640]{2,1,0:T(8,128)(2,1)S(1)} %convolve.1), channel_id=1, replica_groups=mesh['tx'=4,'ty'=4,'sector'=8] {'tx','ty'}, dimensions={0} | all-to-all | bytes 1638400 | tf_op jit(solution)/shard_map/all_to_all | solution.py:295
  102.2 2.4 %assemble.1 = bf16[640,640]{1,0:T(8,128)(2,1)} custom-call(bf16[16,40,640]{2,1,0:T(8,128)(2,1)} %all_to_all.5.packets), custom_call_target="tpu_custom_call" | custom-call | tf_op jit(solution)/shard_map/assemble/pallas_call | solution.py:261
Async XLA Ops:
  0.0 55.9 %copy-start = (f32[1,640]{1,0:T(1,128)S(1)}, f32[1,640]{1,0:T(1,128)}, u32[]{:S(2)}) copy-start(f32[1,640]{1,0:T(1,128)} %param.8) | copy-start | bytes 7684
  0.7 19.8 %copy-start.2 = (bf16[1,640,640]{2,1,0:T(8,128)(2,1)S(1)}, bf16[1,640,640]{2,1,0:T(8,128)(2,1)}, u32[]{:S(2)}) copy-start(bf16[1,640,640]{2,1,0:T(8,128)(2,1)} %param.7) | copy-start | bytes 2457604
  4.7 14.4 %collective-permute-start.1 = (bf16[640,640]{1,0:T(8,128)(2,1)}, bf16[640,640]{1,0:T(8,128)(2,1)S(1)}, u32[]{:S(2)}, u32[]{:S(2)}) collective-permute-start(bf16[640,640]{1,0:T(8,128)(2,1)} %get-tuple-element.16), channel_id=1, source_target_pairs={{0,1},{1,2},{2,3},{3,4},{4,5},{5,6},{6,7},{8,9},{9,10},{10,11},{11... | collective-permute-start | bytes 2457608 | tf_op jit(solution)/shard_map/ppermute | solution.py:22
  6.6 13.8 %collective-permute-start = (bf16[640,640]{1,0:T(8,128)(2,1)}, bf16[640,640]{1,0:T(8,128)(2,1)S(1)}, u32[]{:S(2)}, u32[]{:S(2)}) collective-permute-start(bf16[640,640]{1,0:T(8,128)(2,1)} %get-tuple-element.15.masked), channel_id=1, source_target_pairs={{1,0},{2,1},{3,2},{4,3},{5,4},{6,5},{7,6},{9,8},{10,9},{11,10},{12... | collective-permute-start | bytes 2457608 | tf_op jit(solution)/shard_map/ppermute | solution.py:22
  10.3 1.2 %copy-start.1 = (bf16[640,640]{1,0:T(8,128)(2,1)S(1)}, bf16[640,640]{1,0:T(8,128)(2,1)}, u32[]{:S(2)}) copy-start(bf16[640,640]{1,0:T(8,128)(2,1)} %get-tuple-element.15.masked) | copy-start | bytes 2457604
  11.9 15.2 %collective-permute-start.8 = (bf16[160,640]{1,0:T(8,128)(2,1)S(1)}, bf16[160,640]{1,0:T(8,128)(2,1)S(1)}, u32[]{:S(2)}, u32[]{:S(2)}) collective-permute-start(bf16[160,640]{1,0:T(8,128)(2,1)S(1)} %get-tuple-element.22), channel_id=1, source_target_pairs={{0,8},{8,16},{16,24},{24,0},{1,9},{9,17},{17,25},{25,1},{2,10},{10... | collective-permute-start | bytes 614408 | tf_op jit(solution)/shard_map/ppermute | solution.py:27
  13.6 15.0 %collective-permute-start.9 = (bf16[160,640]{1,0:T(8,128)(2,1)S(1)}, bf16[160,640]{1,0:T(8,128)(2,1)S(1)}, u32[]{:S(2)}, u32[]{:S(2)}) collective-permute-start(bf16[160,640]{1,0:T(8,128)(2,1)S(1)} %get-tuple-element.23), channel_id=1, source_target_pairs={{0,16},{8,24},{16,0},{24,8},{1,17},{9,25},{17,1},{25,9},{2,18},{10... | collective-permute-start | bytes 614408 | tf_op jit(solution)/shard_map/ppermute | solution.py:27
  16.5 12.1 %collective-permute-start.10 = (bf16[160,640]{1,0:T(8,128)(2,1)S(1)}, bf16[160,640]{1,0:T(8,128)(2,1)S(1)}, u32[]{:S(2)}, u32[]{:S(2)}) collective-permute-start(bf16[160,640]{1,0:T(8,128)(2,1)S(1)} %get-tuple-element.24), channel_id=1, source_target_pairs={{0,24},{8,0},{16,8},{24,16},{1,25},{9,1},{17,9},{25,17},{2,26},{10... | collective-permute-start | bytes 614408 | tf_op jit(solution)/shard_map/ppermute | solution.py:27
  22.8 7.8 %collective-permute-start.2 = (bf16[160,640]{1,0:T(8,128)(2,1)S(1)}, bf16[160,640]{1,0:T(8,128)(2,1)S(1)}, u32[]{:S(2)}, u32[]{:S(2)}) collective-permute-start(bf16[160,640]{1,0:T(8,128)(2,1)S(1)} %get-tuple-element.18), channel_id=1, source_target_pairs={{0,32},{32,64},{64,96},{96,0},{1,33},{33,65},{65,97},{97,1},{2,34}... | collective-permute-start | bytes 614408 | tf_op jit(solution)/shard_map/ppermute | solution.py:27
  24.3 11.7 %collective-permute-start.3 = (bf16[160,640]{1,0:T(8,128)(2,1)S(1)}, bf16[160,640]{1,0:T(8,128)(2,1)S(1)}, u32[]{:S(2)}, u32[]{:S(2)}) collective-permute-start(bf16[160,640]{1,0:T(8,128)(2,1)S(1)} %get-tuple-element.19), channel_id=1, source_target_pairs={{0,64},{32,96},{64,0},{96,32},{1,65},{33,97},{65,1},{97,33},{2,66}... | collective-permute-start | bytes 614408 | tf_op jit(solution)/shard_map/ppermute | solution.py:27
  27.1 9.1 %collective-permute-start.4 = (bf16[160,640]{1,0:T(8,128)(2,1)S(1)}, bf16[160,640]{1,0:T(8,128)(2,1)S(1)}, u32[]{:S(2)}, u32[]{:S(2)}) collective-permute-start(bf16[160,640]{1,0:T(8,128)(2,1)S(1)} %get-tuple-element.20), channel_id=1, source_target_pairs={{0,96},{32,0},{64,32},{96,64},{1,97},{33,1},{65,33},{97,65},{2,98}... | collective-permute-start | bytes 614408 | tf_op jit(solution)/shard_map/ppermute | solution.py:27
  28.6 17.2 %collective-permute-start.11 = (bf16[4,160,640]{2,1,0:T(8,128)(2,1)S(1)}, bf16[4,160,640]{2,1,0:T(8,128)(2,1)S(1)}, u32[]{:S(2)}, u32[]{:S(2)}) collective-permute-start(bf16[4,160,640]{2,1,0:T(8,128)(2,1)S(1)} %pad_maximum_fusion.1.refs_4_), channel_id=1, source_target_pairs={{0,32},{1,97},{2,34},{3,99},{4,36},{5,101},{6,38},{7,103},{32,64},... | collective-permute-start | bytes 2457608 | tf_op jit(solution)/shard_map/ppermute | solution.py:41
  36.3 17.6 %collective-permute-start.5 = (bf16[4,160,640]{2,1,0:T(8,128)(2,1)S(1)}, bf16[4,160,640]{2,1,0:T(8,128)(2,1)S(1)}, u32[]{:S(2)}, u32[]{:S(2)}) collective-permute-start(bf16[4,160,640]{2,1,0:T(8,128)(2,1)S(1)} %pad_maximum_fusion.refs_0_), channel_id=1, source_target_pairs={{0,8},{1,25},{2,10},{3,27},{4,12},{5,29},{6,14},{7,31},{8,16},{9,1... | collective-permute-start | bytes 2457608 | tf_op jit(solution)/shard_map/ppermute | solution.py:41
  37.9 18.8 %collective-permute-start.12 = (bf16[4,160,640]{2,1,0:T(8,128)(2,1)S(1)}, bf16[4,160,640]{2,1,0:T(8,128)(2,1)}, u32[]{:S(2)}, u32[]{:S(2)}) collective-permute-start(bf16[4,160,640]{2,1,0:T(8,128)(2,1)S(1)} %pad_maximum_fusion.1.refs_4_), channel_id=1, source_target_pairs={{0,96},{1,33},{2,98},{3,35},{4,100},{5,37},{6,102},{7,39},{32,0},{... | collective-permute-start | bytes 2457608 | tf_op jit(solution)/shard_map/ppermute | solution.py:41
  41.6 21.7 %collective-permute-start.6 = (bf16[4,160,640]{2,1,0:T(8,128)(2,1)S(1)}, bf16[4,160,640]{2,1,0:T(8,128)(2,1)}, u32[]{:S(2)}, u32[]{:S(2)}) collective-permute-start(bf16[4,160,640]{2,1,0:T(8,128)(2,1)S(1)} %pad_maximum_fusion.refs_0_), channel_id=1, source_target_pairs={{0,24},{1,9},{2,26},{3,11},{4,28},{5,13},{6,30},{7,15},{8,0},{9,17... | collective-permute-start | bytes 2457608 | tf_op jit(solution)/shard_map/ppermute | solution.py:41
  45.8 17.5 %collective-permute-start.13 = (bf16[4,160,640]{2,1,0:T(8,128)(2,1)S(1)}, bf16[4,160,640]{2,1,0:T(8,128)(2,1)}, u32[]{:S(2)}, u32[]{:S(2)}) collective-permute-start(bf16[4,160,640]{2,1,0:T(8,128)(2,1)S(1)} %collective-permute-done.11.refs_5_), channel_id=1, source_target_pairs={{0,32},{1,97},{2,34},{3,99},{4,36},{5,101},{6,38},{7,103},{32,64},... | collective-permute-start | bytes 2457608 | tf_op jit(solution)/shard_map/ppermute | solution.py:41
  53.9 14.5 %collective-permute-start.7 = (bf16[4,160,640]{2,1,0:T(8,128)(2,1)S(1)}, bf16[4,160,640]{2,1,0:T(8,128)(2,1)}, u32[]{:S(2)}, u32[]{:S(2)}) collective-permute-start(bf16[4,160,640]{2,1,0:T(8,128)(2,1)S(1)} %collective-permute-done.5.refs_1_), channel_id=1, source_target_pairs={{0,8},{1,25},{2,10},{3,27},{4,12},{5,29},{6,14},{7,31},{8,16},{9,1... | collective-permute-start | bytes 2457608 | tf_op jit(solution)/shard_map/ppermute | solution.py:41

commit v16 on v12

--- a/solution.py
+++ b/solution.py
@@ -226,7 +226,10 @@
     )(sizes, rates, *parts)
 
 
-def assemble_kernel(n, packets, out):
+def assemble_kernel(n, arrived, out, packets, sem):
+    move = pltpu.make_async_copy(arrived, packets, sem.at[0])
+    move.start()
+    move.wait()
     quarter, states = packets.shape[1:]
     rows = states // n
     for x in range(n):
@@ -241,8 +244,13 @@
     return pl.pallas_call(
         functools.partial(assemble_kernel, n),
         out_shape=jax.ShapeDtypeStruct((states, states), jnp.bfloat16),
-        in_specs=[VMEM],
+        in_specs=[ANY],
         out_specs=VMEM,
+        scratch_shapes=[
+            pltpu.VMEM(packets.shape, jnp.bfloat16),
+            pltpu.SemaphoreType.DMA((1,)),
+        ],
+        compiler_params=pltpu.CompilerParams(vmem_limit_bytes=16 * MIB),
         name="assemble",
     )(packets)
 

time: 103 us -> 102 us (level)
  Pallas kernels: 19.9 us -> 18.8 us
    pallas_call x1, Pallas kernels: 2.41 us -> 1.36 us  [assemble(): pl.pallas_call(functools.partial(assemble_kernel, n), out_shape=jax.Shape...]
where the time goes in v16:
time: 102 us; the launch traced here: 101 us
  waiting for transfers between devices  41.6 us (41%)
  starting transfers between devices  22.3 us (22%)
  Pallas kernels  18.8 us (18%)
  blocking collectives  16.1 us (16%)
  between operations  2.22 us (2%)
    ppermute x6, waiting for transfers between devices, turned_ring(): return lax.ppermute(block, (axis, 'sector'), route)  29.3 us
    all_to_all x1, blocking collectives, per_device(): packets = lax.all_to_all(packets, ('tx', 'ty'), 0, 0, tiled=True)  16.1 us
    ppermute x6, starting transfers between devices, ring(): lax.ppermute(block, axis, [(i, (i + distance) % n) for i in range(n)])  11.6 us
    pallas_call x1, Pallas kernels, convolve(): pl.pallas_call(functools.partial(convolve_kernel, plan, n, step_size), ou...  10.6 us
    ppermute x6, waiting for transfers between devices, ring(): lax.ppermute(block, axis, [(i, (i + distance) % n) for i in range(n)])  8.02 us
    ppermute x6, starting transfers between devices, turned_ring(): return lax.ppermute(block, (axis, 'sector'), route)  6.33 us
    pallas_call x1, Pallas kernels, prepare(): pl.pallas_call(prepare_kernel, out_shape=(square,) * 2 + (block,) * n, in...  4.48 us
    ppermute x2, starting transfers between devices, shifted(): return lax.ppermute(block, axis, route)  4.31 us
  transfers between devices with their start and end apart: 14, of which 9 were waited for; matrix products, arithmetic and copies ran while one was open for 0% of the time, Pallas kernels for 2%

profile of v16, /device:TPU:32, one launch (start us, length us, event | category | flops | bytes accessed | tf_op | source)
XLA Modules:
  0.0 101.4 jit_solution(12740797368549301514)
XLA Ops:
  0.0 0.0 copy-start
  0.7 0.0 copy-start.1
  0.7 4.5 %prepare.1 = (bf16[640,640]{1,0:T(8,128)(2,1)}, bf16[640,640]{1,0:T(8,128)(2,1)}, bf16[160,640]{1,0:T(8,128)(2,1)}, bf16[160,640]{1,0:T(8,128)(2,1)}, bf16[160,6...) custom-call(s32[1]{0:T(128)S(6)} %copy.10.sizes, bf16[640,640]{1,0:T(8,128)(2,1)} %bitcast.23, bf16[640,640]{1,0:T(8,128)(2,1)} %bitcast.14), custom_call_target="tpu_custom_call" | custom-call | flops 1048576000 | bytes 4915200 | tf_op jit(solution)/shard_map/prepare/pallas_call | solution.py:83
  5.2 1.9 %collective-permute-start = (bf16[640,640]{1,0:T(8,128)(2,1)}, bf16[640,640]{1,0:T(8,128)(2,1)S(1)}, u32[]{:S(2)}, u32[]{:S(2)}) collective-permute-start(bf16[640,640]{1,0:T(8,128)(2,1)} %get-tuple-element.15), channel_id=1, source_target_pairs={{1,0},{2,1},{3,2},{4,3},{5,4},{6,5},{7,6},{9,8},{10,9},{11,10},{12... | collective-permute-start | bytes 2457608 | tf_op jit(solution)/shard_map/ppermute | solution.py:22
  7.1 2.4 %collective-permute-start.1 = (bf16[640,640]{1,0:T(8,128)(2,1)}, bf16[640,640]{1,0:T(8,128)(2,1)S(1)}, u32[]{:S(2)}, u32[]{:S(2)}) collective-permute-start(bf16[640,640]{1,0:T(8,128)(2,1)} %get-tuple-element.16), channel_id=1, source_target_pairs={{0,1},{1,2},{2,3},{3,4},{4,5},{5,6},{6,7},{8,9},{9,10},{10,11},{11... | collective-permute-start | bytes 2457608 | tf_op jit(solution)/shard_map/ppermute | solution.py:22
  9.5 1.7 %collective-permute-start.8 = (bf16[160,640]{1,0:T(8,128)(2,1)}, bf16[160,640]{1,0:T(8,128)(2,1)S(1)}, u32[]{:S(2)}, u32[]{:S(2)}) collective-permute-start(bf16[160,640]{1,0:T(8,128)(2,1)} %get-tuple-element.22), channel_id=1, source_target_pairs={{0,8},{8,16},{16,24},{24,0},{1,9},{9,17},{17,25},{25,1},{2,10},{10... | collective-permute-start | bytes 614408 | tf_op jit(solution)/shard_map/ppermute | solution.py:27
  11.2 2.9 %collective-permute-start.9 = (bf16[160,640]{1,0:T(8,128)(2,1)}, bf16[160,640]{1,0:T(8,128)(2,1)S(1)}, u32[]{:S(2)}, u32[]{:S(2)}) collective-permute-start(bf16[160,640]{1,0:T(8,128)(2,1)} %get-tuple-element.23), channel_id=1, source_target_pairs={{0,16},{8,24},{16,0},{24,8},{1,17},{9,25},{17,1},{25,9},{2,18},{10... | collective-permute-start | bytes 614408 | tf_op jit(solution)/shard_map/ppermute | solution.py:27
  14.0 1.3 %collective-permute-start.10 = (bf16[160,640]{1,0:T(8,128)(2,1)}, bf16[160,640]{1,0:T(8,128)(2,1)S(1)}, u32[]{:S(2)}, u32[]{:S(2)}) collective-permute-start(bf16[160,640]{1,0:T(8,128)(2,1)} %get-tuple-element.24), channel_id=1, source_target_pairs={{0,24},{8,0},{16,8},{24,16},{1,25},{9,1},{17,9},{25,17},{2,26},{10... | collective-permute-start | bytes 614408 | tf_op jit(solution)/shard_map/ppermute | solution.py:27
  16.7 0.0 copy-start.2
  16.7 0.5 collective-permute-done.refs_0_
  17.2 3.7 %collective-permute-done.1.refs_2_ = bf16[640,640]{1,0:T(8,128)(2,1)S(1)} collective-permute-done((bf16[640,640]{1,0:T(8,128)(2,1)}, bf16[640,640]{1,0:T(8,128)(2,1)S(1)}, u32[]{:S(2)}, u32[]{:S(2)}) %collective-permute-start.1) | collective-permute-done | bytes 819232 | tf_op jit(solution)/shard_map/ppermute | solution.py:22
  20.9 0.0 copy-done.1
  21.0 2.3 %energy_blocks.1 = (bf16[160,640]{1,0:T(8,128)(2,1)S(1)}, bf16[160,640]{1,0:T(8,128)(2,1)S(1)}, bf16[160,640]{1,0:T(8,128)(2,1)S(1)}, bf16[160,640]{1,0:T(8,128)(2,1)S(1)}) custom-call(s32[1]{0:T(128)S(6)} %copy.10.sizes, f32[1]{0:T(128)S(6)} %copy.8.particle, f32[1]{0:T(128)S(6)} %copy.9.hole, bf16[640,640]{1,0:T(8,128)(2,1)S(1)} %collective-permute-done.refs_0_, ...), custom_call_target="tpu_custom_call" | custom-call | flops 1048576000 | bytes 3276800 | tf_op jit(solution)/shard_map/energy_blocks/pallas_call | solution.py:126
  23.3 1.6 %collective-permute-start.2 = (bf16[160,640]{1,0:T(8,128)(2,1)S(1)}, bf16[160,640]{1,0:T(8,128)(2,1)S(1)}, u32[]{:S(2)}, u32[]{:S(2)}) collective-permute-start(bf16[160,640]{1,0:T(8,128)(2,1)S(1)} %get-tuple-element.18), channel_id=1, source_target_pairs={{0,32},{32,64},{64,96},{96,0},{1,33},{33,65},{65,97},{97,1},{2,34}... | collective-permute-start | bytes 614408 | tf_op jit(solution)/shard_map/ppermute | solution.py:27
  24.9 2.7 %collective-permute-start.3 = (bf16[160,640]{1,0:T(8,128)(2,1)S(1)}, bf16[160,640]{1,0:T(8,128)(2,1)S(1)}, u32[]{:S(2)}, u32[]{:S(2)}) collective-permute-start(bf16[160,640]{1,0:T(8,128)(2,1)S(1)} %get-tuple-element.19), channel_id=1, source_target_pairs={{0,64},{32,96},{64,0},{96,32},{1,65},{33,97},{65,1},{97,33},{2,66}... | collective-permute-start | bytes 614408 | tf_op jit(solution)/shard_map/ppermute | solution.py:27
  27.6 0.0 collective-permute-done.8
  27.6 1.4 %collective-permute-start.4 = (bf16[160,640]{1,0:T(8,128)(2,1)S(1)}, bf16[160,640]{1,0:T(8,128)(2,1)S(1)}, u32[]{:S(2)}, u32[]{:S(2)}) collective-permute-start(bf16[160,640]{1,0:T(8,128)(2,1)S(1)} %get-tuple-element.20), channel_id=1, source_target_pairs={{0,96},{32,0},{64,32},{96,64},{1,97},{33,1},{65,33},{97,65},{2,98}... | collective-permute-start | bytes 614408 | tf_op jit(solution)/shard_map/ppermute | solution.py:27
  29.0 0.0 collective-permute-done.9
  29.0 0.0 collective-permute-done.10
  29.0 0.0 copy-done.2
  29.0 0.1 pad_maximum_fusion.1.refs_4_
  29.2 0.7 collective-permute-start.11
  29.8 1.8 %collective-permute-done.2 = bf16[160,640]{1,0:T(8,128)(2,1)S(1)} collective-permute-done((bf16[160,640]{1,0:T(8,128)(2,1)S(1)}, bf16[160,640]{1,0:T(8,128)(2,1)S(1)}, u32[]{:S(2)}, u32[]{:S(2)}) %collective-permute-start.2) | collective-permute-done | bytes 204832 | tf_op jit(solution)/shard_map/ppermute | solution.py:27
  31.6 5.1 %collective-permute-done.3 = bf16[160,640]{1,0:T(8,128)(2,1)S(1)} collective-permute-done((bf16[160,640]{1,0:T(8,128)(2,1)S(1)}, bf16[160,640]{1,0:T(8,128)(2,1)S(1)}, u32[]{:S(2)}, u32[]{:S(2)}) %collective-permute-start.3) | collective-permute-done | bytes 204832 | tf_op jit(solution)/shard_map/ppermute | solution.py:27
  36.7 1.1 %collective-permute-done.4 = bf16[160,640]{1,0:T(8,128)(2,1)S(1)} collective-permute-done((bf16[160,640]{1,0:T(8,128)(2,1)S(1)}, bf16[160,640]{1,0:T(8,128)(2,1)S(1)}, u32[]{:S(2)}, u32[]{:S(2)}) %collective-permute-start.4) | collective-permute-done | bytes 204832 | tf_op jit(solution)/shard_map/ppermute | solution.py:27
  37.8 0.1 pad_maximum_fusion.refs_0_
  38.0 1.7 %collective-permute-start.5 = (bf16[4,160,640]{2,1,0:T(8,128)(2,1)S(1)}, bf16[4,160,640]{2,1,0:T(8,128)(2,1)S(1)}, u32[]{:S(2)}, u32[]{:S(2)}) collective-permute-start(bf16[4,160,640]{2,1,0:T(8,128)(2,1)S(1)} %pad_maximum_fusion.refs_0_), channel_id=1, source_target_pairs={{0,8},{1,25},{2,10},{3,27},{4,12},{5,29},{6,14},{7,31},{8,16},{9,1... | collective-permute-start | bytes 2457608 | tf_op jit(solution)/shard_map/ppermute | solution.py:41
  39.6 1.6 %collective-permute-start.12 = (bf16[4,160,640]{2,1,0:T(8,128)(2,1)S(1)}, bf16[4,160,640]{2,1,0:T(8,128)(2,1)}, u32[]{:S(2)}, u32[]{:S(2)}) collective-permute-start(bf16[4,160,640]{2,1,0:T(8,128)(2,1)S(1)} %pad_maximum_fusion.1.refs_4_), channel_id=1, source_target_pairs={{0,96},{1,33},{2,98},{3,35},{4,100},{5,37},{6,102},{7,39},{32,0},{... | collective-permute-start | bytes 2457608 | tf_op jit(solution)/shard_map/ppermute | solution.py:41
  41.2 1.6 %collective-permute-start.6 = (bf16[4,160,640]{2,1,0:T(8,128)(2,1)S(1)}, bf16[4,160,640]{2,1,0:T(8,128)(2,1)}, u32[]{:S(2)}, u32[]{:S(2)}) collective-permute-start(bf16[4,160,640]{2,1,0:T(8,128)(2,1)S(1)} %pad_maximum_fusion.refs_0_), channel_id=1, source_target_pairs={{0,24},{1,9},{2,26},{3,11},{4,28},{5,13},{6,30},{7,15},{8,0},{9,17... | collective-permute-start | bytes 2457608 | tf_op jit(solution)/shard_map/ppermute | solution.py:41
  42.8 5.6 %collective-permute-done.11.refs_5_ = bf16[4,160,640]{2,1,0:T(8,128)(2,1)S(1)} collective-permute-done((bf16[4,160,640]{2,1,0:T(8,128)(2,1)S(1)}, bf16[4,160,640]{2,1,0:T(8,128)(2,1)S(1)}, u32[]{:S(2)}, u32[]{:S(2)}) %collective-permute-start.11) | collective-permute-done | bytes 819232 | tf_op jit(solution)/shard_map/ppermute | solution.py:41
  48.5 0.0 collective-permute-start.13
  48.5 11.0 %collective-permute-done.5.refs_1_ = bf16[4,160,640]{2,1,0:T(8,128)(2,1)S(1)} collective-permute-done((bf16[4,160,640]{2,1,0:T(8,128)(2,1)S(1)}, bf16[4,160,640]{2,1,0:T(8,128)(2,1)S(1)}, u32[]{:S(2)}, u32[]{:S(2)}) %collective-permute-start.5) | collective-permute-done | bytes 819232 | tf_op jit(solution)/shard_map/ppermute | solution.py:41
  59.5 0.8 collective-permute-start.7
  60.3 0.0 copy-done
  60.3 0.1 dynamic-slice_bitcast_fusion
  60.4 0.1 copy.7.rates
  60.5 0.0 collective-permute-done.12.refs_6_
  60.5 2.5 %collective-permute-done.13.refs_7_ = bf16[4,160,640]{2,1,0:T(8,128)(2,1)} collective-permute-done((bf16[4,160,640]{2,1,0:T(8,128)(2,1)S(1)}, bf16[4,160,640]{2,1,0:T(8,128)(2,1)}, u32[]{:S(2)}, u32[]{:S(2)}) %collective-permute-start.13) | collective-permute-done | bytes 819232 | tf_op jit(solution)/shard_map/ppermute | solution.py:41
  63.0 0.0 collective-permute-done.6.refs_2_
  63.0 10.1 %collective-permute-done.7.refs_3_ = bf16[4,160,640]{2,1,0:T(8,128)(2,1)} collective-permute-done((bf16[4,160,640]{2,1,0:T(8,128)(2,1)S(1)}, bf16[4,160,640]{2,1,0:T(8,128)(2,1)}, u32[]{:S(2)}, u32[]{:S(2)}) %collective-permute-start.7) | collective-permute-done | bytes 819232 | tf_op jit(solution)/shard_map/ppermute | solution.py:41
  73.2 10.6 %convolve.1 = bf16[16,40,640]{2,1,0:T(8,128)(2,1)S(1)} custom-call(s32[1]{0:T(128)S(6)} %copy.10.sizes, f32[160,1]{1,0:T(8,128)S(1)} %copy.7.rates, bf16[4,160,640]{2,1,0:T(8,128)(2,1)S(1)} %pad_maximum_fusion.refs_0_, bf16[4,160,640]{2,1,0:T(8,128)(2,1)S(1)} %collective-permute-done.5.refs_1_, bf16[4,160,640]{2,1,0:T(8,128)(2,1)} %collective-permute-done.6.refs_2_, ...), custom_call_target="tpu_custom_call" | custom-call | flops 4456448000 | bytes 6553600 | tf_op jit(solution)/shard_map/convolve/pallas_call | solution.py:208
  83.8 16.1 %all_to_all.5.arrived = bf16[16,40,640]{2,1,0:T(8,128)(2,1)S(1)} all-to-all(bf16[16,40,640]{2,1,0:T(8,128)(2,1)S(1)} %convolve.1), channel_id=1, replica_groups=mesh['tx'=4,'ty'=4,'sector'=8] {'tx','ty'}, dimensions={0} | all-to-all | bytes 1638400 | tf_op jit(solution)/shard_map/all_to_all | solution.py:284
  99.9 1.4 %assemble.1 = bf16[640,640]{1,0:T(8,128)(2,1)} custom-call(bf16[16,40,640]{2,1,0:T(8,128)(2,1)S(1)} %all_to_all.5.arrived), custom_call_target="tpu_custom_call" | custom-call | tf_op jit(solution)/shard_map/assemble/pallas_call | solution.py:244
Async XLA Ops:
  0.0 60.3 %copy-start = (f32[1,640]{1,0:T(1,128)S(1)}, f32[1,640]{1,0:T(1,128)}, u32[]{:S(2)}) copy-start(f32[1,640]{1,0:T(1,128)} %param.8) | copy-start | bytes 7684
  0.7 20.3 %copy-start.1 = (bf16[1,640,640]{2,1,0:T(8,128)(2,1)S(1)}, bf16[1,640,640]{2,1,0:T(8,128)(2,1)}, u32[]{:S(2)}) copy-start(bf16[1,640,640]{2,1,0:T(8,128)(2,1)} %param.7) | copy-start | bytes 2457604
  5.2 12.1 %collective-permute-start = (bf16[640,640]{1,0:T(8,128)(2,1)}, bf16[640,640]{1,0:T(8,128)(2,1)S(1)}, u32[]{:S(2)}, u32[]{:S(2)}) collective-permute-start(bf16[640,640]{1,0:T(8,128)(2,1)} %get-tuple-element.15), channel_id=1, source_target_pairs={{1,0},{2,1},{3,2},{4,3},{5,4},{6,5},{7,6},{9,8},{10,9},{11,10},{12... | collective-permute-start | bytes 2457608 | tf_op jit(solution)/shard_map/ppermute | solution.py:22
  7.1 13.9 %collective-permute-start.1 = (bf16[640,640]{1,0:T(8,128)(2,1)}, bf16[640,640]{1,0:T(8,128)(2,1)S(1)}, u32[]{:S(2)}, u32[]{:S(2)}) collective-permute-start(bf16[640,640]{1,0:T(8,128)(2,1)} %get-tuple-element.16), channel_id=1, source_target_pairs={{0,1},{1,2},{2,3},{3,4},{4,5},{5,6},{6,7},{8,9},{9,10},{10,11},{11... | collective-permute-start | bytes 2457608 | tf_op jit(solution)/shard_map/ppermute | solution.py:22
  9.5 18.1 %collective-permute-start.8 = (bf16[160,640]{1,0:T(8,128)(2,1)}, bf16[160,640]{1,0:T(8,128)(2,1)S(1)}, u32[]{:S(2)}, u32[]{:S(2)}) collective-permute-start(bf16[160,640]{1,0:T(8,128)(2,1)} %get-tuple-element.22), channel_id=1, source_target_pairs={{0,8},{8,16},{16,24},{24,0},{1,9},{9,17},{17,25},{25,1},{2,10},{10... | collective-permute-start | bytes 614408 | tf_op jit(solution)/shard_map/ppermute | solution.py:27
  11.2 17.9 %collective-permute-start.9 = (bf16[160,640]{1,0:T(8,128)(2,1)}, bf16[160,640]{1,0:T(8,128)(2,1)S(1)}, u32[]{:S(2)}, u32[]{:S(2)}) collective-permute-start(bf16[160,640]{1,0:T(8,128)(2,1)} %get-tuple-element.23), channel_id=1, source_target_pairs={{0,16},{8,24},{16,0},{24,8},{1,17},{9,25},{17,1},{25,9},{2,18},{10... | collective-permute-start | bytes 614408 | tf_op jit(solution)/shard_map/ppermute | solution.py:27
  14.0 15.0 %collective-permute-start.10 = (bf16[160,640]{1,0:T(8,128)(2,1)}, bf16[160,640]{1,0:T(8,128)(2,1)S(1)}, u32[]{:S(2)}, u32[]{:S(2)}) collective-permute-start(bf16[160,640]{1,0:T(8,128)(2,1)} %get-tuple-element.24), channel_id=1, source_target_pairs={{0,24},{8,0},{16,8},{24,16},{1,25},{9,1},{17,9},{25,17},{2,26},{10... | collective-permute-start | bytes 614408 | tf_op jit(solution)/shard_map/ppermute | solution.py:27
  16.7 12.3 %copy-start.2 = (bf16[160,640]{1,0:T(8,128)(2,1)S(1)}, bf16[160,640]{1,0:T(8,128)(2,1)}, u32[]{:S(2)}) copy-start(bf16[160,640]{1,0:T(8,128)(2,1)} %get-tuple-element.21) | copy-start | bytes 614404
  23.3 8.3 %collective-permute-start.2 = (bf16[160,640]{1,0:T(8,128)(2,1)S(1)}, bf16[160,640]{1,0:T(8,128)(2,1)S(1)}, u32[]{:S(2)}, u32[]{:S(2)}) collective-permute-start(bf16[160,640]{1,0:T(8,128)(2,1)S(1)} %get-tuple-element.18), channel_id=1, source_target_pairs={{0,32},{32,64},{64,96},{96,0},{1,33},{33,65},{65,97},{97,1},{2,34}... | collective-permute-start | bytes 614408 | tf_op jit(solution)/shard_map/ppermute | solution.py:27
  24.9 11.8 %collective-permute-start.3 = (bf16[160,640]{1,0:T(8,128)(2,1)S(1)}, bf16[160,640]{1,0:T(8,128)(2,1)S(1)}, u32[]{:S(2)}, u32[]{:S(2)}) collective-permute-start(bf16[160,640]{1,0:T(8,128)(2,1)S(1)} %get-tuple-element.19), channel_id=1, source_target_pairs={{0,64},{32,96},{64,0},{96,32},{1,65},{33,97},{65,1},{97,33},{2,66}... | collective-permute-start | bytes 614408 | tf_op jit(solution)/shard_map/ppermute | solution.py:27
  27.6 10.2 %collective-permute-start.4 = (bf16[160,640]{1,0:T(8,128)(2,1)S(1)}, bf16[160,640]{1,0:T(8,128)(2,1)S(1)}, u32[]{:S(2)}, u32[]{:S(2)}) collective-permute-start(bf16[160,640]{1,0:T(8,128)(2,1)S(1)} %get-tuple-element.20), channel_id=1, source_target_pairs={{0,96},{32,0},{64,32},{96,64},{1,97},{33,1},{65,33},{97,65},{2,98}... | collective-permute-start | bytes 614408 | tf_op jit(solution)/shard_map/ppermute | solution.py:27
  29.2 19.3 %collective-permute-start.11 = (bf16[4,160,640]{2,1,0:T(8,128)(2,1)S(1)}, bf16[4,160,640]{2,1,0:T(8,128)(2,1)S(1)}, u32[]{:S(2)}, u32[]{:S(2)}) collective-permute-start(bf16[4,160,640]{2,1,0:T(8,128)(2,1)S(1)} %pad_maximum_fusion.1.refs_4_), channel_id=1, source_target_pairs={{0,32},{1,97},{2,34},{3,99},{4,36},{5,101},{6,38},{7,103},{32,64},... | collective-permute-start | bytes 2457608 | tf_op jit(solution)/shard_map/ppermute | solution.py:41
  38.0 21.5 %collective-permute-start.5 = (bf16[4,160,640]{2,1,0:T(8,128)(2,1)S(1)}, bf16[4,160,640]{2,1,0:T(8,128)(2,1)S(1)}, u32[]{:S(2)}, u32[]{:S(2)}) collective-permute-start(bf16[4,160,640]{2,1,0:T(8,128)(2,1)S(1)} %pad_maximum_fusion.refs_0_), channel_id=1, source_target_pairs={{0,8},{1,25},{2,10},{3,27},{4,12},{5,29},{6,14},{7,31},{8,16},{9,1... | collective-permute-start | bytes 2457608 | tf_op jit(solution)/shard_map/ppermute | solution.py:41
  39.6 20.9 %collective-permute-start.12 = (bf16[4,160,640]{2,1,0:T(8,128)(2,1)S(1)}, bf16[4,160,640]{2,1,0:T(8,128)(2,1)}, u32[]{:S(2)}, u32[]{:S(2)}) collective-permute-start(bf16[4,160,640]{2,1,0:T(8,128)(2,1)S(1)} %pad_maximum_fusion.1.refs_4_), channel_id=1, source_target_pairs={{0,96},{1,33},{2,98},{3,35},{4,100},{5,37},{6,102},{7,39},{32,0},{... | collective-permute-start | bytes 2457608 | tf_op jit(solution)/shard_map/ppermute | solution.py:41
  41.2 21.8 %collective-permute-start.6 = (bf16[4,160,640]{2,1,0:T(8,128)(2,1)S(1)}, bf16[4,160,640]{2,1,0:T(8,128)(2,1)}, u32[]{:S(2)}, u32[]{:S(2)}) collective-permute-start(bf16[4,160,640]{2,1,0:T(8,128)(2,1)S(1)} %pad_maximum_fusion.refs_0_), channel_id=1, source_target_pairs={{0,24},{1,9},{2,26},{3,11},{4,28},{5,13},{6,30},{7,15},{8,0},{9,17... | collective-permute-start | bytes 2457608 | tf_op jit(solution)/shard_map/ppermute | solution.py:41
  48.5 14.6 %collective-permute-start.13 = (bf16[4,160,640]{2,1,0:T(8,128)(2,1)S(1)}, bf16[4,160,640]{2,1,0:T(8,128)(2,1)}, u32[]{:S(2)}, u32[]{:S(2)}) collective-permute-start(bf16[4,160,640]{2,1,0:T(8,128)(2,1)S(1)} %collective-permute-done.11.refs_5_), channel_id=1, source_target_pairs={{0,32},{1,97},{2,34},{3,99},{4,36},{5,101},{6,38},{7,103},{32,64},... | collective-permute-start | bytes 2457608 | tf_op jit(solution)/shard_map/ppermute | solution.py:41
  59.5 13.7 %collective-permute-start.7 = (bf16[4,160,640]{2,1,0:T(8,128)(2,1)S(1)}, bf16[4,160,640]{2,1,0:T(8,128)(2,1)}, u32[]{:S(2)}, u32[]{:S(2)}) collective-permute-start(bf16[4,160,640]{2,1,0:T(8,128)(2,1)S(1)} %collective-permute-done.5.refs_1_), channel_id=1, source_target_pairs={{0,8},{1,25},{2,10},{3,27},{4,12},{5,29},{6,14},{7,31},{8,16},{9,1... | collective-permute-start | bytes 2457608 | tf_op jit(solution)/shard_map/ppermute | solution.py:41
